TPU v7x, 512 devices: a whole 4x4x16 slice. The times are simulated.
512 devices in a mesh: grp: 16 (over y, x), sp: 32 (over z, core).
Axes of the slice: x: 4, y: 4, z: 16, core: 2. Of those that a mesh axis runs over, the one named last changes fastest.
Arguments:
- coarse: bfloat16 [1024, 48, 1024], P(('grp', 'sp')), parts along dimension 0, may hold values from -30 to 30
- conv_weight: bfloat16 [1024, 3, 3, 1024], P('sp'), may hold values from -0.104166667 to 0.104166667
- conv_bias: float32 [1024], P('sp'), may hold values from -5 to 5
- norm_gain: float32 [1024], P('sp'), may hold values from 0.5 to 1.5
- norm_shift: float32 [1024], P('sp'), may hold values from -3 to 3
- up_weight: bfloat16 [512, 2, 2, 1024], P('sp'), may hold values from -0.1875 to 0.1875
- up_bias: bfloat16 [512], P('sp'), may hold values from -3 to 3
Outputs:
- fine: bfloat16 [2048, 96, 512], P(('grp', 'sp')), parts along dimension 0
There are 16 independent parts, one for each index of `grp`. A program takes and returns all parts, laid end to end along the dimension named above; an argument that names none is the same for every part. Nothing has to cross between parts.
All inputs are finite; a program needn't handle non-finite values.
Results may differ from a plain program's by a relative error of at most 0.0042.
Values may be sent and summed in bfloat16 or wider, within the bound.
No kernel may reach another device: no remote copies, remote signals or barrier semaphores. Data moves between devices by JAX's collectives and lax.ppermute only.
A program may use at most 64 MiB of HBM per device.

v0:
```python
import jax
import jax.numpy as jnp
from jax import lax
from jax.sharding import PartitionSpec as P

GSIZE = 32


def conv_rows(weights_cat, width_cols, channels, outputs, tile_rows):
    how_many = tile_rows.shape[0]
    padded = jnp.pad(tile_rows, ((0, 0), (1, 1), (0, 0)))
    partial_sum = jnp.zeros((how_many * width_cols, 3 * outputs), jnp.float32)
    for offset in range(3):
        window = padded[:, offset : offset + width_cols, :].reshape(how_many * width_cols, channels)
        partial_sum = partial_sum + jnp.dot(
            window, weights_cat[offset], preferred_element_type=jnp.float32
        )
    partial_sum = partial_sum.reshape(how_many, width_cols, 3, outputs)
    contrib = jnp.zeros((how_many + 2, width_cols, outputs), jnp.float32)
    for kernel_row in range(3):
        contrib = contrib.at[2 - kernel_row : 2 - kernel_row + how_many].add(
            partial_sum[:, :, kernel_row]
        )
    return contrib


def normalize(convolved, height, width_cols, outputs, norm_gain, norm_shift):
    grouped = convolved.reshape(height, width_cols, outputs // GSIZE, GSIZE)
    centre = jnp.mean(grouped, axis=(0, 1, 3), keepdims=True)
    spread = jnp.mean(jnp.square(grouped - centre), axis=(0, 1, 3), keepdims=True)
    normed = ((grouped - centre) * lax.rsqrt(spread + 1e-05)).reshape(height, width_cols, outputs)
    return jax.nn.silu(normed * norm_gain + norm_shift).astype(jnp.bfloat16)


def full_conv(coarse, conv_weight, conv_bias, norm_gain, norm_shift):
    tile_count = lax.axis_size("sp")
    local_rows, width_cols, channels = coarse.shape
    height = local_rows * tile_count
    outputs = conv_weight.shape[0]
    weights_cat = jnp.transpose(conv_weight, (2, 3, 1, 0)).reshape(3, channels, 3 * outputs)
    summed = conv_rows(
        weights_cat, width_cols, channels, outputs, lax.all_gather(coarse, "sp", axis=0, tiled=True)
    )
    convolved = summed[1 : height + 1] + conv_bias
    return normalize(convolved, height, width_cols, outputs, norm_gain, norm_shift)


def body(coarse, conv_weight, conv_bias, norm_gain, norm_shift, up_weight, up_bias):
    activated = full_conv(coarse, conv_weight, conv_bias, norm_gain, norm_shift)
    height, width_cols, channels = (activated.shape[0], activated.shape[1], conv_weight.shape[3])
    slice_out = up_weight.shape[0]
    flat_weight = jnp.transpose(up_weight, (3, 1, 2, 0)).reshape(channels, 4 * slice_out)
    features = lax.all_gather(activated, "sp", axis=2, tiled=True)
    chosen_width = features.shape[2]
    flat_features = features.reshape(height * width_cols, chosen_width)
    decoded = jnp.dot(flat_features, flat_weight, preferred_element_type=jnp.float32)
    decoded = (decoded.reshape(height, width_cols, 2, 2, slice_out) + up_bias).astype(jnp.bfloat16)
    decoded = jnp.transpose(decoded, (0, 2, 1, 3, 4)).reshape(2 * height, 2 * width_cols, slice_out)
    return lax.all_to_all(decoded, "sp", split_axis=0, concat_axis=2, tiled=True)


def solution(mesh):
    return jax.shard_map(
        body,
        mesh=mesh,
        in_specs=(
            P(("grp", "sp"), None, None),
            P("sp", None, None, None),
            P("sp"),
            P("sp"),
            P("sp"),
            P("sp", None, None, None),
            P("sp"),
        ),
        out_specs=P(("grp", "sp"), None, None),
        check_vma=False,
    )
```

profile of v0, /device:TPU:1, one launch (start us, length us, event | category | flops | bytes accessed | tf_op | source)
XLA Modules:
  0.0 294.0 jit_solution(15745474738051141578)
XLA Ops:
  6.5 0.0 all-gather.3.cloned.1.call-start
  6.5 0.7 all-gather.3.cloned.1.call-update
  7.3 0.0 all-gather.5.cloned.1.call-start
  7.3 1.2 fusion.14
  8.5 83.6 %all-gather.3.cloned.1.call-done = bf16[64,48,1024]{2,1,0:T(8,128)(2,1)} async-done(((bf16[2,48,1024]{2,1,0:T(8,128)(2,1)}), bf16[64,48,1024]{2,1,0:T(8,128)(2,1)}) %all-gather.3.cloned.1.call-update) | async-done | bytes 6291472 | tf_op jit(solution)/shard_map/all_gather | solution.py:42
  92.1 10.7 %pad_slice_fusion = (bf16[64,48,1024]{2,1,0:T(8,128)(2,1)S(1)}, bf16[64,48,1024]{2,1,0:T(8,128)(2,1)S(1)}) fusion(bf16[64,48,1024]{2,1,0:T(8,128)(2,1)} %all-gather.3.cloned.1.call-done), kind=kLoop, calls=%fused_computation.2 | loop fusion | bytes 18874368 | tf_op jit(solution)/shard_map/slice | solution.py:14
  102.9 0.0 copy-start
  102.9 2.0 fusion.15
  104.9 0.7 copy-done
  105.7 2.0 convolution_add_fusion.1
  107.7 3.1 %convolution_add_fusion = f32[3072,96]{0,1:T(8,128)} fusion(f32[3072,96]{0,1:T(8,128)S(1)} %convolution_add_fusion.1, bf16[3072,1024]{1,0:T(8,128)(2,1)S(1)} %bitcast.56, bf16[1024,96]{0,1:T(8,128)(2,1)S(1)} %bitcast.62), kind=kOutput, calls=%fused_computation.4 | convolution fusion | flops 604274688 | bytes 8847360 | tf_op jit(solution)/shard_map/dot_general | solution.py:15
  110.8 2.6 reshape.152
  113.4 0.2 fusion.13
  113.7 0.6 copy.44
  114.3 0.1 scatter-add.10
  114.4 0.0 copy-start.2
  114.4 1.0 fusion.9
  115.4 0.0 copy-start.3
  115.4 0.0 copy-start.4
  115.4 0.0 copy-start.5
  115.4 0.0 copy-start.1
  115.4 1.0 fusion.7
  116.4 0.0 copy-done.2
  116.4 1.0 fusion.10
  118.0 0.9 multiply_reduce_fusion
  119.7 0.0 copy-done.3
  119.7 0.0 copy-done.4
  119.7 1.3 multiply_convert_fusion
  120.9 0.0 all-gather.5.cloned.1.call-update
  121.0 0.0 copy-done.5
  121.0 104.1 %all-gather.5.cloned.1.call-done = bf16[64,48,1024]{1,2,0:T(8,128)(2,1)} async-done(((bf16[64,48,32]{1,2,0:T(8,128)(2,1)}), bf16[64,48,1024]{1,2,0:T(8,128)(2,1)}) %all-gather.5.cloned.1.call-update) | async-done | bytes 6291472 | tf_op jit(solution)/shard_map/all_gather | solution.py:53
  225.0 0.0 copy-done.1
  225.1 9.7 %fusion.4 = bf16[64,2,48,2,16]{2,4,3,1,0:T(8,128)(2,1)} fusion(bf16[64,48,1024]{1,2,0:T(8,128)(2,1)} %all-gather.5.cloned.1.call-done, f32[16]{0:T(128)S(1)} %convert_element_type.16, bf16[16,2,2,1024]{3,2,1,0:T(2,128)(2,1)S(1)} %copy-done.1), kind=kOutput, calls=%fused_computation.7 | convolution fusion | flops 403046400 | bytes 6815808 | tf_op jit(solution)/shard_map/dot_general | solution.py:56
  234.8 6.1 %copy.23 = bf16[64,2,48,2,16]{4,3,2,1,0:T(2,128)(2,1)S(1)} copy(bf16[64,2,48,2,16]{2,4,3,1,0:T(8,128)(2,1)} %fusion.4) | data formatting | bytes 786432 | tf_op jit(solution)/shard_map/convert_element_type | solution.py:57
  240.9 2.7 copy.24
  243.5 42.6 %all_to_all.18 = bf16[128,96,16]{1,2,0:T(8,128)(2,1)S(1)} all-to-all(bf16[128,96,16]{1,2,0:T(8,128)(2,1)} %copy.24), channel_id=1, replica_groups=mesh['grp'=16,'sp'=32] {'sp'}, dimensions={0} | all-to-all | bytes 786432 | tf_op jit(solution)/shard_map/all_to_all | solution.py:59
  286.2 1.0 copy.26
  (2 shorter events, 0.0 us)
Async XLA Ops:
  6.5 85.6 %all-gather.3.cloned.1.call-start = ((), (), s32[]{:S(2)}) async-start(), calls=%async_computation.1 | async-start | bytes 6488064 | tf_op jit(solution)/shard_map/all_gather | solution.py:42
  7.3 217.8 %all-gather.5.cloned.1.call-start = ((), (), s32[]{:S(2)}) async-start(), calls=%async_computation.2 | async-start | bytes 17301504 | tf_op jit(solution)/shard_map/all_gather | solution.py:53
  102.9 2.8 copy-start
  114.4 2.0 copy-start.2
  115.4 4.3 %copy-start.3 = (f32[32]{0:T(128)S(1)}, f32[32]{0:T(128)}, u32[]{:S(2)}) copy-start(f32[32]{0:T(128)} %param.17) | copy-start | bytes 388
  115.4 4.3 %copy-start.4 = (f32[32]{0:T(128)S(1)}, f32[32]{0:T(128)}, u32[]{:S(2)}) copy-start(f32[32]{0:T(128)} %param.16) | copy-start | bytes 388
  115.4 5.6 %copy-start.5 = (bf16[16]{0:T(256)(128)(2,1)S(1)}, bf16[16]{0:T(256)(128)(2,1)}, u32[]{:S(2)}) copy-start(bf16[16]{0:T(256)(128)(2,1)} %param.19) | copy-start | bytes 100
  115.4 109.6 %copy-start.1 = (bf16[16,2,2,1024]{3,2,1,0:T(2,128)(2,1)S(1)}, bf16[16,2,2,1024]{3,2,1,0:T(2,128)(2,1)}, u32[]{:S(2)}) copy-start(bf16[16,2,2,1024]{3,2,1,0:T(2,128)(2,1)} %param.18) | copy-start | bytes 393220
Sparse Core Ops, SparseCore 0:
  9.5 82.6 all-gather.2
  121.1 103.9 all-gather.4
where the time goes:
time: 294 us
  waiting for transfers between devices  188 us (64%)
  blocking collectives  42.6 us (14%)
  local copies, waits for them, and re-layouts  26 us (9%)
  matrix products  16.9 us (6%)
  between operations  14.9 us (5%)
  other arithmetic  5.12 us (2%)
    all_gather x1, waiting for transfers between devices, body(): features = lax.all_gather(activated, 'sp', axis=2, tiled=True)  104 us
    all_gather x1, waiting for transfers between devices, full_conv(): lax.all_gather(coarse, 'sp', axis=0, tiled=True)  83.6 us
    all_to_all x1, blocking collectives, body(): lax.all_to_all(decoded, 'sp', split_axis=0, concat_axis=2, tiled=True)  42.6 us
    slice x1, local copies, waits for them, and re-layouts, conv_rows(): padded[:, offset:offset + width_cols, :]  10.7 us
    dot_general x1, matrix products, body(): jnp.dot(flat_features, flat_weight, preferred_element_type=jnp.float32)  9.72 us
    dot_general x3, matrix products, conv_rows(): jnp.dot(window, weights_cat[offset], preferred_element_type=jnp.float32)  7.18 us
    convert_element_type x1, local copies, waits for them, and re-layouts, body(): (decoded.reshape(height, width_cols, 2, 2, slice_out) + up_bias).astype(j...  6.09 us
  transfers between devices with their start and end apart: 2, of which 2 were waited for; matrix products, arithmetic and copies ran while one was open for 0% of the time, Pallas kernels for 0%

commit v1 on v0

v1 whole, which is shorter than its diff:
```python
import jax
import jax.numpy as jnp
from jax import lax
from jax.sharding import Mesh, PartitionSpec as P

GSIZE = 32


def gather_rows(local, axis):
    by_z = lax.all_gather(local, "z", axis=0, tiled=False)
    both = lax.all_gather(by_z, "core", axis=1, tiled=False)
    return both.reshape((-1,) + local.shape[1:])


def normalize(convolved, norm_gain, norm_shift):
    height, width_cols, outputs = convolved.shape
    grouped = convolved.reshape(height, width_cols, outputs // GSIZE, GSIZE)
    centre = jnp.mean(grouped, axis=(0, 1, 3), keepdims=True)
    spread = jnp.mean(jnp.square(grouped - centre), axis=(0, 1, 3), keepdims=True)
    normed = ((grouped - centre) * lax.rsqrt(spread + 1e-05)).reshape(height, width_cols, outputs)
    return jax.nn.silu(normed * norm_gain + norm_shift).astype(jnp.bfloat16)


def body(coarse, conv_weight, conv_bias, norm_gain, norm_shift, up_weight, up_bias):
    whole = gather_rows(coarse, 0)
    up_weight, up_bias, whole = lax.optimization_barrier((up_weight, up_bias, whole))
    convolved = lax.conv_general_dilated(
        whole[None],
        conv_weight,
        (1, 1),
        "SAME",
        dimension_numbers=("NHWC", "OHWI", "NHWC"),
        preferred_element_type=jnp.float32,
    )[0]
    activated = normalize(convolved + conv_bias, norm_gain, norm_shift)
    slice_out = up_weight.shape[0]
    flat = up_weight.reshape(slice_out, -1)
    packed = jnp.concatenate([flat, jnp.pad(up_bias[:, None], ((0, 0), (0, 127)))], axis=1)
    packed_all = lax.all_gather(packed, ("z", "core"), axis=0, tiled=True)
    weight_all = packed_all[:, : flat.shape[1]].reshape((-1,) + up_weight.shape[1:])
    bias_all = packed_all[:, flat.shape[1]]
    rows = lax.all_to_all(activated, ("z", "core"), split_axis=0, concat_axis=2, tiled=True)
    decoded = jnp.einsum("ijc,oabc->iajbo", rows, weight_all, preferred_element_type=jnp.float32)
    decoded = decoded + bias_all.astype(jnp.float32)
    height, _, width_cols, _, outputs = decoded.shape
    return decoded.astype(jnp.bfloat16).reshape(2 * height, 2 * width_cols, outputs)


def solution(mesh):
    grp, sp = mesh.devices.shape
    fine_mesh = Mesh(mesh.devices.reshape(grp, sp // 2, 2), ("grp", "z", "core"))
    rows = ("grp", "z", "core")
    chans = ("z", "core")
    return jax.shard_map(
        body,
        mesh=fine_mesh,
        in_specs=(
            P(rows, None, None),
            P(chans, None, None, None),
            P(chans),
            P(chans),
            P(chans),
            P(chans, None, None, None),
            P(chans),
        ),
        out_specs=P(rows, None, None),
        check_vma=False,
    )
```

time: 294 us -> 246 us (0.84)
  waiting for transfers between devices: 188 us -> 117 us
  local copies, waits for them, and re-layouts: 26 us -> 55 us
  blocking collectives: 42.6 us -> 32 us
  matrix products: 16.9 us -> 22.9 us
    all_gather x2 -> x3, waiting for transfers between devices: 188 us -> 116 us  [the longest x1 75.1 us: gather_rows(): by_z = lax.all_gather(local, 'z', axis=0, tiled=False)]
    conv_general_dilated x0 -> x1, matrix products: none -> 19.9 us  [body(): lax.conv_general_dilated(whole[None], conv_weight, (1, 1), 'SAME', dimens...]
    all_gather x0 -> x2, local copies, waits for them, and re-layouts: none -> 14.4 us  [the longest x1 10.3 us: gather_rows(): both = lax.all_gather(by_z, 'core', axis=1, tiled=False)]
    dot_general x4 -> x1, matrix products: 16.9 us -> 2.99 us  [body(): jnp.einsum('ijc,oabc->iajbo', rows, weight_all, preferred_element_type=jn...]
    all_to_all x1, blocking collectives: 42.6 us -> 32 us  [body(): lax.all_to_all(activated, ('z', 'core'), split_axis=0, concat_axis=2, til...]
    conv_general_dilated x0 -> x3, local copies, waits for them, and re-layouts: none -> 9.91 us  [body(): lax.conv_general_dilated(whole[None], conv_weight, (1, 1), 'SAME', dimens...]
    slice x3 -> x1, local copies, waits for them, and re-layouts: 12.1 us -> 4.72 us  [body(): packed_all[:, :flat.shape[1]].reshape((-1,) + up_weight.shape[1:])]
    unnamed x13 -> x18, local copies, waits for them, and re-layouts: 1.37 us -> 7.91 us
  transfers between devices with their start and end apart: 2 -> 3, of which waited for: 2 -> 3; matrix products, arithmetic and copies ran while one was open for 0% -> 16% of each run, Pallas kernels for 0% -> 0%
where the time goes in v1:
time: 246 us; the launch traced here: 245 us
  waiting for transfers between devices  117 us (48%)
  local copies, waits for them, and re-layouts  55 us (22%)
  blocking collectives  32 us (13%)
  matrix products  22.9 us (9%)
  between operations  14.4 us (6%)
  other arithmetic  3.79 us (2%)
    all_gather x1, waiting for transfers between devices, gather_rows(): by_z = lax.all_gather(local, 'z', axis=0, tiled=False)  75.1 us
    all_gather x1, waiting for transfers between devices, gather_rows(): both = lax.all_gather(by_z, 'core', axis=1, tiled=False)  34.4 us
    all_to_all x1, blocking collectives, body(): lax.all_to_all(activated, ('z', 'core'), split_axis=0, concat_axis=2, til...  32 us
    conv_general_dilated x1, matrix products, body(): lax.conv_general_dilated(whole[None], conv_weight, (1, 1), 'SAME', dimens...  19.9 us
    all_gather x1, local copies, waits for them, and re-layouts, gather_rows(): both = lax.all_gather(by_z, 'core', axis=1, tiled=False)  10.3 us
    conv_general_dilated x3, local copies, waits for them, and re-layouts, body(): lax.conv_general_dilated(whole[None], conv_weight, (1, 1), 'SAME', dimens...  9.91 us
    reshape x1, local copies, waits for them, and re-layouts, gather_rows(): return both.reshape((-1,) + local.shape[1:])  9.72 us
    unnamed x18, local copies, waits for them, and re-layouts  7.91 us
  transfers between devices with their start and end apart: 3, of which 3 were waited for; matrix products, arithmetic and copies ran while one was open for 16% of the time, Pallas kernels for 0%

profile of v1, /device:TPU:1, one launch (start us, length us, event | category | flops | bytes accessed | tf_op | source)
XLA Modules:
  0.0 245.1 jit_solution(8571424381882101060)
XLA Ops:
  6.5 0.0 copy-start
  6.5 0.0 all-gather.8.cloned.1.call-start
  6.5 0.7 all-gather.8.cloned.1.call-update
  7.3 0.0 all-gather.10.cloned.1.call-start
  7.3 75.1 %all-gather.8.cloned.1.call-done = bf16[32,48,1024]{2,1,0:T(8,128)(2,1)} async-done(((bf16[2,48,1024]{2,1,0:T(8,128)(2,1)}), bf16[32,48,1024]{2,1,0:T(8,128)(2,1)}) %all-gather.8.cloned.1.call-update) | async-done | bytes 3145744 | tf_op jit(solution)/shard_map/all_gather | solution.py:10
  82.4 4.1 %copy.30 = bf16[16,2,48,1024]{3,2,0,1:T(8,128)(2,1)} copy(bf16[16,2,48,1024]{3,2,1,0:T(8,128)(2,1)} %bitcast.55) | data formatting | bytes 6291456 | tf_op jit(solution)/shard_map/all_gather | solution.py:10
  86.4 0.0 all-gather.10.cloned.1.call-update
  86.5 0.0 all-gather.6.cloned.1.call-start
  86.5 34.4 %all-gather.10.cloned.1.call-done = bf16[16,4,48,1024]{3,2,0,1:T(8,128)(2,1)} async-done(((bf16[16,2,48,1024]{3,2,0,1:T(8,128)(2,1)}), bf16[16,4,48,1024]{3,2,0,1:T(8,128)(2,1)}) %all-gather.10.cloned.1.call-update) | async-done | bytes 6291472 | tf_op jit(solution)/shard_map/all_gather | solution.py:11
  121.0 10.3 %copy.31 = bf16[16,4,48,1024]{3,1,0,2:T(4,128)(2,1)} copy(bf16[16,4,48,1024]{3,2,0,1:T(8,128)(2,1)} %all-gather.10.cloned.1.call-done) | data formatting | bytes 12582912 | tf_op jit(solution)/shard_map/all_gather | solution.py:11
  131.2 0.0 copy-start.1
  131.2 9.7 %reshape.66 = bf16[64,48,1024]{2,0,1:T(8,128)(2,1)} reshape(bf16[16,4,48,1024]{3,1,0,2:T(4,128)(2,1)} %copy.31) | data formatting | bytes 12582912 | tf_op jit(solution)/shard_map/reshape | solution.py:12
  140.9 0.0 copy-done.1
  140.9 0.1 reshape.67
  141.0 0.0 copy-done.5
  141.0 0.1 copy.46
  141.1 0.7 fusion.18
  141.8 0.0 all-gather.6.cloned.1.call-update
  141.8 4.1 %pad.5 = bf16[64,1,56,1024]{3,0,2,1:T(8,128)(2,1)S(1)} pad(bf16[64,1,48,1024]{3,0,2,1:T(8,128)(2,1)} %bitcast.50, bf16[]{:T(256)} %constant.12.clone.1), padding=0_0x0_0x1_7x0_0 | pad | bytes 13631490 | tf_op jit(solution)/shard_map/broadcast_in_dim | solution.py:28
  146.0 0.0 copy-start.6
  146.0 7.1 %copy.35 = bf16[64,1,8,7,1024]{4,2,3,0,1:T(8,128)(2,1)} copy(bf16[64,1,8,7,1024]{4,0,3,2,1:T(8,128)(2,1)S(1)} %bitcast.49) | data formatting | bytes 14680064 | tf_op jit(solution)/shard_map/conv_general_dilated | solution.py:27
  153.0 2.2 slice.11
  155.3 0.0 copy-done
  155.3 0.0 copy-done.6
  155.3 0.0 copy-start.2
  155.3 0.0 copy-start.3
  155.3 0.0 copy-start.4
  155.3 19.9 %fusion.6 = f32[64,8,7,32]{3,1,2,0:T(8,128)S(1)} fusion(bf16[32,3,3,1024]{3,0,2,1:T(8,128)(2,1)S(1)} %copy-done, bf16[64,1,7,2,1024]{4,2,3,0,1:T(8,128)(2,1)S(1)} %slice.11, bf16[64,1,8,7,1024]{4,2,3,0,1:T(8,128)(2,1)} %copy.35, pred[8,7]{0,1:T(8,128)(4,1)S(1)} %copy-done.6), kind=kOutput, calls=%fused_computation.6 | convolution fusion | flops 2120335360 | bytes 10223672 | tf_op jit(solution)/shard_map/conv_general_dilated | solution.py:27
  175.2 0.6 copy.36
  175.9 0.0 copy-done.2
  175.9 0.9 fusion.15
  177.3 0.9 multiply_reduce_fusion
  178.8 0.0 copy-done.3
  178.8 0.0 copy-done.4
  178.8 0.4 multiply_convert_fusion
  179.2 1.0 copy.37
  180.1 0.8 reshape.93
  180.9 32.0 %all_to_all.18 = bf16[32,2,1536]{2,1,0:T(2,128)(2,1)S(1)} all-to-all(bf16[32,2,1536]{2,1,0:T(2,128)(2,1)S(1)} %reshape.93), channel_id=1, replica_groups=mesh['grp'=16,'z'=16,'core'=2] {'z','core'}, dimensions={0} | all-to-all | bytes 393216 | tf_op jit(solution)/shard_map/all_to_all | solution.py:42
  212.9 0.5 reshape.94
  213.4 1.2 copy.38
  214.6 0.8 reshape.90
  215.4 6.6 %all-gather.6.cloned.1.call-done = bf16[512,4224]{1,0:T(8,128)(2,1)} async-done(((bf16[16,4224]{1,0:T(8,128)(2,1)}), bf16[512,4224]{1,0:T(8,128)(2,1)}) %all-gather.6.cloned.1.call-update) | async-done | bytes 4325392 | tf_op jit(solution)/shard_map/all_gather | solution.py:39
  222.0 4.7 %slice.10 = bf16[512,4096]{1,0:T(8,128)(2,1)} slice(bf16[512,4224]{1,0:T(8,128)(2,1)} %all-gather.6.cloned.1.call-done), slice={[0:512], [0:4096]} | slice | bytes 8388608 | tf_op jit(solution)/shard_map/slice | solution.py:40
  226.8 6.5 %copy.45 = bf16[512,4096]{0,1:T(8,128)(2,1)} copy(bf16[512,4096]{1,0:T(8,128)(2,1)} %slice.10) | data formatting | bytes 8388608
  233.2 1.0 convert_reduce_fusion
  234.2 3.0 %fusion.10 = bf16[2,2,48,2,512]{4,2,0,3,1:T(8,128)(2,1)S(1)} fusion(bf16[512,2,2,1024,1]{0,3,4,2,1:T(8,128)(2,1)} %bitcast.51, f32[512]{0:T(512)S(1)} %convert_reduce_fusion, bf16[2,48,1024,1,1]{2,1,0,3,4:T(8,128)(2,1)S(1)} %reshape.90), kind=kOutput, calls=%fused_computation.9 | convolution fusion | flops 403046400 | bytes 4786176 | tf_op jit(solution)/shard_map/ijc,oabc->iajbo/dot_general | solution.py:43
  237.2 0.4 copy.40
  237.6 0.9 reshape.69
  (1 shorter events, 0.0 us)
Async XLA Ops:
  6.5 148.7 %copy-start = (bf16[32,3,3,1024]{3,0,2,1:T(8,128)(2,1)S(1)}, bf16[32,3,3,1024]{3,0,2,1:T(8,128)(2,1)}, u32[]{:S(2)}) copy-start(bf16[32,3,3,1024]{3,0,2,1:T(8,128)(2,1)} %param.8) | copy-start | bytes 1769476
  6.5 75.8 %all-gather.8.cloned.1.call-start = ((), (), s32[]{:S(2)}) async-start(), calls=%async_computation.2 | async-start | bytes 3342336 | tf_op jit(solution)/shard_map/all_gather | solution.py:10
  7.3 113.7 %all-gather.10.cloned.1.call-start = ((), (), s32[]{:S(2)}) async-start(), calls=%async_computation.3 | async-start | bytes 9437184 | tf_op jit(solution)/shard_map/all_gather | solution.py:11
  86.5 135.6 %all-gather.6.cloned.1.call-start = ((), (), s32[]{:S(2)}) async-start(), calls=%async_computation.1 | async-start | bytes 4460544 | tf_op jit(solution)/shard_map/all_gather | solution.py:39
  131.2 9.7 %copy-start.1 = (bf16[16,2,2,1024]{3,2,1,0:T(2,128)(2,1)S(1)}, bf16[16,2,2,1024]{3,2,1,0:T(2,128)(2,1)}, u32[]{:S(2)}) copy-start(bf16[16,2,2,1024]{3,2,1,0:T(2,128)(2,1)} %param.12) | copy-start | bytes 393220
  131.2 9.8 %copy-start.5 = (bf16[16]{0:T(256)(128)(2,1)S(1)}, bf16[16]{0:T(256)(128)(2,1)}, u32[]{:S(2)}) copy-start(bf16[16]{0:T(256)(128)(2,1)} %param.13) | copy-start | bytes 100
  146.0 9.3 %copy-start.6 = (pred[8,7]{0,1:T(8,128)(4,1)S(1)}, pred[8,7]{0,1:T(8,128)(4,1)}, u32[]{:S(2)}) copy-start(pred[8,7]{0,1:T(8,128)(4,1)} %constant.26) | copy-start | bytes 172
  155.3 20.6 %copy-start.2 = (f32[32]{0:T(128)S(1)}, f32[32]{0:T(128)}, u32[]{:S(2)}) copy-start(f32[32]{0:T(128)} %param.9) | copy-start | bytes 388
  155.3 23.5 %copy-start.3 = (f32[32]{0:T(128)S(1)}, f32[32]{0:T(128)}, u32[]{:S(2)}) copy-start(f32[32]{0:T(128)} %param.11) | copy-start | bytes 388
  155.3 23.5 %copy-start.4 = (f32[32]{0:T(128)S(1)}, f32[32]{0:T(128)}, u32[]{:S(2)}) copy-start(f32[32]{0:T(128)} %param.10) | copy-start | bytes 388
Sparse Core Ops, SparseCore 0:
  9.4 72.8 all-gather.7
  86.6 34.3 all-gather.9
  142.0 80.0 all-gather.5

commit v2 on v1

v2 whole, which is shorter than its diff:
```python
import jax
import jax.numpy as jnp
from jax import lax
from jax.sharding import Mesh, PartitionSpec as P

GSIZE = 32


def conv_rows(weights_cat, width_cols, channels, outputs, tile_rows):
    how_many = tile_rows.shape[0]
    padded = jnp.pad(tile_rows, ((0, 0), (1, 1), (0, 0)))
    partial_sum = jnp.zeros((how_many * width_cols, 3 * outputs), jnp.float32)
    for offset in range(3):
        window = padded[:, offset : offset + width_cols, :].reshape(how_many * width_cols, channels)
        partial_sum = partial_sum + jnp.dot(
            window, weights_cat[offset], preferred_element_type=jnp.float32
        )
    partial_sum = partial_sum.reshape(how_many, width_cols, 3, outputs)
    contrib = jnp.zeros((how_many + 2, width_cols, outputs), jnp.float32)
    for kernel_row in range(3):
        contrib = contrib.at[2 - kernel_row : 2 - kernel_row + how_many].add(
            partial_sum[:, :, kernel_row]
        )
    return contrib


def normalize(convolved, norm_gain, norm_shift):
    height, width_cols, outputs = convolved.shape
    grouped = convolved.reshape(height, width_cols, outputs // GSIZE, GSIZE)
    centre = jnp.mean(grouped, axis=(0, 1, 3), keepdims=True)
    spread = jnp.mean(jnp.square(grouped - centre), axis=(0, 1, 3), keepdims=True)
    normed = ((grouped - centre) * lax.rsqrt(spread + 1e-05)).reshape(height, width_cols, outputs)
    return jax.nn.silu(normed * norm_gain + norm_shift).astype(jnp.bfloat16)


def body(coarse, conv_weight, conv_bias, norm_gain, norm_shift, up_weight, up_bias):
    chips = lax.axis_size("z")
    core = lax.axis_index("core")
    _, width_cols, channels = coarse.shape
    outputs = conv_weight.shape[0]
    slice_out = up_weight.shape[0]

    whole = lax.all_gather(coarse, ("z", "core"), axis=0, tiled=True)
    height = whole.shape[0]
    flat = up_weight.reshape(slice_out, -1)
    packed = jnp.concatenate([flat, jnp.pad(up_bias[:, None], ((0, 0), (0, 127)))], axis=1)
    packed, whole = lax.optimization_barrier((packed, whole))
    packed_z = lax.all_gather(packed, "z", axis=0, tiled=False)
    weight_half = packed_z[:, :, : flat.shape[1]].reshape((chips, slice_out) + up_weight.shape[1:])
    bias_half = packed_z[:, :, flat.shape[1]].astype(jnp.float32)

    weights_cat = jnp.transpose(conv_weight, (2, 3, 1, 0)).reshape(3, channels, 3 * outputs)
    summed = conv_rows(weights_cat, width_cols, channels, outputs, whole)
    activated = normalize(summed[1 : height + 1] + conv_bias, norm_gain, norm_shift)

    chip_rows = lax.all_to_all(activated, "z", split_axis=0, concat_axis=2, tiled=True)
    both = lax.all_gather(chip_rows, "core", axis=0, tiled=False)
    local_rows = chip_rows.shape[0]
    both = both.reshape(2, local_rows, width_cols, chips, outputs)
    act = jnp.transpose(both, (1, 2, 3, 0, 4)).reshape(local_rows, width_cols, chips * 2 * outputs)

    decoded = jnp.einsum("ijc,zoabc->iajbzo", act, weight_half, preferred_element_type=jnp.float32)
    decoded = (decoded + bias_half).astype(jnp.bfloat16)
    half = local_rows // 2
    own = lax.dynamic_slice_in_dim(decoded, core * half, half, axis=0)
    other = lax.dynamic_slice_in_dim(decoded, (1 - core) * half, half, axis=0)
    received = lax.ppermute(other, "core", [(0, 1), (1, 0)])
    low = jnp.where(core == 0, own, received)
    high = jnp.where(core == 0, received, own)
    fine = jnp.stack([low, high], axis=5)
    return fine.reshape(2 * half, 2 * width_cols, chips * 2 * slice_out)


def solution(mesh):
    grp, sp = mesh.devices.shape
    fine_mesh = Mesh(mesh.devices.reshape(grp, sp // 2, 2), ("grp", "z", "core"))
    rows = ("grp", "z", "core")
    chans = ("z", "core")
    return jax.shard_map(
        body,
        mesh=fine_mesh,
        in_specs=(
            P(rows, None, None),
            P(chans, None, None, None),
            P(chans),
            P(chans),
            P(chans),
            P(chans, None, None, None),
            P(chans),
        ),
        out_specs=P(rows, None, None),
        check_vma=False,
    )
```

time: 246 us -> 205 us (0.83)
  blocking collectives: 32 us -> 4.98 us
  starting transfers between devices: 0.08 us -> 19.7 us
  waiting for transfers between devices: 117 us -> 102 us
  matrix products: 22.9 us -> 10 us
  local copies, waits for them, and re-layouts: 55 us -> 43.9 us
  other arithmetic: 3.79 us -> 8.48 us
    all_gather x3 -> x2, waiting for transfers between devices: 116 us -> 83.1 us  [the longest x1 81.3 us: body(): whole = lax.all_gather(coarse, ('z', 'core'), axis=0, tiled=True)]
    all_to_all x1 -> x0, blocking collectives: 32 us -> none  [body(): lax.all_to_all(activated, ('z', 'core'), split_axis=0, concat_axis=2, til...]
    conv_general_dilated x1 -> x0, matrix products: 19.9 us -> none  [body(): lax.conv_general_dilated(whole[None], conv_weight, (1, 1), 'SAME', dimens...]
    all_to_all x0 -> x1, waiting for transfers between devices: none -> 16.4 us  [body(): lax.all_to_all(activated, 'z', split_axis=0, concat_axis=2, tiled=True)]
    all_gather x2 -> x1, local copies, waits for them, and re-layouts: 14.4 us -> 0.73 us  [body(): both = lax.all_gather(chip_rows, 'core', axis=0, tiled=False)]
    ppermute x0 -> x1, starting transfers between devices: none -> 11.8 us  [body(): received = lax.ppermute(other, 'core', [(0, 1), (1, 0)])]
    conv_general_dilated x3 -> x0, local copies, waits for them, and re-layouts: 9.91 us -> none  [body(): lax.conv_general_dilated(whole[None], conv_weight, (1, 1), 'SAME', dimens...]
    slice x1 -> x3, local copies, waits for them, and re-layouts: 4.72 us -> 13.6 us  [the longest x1 10.8 us: conv_rows(): padded[:, offset:offset + width_cols, :]]
  transfers between devices with their start and end apart: 3 -> 4, of which waited for: 3 -> 4; matrix products, arithmetic and copies ran while one was open for 16% -> 18% of each run, Pallas kernels for 0% -> 0%
where the time goes in v2:
time: 205 us; the launch traced here: 204 us
  waiting for transfers between devices  102 us (50%)
  local copies, waits for them, and re-layouts  43.9 us (21%)
  starting transfers between devices  19.7 us (10%)
  between operations  15 us (7%)
  matrix products  10 us (5%)
  other arithmetic  8.48 us (4%)
  blocking collectives  4.98 us (2%)
    all_gather x1, waiting for transfers between devices, body(): whole = lax.all_gather(coarse, ('z', 'core'), axis=0, tiled=True)  81.3 us
    all_to_all x1, waiting for transfers between devices, body(): lax.all_to_all(activated, 'z', split_axis=0, concat_axis=2, tiled=True)  16.4 us
    ppermute x1, starting transfers between devices, body(): received = lax.ppermute(other, 'core', [(0, 1), (1, 0)])  11.8 us
    slice x1, local copies, waits for them, and re-layouts, conv_rows(): padded[:, offset:offset + width_cols, :]  10.8 us
    all_to_all x1, starting transfers between devices, body(): lax.all_to_all(activated, 'z', split_axis=0, concat_axis=2, tiled=True)  7.81 us
    dot_general x3, matrix products, conv_rows(): jnp.dot(window, weights_cat[offset], preferred_element_type=jnp.float32)  7.19 us
    another operation x1, local copies, waits for them, and re-layouts, body(): fine = jnp.stack([low, high], axis=5)  6.69 us
    reshape x1, local copies, waits for them, and re-layouts, body(): return fine.reshape(2 * half, 2 * width_cols, chips * 2 * slice_out)  6.03 us
  transfers between devices with their start and end apart: 4, of which 4 were waited for; matrix products, arithmetic and copies ran while one was open for 18% of the time, Pallas kernels for 0%

profile of v2, /device:TPU:1, one launch (start us, length us, event | category | flops | bytes accessed | tf_op | source)
XLA Modules:
  0.0 203.8 jit_solution(14903558580625342563)
XLA Ops:
  6.5 0.0 all-gather.4.cloned.1.call-start
  6.5 0.7 all-gather.4.cloned.1.call-update
  7.3 0.0 all-gather.6.cloned.1.call-start
  7.3 1.0 reshape.160
  8.3 0.7 copy.34
  9.0 1.2 fusion.12
  10.2 0.7 fusion.11
  10.9 81.3 %all-gather.4.cloned.1.call-done = bf16[64,48,1024]{2,1,0:T(8,128)(2,1)} async-done(((bf16[2,48,1024]{2,1,0:T(8,128)(2,1)}), bf16[64,48,1024]{2,1,0:T(8,128)(2,1)}) %all-gather.4.cloned.1.call-update) | async-done | bytes 6291472 | tf_op jit(solution)/shard_map/all_gather | solution.py:43
  92.1 0.0 all-gather.6.cloned.1.call-update
  92.2 10.8 %pad_slice_fusion = (bf16[64,48,1024]{2,1,0:T(8,128)(2,1)S(1)}, bf16[64,48,1024]{2,1,0:T(8,128)(2,1)S(1)}) fusion(bf16[64,48,1024]{2,1,0:T(8,128)(2,1)} %all-gather.4.cloned.1.call-done), kind=kLoop, calls=%fused_computation | loop fusion | bytes 18874368 | tf_op jit(solution)/shard_map/slice | solution.py:14
  102.9 2.0 %fusion.13 = f32[3072,96]{0,1:T(8,128)S(1)} fusion(bf16[3072,1024]{1,0:T(8,128)(2,1)S(1)} %bitcast.60, bf16[1024,96]{0,1:T(8,128)(2,1)S(1)} %bitcast.71), kind=kOutput, calls=%fused_computation.29 | convolution fusion | flops 603979776 | bytes 7667712 | tf_op jit(solution)/shard_map/dot_general | solution.py:15
  105.0 0.7 copy-done
  105.7 2.0 %convolution_add_fusion.1 = f32[3072,96]{0,1:T(8,128)S(1)} fusion(f32[3072,96]{0,1:T(8,128)S(1)} %fusion.13, bf16[3072,1024]{1,0:T(8,128)(2,1)S(1)} %bitcast.58, bf16[1024,96]{0,1:T(8,128)(2,1)S(1)} %bitcast.70), kind=kOutput, calls=%fused_computation.3 | convolution fusion | flops 604274688 | bytes 8847360 | tf_op jit(solution)/shard_map/dot_general | solution.py:15
  107.8 3.1 %convolution_add_fusion = f32[3072,96]{0,1:T(8,128)} fusion(f32[3072,96]{0,1:T(8,128)S(1)} %convolution_add_fusion.1, bf16[3072,1024]{1,0:T(8,128)(2,1)S(1)} %bitcast.59, bf16[1024,96]{0,1:T(8,128)(2,1)S(1)} %bitcast.69), kind=kOutput, calls=%fused_computation.2 | convolution fusion | flops 604274688 | bytes 8847360 | tf_op jit(solution)/shard_map/dot_general | solution.py:15
  110.9 2.4 %reshape.165 = f32[64,48,3,32]{1,0,3,2:T(8,128)S(1)} reshape(f32[3072,96]{0,1:T(8,128)} %convolution_add_fusion) | data formatting | bytes 2359296 | tf_op jit(solution)/shard_map/reshape | solution.py:18
  113.3 1.6 copy-done.1
  114.9 0.1 slice_bitcast_fusion.2
  115.0 0.1 scatter-add.10
  115.1 1.5 fusion.6
  116.6 2.0 %scatter-add.11 = f32[66,48,32]{1,0,2:T(8,128)S(1)} dynamic-update-slice(f32[66,48,32]{1,0,2:T(8,128)S(1)} %scatter-add.10, f32[64,48,32]{1,0,2:T(8,128)S(1)} %fusion.6, s32[]{:T(128)} %constant.102.clone.1, s32[]{:T(128)} %constant.99.clone.1, s32[]{:T(128)} %constant.99.clone.1) | dynamic-update-slice | bytes 786436 | tf_op jit(solution)/shard_map/scatter-add | solution.py:21
  118.7 0.0 copy-start.2
  118.7 0.0 copy-start.3
  118.7 0.0 copy-start.4
  118.7 1.5 fusion.5
  120.2 1.0 fusion.7
  121.8 1.0 multiply_reduce_fusion
  123.6 0.6 multiply_convert_fusion
  124.2 0.3 copy.40
  124.5 1.5 reshape.176
  126.0 7.8 %all-to-all-start = ((bf16[16,2,3072]{2,1,0:T(2,128)(2,1)}), bf16[16,2,3072]{2,1,0:T(2,128)(2,1)S(1)}, u32[]{:S(2)}, u32[]{:S(2)}) async-start(bf16[16,2,3072]{2,1,0:T(2,128)(2,1)} %reshape.176), calls=%async_computation | async-start | bytes 393216 | tf_op jit(solution)/shard_map/all_to_all | solution.py:56
  133.8 16.4 %all-to-all-done = bf16[16,2,3072]{2,1,0:T(2,128)(2,1)S(1)} async-done(((bf16[16,2,3072]{2,1,0:T(2,128)(2,1)}), bf16[16,2,3072]{2,1,0:T(2,128)(2,1)S(1)}, u32[]{:S(2)}, u32[]{:S(2)}) %all-to-all-start) | async-done | bytes 196640 | tf_op jit(solution)/shard_map/all_to_all | solution.py:56
  150.2 0.5 reshape.177
  150.7 0.6 copy.24
  151.4 0.7 all_gather.18
  152.1 5.0 %all_gather.19 = bf16[2,4,48,512]{3,2,1,0:T(8,128)(2,1)S(1)} all-gather(bf16[1,4,48,512]{3,2,1,0:T(8,128)(2,1)S(1)} %all_gather.18), channel_id=1, replica_groups=mesh['grp'=16,'z'=16,'core'=2] {'core'}, dimensions={0}, use_global_device_ids=true | all-gather | bytes 589824 | tf_op jit(solution)/shard_map/all_gather | solution.py:57
  157.1 0.9 reshape.168
  157.9 1.4 copy.25
  159.4 1.8 all-gather.6.cloned.1.call-done
  161.2 1.7 slice.119
  162.9 0.9 convert_reduce_fusion
  163.9 2.8 %reshape.161 = bf16[16,16,2,2,1024]{4,3,2,1,0:T(2,128)(2,1)} reshape(bf16[16,16,4096]{2,1,0:T(8,128)(2,1)S(1)} %slice.119) | data formatting | bytes 4194304 | tf_op jit(solution)/shard_map/reshape | solution.py:49
  166.6 2.8 %add_convert_fusion = bf16[16,16,2,2,4,48]{5,1,4,3,2,0:T(8,128)(2,1)S(1)} fusion(bf16[4,48,1024,1,1,1]{1,2,0,5,4,3:T(8,128)(2,1)S(1)} %bitcast.68, bf16[16,16,2,2,1024,1]{4,3,2,1,0,5:T(2,128)(2,1)} %bitcast.65, f32[16,16]{1,0:T(8,128)S(1)} %convert_reduce_fusion), kind=kOutput, calls=%fused_computation.6 | convolution fusion | flops 403046400 | bytes 2884608 | tf_op jit(solution)/shard_map/ijc,zoabc->iajbzo/dot_general | solution.py:62
  169.6 11.8 %collective-permute-start = (bf16[2,2,48,2,16,16]{2,5,0,3,1,4:T(8,128)(2,1)S(1)}, bf16[2,2,48,2,16,16]{2,5,0,3,1,4:T(8,128)(2,1)S(1)}, u32[]{:S(2)}, u32[]{:S(2)}) collective-permute-start(bf16[2,2,48,2,16,16]{2,5,0,3,1,4:T(8,128)(2,1)S(1)} %dynamic-slice_bitcast_fusion), channel_id=1, source_target_pairs={{0,1},{1,0},{2,3},{3,2},{4,5},{5,4},{6,7},{7,6},{8,9},{9,8},{10,11... | collective-permute-start | bytes 589832 | tf_op jit(solution)/shard_map/ppermute | solution.py:67
  181.4 1.5 collective-permute-done
  182.9 0.1 fusion.8
  183.0 1.2 pad_maximum_fusion
  184.2 6.7 %copy.28 = bf16[2,2,48,2,16,2,16]{6,5,4,3,2,1,0:T(2,128)(2,1)S(1)} copy(bf16[2,2,48,2,16,2,16]{2,6,0,3,1,4,5:T(8,128)(2,1)} %pad_maximum_fusion) | data formatting | bytes 786432 | tf_op jit(solution)/shard_map/stack | solution.py:70
  190.9 6.0 %reshape.170 = bf16[4,96,512]{2,1,0:T(8,128)(2,1)} reshape(bf16[2,2,48,2,16,2,16]{6,5,4,3,2,1,0:T(2,128)(2,1)S(1)} %copy.28) | data formatting | bytes 786432 | tf_op jit(solution)/shard_map/reshape | solution.py:71
  (6 shorter events, 0.1 us)
Async XLA Ops:
  6.5 85.6 %all-gather.4.cloned.1.call-start = ((), (), s32[]{:S(2)}) async-start(), calls=%async_computation.1 | async-start | bytes 6488064 | tf_op jit(solution)/shard_map/all_gather | solution.py:43
  7.3 153.9 %all-gather.6.cloned.1.call-start = ((), (), s32[]{:S(2)}) async-start(), calls=%async_computation.2 | async-start | bytes 2297856 | tf_op jit(solution)/shard_map/all_gather | solution.py:48
  102.9 2.8 %copy-start = (bf16[64,48,1024]{2,1,0:T(8,128)(2,1)S(1)}, bf16[64,48,1024]{2,1,0:T(8,128)(2,1)}, u32[]{:S(2)}) copy-start(bf16[64,48,1024]{2,1,0:T(8,128)(2,1)} %all-gather.4.cloned.1.call-done) | copy-start | bytes 18874372
  113.3 1.6 copy-start.1
  118.7 1.5 copy-start.2
  118.7 4.9 %copy-start.3 = (f32[32]{0:T(128)S(1)}, f32[32]{0:T(128)}, u32[]{:S(2)}) copy-start(f32[32]{0:T(128)} %param.17) | copy-start | bytes 388
  118.7 4.9 %copy-start.4 = (f32[32]{0:T(128)S(1)}, f32[32]{0:T(128)}, u32[]{:S(2)}) copy-start(f32[32]{0:T(128)} %param.16) | copy-start | bytes 388
  126.0 24.2 %all-to-all-start = ((bf16[16,2,3072]{2,1,0:T(2,128)(2,1)}), bf16[16,2,3072]{2,1,0:T(2,128)(2,1)S(1)}, u32[]{:S(2)}, u32[]{:S(2)}) async-start(bf16[16,2,3072]{2,1,0:T(2,128)(2,1)} %reshape.176), calls=%async_computation | async-start | bytes 393216 | tf_op jit(solution)/shard_map/all_to_all | solution.py:56
  169.6 13.3 %collective-permute-start = (bf16[2,2,48,2,16,16]{2,5,0,3,1,4:T(8,128)(2,1)S(1)}, bf16[2,2,48,2,16,16]{2,5,0,3,1,4:T(8,128)(2,1)S(1)}, u32[]{:S(2)}, u32[]{:S(2)}) collective-permute-start(bf16[2,2,48,2,16,16]{2,5,0,3,1,4:T(8,128)(2,1)S(1)} %dynamic-slice_bitcast_fusion), channel_id=1, source_target_pairs={{0,1},{1,0},{2,3},{3,2},{4,5},{5,4},{6,7},{7,6},{8,9},{9,8},{10,11... | collective-permute-start | bytes 589832 | tf_op jit(solution)/shard_map/ppermute | solution.py:67
Sparse Core Ops, SparseCore 0:
  9.5 82.6 all-gather.3
  94.2 66.9 all-gather.5

commit v3 on v2

--- a/solution.py
+++ b/solution.py
@@ -24,6 +24,22 @@
     return contrib
 
 
+def ring_gather(block, axis):
+    chips = lax.axis_size(axis)
+    step_up = [(i, (i - 1) % chips) for i in range(chips)]
+    step_down = [(i, (i + 1) % chips) for i in range(chips)]
+    ahead, behind = block, block
+    from_ahead, from_behind = [], []
+    for k in range(1, chips // 2 + 1):
+        ahead = lax.ppermute(ahead, axis, step_up)
+        from_ahead.append(ahead)
+        if k < chips - chips // 2:
+            behind = lax.ppermute(behind, axis, step_down)
+            from_behind.append(behind)
+    stacked = jnp.stack([block] + from_ahead + from_behind[::-1])
+    return jnp.roll(stacked, lax.axis_index(axis), axis=0)
+
+
 def normalize(convolved, norm_gain, norm_shift):
     height, width_cols, outputs = convolved.shape
     grouped = convolved.reshape(height, width_cols, outputs // GSIZE, GSIZE)
@@ -44,8 +60,7 @@
     height = whole.shape[0]
     flat = up_weight.reshape(slice_out, -1)
     packed = jnp.concatenate([flat, jnp.pad(up_bias[:, None], ((0, 0), (0, 127)))], axis=1)
-    packed, whole = lax.optimization_barrier((packed, whole))
-    packed_z = lax.all_gather(packed, "z", axis=0, tiled=False)
+    packed_z = ring_gather(packed, "z")
     weight_half = packed_z[:, :, : flat.shape[1]].reshape((chips, slice_out) + up_weight.shape[1:])
     bias_half = packed_z[:, :, flat.shape[1]].astype(jnp.float32)
 

time: 205 us -> 205 us (level); the launches traced: 204 us -> 201 us
  waiting for transfers between devices: 102 us -> 18.1 us
  starting transfers between devices: 19.7 us -> 72.3 us
  local copies, waits for them, and re-layouts: 43.9 us -> 66.7 us
  blocking collectives: 4.98 us -> 10.1 us
    all_gather x1, waiting for transfers between devices: 81.3 us -> 0.01 us  [body(): whole = lax.all_gather(coarse, ('z', 'core'), axis=0, tiled=True)]
    ppermute x0 -> x15, starting transfers between devices: none -> 59.8 us  [the longest x8 46.2 us: ring_gather(): ahead = lax.ppermute(ahead, axis, step_up)]
    unnamed x13 -> x42, local copies, waits for them, and re-layouts: 5.1 us -> 24.2 us
    ppermute x0 -> x15, waiting for transfers between devices: none -> 10.3 us  [the longest x8 6.51 us: ring_gather(): ahead = lax.ppermute(ahead, axis, step_up)]
    all_to_all x1, waiting for transfers between devices: 16.4 us -> 6.3 us  [body(): lax.all_to_all(activated, 'z', split_axis=0, concat_axis=2, tiled=True)]
    ppermute x1, starting transfers between devices: 11.8 us -> 2.27 us  [body(): received = lax.ppermute(other, 'core', [(0, 1), (1, 0)])]
    all_gather x1, blocking collectives: 4.98 us -> 10.1 us  [body(): both = lax.all_gather(chip_rows, 'core', axis=0, tiled=False)]
    scatter-add x2, local copies, waits for them, and re-layouts: 2.17 us -> 5.18 us  [conv_rows(): contrib.at[2 - kernel_row:2 - kernel_row + how_many]]
  transfers between devices with their start and end apart: 4 -> 18, of which waited for: 4 -> 8; matrix products, arithmetic and copies ran while one was open for 18% -> 14% of each run, Pallas kernels for 0% -> 0%
where the time goes in v3:
time: 205 us; the launch traced here: 201 us
  starting transfers between devices  72.3 us (35%)
  local copies, waits for them, and re-layouts  66.7 us (33%)
  waiting for transfers between devices  18.1 us (9%)
  between operations  15.1 us (7%)
  blocking collectives  10.1 us (5%)
  matrix products  10 us (5%)
  other arithmetic  8.92 us (4%)
    ppermute x8, starting transfers between devices, ring_gather(): ahead = lax.ppermute(ahead, axis, step_up)  46.2 us
    unnamed x42, local copies, waits for them, and re-layouts  24.2 us
    ppermute x7, starting transfers between devices, ring_gather(): behind = lax.ppermute(behind, axis, step_down)  13.6 us
    slice x1, local copies, waits for them, and re-layouts, conv_rows(): padded[:, offset:offset + width_cols, :]  10.7 us
    all_to_all x1, starting transfers between devices, body(): lax.all_to_all(activated, 'z', split_axis=0, concat_axis=2, tiled=True)  10.3 us
    all_gather x1, blocking collectives, body(): both = lax.all_gather(chip_rows, 'core', axis=0, tiled=False)  10.1 us
    dot_general x3, matrix products, conv_rows(): jnp.dot(window, weights_cat[offset], preferred_element_type=jnp.float32)  7.2 us
    another operation x1, local copies, waits for them, and re-layouts, body(): fine = jnp.stack([low, high], axis=5)  6.69 us
  transfers between devices with their start and end apart: 18, of which 8 were waited for; matrix products, arithmetic and copies ran while one was open for 14% of the time, Pallas kernels for 0%

profile of v3, /device:TPU:1, one launch (start us, length us, event | category | flops | bytes accessed | tf_op | source)
XLA Modules:
  0.0 201.3 jit_solution(6216756522650430417)
XLA Ops:
  7.3 1.0 reshape.160
  8.3 12.0 %collective-permute-start = (bf16[16,4224]{1,0:T(8,128)(2,1)S(1)}, bf16[16,4224]{1,0:T(8,128)(2,1)S(1)}, u32[]{:S(2)}, u32[]{:S(2)}) collective-permute-start(bf16[16,4224]{1,0:T(8,128)(2,1)S(1)} %fusion.11), channel_id=1, source_target_pairs={{0,30},{2,0},{4,2},{6,4},{8,6},{10,8},{12,10},{14,12},{16,14},{18,... | collective-permute-start | bytes 405512 | tf_op jit(solution)/shard_map/ppermute | solution.py:34
  20.2 1.9 collective-permute-start.8
  22.9 1.2 fusion.12
  24.1 4.6 %collective-permute-start.1 = (bf16[16,4224]{1,0:T(8,128)(2,1)S(1)}, bf16[16,4224]{1,0:T(8,128)(2,1)S(1)}, u32[]{:S(2)}, u32[]{:S(2)}) collective-permute-start(bf16[16,4224]{1,0:T(8,128)(2,1)S(1)} %collective-permute-done), channel_id=1, source_target_pairs={{0,30},{2,0},{4,2},{6,4},{8,6},{10,8},{12,10},{14,12},{16,14},{18,... | collective-permute-start | bytes 405512 | tf_op jit(solution)/shard_map/ppermute | solution.py:34
  29.3 1.9 collective-permute-start.9
  31.2 4.6 %collective-permute-start.2 = (bf16[16,4224]{1,0:T(8,128)(2,1)S(1)}, bf16[16,4224]{1,0:T(8,128)(2,1)S(1)}, u32[]{:S(2)}, u32[]{:S(2)}) collective-permute-start(bf16[16,4224]{1,0:T(8,128)(2,1)S(1)} %collective-permute-done.1), channel_id=1, source_target_pairs={{0,30},{2,0},{4,2},{6,4},{8,6},{10,8},{12,10},{14,12},{16,14},{18,... | collective-permute-start | bytes 405512 | tf_op jit(solution)/shard_map/ppermute | solution.py:34
  36.5 1.9 collective-permute-start.10
  38.4 0.9 collective-permute-done.2
  39.3 5.4 %collective-permute-start.3 = (bf16[16,4224]{1,0:T(8,128)(2,1)S(1)}, bf16[16,4224]{1,0:T(8,128)(2,1)S(1)}, u32[]{:S(2)}, u32[]{:S(2)}) collective-permute-start(bf16[16,4224]{1,0:T(8,128)(2,1)S(1)} %collective-permute-done.2), channel_id=1, source_target_pairs={{0,30},{2,0},{4,2},{6,4},{8,6},{10,8},{12,10},{14,12},{16,14},{18,... | collective-permute-start | bytes 405512 | tf_op jit(solution)/shard_map/ppermute | solution.py:34
  45.4 1.9 collective-permute-start.11
  47.3 5.2 %collective-permute-start.4 = (bf16[16,4224]{1,0:T(8,128)(2,1)S(1)}, bf16[16,4224]{1,0:T(8,128)(2,1)S(1)}, u32[]{:S(2)}, u32[]{:S(2)}) collective-permute-start(bf16[16,4224]{1,0:T(8,128)(2,1)S(1)} %collective-permute-done.3), channel_id=1, source_target_pairs={{0,30},{2,0},{4,2},{6,4},{8,6},{10,8},{12,10},{14,12},{16,14},{18,... | collective-permute-start | bytes 405512 | tf_op jit(solution)/shard_map/ppermute | solution.py:34
  53.7 2.1 %collective-permute-start.12 = (bf16[16,4224]{1,0:T(8,128)(2,1)S(1)}, bf16[16,4224]{1,0:T(8,128)(2,1)S(1)}, u32[]{:S(2)}, u32[]{:S(2)}) collective-permute-start(bf16[16,4224]{1,0:T(8,128)(2,1)S(1)} %collective-permute-done.11), channel_id=1, source_target_pairs={{0,2},{2,4},{4,6},{6,8},{8,10},{10,12},{12,14},{14,16},{16,18},{18... | collective-permute-start | bytes 405512 | tf_op jit(solution)/shard_map/ppermute | solution.py:37
  55.9 4.5 %collective-permute-start.5 = (bf16[16,4224]{1,0:T(8,128)(2,1)S(1)}, bf16[16,4224]{1,0:T(8,128)(2,1)S(1)}, u32[]{:S(2)}, u32[]{:S(2)}) collective-permute-start(bf16[16,4224]{1,0:T(8,128)(2,1)S(1)} %collective-permute-done.4), channel_id=1, source_target_pairs={{0,30},{2,0},{4,2},{6,4},{8,6},{10,8},{12,10},{14,12},{16,14},{18,... | collective-permute-start | bytes 405512 | tf_op jit(solution)/shard_map/ppermute | solution.py:34
  61.0 1.5 collective-permute-done.12
  62.6 1.9 collective-permute-start.13
  64.5 4.6 %collective-permute-start.6 = (bf16[16,4224]{1,0:T(8,128)(2,1)S(1)}, bf16[16,4224]{1,0:T(8,128)(2,1)S(1)}, u32[]{:S(2)}, u32[]{:S(2)}) collective-permute-start(bf16[16,4224]{1,0:T(8,128)(2,1)S(1)} %collective-permute-done.5), channel_id=1, source_target_pairs={{0,30},{2,0},{4,2},{6,4},{8,6},{10,8},{12,10},{14,12},{16,14},{18,... | collective-permute-start | bytes 405512 | tf_op jit(solution)/shard_map/ppermute | solution.py:34
  69.7 1.7 collective-permute-done.13
  71.4 1.9 collective-permute-start.14
  73.3 1.0 collective-permute-done.6
  74.3 5.4 %collective-permute-start.7 = (bf16[16,4224]{1,0:T(8,128)(2,1)S(1)}, bf16[16,4224]{1,0:T(8,128)(2,1)S(1)}, u32[]{:S(2)}, u32[]{:S(2)}) collective-permute-start(bf16[16,4224]{1,0:T(8,128)(2,1)S(1)} %collective-permute-done.6), channel_id=1, source_target_pairs={{0,30},{2,0},{4,2},{6,4},{8,6},{10,8},{12,10},{14,12},{16,14},{18,... | collective-permute-start | bytes 405512 | tf_op jit(solution)/shard_map/ppermute | solution.py:34
  80.4 4.6 %collective-permute-done.7 = bf16[16,4224]{1,0:T(8,128)(2,1)S(1)} collective-permute-done((bf16[16,4224]{1,0:T(8,128)(2,1)S(1)}, bf16[16,4224]{1,0:T(8,128)(2,1)S(1)}, u32[]{:S(2)}, u32[]{:S(2)}) %collective-permute-start.7) | collective-permute-done | bytes 135200 | tf_op jit(solution)/shard_map/ppermute | solution.py:34
  100.3 10.7 %pad_slice_fusion = (bf16[64,48,1024]{2,1,0:T(8,128)(2,1)S(1)}, bf16[64,48,1024]{2,1,0:T(8,128)(2,1)S(1)}) fusion(bf16[64,48,1024]{2,1,0:T(8,128)(2,1)} %all-gather.2.cloned.1.call-done), kind=kLoop, calls=%fused_computation | loop fusion | bytes 18874368 | tf_op jit(solution)/shard_map/slice | solution.py:14
  111.0 2.0 %fusion.13 = f32[3072,96]{0,1:T(8,128)S(1)} fusion(bf16[3072,1024]{1,0:T(8,128)(2,1)S(1)} %bitcast.107, bf16[1024,96]{0,1:T(8,128)(2,1)S(1)} %bitcast.116), kind=kOutput, calls=%fused_computation.62 | convolution fusion | flops 603979776 | bytes 7667712 | tf_op jit(solution)/shard_map/dot_general | solution.py:15
  113.8 2.0 %convolution_add_fusion.1 = f32[3072,96]{0,1:T(8,128)S(1)} fusion(f32[3072,96]{0,1:T(8,128)S(1)} %fusion.13, bf16[3072,1024]{1,0:T(8,128)(2,1)S(1)} %bitcast.105, bf16[1024,96]{0,1:T(8,128)(2,1)S(1)} %bitcast.115), kind=kOutput, calls=%fused_computation.3 | convolution fusion | flops 604274688 | bytes 8847360 | tf_op jit(solution)/shard_map/dot_general | solution.py:15
  115.9 3.1 %convolution_add_fusion = f32[3072,96]{0,1:T(8,128)} fusion(f32[3072,96]{0,1:T(8,128)S(1)} %convolution_add_fusion.1, bf16[3072,1024]{1,0:T(8,128)(2,1)S(1)} %bitcast.106, bf16[1024,96]{0,1:T(8,128)(2,1)S(1)} %bitcast.114), kind=kOutput, calls=%fused_computation.2 | convolution fusion | flops 604274688 | bytes 8847360 | tf_op jit(solution)/shard_map/dot_general | solution.py:15
  119.0 2.4 %reshape.165 = f32[64,48,3,32]{1,0,3,2:T(8,128)S(1)} reshape(f32[3072,96]{0,1:T(8,128)} %convolution_add_fusion) | data formatting | bytes 2359296 | tf_op jit(solution)/shard_map/reshape | solution.py:18
  121.5 1.6 copy-done.1
  123.1 1.2 fusion.6
  124.4 5.1 %scatter-add.11 = f32[66,48,32]{1,0,2:T(8,128)S(1)} dynamic-update-slice(f32[66,48,32]{1,0,2:T(8,128)S(1)} %scatter-add.10, f32[64,48,32]{1,0,2:T(8,128)} %fusion.6, s32[]{:T(128)} %constant.127.clone.1, s32[]{:T(128)} %constant.120.clone.1, s32[]{:T(128)} %constant.120.clone.1) | dynamic-update-slice | bytes 786436 | tf_op jit(solution)/shard_map/scatter-add | solution.py:21
  129.5 1.5 fusion.5
  131.0 1.0 fusion.7
  132.6 1.0 multiply_reduce_fusion
  135.3 1.5 reshape.175
  136.8 10.3 %all-to-all-start = ((bf16[16,2,3072]{2,1,0:T(2,128)(2,1)}), bf16[16,2,3072]{2,1,0:T(2,128)(2,1)S(1)}, u32[]{:S(2)}, u32[]{:S(2)}) async-start(bf16[16,2,3072]{2,1,0:T(2,128)(2,1)} %reshape.175), calls=%async_computation | async-start | bytes 393216 | tf_op jit(solution)/shard_map/all_to_all | solution.py:71
  147.7 1.7 constant_dynamic-slice_fusion
  149.4 2.8 %reshape.161 = bf16[16,16,2,2,1024]{4,3,2,1,0:T(2,128)(2,1)} reshape(bf16[16,16,4096]{2,1,0:T(8,128)(2,1)S(1)} %constant_dynamic-slice_fusion) | data formatting | bytes 4194304 | tf_op jit(solution)/shard_map/reshape | solution.py:64
  152.2 0.9 convert_reduce_fusion
  153.2 6.3 %all-to-all-done = bf16[16,2,3072]{2,1,0:T(2,128)(2,1)S(1)} async-done(((bf16[16,2,3072]{2,1,0:T(2,128)(2,1)}), bf16[16,2,3072]{2,1,0:T(2,128)(2,1)S(1)}, u32[]{:S(2)}, u32[]{:S(2)}) %all-to-all-start) | async-done | bytes 196640 | tf_op jit(solution)/shard_map/all_to_all | solution.py:71
  161.3 10.1 %all_gather.11 = bf16[2,4,48,512]{3,2,1,0:T(8,128)(2,1)S(1)} all-gather(bf16[1,4,48,512]{3,2,1,0:T(8,128)(2,1)S(1)} %all_gather.10), channel_id=1, replica_groups=mesh['grp'=16,'z'=16,'core'=2] {'core'}, dimensions={0}, use_global_device_ids=true | all-gather | bytes 589824 | tf_op jit(solution)/shard_map/all_gather | solution.py:72
  171.4 0.9 reshape.168
  172.3 1.4 copy.54
  173.7 2.8 %add_convert_fusion = bf16[16,16,2,2,4,48]{5,1,4,3,2,0:T(8,128)(2,1)S(1)} fusion(bf16[4,48,1024,1,1,1]{1,2,0,5,4,3:T(8,128)(2,1)S(1)} %bitcast.113, bf16[16,16,2,2,1024,1]{4,3,2,1,0,5:T(2,128)(2,1)} %bitcast.110, f32[16,16]{1,0:T(8,128)S(1)} %convert_reduce_fusion), kind=kOutput, calls=%fused_computation.6 | convolution fusion | flops 403046400 | bytes 2884608 | tf_op jit(solution)/shard_map/ijc,zoabc->iajbzo/dot_general | solution.py:77
  176.6 2.3 %collective-permute-start.15 = (bf16[2,2,48,2,16,16]{2,5,0,3,1,4:T(8,128)(2,1)S(1)}, bf16[2,2,48,2,16,16]{2,5,0,3,1,4:T(8,128)(2,1)S(1)}, u32[]{:S(2)}, u32[]{:S(2)}) collective-permute-start(bf16[2,2,48,2,16,16]{2,5,0,3,1,4:T(8,128)(2,1)S(1)} %dynamic-slice_bitcast_fusion), channel_id=1, source_target_pairs={{0,1},{1,0},{2,3},{3,2},{4,5},{5,4},{6,7},{7,6},{8,9},{9,8},{10,11... | collective-permute-start | bytes 589832 | tf_op jit(solution)/shard_map/ppermute | solution.py:82
  178.9 1.5 collective-permute-done.15
  180.5 1.2 pad_maximum_fusion
  181.8 6.7 %copy.57 = bf16[2,2,48,2,16,2,16]{6,5,4,3,2,1,0:T(2,128)(2,1)S(1)} copy(bf16[2,2,48,2,16,2,16]{2,6,0,3,1,4,5:T(8,128)(2,1)} %pad_maximum_fusion) | data formatting | bytes 786432 | tf_op jit(solution)/shard_map/stack | solution.py:85
  188.4 6.0 %reshape.170 = bf16[4,96,512]{2,1,0:T(8,128)(2,1)} reshape(bf16[2,2,48,2,16,2,16]{6,5,4,3,2,1,0:T(2,128)(2,1)S(1)} %copy.57) | data formatting | bytes 786432 | tf_op jit(solution)/shard_map/reshape | solution.py:86
  (65 shorter events, 26.5 us)
Async XLA Ops:
  6.5 93.7 %all-gather.2.cloned.1.call-start = ((), (), s32[]{:S(2)}) async-start(), calls=%async_computation.1 | async-start | bytes 6488064 | tf_op jit(solution)/shard_map/all_gather | solution.py:59
  8.3 15.8 %collective-permute-start = (bf16[16,4224]{1,0:T(8,128)(2,1)S(1)}, bf16[16,4224]{1,0:T(8,128)(2,1)S(1)}, u32[]{:S(2)}, u32[]{:S(2)}) collective-permute-start(bf16[16,4224]{1,0:T(8,128)(2,1)S(1)} %fusion.11), channel_id=1, source_target_pairs={{0,30},{2,0},{4,2},{6,4},{8,6},{10,8},{12,10},{14,12},{16,14},{18,... | collective-permute-start | bytes 405512 | tf_op jit(solution)/shard_map/ppermute | solution.py:34
  20.2 9.1 %collective-permute-start.8 = (bf16[16,4224]{1,0:T(8,128)(2,1)S(1)}, bf16[16,4224]{1,0:T(8,128)(2,1)S(1)}, u32[]{:S(2)}, u32[]{:S(2)}) collective-permute-start(bf16[16,4224]{1,0:T(8,128)(2,1)S(1)} %fusion.11), channel_id=1, source_target_pairs={{0,2},{2,4},{4,6},{6,8},{8,10},{10,12},{12,14},{14,16},{16,18},{18... | collective-permute-start | bytes 405512 | tf_op jit(solution)/shard_map/ppermute | solution.py:37
  24.1 7.2 %collective-permute-start.1 = (bf16[16,4224]{1,0:T(8,128)(2,1)S(1)}, bf16[16,4224]{1,0:T(8,128)(2,1)S(1)}, u32[]{:S(2)}, u32[]{:S(2)}) collective-permute-start(bf16[16,4224]{1,0:T(8,128)(2,1)S(1)} %collective-permute-done), channel_id=1, source_target_pairs={{0,30},{2,0},{4,2},{6,4},{8,6},{10,8},{12,10},{14,12},{16,14},{18,... | collective-permute-start | bytes 405512 | tf_op jit(solution)/shard_map/ppermute | solution.py:34
  29.3 7.2 %collective-permute-start.9 = (bf16[16,4224]{1,0:T(8,128)(2,1)S(1)}, bf16[16,4224]{1,0:T(8,128)(2,1)S(1)}, u32[]{:S(2)}, u32[]{:S(2)}) collective-permute-start(bf16[16,4224]{1,0:T(8,128)(2,1)S(1)} %collective-permute-done.8), channel_id=1, source_target_pairs={{0,2},{2,4},{4,6},{6,8},{8,10},{10,12},{12,14},{14,16},{16,18},{18... | collective-permute-start | bytes 405512 | tf_op jit(solution)/shard_map/ppermute | solution.py:37
  31.2 8.1 %collective-permute-start.2 = (bf16[16,4224]{1,0:T(8,128)(2,1)S(1)}, bf16[16,4224]{1,0:T(8,128)(2,1)S(1)}, u32[]{:S(2)}, u32[]{:S(2)}) collective-permute-start(bf16[16,4224]{1,0:T(8,128)(2,1)S(1)} %collective-permute-done.1), channel_id=1, source_target_pairs={{0,30},{2,0},{4,2},{6,4},{8,6},{10,8},{12,10},{14,12},{16,14},{18,... | collective-permute-start | bytes 405512 | tf_op jit(solution)/shard_map/ppermute | solution.py:34
  36.5 8.9 %collective-permute-start.10 = (bf16[16,4224]{1,0:T(8,128)(2,1)S(1)}, bf16[16,4224]{1,0:T(8,128)(2,1)S(1)}, u32[]{:S(2)}, u32[]{:S(2)}) collective-permute-start(bf16[16,4224]{1,0:T(8,128)(2,1)S(1)} %collective-permute-done.9), channel_id=1, source_target_pairs={{0,2},{2,4},{4,6},{6,8},{8,10},{10,12},{12,14},{14,16},{16,18},{18... | collective-permute-start | bytes 405512 | tf_op jit(solution)/shard_map/ppermute | solution.py:37
  39.3 8.0 %collective-permute-start.3 = (bf16[16,4224]{1,0:T(8,128)(2,1)S(1)}, bf16[16,4224]{1,0:T(8,128)(2,1)S(1)}, u32[]{:S(2)}, u32[]{:S(2)}) collective-permute-start(bf16[16,4224]{1,0:T(8,128)(2,1)S(1)} %collective-permute-done.2), channel_id=1, source_target_pairs={{0,30},{2,0},{4,2},{6,4},{8,6},{10,8},{12,10},{14,12},{16,14},{18,... | collective-permute-start | bytes 405512 | tf_op jit(solution)/shard_map/ppermute | solution.py:34
  45.4 8.4 %collective-permute-start.11 = (bf16[16,4224]{1,0:T(8,128)(2,1)S(1)}, bf16[16,4224]{1,0:T(8,128)(2,1)S(1)}, u32[]{:S(2)}, u32[]{:S(2)}) collective-permute-start(bf16[16,4224]{1,0:T(8,128)(2,1)S(1)} %collective-permute-done.10), channel_id=1, source_target_pairs={{0,2},{2,4},{4,6},{6,8},{8,10},{10,12},{12,14},{14,16},{16,18},{18... | collective-permute-start | bytes 405512 | tf_op jit(solution)/shard_map/ppermute | solution.py:37
  47.3 8.6 %collective-permute-start.4 = (bf16[16,4224]{1,0:T(8,128)(2,1)S(1)}, bf16[16,4224]{1,0:T(8,128)(2,1)S(1)}, u32[]{:S(2)}, u32[]{:S(2)}) collective-permute-start(bf16[16,4224]{1,0:T(8,128)(2,1)S(1)} %collective-permute-done.3), channel_id=1, source_target_pairs={{0,30},{2,0},{4,2},{6,4},{8,6},{10,8},{12,10},{14,12},{16,14},{18,... | collective-permute-start | bytes 405512 | tf_op jit(solution)/shard_map/ppermute | solution.py:34
  53.7 8.8 %collective-permute-start.12 = (bf16[16,4224]{1,0:T(8,128)(2,1)S(1)}, bf16[16,4224]{1,0:T(8,128)(2,1)S(1)}, u32[]{:S(2)}, u32[]{:S(2)}) collective-permute-start(bf16[16,4224]{1,0:T(8,128)(2,1)S(1)} %collective-permute-done.11), channel_id=1, source_target_pairs={{0,2},{2,4},{4,6},{6,8},{8,10},{10,12},{12,14},{14,16},{16,18},{18... | collective-permute-start | bytes 405512 | tf_op jit(solution)/shard_map/ppermute | solution.py:37
  55.9 8.6 %collective-permute-start.5 = (bf16[16,4224]{1,0:T(8,128)(2,1)S(1)}, bf16[16,4224]{1,0:T(8,128)(2,1)S(1)}, u32[]{:S(2)}, u32[]{:S(2)}) collective-permute-start(bf16[16,4224]{1,0:T(8,128)(2,1)S(1)} %collective-permute-done.4), channel_id=1, source_target_pairs={{0,30},{2,0},{4,2},{6,4},{8,6},{10,8},{12,10},{14,12},{16,14},{18,... | collective-permute-start | bytes 405512 | tf_op jit(solution)/shard_map/ppermute | solution.py:34
  62.6 8.8 %collective-permute-start.13 = (bf16[16,4224]{1,0:T(8,128)(2,1)S(1)}, bf16[16,4224]{1,0:T(8,128)(2,1)S(1)}, u32[]{:S(2)}, u32[]{:S(2)}) collective-permute-start(bf16[16,4224]{1,0:T(8,128)(2,1)S(1)} %collective-permute-done.12), channel_id=1, source_target_pairs={{0,2},{2,4},{4,6},{6,8},{8,10},{10,12},{12,14},{14,16},{16,18},{18... | collective-permute-start | bytes 405512 | tf_op jit(solution)/shard_map/ppermute | solution.py:37
  64.5 9.9 %collective-permute-start.6 = (bf16[16,4224]{1,0:T(8,128)(2,1)S(1)}, bf16[16,4224]{1,0:T(8,128)(2,1)S(1)}, u32[]{:S(2)}, u32[]{:S(2)}) collective-permute-start(bf16[16,4224]{1,0:T(8,128)(2,1)S(1)} %collective-permute-done.5), channel_id=1, source_target_pairs={{0,30},{2,0},{4,2},{6,4},{8,6},{10,8},{12,10},{14,12},{16,14},{18,... | collective-permute-start | bytes 405512 | tf_op jit(solution)/shard_map/ppermute | solution.py:34
  71.4 14.3 %collective-permute-start.14 = (bf16[16,4224]{1,0:T(8,128)(2,1)S(1)}, bf16[16,4224]{1,0:T(8,128)(2,1)S(1)}, u32[]{:S(2)}, u32[]{:S(2)}) collective-permute-start(bf16[16,4224]{1,0:T(8,128)(2,1)S(1)} %collective-permute-done.13), channel_id=1, source_target_pairs={{0,2},{2,4},{4,6},{6,8},{8,10},{10,12},{12,14},{14,16},{16,18},{18... | collective-permute-start | bytes 405512 | tf_op jit(solution)/shard_map/ppermute | solution.py:37
  74.3 10.7 %collective-permute-start.7 = (bf16[16,4224]{1,0:T(8,128)(2,1)S(1)}, bf16[16,4224]{1,0:T(8,128)(2,1)S(1)}, u32[]{:S(2)}, u32[]{:S(2)}) collective-permute-start(bf16[16,4224]{1,0:T(8,128)(2,1)S(1)} %collective-permute-done.6), channel_id=1, source_target_pairs={{0,30},{2,0},{4,2},{6,4},{8,6},{10,8},{12,10},{14,12},{16,14},{18,... | collective-permute-start | bytes 405512 | tf_op jit(solution)/shard_map/ppermute | solution.py:34
  111.0 2.8 %copy-start = (bf16[64,48,1024]{2,1,0:T(8,128)(2,1)S(1)}, bf16[64,48,1024]{2,1,0:T(8,128)(2,1)}, u32[]{:S(2)}) copy-start(bf16[64,48,1024]{2,1,0:T(8,128)(2,1)} %all-gather.2.cloned.1.call-done) | copy-start | bytes 18874372
  121.4 1.7 copy-start.1
  124.3 6.7 %copy-start.2 = (f32[32]{0:T(128)S(1)}, f32[32]{0:T(128)}, u32[]{:S(2)}) copy-start(f32[32]{0:T(128)} %param.15) | copy-start | bytes 388
  124.3 10.0 %copy-start.3 = (f32[32]{0:T(128)S(1)}, f32[32]{0:T(128)}, u32[]{:S(2)}) copy-start(f32[32]{0:T(128)} %param.17) | copy-start | bytes 388
  124.3 10.0 %copy-start.4 = (f32[32]{0:T(128)S(1)}, f32[32]{0:T(128)}, u32[]{:S(2)}) copy-start(f32[32]{0:T(128)} %param.16) | copy-start | bytes 388
  136.8 22.7 %all-to-all-start = ((bf16[16,2,3072]{2,1,0:T(2,128)(2,1)}), bf16[16,2,3072]{2,1,0:T(2,128)(2,1)S(1)}, u32[]{:S(2)}, u32[]{:S(2)}) async-start(bf16[16,2,3072]{2,1,0:T(2,128)(2,1)} %reshape.175), calls=%async_computation | async-start | bytes 393216 | tf_op jit(solution)/shard_map/all_to_all | solution.py:71
  176.6 3.8 %collective-permute-start.15 = (bf16[2,2,48,2,16,16]{2,5,0,3,1,4:T(8,128)(2,1)S(1)}, bf16[2,2,48,2,16,16]{2,5,0,3,1,4:T(8,128)(2,1)S(1)}, u32[]{:S(2)}, u32[]{:S(2)}) collective-permute-start(bf16[2,2,48,2,16,16]{2,5,0,3,1,4:T(8,128)(2,1)S(1)} %dynamic-slice_bitcast_fusion), channel_id=1, source_target_pairs={{0,1},{1,0},{2,3},{3,2},{4,5},{5,4},{6,7},{7,6},{8,9},{9,8},{10,11... | collective-permute-start | bytes 589832 | tf_op jit(solution)/shard_map/ppermute | solution.py:82
Sparse Core Ops, SparseCore 0:
  22.3 77.8 all-gather.1

commit v4 on v3

--- a/solution.py
+++ b/solution.py
@@ -1,27 +1,62 @@
+import functools
+
 import jax
 import jax.numpy as jnp
 from jax import lax
+from jax.experimental import pallas as pl
+from jax.experimental.pallas import tpu as pltpu
 from jax.sharding import Mesh, PartitionSpec as P
 
 GSIZE = 32
 
 
-def conv_rows(weights_cat, width_cols, channels, outputs, tile_rows):
-    how_many = tile_rows.shape[0]
-    padded = jnp.pad(tile_rows, ((0, 0), (1, 1), (0, 0)))
-    partial_sum = jnp.zeros((how_many * width_cols, 3 * outputs), jnp.float32)
-    for offset in range(3):
-        window = padded[:, offset : offset + width_cols, :].reshape(how_many * width_cols, channels)
-        partial_sum = partial_sum + jnp.dot(
-            window, weights_cat[offset], preferred_element_type=jnp.float32
-        )
-    partial_sum = partial_sum.reshape(how_many, width_cols, 3, outputs)
-    contrib = jnp.zeros((how_many + 2, width_cols, outputs), jnp.float32)
-    for kernel_row in range(3):
-        contrib = contrib.at[2 - kernel_row : 2 - kernel_row + how_many].add(
-            partial_sum[:, :, kernel_row]
-        )
-    return contrib
+def conv_norm_kernel(x_ref, w_ref, bias_ref, gain_ref, shift_ref, out_ref, *, height, width_cols):
+    outputs = out_ref.shape[0]
+    positions = height * width_cols
+    taps = lax.dot_general(w_ref[...], x_ref[...], (((1,), (1,)), ((), ())),
+                           preferred_element_type=jnp.float32)
+    pos = lax.broadcasted_iota(jnp.int32, (1, positions), 1)
+    row = pos // width_cols
+    col = pos % width_cols
+    acc = jnp.zeros((outputs, positions), jnp.float32)
+    for t in range(9):
+        r, s = divmod(t, 3)
+        off = (r - 1) * width_cols + (s - 1)
+        part = taps[t * outputs:(t + 1) * outputs, :]
+        if off:
+            part = pltpu.roll(part, (-off) % positions, 1)
+        valid = ((row + (r - 1) >= 0) & (row + (r - 1) < height)
+                 & (col + (s - 1) >= 0) & (col + (s - 1) < width_cols))
+        acc = acc + jnp.where(valid, part, 0.0)
+    conv = acc + bias_ref[...]
+    groups = outputs // GSIZE
+    grouped = conv.reshape(groups, GSIZE, positions)
+    count = GSIZE * positions
+    centre = jnp.sum(jnp.sum(grouped, axis=2, keepdims=True), axis=1, keepdims=True) / count
+    dev = grouped - centre
+    spread = jnp.sum(jnp.sum(dev * dev, axis=2, keepdims=True), axis=1, keepdims=True) / count
+    normed = (dev * lax.rsqrt(spread + 1e-05)).reshape(outputs, positions)
+    v = normed * gain_ref[...] + shift_ref[...]
+    out_ref[...] = (v / (1.0 + jnp.exp(-v))).astype(out_ref.dtype)
+
+
+def conv_norm(whole, conv_weight, conv_bias, norm_gain, norm_shift):
+    height, width_cols, channels = whole.shape
+    outputs = conv_weight.shape[0]
+    x = whole.reshape(height * width_cols, channels)
+    w = jnp.transpose(conv_weight.reshape(outputs, 9, channels), (1, 0, 2)).reshape(9 * outputs, channels)
+    col = lambda v: v.astype(jnp.float32).reshape(outputs, 1)
+    vmem = pl.BlockSpec(memory_space=pltpu.VMEM)
+    return pl.pallas_call(
+        functools.partial(conv_norm_kernel, height=height, width_cols=width_cols),
+        out_shape=jax.ShapeDtypeStruct((outputs, height * width_cols), jnp.bfloat16),
+        in_specs=[vmem] * 5,
+        out_specs=vmem,
+        cost_estimate=pl.CostEstimate(
+            flops=2 * height * width_cols * channels * 9 * outputs,
+            transcendentals=height * width_cols * outputs,
+            bytes_accessed=x.size * 2 + w.size * 2 + outputs * height * width_cols * 2),
+    )(x, w, col(conv_bias), col(norm_gain), col(norm_shift))
 
 
 def ring_gather(block, axis):
@@ -40,15 +75,6 @@
     return jnp.roll(stacked, lax.axis_index(axis), axis=0)
 
 
-def normalize(convolved, norm_gain, norm_shift):
-    height, width_cols, outputs = convolved.shape
-    grouped = convolved.reshape(height, width_cols, outputs // GSIZE, GSIZE)
-    centre = jnp.mean(grouped, axis=(0, 1, 3), keepdims=True)
-    spread = jnp.mean(jnp.square(grouped - centre), axis=(0, 1, 3), keepdims=True)
-    normed = ((grouped - centre) * lax.rsqrt(spread + 1e-05)).reshape(height, width_cols, outputs)
-    return jax.nn.silu(normed * norm_gain + norm_shift).astype(jnp.bfloat16)
-
-
 def body(coarse, conv_weight, conv_bias, norm_gain, norm_shift, up_weight, up_bias):
     chips = lax.axis_size("z")
     core = lax.axis_index("core")
@@ -64,9 +90,8 @@
     weight_half = packed_z[:, :, : flat.shape[1]].reshape((chips, slice_out) + up_weight.shape[1:])
     bias_half = packed_z[:, :, flat.shape[1]].astype(jnp.float32)
 
-    weights_cat = jnp.transpose(conv_weight, (2, 3, 1, 0)).reshape(3, channels, 3 * outputs)
-    summed = conv_rows(weights_cat, width_cols, channels, outputs, whole)
-    activated = normalize(summed[1 : height + 1] + conv_bias, norm_gain, norm_shift)
+    activated = conv_norm(whole, conv_weight, conv_bias, norm_gain, norm_shift)
+    activated = jnp.transpose(activated).reshape(height, width_cols, outputs)
 
     chip_rows = lax.all_to_all(activated, "z", split_axis=0, concat_axis=2, tiled=True)
     both = lax.all_gather(chip_rows, "core", axis=0, tiled=False)

time: 205 us -> 179 us (0.87)
  local copies, waits for them, and re-layouts: 66.7 us -> 50.4 us
  matrix products: 10 us -> 2.85 us
  Pallas kernels: 0 us -> 6.3 us
  other arithmetic: 8.92 us -> 3.6 us
  starting transfers between devices: 72.3 us -> 68.3 us
  waiting for transfers between devices: 18.1 us -> 22.1 us
    slice x2 -> x0, local copies, waits for them, and re-layouts: 11.9 us -> none  [the longest x1 10.7 us: conv_rows(): padded[:, offset:offset + width_cols, :]]
    dot_general x3 -> x0, matrix products: 7.2 us -> none  [conv_rows(): jnp.dot(window, weights_cat[offset], preferred_element_type=jnp.float32)]
    pallas_call x0 -> x1, Pallas kernels: none -> 6.3 us  [conv_norm(): pl.pallas_call(functools.partial(conv_norm_kernel, height=height, width_c...]
    scatter-add x2 -> x0, local copies, waits for them, and re-layouts: 5.18 us -> none  [conv_rows(): contrib.at[2 - kernel_row:2 - kernel_row + how_many]]
    ppermute x8, starting transfers between devices: 46.2 us -> 41.1 us  [ring_gather(): ahead = lax.ppermute(ahead, axis, step_up)]
    ppermute x8, waiting for transfers between devices: 6.51 us -> 10.6 us  [ring_gather(): ahead = lax.ppermute(ahead, axis, step_up)]
    reshape x1 -> x5, local copies, waits for them, and re-layouts: 2.43 us -> 5.78 us  [the longest x3 4 us: conv_norm(): col = lambda v: v.astype(jnp.float32).reshape(outputs, 1)]
    unnamed x42 -> x32, local copies, waits for them, and re-layouts: 24.2 us -> 22 us
  transfers between devices with their start and end apart: 18 -> 18, of which waited for: 8 -> 11; matrix products, arithmetic and copies ran while one was open for 14% -> 17% of each run, Pallas kernels for 0% -> 0%
where the time goes in v4:
time: 179 us; the launch traced here: 176 us
  starting transfers between devices  68.3 us (38%)
  local copies, waits for them, and re-layouts  50.4 us (28%)
  waiting for transfers between devices  22.1 us (12%)
  between operations  13.7 us (8%)
  blocking collectives  9.27 us (5%)
  Pallas kernels  6.3 us (4%)
  other arithmetic  3.6 us (2%)
  matrix products  2.85 us (2%)
    ppermute x8, starting transfers between devices, ring_gather(): ahead = lax.ppermute(ahead, axis, step_up)  41.1 us
    unnamed x32, local copies, waits for them, and re-layouts  22 us
    ppermute x7, starting transfers between devices, ring_gather(): behind = lax.ppermute(behind, axis, step_down)  13.4 us
    all_to_all x1, starting transfers between devices, body(): lax.all_to_all(activated, 'z', split_axis=0, concat_axis=2, tiled=True)  11.4 us
    ppermute x8, waiting for transfers between devices, ring_gather(): ahead = lax.ppermute(ahead, axis, step_up)  10.6 us
    all_gather x1, blocking collectives, body(): both = lax.all_gather(chip_rows, 'core', axis=0, tiled=False)  9.27 us
    another operation x1, local copies, waits for them, and re-layouts, body(): fine = jnp.stack([low, high], axis=5)  6.69 us
    pallas_call x1, Pallas kernels, conv_norm(): pl.pallas_call(functools.partial(conv_norm_kernel, height=height, width_c...  6.3 us
  transfers between devices with their start and end apart: 18, of which 11 were waited for; matrix products, arithmetic and copies ran while one was open for 17% of the time, Pallas kernels for 0%

profile of v4, /device:TPU:1, one launch (start us, length us, event | category | flops | bytes accessed | tf_op | source)
XLA Modules:
  0.0 176.4 jit_solution(10183762096593106986)
XLA Ops:
  6.5 1.0 reshape.44
  7.5 0.7 copy.75
  8.3 12.0 %collective-permute-start = (bf16[16,4224]{1,0:T(8,128)(2,1)S(1)}, bf16[16,4224]{1,0:T(8,128)(2,1)S(1)}, u32[]{:S(2)}, u32[]{:S(2)}) collective-permute-start(bf16[16,4224]{1,0:T(8,128)(2,1)S(1)} %fusion.7), channel_id=1, source_target_pairs={{0,30},{2,0},{4,2},{6,4},{8,6},{10,8},{12,10},{14,12},{16,14},{18,... | collective-permute-start | bytes 405512 | tf_op jit(solution)/shard_map/ppermute | solution.py:69
  20.2 1.9 %collective-permute-start.8 = (bf16[16,4224]{1,0:T(8,128)(2,1)S(1)}, bf16[16,4224]{1,0:T(8,128)(2,1)S(1)}, u32[]{:S(2)}, u32[]{:S(2)}) collective-permute-start(bf16[16,4224]{1,0:T(8,128)(2,1)S(1)} %fusion.7), channel_id=1, source_target_pairs={{0,2},{2,4},{4,6},{6,8},{8,10},{10,12},{12,14},{14,16},{16,18},{18... | collective-permute-start | bytes 405512 | tf_op jit(solution)/shard_map/ppermute | solution.py:72
  22.9 1.3 copy.61.bias_ref
  24.2 1.3 copy.62.gain_ref
  25.5 1.3 copy.63.shift_ref
  26.9 4.6 %collective-permute-start.1 = (bf16[16,4224]{1,0:T(8,128)(2,1)S(1)}, bf16[16,4224]{1,0:T(8,128)(2,1)S(1)}, u32[]{:S(2)}, u32[]{:S(2)}) collective-permute-start(bf16[16,4224]{1,0:T(8,128)(2,1)S(1)} %collective-permute-done), channel_id=1, source_target_pairs={{0,30},{2,0},{4,2},{6,4},{8,6},{10,8},{12,10},{14,12},{16,14},{18,... | collective-permute-start | bytes 405512 | tf_op jit(solution)/shard_map/ppermute | solution.py:69
  32.1 1.9 %collective-permute-start.9 = (bf16[16,4224]{1,0:T(8,128)(2,1)S(1)}, bf16[16,4224]{1,0:T(8,128)(2,1)S(1)}, u32[]{:S(2)}, u32[]{:S(2)}) collective-permute-start(bf16[16,4224]{1,0:T(8,128)(2,1)S(1)} %collective-permute-done.8), channel_id=1, source_target_pairs={{0,2},{2,4},{4,6},{6,8},{8,10},{10,12},{12,14},{14,16},{16,18},{18... | collective-permute-start | bytes 405512 | tf_op jit(solution)/shard_map/ppermute | solution.py:72
  34.0 4.6 %collective-permute-start.2 = (bf16[16,4224]{1,0:T(8,128)(2,1)S(1)}, bf16[16,4224]{1,0:T(8,128)(2,1)S(1)}, u32[]{:S(2)}, u32[]{:S(2)}) collective-permute-start(bf16[16,4224]{1,0:T(8,128)(2,1)S(1)} %collective-permute-done.1), channel_id=1, source_target_pairs={{0,30},{2,0},{4,2},{6,4},{8,6},{10,8},{12,10},{14,12},{16,14},{18,... | collective-permute-start | bytes 405512 | tf_op jit(solution)/shard_map/ppermute | solution.py:69
  39.3 1.9 %collective-permute-start.10 = (bf16[16,4224]{1,0:T(8,128)(2,1)S(1)}, bf16[16,4224]{1,0:T(8,128)(2,1)S(1)}, u32[]{:S(2)}, u32[]{:S(2)}) collective-permute-start(bf16[16,4224]{1,0:T(8,128)(2,1)S(1)} %collective-permute-done.9), channel_id=1, source_target_pairs={{0,2},{2,4},{4,6},{6,8},{8,10},{10,12},{12,14},{14,16},{16,18},{18... | collective-permute-start | bytes 405512 | tf_op jit(solution)/shard_map/ppermute | solution.py:72
  41.2 1.7 collective-permute-done.2
  42.9 2.9 %collective-permute-start.3 = (bf16[16,4224]{1,0:T(8,128)(2,1)S(1)}, bf16[16,4224]{1,0:T(8,128)(2,1)S(1)}, u32[]{:S(2)}, u32[]{:S(2)}) collective-permute-start(bf16[16,4224]{1,0:T(8,128)(2,1)S(1)} %collective-permute-done.2), channel_id=1, source_target_pairs={{0,30},{2,0},{4,2},{6,4},{8,6},{10,8},{12,10},{14,12},{16,14},{18,... | collective-permute-start | bytes 405512 | tf_op jit(solution)/shard_map/ppermute | solution.py:69
  46.4 1.2 collective-permute-done.10
  47.7 1.9 %collective-permute-start.11 = (bf16[16,4224]{1,0:T(8,128)(2,1)S(1)}, bf16[16,4224]{1,0:T(8,128)(2,1)S(1)}, u32[]{:S(2)}, u32[]{:S(2)}) collective-permute-start(bf16[16,4224]{1,0:T(8,128)(2,1)S(1)} %collective-permute-done.10), channel_id=1, source_target_pairs={{0,2},{2,4},{4,6},{6,8},{8,10},{10,12},{12,14},{14,16},{16,18},{18... | collective-permute-start | bytes 405512 | tf_op jit(solution)/shard_map/ppermute | solution.py:72
  49.6 2.2 %collective-permute-done.3 = bf16[16,4224]{1,0:T(8,128)(2,1)S(1)} collective-permute-done((bf16[16,4224]{1,0:T(8,128)(2,1)S(1)}, bf16[16,4224]{1,0:T(8,128)(2,1)S(1)}, u32[]{:S(2)}, u32[]{:S(2)}) %collective-permute-start.3) | collective-permute-done | bytes 135200 | tf_op jit(solution)/shard_map/ppermute | solution.py:69
  51.8 3.4 %collective-permute-start.4 = (bf16[16,4224]{1,0:T(8,128)(2,1)S(1)}, bf16[16,4224]{1,0:T(8,128)(2,1)S(1)}, u32[]{:S(2)}, u32[]{:S(2)}) collective-permute-start(bf16[16,4224]{1,0:T(8,128)(2,1)S(1)} %collective-permute-done.3), channel_id=1, source_target_pairs={{0,30},{2,0},{4,2},{6,4},{8,6},{10,8},{12,10},{14,12},{16,14},{18,... | collective-permute-start | bytes 405512 | tf_op jit(solution)/shard_map/ppermute | solution.py:69
  55.9 1.9 %collective-permute-start.12 = (bf16[16,4224]{1,0:T(8,128)(2,1)S(1)}, bf16[16,4224]{1,0:T(8,128)(2,1)S(1)}, u32[]{:S(2)}, u32[]{:S(2)}) collective-permute-start(bf16[16,4224]{1,0:T(8,128)(2,1)S(1)} %collective-permute-done.11), channel_id=1, source_target_pairs={{0,2},{2,4},{4,6},{6,8},{8,10},{10,12},{12,14},{14,16},{16,18},{18... | collective-permute-start | bytes 405512 | tf_op jit(solution)/shard_map/ppermute | solution.py:72
  57.9 2.4 %collective-permute-done.4 = bf16[16,4224]{1,0:T(8,128)(2,1)S(1)} collective-permute-done((bf16[16,4224]{1,0:T(8,128)(2,1)S(1)}, bf16[16,4224]{1,0:T(8,128)(2,1)S(1)}, u32[]{:S(2)}, u32[]{:S(2)}) %collective-permute-start.4) | collective-permute-done | bytes 135200 | tf_op jit(solution)/shard_map/ppermute | solution.py:69
  60.3 3.3 %collective-permute-start.5 = (bf16[16,4224]{1,0:T(8,128)(2,1)S(1)}, bf16[16,4224]{1,0:T(8,128)(2,1)S(1)}, u32[]{:S(2)}, u32[]{:S(2)}) collective-permute-start(bf16[16,4224]{1,0:T(8,128)(2,1)S(1)} %collective-permute-done.4), channel_id=1, source_target_pairs={{0,30},{2,0},{4,2},{6,4},{8,6},{10,8},{12,10},{14,12},{16,14},{18,... | collective-permute-start | bytes 405512 | tf_op jit(solution)/shard_map/ppermute | solution.py:69
  64.2 1.1 collective-permute-done.12
  65.4 1.9 %collective-permute-start.13 = (bf16[16,4224]{1,0:T(8,128)(2,1)S(1)}, bf16[16,4224]{1,0:T(8,128)(2,1)S(1)}, u32[]{:S(2)}, u32[]{:S(2)}) collective-permute-start(bf16[16,4224]{1,0:T(8,128)(2,1)S(1)} %collective-permute-done.12), channel_id=1, source_target_pairs={{0,2},{2,4},{4,6},{6,8},{8,10},{10,12},{12,14},{14,16},{16,18},{18... | collective-permute-start | bytes 405512 | tf_op jit(solution)/shard_map/ppermute | solution.py:72
  67.8 5.2 %collective-permute-start.6 = (bf16[16,4224]{1,0:T(8,128)(2,1)S(1)}, bf16[16,4224]{1,0:T(8,128)(2,1)S(1)}, u32[]{:S(2)}, u32[]{:S(2)}) collective-permute-start(bf16[16,4224]{1,0:T(8,128)(2,1)S(1)} %collective-permute-done.5), channel_id=1, source_target_pairs={{0,30},{2,0},{4,2},{6,4},{8,6},{10,8},{12,10},{14,12},{16,14},{18,... | collective-permute-start | bytes 405512 | tf_op jit(solution)/shard_map/ppermute | solution.py:69
  73.7 1.3 collective-permute-done.13
  75.0 1.9 %collective-permute-start.14 = (bf16[16,4224]{1,0:T(8,128)(2,1)S(1)}, bf16[16,4224]{1,0:T(8,128)(2,1)S(1)}, u32[]{:S(2)}, u32[]{:S(2)}) collective-permute-start(bf16[16,4224]{1,0:T(8,128)(2,1)S(1)} %collective-permute-done.13), channel_id=1, source_target_pairs={{0,2},{2,4},{4,6},{6,8},{8,10},{10,12},{12,14},{14,16},{16,18},{18... | collective-permute-start | bytes 405512 | tf_op jit(solution)/shard_map/ppermute | solution.py:72
  76.9 5.3 %collective-permute-start.7 = (bf16[16,4224]{1,0:T(8,128)(2,1)S(1)}, bf16[16,4224]{1,0:T(8,128)(2,1)S(1)}, u32[]{:S(2)}, u32[]{:S(2)}) collective-permute-start(bf16[16,4224]{1,0:T(8,128)(2,1)S(1)} %collective-permute-done.6), channel_id=1, source_target_pairs={{0,30},{2,0},{4,2},{6,4},{8,6},{10,8},{12,10},{14,12},{16,14},{18,... | collective-permute-start | bytes 405512 | tf_op jit(solution)/shard_map/ppermute | solution.py:69
  82.9 3.8 %collective-permute-done.7 = bf16[16,4224]{1,0:T(8,128)(2,1)S(1)} collective-permute-done((bf16[16,4224]{1,0:T(8,128)(2,1)S(1)}, bf16[16,4224]{1,0:T(8,128)(2,1)S(1)}, u32[]{:S(2)}, u32[]{:S(2)}) %collective-permute-start.7) | collective-permute-done | bytes 135200 | tf_op jit(solution)/shard_map/ppermute | solution.py:69
  89.3 0.7 bitcast_dynamic-update-slice_fusion.6
  90.0 0.7 bitcast_dynamic-update-slice_fusion.4
  100.6 0.7 bitcast_dynamic-update-slice_fusion.5
  102.0 6.3 %shard_map.73 = bf16[32,3072]{1,0:T(8,128)(2,1)} custom-call(bf16[3072,1024]{1,0:T(8,128)(2,1)} %bitcast.90, bf16[288,1024]{1,0:T(8,128)(2,1)} %bitcast.98, f32[32,1]{1,0:T(8,128)} %copy.61.bias_ref, f32[32,1]{1,0:T(8,128)} %copy.62.gain_ref, f32[32,1]{1,0:T(8,128)} %copy.63.shift_ref), custom_call_target="tpu_custom_call" | custom-call | flops 1811939328 | bytes 7077888 | tf_op jit(solution)/shard_map/pallas_call | solution.py:50
  108.3 1.4 reshape.52
  110.1 1.5 reshape.60
  111.5 11.4 %all-to-all-start = ((bf16[16,2,3072]{2,1,0:T(2,128)(2,1)}), bf16[16,2,3072]{2,1,0:T(2,128)(2,1)S(1)}, u32[]{:S(2)}, u32[]{:S(2)}) async-start(bf16[16,2,3072]{2,1,0:T(2,128)(2,1)} %reshape.60), calls=%async_computation | async-start | bytes 393216 | tf_op jit(solution)/shard_map/all_to_all | solution.py:96
  123.6 1.7 constant_dynamic-slice_fusion
  125.3 2.8 %reshape.45 = bf16[16,16,2,2,1024]{4,3,2,1,0:T(2,128)(2,1)} reshape(bf16[16,16,4096]{2,1,0:T(8,128)(2,1)S(1)} %constant_dynamic-slice_fusion) | data formatting | bytes 4194304 | tf_op jit(solution)/shard_map/reshape | solution.py:90
  128.1 0.9 convert_reduce_fusion
  129.1 6.3 %all-to-all-done = bf16[16,2,3072]{2,1,0:T(2,128)(2,1)S(1)} async-done(((bf16[16,2,3072]{2,1,0:T(2,128)(2,1)}), bf16[16,2,3072]{2,1,0:T(2,128)(2,1)S(1)}, u32[]{:S(2)}, u32[]{:S(2)}) %all-to-all-start) | async-done | bytes 196640 | tf_op jit(solution)/shard_map/all_to_all | solution.py:96
  136.5 0.7 all_gather.10
  137.3 9.3 %all_gather.11 = bf16[2,4,48,512]{3,2,1,0:T(8,128)(2,1)S(1)} all-gather(bf16[1,4,48,512]{3,2,1,0:T(8,128)(2,1)S(1)} %all_gather.10), channel_id=1, replica_groups=mesh['grp'=16,'z'=16,'core'=2] {'core'}, dimensions={0}, use_global_device_ids=true | all-gather | bytes 589824 | tf_op jit(solution)/shard_map/all_gather | solution.py:97
  146.5 0.9 reshape.53
  147.4 1.4 copy.66
  148.8 2.8 %add_convert_fusion = bf16[16,16,2,2,4,48]{5,1,4,3,2,0:T(8,128)(2,1)S(1)} fusion(bf16[4,48,1024,1,1,1]{1,2,0,5,4,3:T(8,128)(2,1)S(1)} %bitcast.96, bf16[16,16,2,2,1024,1]{4,3,2,1,0,5:T(2,128)(2,1)} %bitcast.93, f32[16,16]{1,0:T(8,128)S(1)} %convert_reduce_fusion), kind=kOutput, calls=%fused_computation.2 | convolution fusion | flops 403046400 | bytes 2884608 | tf_op jit(solution)/shard_map/ijc,zoabc->iajbzo/dot_general | solution.py:102
  151.7 2.5 %collective-permute-start.15 = (bf16[2,2,48,2,16,16]{2,5,0,3,1,4:T(8,128)(2,1)S(1)}, bf16[2,2,48,2,16,16]{2,5,0,3,1,4:T(8,128)(2,1)S(1)}, u32[]{:S(2)}, u32[]{:S(2)}) collective-permute-start(bf16[2,2,48,2,16,16]{2,5,0,3,1,4:T(8,128)(2,1)S(1)} %dynamic-slice_bitcast_fusion), channel_id=1, source_target_pairs={{0,1},{1,0},{2,3},{3,2},{4,5},{5,4},{6,7},{7,6},{8,9},{9,8},{10,11... | collective-permute-start | bytes 589832 | tf_op jit(solution)/shard_map/ppermute | solution.py:107
  154.2 1.3 collective-permute-done.15
  155.6 1.2 pad_maximum_fusion
  156.9 6.7 %copy.69 = bf16[2,2,48,2,16,2,16]{6,5,4,3,2,1,0:T(2,128)(2,1)S(1)} copy(bf16[2,2,48,2,16,2,16]{2,6,0,3,1,4,5:T(8,128)(2,1)} %pad_maximum_fusion) | data formatting | bytes 786432 | tf_op jit(solution)/shard_map/stack | solution.py:110
  163.6 6.0 %reshape.55 = bf16[4,96,512]{2,1,0:T(8,128)(2,1)} reshape(bf16[2,2,48,2,16,2,16]{6,5,4,3,2,1,0:T(2,128)(2,1)S(1)} %copy.69) | data formatting | bytes 786432 | tf_op jit(solution)/shard_map/reshape | solution.py:111
  (46 shorter events, 21.5 us)
Async XLA Ops:
  6.5 95.4 %all-gather.2.cloned.1.call-start = ((), (), s32[]{:S(2)}) async-start(), calls=%async_computation.1 | async-start | bytes 6488064 | tf_op jit(solution)/shard_map/all_gather | solution.py:85
  8.3 18.6 %collective-permute-start = (bf16[16,4224]{1,0:T(8,128)(2,1)S(1)}, bf16[16,4224]{1,0:T(8,128)(2,1)S(1)}, u32[]{:S(2)}, u32[]{:S(2)}) collective-permute-start(bf16[16,4224]{1,0:T(8,128)(2,1)S(1)} %fusion.7), channel_id=1, source_target_pairs={{0,30},{2,0},{4,2},{6,4},{8,6},{10,8},{12,10},{14,12},{16,14},{18,... | collective-permute-start | bytes 405512 | tf_op jit(solution)/shard_map/ppermute | solution.py:69
  20.2 11.9 %collective-permute-start.8 = (bf16[16,4224]{1,0:T(8,128)(2,1)S(1)}, bf16[16,4224]{1,0:T(8,128)(2,1)S(1)}, u32[]{:S(2)}, u32[]{:S(2)}) collective-permute-start(bf16[16,4224]{1,0:T(8,128)(2,1)S(1)} %fusion.7), channel_id=1, source_target_pairs={{0,2},{2,4},{4,6},{6,8},{8,10},{10,12},{12,14},{14,16},{16,18},{18... | collective-permute-start | bytes 405512 | tf_op jit(solution)/shard_map/ppermute | solution.py:72
  26.9 7.2 %collective-permute-start.1 = (bf16[16,4224]{1,0:T(8,128)(2,1)S(1)}, bf16[16,4224]{1,0:T(8,128)(2,1)S(1)}, u32[]{:S(2)}, u32[]{:S(2)}) collective-permute-start(bf16[16,4224]{1,0:T(8,128)(2,1)S(1)} %collective-permute-done), channel_id=1, source_target_pairs={{0,30},{2,0},{4,2},{6,4},{8,6},{10,8},{12,10},{14,12},{16,14},{18,... | collective-permute-start | bytes 405512 | tf_op jit(solution)/shard_map/ppermute | solution.py:69
  32.1 7.2 %collective-permute-start.9 = (bf16[16,4224]{1,0:T(8,128)(2,1)S(1)}, bf16[16,4224]{1,0:T(8,128)(2,1)S(1)}, u32[]{:S(2)}, u32[]{:S(2)}) collective-permute-start(bf16[16,4224]{1,0:T(8,128)(2,1)S(1)} %collective-permute-done.8), channel_id=1, source_target_pairs={{0,2},{2,4},{4,6},{6,8},{8,10},{10,12},{12,14},{14,16},{16,18},{18... | collective-permute-start | bytes 405512 | tf_op jit(solution)/shard_map/ppermute | solution.py:72
  34.0 8.9 %collective-permute-start.2 = (bf16[16,4224]{1,0:T(8,128)(2,1)S(1)}, bf16[16,4224]{1,0:T(8,128)(2,1)S(1)}, u32[]{:S(2)}, u32[]{:S(2)}) collective-permute-start(bf16[16,4224]{1,0:T(8,128)(2,1)S(1)} %collective-permute-done.1), channel_id=1, source_target_pairs={{0,30},{2,0},{4,2},{6,4},{8,6},{10,8},{12,10},{14,12},{16,14},{18,... | collective-permute-start | bytes 405512 | tf_op jit(solution)/shard_map/ppermute | solution.py:69
  39.3 8.4 %collective-permute-start.10 = (bf16[16,4224]{1,0:T(8,128)(2,1)S(1)}, bf16[16,4224]{1,0:T(8,128)(2,1)S(1)}, u32[]{:S(2)}, u32[]{:S(2)}) collective-permute-start(bf16[16,4224]{1,0:T(8,128)(2,1)S(1)} %collective-permute-done.9), channel_id=1, source_target_pairs={{0,2},{2,4},{4,6},{6,8},{8,10},{10,12},{12,14},{14,16},{16,18},{18... | collective-permute-start | bytes 405512 | tf_op jit(solution)/shard_map/ppermute | solution.py:72
  42.9 8.8 %collective-permute-start.3 = (bf16[16,4224]{1,0:T(8,128)(2,1)S(1)}, bf16[16,4224]{1,0:T(8,128)(2,1)S(1)}, u32[]{:S(2)}, u32[]{:S(2)}) collective-permute-start(bf16[16,4224]{1,0:T(8,128)(2,1)S(1)} %collective-permute-done.2), channel_id=1, source_target_pairs={{0,30},{2,0},{4,2},{6,4},{8,6},{10,8},{12,10},{14,12},{16,14},{18,... | collective-permute-start | bytes 405512 | tf_op jit(solution)/shard_map/ppermute | solution.py:69
  47.7 8.3 %collective-permute-start.11 = (bf16[16,4224]{1,0:T(8,128)(2,1)S(1)}, bf16[16,4224]{1,0:T(8,128)(2,1)S(1)}, u32[]{:S(2)}, u32[]{:S(2)}) collective-permute-start(bf16[16,4224]{1,0:T(8,128)(2,1)S(1)} %collective-permute-done.10), channel_id=1, source_target_pairs={{0,2},{2,4},{4,6},{6,8},{8,10},{10,12},{12,14},{14,16},{16,18},{18... | collective-permute-start | bytes 405512 | tf_op jit(solution)/shard_map/ppermute | solution.py:72
  51.8 8.5 %collective-permute-start.4 = (bf16[16,4224]{1,0:T(8,128)(2,1)S(1)}, bf16[16,4224]{1,0:T(8,128)(2,1)S(1)}, u32[]{:S(2)}, u32[]{:S(2)}) collective-permute-start(bf16[16,4224]{1,0:T(8,128)(2,1)S(1)} %collective-permute-done.3), channel_id=1, source_target_pairs={{0,30},{2,0},{4,2},{6,4},{8,6},{10,8},{12,10},{14,12},{16,14},{18,... | collective-permute-start | bytes 405512 | tf_op jit(solution)/shard_map/ppermute | solution.py:69
  55.9 9.4 %collective-permute-start.12 = (bf16[16,4224]{1,0:T(8,128)(2,1)S(1)}, bf16[16,4224]{1,0:T(8,128)(2,1)S(1)}, u32[]{:S(2)}, u32[]{:S(2)}) collective-permute-start(bf16[16,4224]{1,0:T(8,128)(2,1)S(1)} %collective-permute-done.11), channel_id=1, source_target_pairs={{0,2},{2,4},{4,6},{6,8},{8,10},{10,12},{12,14},{14,16},{16,18},{18... | collective-permute-start | bytes 405512 | tf_op jit(solution)/shard_map/ppermute | solution.py:72
  60.3 7.5 %collective-permute-start.5 = (bf16[16,4224]{1,0:T(8,128)(2,1)S(1)}, bf16[16,4224]{1,0:T(8,128)(2,1)S(1)}, u32[]{:S(2)}, u32[]{:S(2)}) collective-permute-start(bf16[16,4224]{1,0:T(8,128)(2,1)S(1)} %collective-permute-done.4), channel_id=1, source_target_pairs={{0,30},{2,0},{4,2},{6,4},{8,6},{10,8},{12,10},{14,12},{16,14},{18,... | collective-permute-start | bytes 405512 | tf_op jit(solution)/shard_map/ppermute | solution.py:69
  65.4 9.6 %collective-permute-start.13 = (bf16[16,4224]{1,0:T(8,128)(2,1)S(1)}, bf16[16,4224]{1,0:T(8,128)(2,1)S(1)}, u32[]{:S(2)}, u32[]{:S(2)}) collective-permute-start(bf16[16,4224]{1,0:T(8,128)(2,1)S(1)} %collective-permute-done.12), channel_id=1, source_target_pairs={{0,2},{2,4},{4,6},{6,8},{8,10},{10,12},{12,14},{14,16},{16,18},{18... | collective-permute-start | bytes 405512 | tf_op jit(solution)/shard_map/ppermute | solution.py:72
  67.8 9.2 %collective-permute-start.6 = (bf16[16,4224]{1,0:T(8,128)(2,1)S(1)}, bf16[16,4224]{1,0:T(8,128)(2,1)S(1)}, u32[]{:S(2)}, u32[]{:S(2)}) collective-permute-start(bf16[16,4224]{1,0:T(8,128)(2,1)S(1)} %collective-permute-done.5), channel_id=1, source_target_pairs={{0,30},{2,0},{4,2},{6,4},{8,6},{10,8},{12,10},{14,12},{16,14},{18,... | collective-permute-start | bytes 405512 | tf_op jit(solution)/shard_map/ppermute | solution.py:69
  75.0 12.3 %collective-permute-start.14 = (bf16[16,4224]{1,0:T(8,128)(2,1)S(1)}, bf16[16,4224]{1,0:T(8,128)(2,1)S(1)}, u32[]{:S(2)}, u32[]{:S(2)}) collective-permute-start(bf16[16,4224]{1,0:T(8,128)(2,1)S(1)} %collective-permute-done.13), channel_id=1, source_target_pairs={{0,2},{2,4},{4,6},{6,8},{8,10},{10,12},{12,14},{14,16},{16,18},{18... | collective-permute-start | bytes 405512 | tf_op jit(solution)/shard_map/ppermute | solution.py:72
  76.9 9.7 %collective-permute-start.7 = (bf16[16,4224]{1,0:T(8,128)(2,1)S(1)}, bf16[16,4224]{1,0:T(8,128)(2,1)S(1)}, u32[]{:S(2)}, u32[]{:S(2)}) collective-permute-start(bf16[16,4224]{1,0:T(8,128)(2,1)S(1)} %collective-permute-done.6), channel_id=1, source_target_pairs={{0,30},{2,0},{4,2},{6,4},{8,6},{10,8},{12,10},{14,12},{16,14},{18,... | collective-permute-start | bytes 405512 | tf_op jit(solution)/shard_map/ppermute | solution.py:69
  111.5 23.8 %all-to-all-start = ((bf16[16,2,3072]{2,1,0:T(2,128)(2,1)}), bf16[16,2,3072]{2,1,0:T(2,128)(2,1)S(1)}, u32[]{:S(2)}, u32[]{:S(2)}) async-start(bf16[16,2,3072]{2,1,0:T(2,128)(2,1)} %reshape.60), calls=%async_computation | async-start | bytes 393216 | tf_op jit(solution)/shard_map/all_to_all | solution.py:96
  151.7 3.8 %collective-permute-start.15 = (bf16[2,2,48,2,16,16]{2,5,0,3,1,4:T(8,128)(2,1)S(1)}, bf16[2,2,48,2,16,16]{2,5,0,3,1,4:T(8,128)(2,1)S(1)}, u32[]{:S(2)}, u32[]{:S(2)}) collective-permute-start(bf16[2,2,48,2,16,16]{2,5,0,3,1,4:T(8,128)(2,1)S(1)} %dynamic-slice_bitcast_fusion), channel_id=1, source_target_pairs={{0,1},{1,0},{2,3},{3,2},{4,5},{5,4},{6,7},{7,6},{8,9},{9,8},{10,11... | collective-permute-start | bytes 589832 | tf_op jit(solution)/shard_map/ppermute | solution.py:107
Sparse Core Ops, SparseCore 0:
  22.3 78.4 all-gather.1

commit v5 on v4

--- a/solution.py
+++ b/solution.py
@@ -87,28 +87,26 @@
     flat = up_weight.reshape(slice_out, -1)
     packed = jnp.concatenate([flat, jnp.pad(up_bias[:, None], ((0, 0), (0, 127)))], axis=1)
     packed_z = ring_gather(packed, "z")
-    weight_half = packed_z[:, :, : flat.shape[1]].reshape((chips, slice_out) + up_weight.shape[1:])
-    bias_half = packed_z[:, :, flat.shape[1]].astype(jnp.float32)
+    packed_other = lax.ppermute(packed_z, "core", [(0, 1), (1, 0)])
+    low = jnp.where(core == 0, packed_z, packed_other)
+    high = jnp.where(core == 0, packed_other, packed_z)
+    packed_all = jnp.stack([low, high], axis=1).reshape(chips * 2 * slice_out, -1)
+    up_all = packed_all[:, : flat.shape[1]].reshape((chips * 2 * slice_out,) + up_weight.shape[1:])
+    bias_all = packed_all[:, flat.shape[1]].astype(jnp.float32)
+    up_all = up_all.reshape(up_all.shape[:3] + (chips, 2, outputs))
+    up_all = jnp.transpose(up_all, (4, 3, 5, 1, 2, 0)).reshape(channels, 2, 2, -1)
 
     activated = conv_norm(whole, conv_weight, conv_bias, norm_gain, norm_shift)
     activated = jnp.transpose(activated).reshape(height, width_cols, outputs)
 
     chip_rows = lax.all_to_all(activated, "z", split_axis=0, concat_axis=2, tiled=True)
-    both = lax.all_gather(chip_rows, "core", axis=0, tiled=False)
-    local_rows = chip_rows.shape[0]
-    both = both.reshape(2, local_rows, width_cols, chips, outputs)
-    act = jnp.transpose(both, (1, 2, 3, 0, 4)).reshape(local_rows, width_cols, chips * 2 * outputs)
+    both = lax.all_gather(chip_rows, "core", axis=2, tiled=True)
+    half = chip_rows.shape[0] // 2
+    own = lax.dynamic_slice_in_dim(both, core * half, half, axis=0)
 
-    decoded = jnp.einsum("ijc,zoabc->iajbzo", act, weight_half, preferred_element_type=jnp.float32)
-    decoded = (decoded + bias_half).astype(jnp.bfloat16)
-    half = local_rows // 2
-    own = lax.dynamic_slice_in_dim(decoded, core * half, half, axis=0)
-    other = lax.dynamic_slice_in_dim(decoded, (1 - core) * half, half, axis=0)
-    received = lax.ppermute(other, "core", [(0, 1), (1, 0)])
-    low = jnp.where(core == 0, own, received)
-    high = jnp.where(core == 0, received, own)
-    fine = jnp.stack([low, high], axis=5)
-    return fine.reshape(2 * half, 2 * width_cols, chips * 2 * slice_out)
+    decoded = jnp.einsum("ijc,cabo->iajbo", own, up_all, preferred_element_type=jnp.float32)
+    decoded = (decoded + bias_all).astype(jnp.bfloat16)
+    return decoded.reshape(2 * half, 2 * width_cols, -1)
 
 
 def solution(mesh):

time: 179 us -> 178 us (level)
  the two profiles are of different devices: /device:TPU:1 before, /device:TPU:47 now
where the time goes in v5:
time: 178 us; the launch traced here: 177 us
  starting transfers between devices  84.9 us (48%)
  local copies, waits for them, and re-layouts  47.7 us (27%)
  between operations  13.7 us (8%)
  waiting for transfers between devices  9.84 us (6%)
  other arithmetic  8.43 us (5%)
  Pallas kernels  6.3 us (4%)
  matrix products  3 us (2%)
  blocking collectives  2.65 us (1%)
    ppermute x8, starting transfers between devices, ring_gather(): ahead = lax.ppermute(ahead, axis, step_up)  44 us
    unnamed x40, local copies, waits for them, and re-layouts  24 us
    all_to_all x1, starting transfers between devices, body(): lax.all_to_all(activated, 'z', split_axis=0, concat_axis=2, tiled=True)  18 us
    ppermute x7, starting transfers between devices, ring_gather(): behind = lax.ppermute(behind, axis, step_down)  15.1 us
    slice x2, local copies, waits for them, and re-layouts, body(): packed_all[:, :flat.shape[1]]  9.06 us
    ppermute x1, starting transfers between devices, body(): packed_other = lax.ppermute(packed_z, 'core', [(0, 1), (1, 0)])  7.84 us
    pallas_call x1, Pallas kernels, conv_norm(): pl.pallas_call(functools.partial(conv_norm_kernel, height=height, width_c...  6.3 us
    another operation x2, other arithmetic, body(): jnp.stack([low, high], axis=1).reshape(chips * 2 * slice_out, -1)  6.07 us
  transfers between devices with their start and end apart: 18, of which 9 were waited for; matrix products, arithmetic and copies ran while one was open for 26% of the time, Pallas kernels for 0%

profile of v5, /device:TPU:47, one launch (start us, length us, event | category | flops | bytes accessed | tf_op | source)
XLA Modules:
  0.0 176.6 jit_solution(11667008704032036644)
XLA Ops:
  6.5 0.7 copy.34
  7.3 1.0 reshape.40
  8.3 1.9 %collective-permute-start = (bf16[16,4224]{1,0:T(8,128)(2,1)S(1)}, bf16[16,4224]{1,0:T(8,128)(2,1)S(1)}, u32[]{:S(2)}, u32[]{:S(2)}) collective-permute-start(bf16[16,4224]{1,0:T(8,128)(2,1)S(1)} %fusion.5), channel_id=1, source_target_pairs={{0,30},{2,0},{4,2},{6,4},{8,6},{10,8},{12,10},{14,12},{16,14},{18,... | collective-permute-start | bytes 405512 | tf_op jit(solution)/shard_map/ppermute | solution.py:69
  10.2 3.5 %collective-permute-start.8 = (bf16[16,4224]{1,0:T(8,128)(2,1)S(1)}, bf16[16,4224]{1,0:T(8,128)(2,1)S(1)}, u32[]{:S(2)}, u32[]{:S(2)}) collective-permute-start(bf16[16,4224]{1,0:T(8,128)(2,1)S(1)} %fusion.5), channel_id=1, source_target_pairs={{0,2},{2,4},{4,6},{6,8},{8,10},{10,12},{12,14},{14,16},{16,18},{18... | collective-permute-start | bytes 405512 | tf_op jit(solution)/shard_map/ppermute | solution.py:72
  15.0 8.7 %collective-permute-start.1 = (bf16[16,4224]{1,0:T(8,128)(2,1)S(1)}, bf16[16,4224]{1,0:T(8,128)(2,1)S(1)}, u32[]{:S(2)}, u32[]{:S(2)}) collective-permute-start(bf16[16,4224]{1,0:T(8,128)(2,1)S(1)} %collective-permute-done), channel_id=1, source_target_pairs={{0,30},{2,0},{4,2},{6,4},{8,6},{10,8},{12,10},{14,12},{16,14},{18,... | collective-permute-start | bytes 405512 | tf_op jit(solution)/shard_map/ppermute | solution.py:69
  24.1 1.9 %collective-permute-start.9 = (bf16[16,4224]{1,0:T(8,128)(2,1)S(1)}, bf16[16,4224]{1,0:T(8,128)(2,1)S(1)}, u32[]{:S(2)}, u32[]{:S(2)}) collective-permute-start(bf16[16,4224]{1,0:T(8,128)(2,1)S(1)} %collective-permute-done.8), channel_id=1, source_target_pairs={{0,2},{2,4},{4,6},{6,8},{8,10},{10,12},{12,14},{14,16},{16,18},{18... | collective-permute-start | bytes 405512 | tf_op jit(solution)/shard_map/ppermute | solution.py:72
  26.7 4.6 %collective-permute-start.2 = (bf16[16,4224]{1,0:T(8,128)(2,1)S(1)}, bf16[16,4224]{1,0:T(8,128)(2,1)S(1)}, u32[]{:S(2)}, u32[]{:S(2)}) collective-permute-start(bf16[16,4224]{1,0:T(8,128)(2,1)S(1)} %collective-permute-done.1), channel_id=1, source_target_pairs={{0,30},{2,0},{4,2},{6,4},{8,6},{10,8},{12,10},{14,12},{16,14},{18,... | collective-permute-start | bytes 405512 | tf_op jit(solution)/shard_map/ppermute | solution.py:69
  31.3 1.9 %collective-permute-start.10 = (bf16[16,4224]{1,0:T(8,128)(2,1)S(1)}, bf16[16,4224]{1,0:T(8,128)(2,1)S(1)}, u32[]{:S(2)}, u32[]{:S(2)}) collective-permute-start(bf16[16,4224]{1,0:T(8,128)(2,1)S(1)} %collective-permute-done.9), channel_id=1, source_target_pairs={{0,2},{2,4},{4,6},{6,8},{8,10},{10,12},{12,14},{14,16},{16,18},{18... | collective-permute-start | bytes 405512 | tf_op jit(solution)/shard_map/ppermute | solution.py:72
  33.2 0.7 bitcast_dynamic-update-slice_fusion.26
  33.9 6.0 %collective-permute-start.3 = (bf16[16,4224]{1,0:T(8,128)(2,1)S(1)}, bf16[16,4224]{1,0:T(8,128)(2,1)S(1)}, u32[]{:S(2)}, u32[]{:S(2)}) collective-permute-start(bf16[16,4224]{1,0:T(8,128)(2,1)S(1)} %collective-permute-done.2), channel_id=1, source_target_pairs={{0,30},{2,0},{4,2},{6,4},{8,6},{10,8},{12,10},{14,12},{16,14},{18,... | collective-permute-start | bytes 405512 | tf_op jit(solution)/shard_map/ppermute | solution.py:69
  39.9 1.9 %collective-permute-start.11 = (bf16[16,4224]{1,0:T(8,128)(2,1)S(1)}, bf16[16,4224]{1,0:T(8,128)(2,1)S(1)}, u32[]{:S(2)}, u32[]{:S(2)}) collective-permute-start(bf16[16,4224]{1,0:T(8,128)(2,1)S(1)} %collective-permute-done.10), channel_id=1, source_target_pairs={{0,2},{2,4},{4,6},{6,8},{8,10},{10,12},{12,14},{14,16},{16,18},{18... | collective-permute-start | bytes 405512 | tf_op jit(solution)/shard_map/ppermute | solution.py:72
  41.8 0.7 bitcast_dynamic-update-slice_fusion.24
  42.5 7.6 %collective-permute-start.4 = (bf16[16,4224]{1,0:T(8,128)(2,1)S(1)}, bf16[16,4224]{1,0:T(8,128)(2,1)S(1)}, u32[]{:S(2)}, u32[]{:S(2)}) collective-permute-start(bf16[16,4224]{1,0:T(8,128)(2,1)S(1)} %collective-permute-done.3), channel_id=1, source_target_pairs={{0,30},{2,0},{4,2},{6,4},{8,6},{10,8},{12,10},{14,12},{16,14},{18,... | collective-permute-start | bytes 405512 | tf_op jit(solution)/shard_map/ppermute | solution.py:69
  50.1 1.8 %collective-permute-done.11 = bf16[16,4224]{1,0:T(8,128)(2,1)S(1)} collective-permute-done((bf16[16,4224]{1,0:T(8,128)(2,1)S(1)}, bf16[16,4224]{1,0:T(8,128)(2,1)S(1)}, u32[]{:S(2)}, u32[]{:S(2)}) %collective-permute-start.11) | collective-permute-done | bytes 135200 | tf_op jit(solution)/shard_map/ppermute | solution.py:72
  52.0 1.9 %collective-permute-start.12 = (bf16[16,4224]{1,0:T(8,128)(2,1)S(1)}, bf16[16,4224]{1,0:T(8,128)(2,1)S(1)}, u32[]{:S(2)}, u32[]{:S(2)}) collective-permute-start(bf16[16,4224]{1,0:T(8,128)(2,1)S(1)} %collective-permute-done.11), channel_id=1, source_target_pairs={{0,2},{2,4},{4,6},{6,8},{8,10},{10,12},{12,14},{14,16},{16,18},{18... | collective-permute-start | bytes 405512 | tf_op jit(solution)/shard_map/ppermute | solution.py:72
  54.5 4.7 %collective-permute-start.5 = (bf16[16,4224]{1,0:T(8,128)(2,1)S(1)}, bf16[16,4224]{1,0:T(8,128)(2,1)S(1)}, u32[]{:S(2)}, u32[]{:S(2)}) collective-permute-start(bf16[16,4224]{1,0:T(8,128)(2,1)S(1)} %collective-permute-done.4), channel_id=1, source_target_pairs={{0,30},{2,0},{4,2},{6,4},{8,6},{10,8},{12,10},{14,12},{16,14},{18,... | collective-permute-start | bytes 405512 | tf_op jit(solution)/shard_map/ppermute | solution.py:69
  59.3 2.0 %collective-permute-start.13 = (bf16[16,4224]{1,0:T(8,128)(2,1)S(1)}, bf16[16,4224]{1,0:T(8,128)(2,1)S(1)}, u32[]{:S(2)}, u32[]{:S(2)}) collective-permute-start(bf16[16,4224]{1,0:T(8,128)(2,1)S(1)} %collective-permute-done.12), channel_id=1, source_target_pairs={{0,2},{2,4},{4,6},{6,8},{8,10},{10,12},{12,14},{14,16},{16,18},{18... | collective-permute-start | bytes 405512 | tf_op jit(solution)/shard_map/ppermute | solution.py:72
  62.1 5.5 %collective-permute-start.6 = (bf16[16,4224]{1,0:T(8,128)(2,1)S(1)}, bf16[16,4224]{1,0:T(8,128)(2,1)S(1)}, u32[]{:S(2)}, u32[]{:S(2)}) collective-permute-start(bf16[16,4224]{1,0:T(8,128)(2,1)S(1)} %collective-permute-done.5), channel_id=1, source_target_pairs={{0,30},{2,0},{4,2},{6,4},{8,6},{10,8},{12,10},{14,12},{16,14},{18,... | collective-permute-start | bytes 405512 | tf_op jit(solution)/shard_map/ppermute | solution.py:69
  67.6 1.1 collective-permute-done.13
  68.7 1.9 %collective-permute-start.14 = (bf16[16,4224]{1,0:T(8,128)(2,1)S(1)}, bf16[16,4224]{1,0:T(8,128)(2,1)S(1)}, u32[]{:S(2)}, u32[]{:S(2)}) collective-permute-start(bf16[16,4224]{1,0:T(8,128)(2,1)S(1)} %collective-permute-done.13), channel_id=1, source_target_pairs={{0,2},{2,4},{4,6},{6,8},{8,10},{10,12},{12,14},{14,16},{16,18},{18... | collective-permute-start | bytes 405512 | tf_op jit(solution)/shard_map/ppermute | solution.py:72
  71.9 5.0 %collective-permute-start.7 = (bf16[16,4224]{1,0:T(8,128)(2,1)S(1)}, bf16[16,4224]{1,0:T(8,128)(2,1)S(1)}, u32[]{:S(2)}, u32[]{:S(2)}) collective-permute-start(bf16[16,4224]{1,0:T(8,128)(2,1)S(1)} %collective-permute-done.6), channel_id=1, source_target_pairs={{0,30},{2,0},{4,2},{6,4},{8,6},{10,8},{12,10},{14,12},{16,14},{18,... | collective-permute-start | bytes 405512 | tf_op jit(solution)/shard_map/ppermute | solution.py:69
  77.6 3.2 %collective-permute-done.7 = bf16[16,4224]{1,0:T(8,128)(2,1)S(1)} collective-permute-done((bf16[16,4224]{1,0:T(8,128)(2,1)S(1)}, bf16[16,4224]{1,0:T(8,128)(2,1)S(1)}, u32[]{:S(2)}, u32[]{:S(2)}) %collective-permute-start.7) | collective-permute-done | bytes 135200 | tf_op jit(solution)/shard_map/ppermute | solution.py:69
  81.5 0.7 bitcast_dynamic-update-slice_fusion.12
  83.4 0.7 bitcast_dynamic-update-slice_fusion.6
  84.1 0.7 bitcast_dynamic-update-slice_fusion.4
  84.8 0.7 bitcast_dynamic-update-slice_fusion.2
  86.1 0.7 bitcast_dynamic-update-slice_fusion.31
  96.8 1.8 constant_dynamic-slice_fusion
  98.5 7.8 %collective-permute-start.15 = (bf16[16,16,4224]{2,1,0:T(8,128)(2,1)S(1)}, bf16[16,16,4224]{2,1,0:T(8,128)(2,1)}, u32[]{:S(2)}, u32[]{:S(2)}) collective-permute-start(bf16[16,16,4224]{2,1,0:T(8,128)(2,1)S(1)} %constant_dynamic-slice_fusion), channel_id=1, source_target_pairs={{0,1},{1,0},{2,3},{3,2},{4,5},{5,4},{6,7},{7,6},{8,9},{9,8},{10,11... | collective-permute-start | bytes 6488072 | tf_op jit(solution)/shard_map/ppermute | solution.py:90
  106.4 0.7 copy.26.bias_ref
  107.1 0.7 copy.27.gain_ref
  107.8 0.7 copy.28.shift_ref
  108.5 1.9 %collective-permute-done.15 = bf16[16,16,4224]{2,1,0:T(8,128)(2,1)} collective-permute-done((bf16[16,16,4224]{2,1,0:T(8,128)(2,1)S(1)}, bf16[16,16,4224]{2,1,0:T(8,128)(2,1)}, u32[]{:S(2)}, u32[]{:S(2)}) %collective-permute-start.15) | collective-permute-done | bytes 2162720 | tf_op jit(solution)/shard_map/ppermute | solution.py:90
  110.4 4.0 %select_bitcast_fusion.1 = (bf16[16,1,16,4224]{3,2,1,0:T(8,128)(2,1)S(1)}, bf16[16,1,16,4224]{3,2,1,0:T(8,128)(2,1)}) fusion(bf16[16,16,4224]{2,1,0:T(8,128)(2,1)} %collective-permute-done.15, pred[]{:T(512)S(6)} %eq.7, bf16[32,16,4224]{2,1,0:T(8,128)(2,1)} %bitcast_dynamic-update-slice_fusion.1, s32[]{:T(128)S(6)} %select_n.30), kind=kLoop, calls=%fused_computation.2 | loop fusion | flops 2162688 | bytes 8650757 | tf_op jit(solution)/shard_map/stack | solution.py:93
  114.4 6.3 %shard_map.73 = bf16[32,3072]{1,0:T(8,128)(2,1)} custom-call(bf16[3072,1024]{1,0:T(8,128)(2,1)} %bitcast.95, bf16[288,1024]{1,0:T(8,128)(2,1)} %bitcast.101, f32[32,1]{1,0:T(8,128)} %copy.26.bias_ref, f32[32,1]{1,0:T(8,128)} %copy.27.gain_ref, f32[32,1]{1,0:T(8,128)} %copy.28.shift_ref), custom_call_target="tpu_custom_call" | custom-call | flops 1811939328 | bytes 7077888 | tf_op jit(solution)/shard_map/pallas_call | solution.py:50
  120.7 1.4 reshape.49
  122.5 1.5 reshape.55
  124.0 18.0 %all-to-all-start = ((bf16[16,2,3072]{2,1,0:T(2,128)(2,1)}), bf16[16,2,3072]{2,1,0:T(2,128)(2,1)S(1)}, u32[]{:S(2)}, u32[]{:S(2)}) async-start(bf16[16,2,3072]{2,1,0:T(2,128)(2,1)} %reshape.55), calls=%async_computation | async-start | bytes 393216 | tf_op jit(solution)/shard_map/all_to_all | solution.py:102
  141.9 2.0 %pad_maximum_fusion = bf16[16,2,16,4224]{3,2,1,0:T(8,128)(2,1)S(1)} fusion(bf16[16,1,16,4224]{3,2,1,0:T(8,128)(2,1)} %get-tuple-element.6, bf16[16,1,16,4224]{3,2,1,0:T(8,128)(2,1)S(1)} %get-tuple-element.5), kind=kLoop, calls=%fused_computation | loop fusion | flops 2162688 | bytes 8650752 | tf_op jit(solution)/shard_map/stack | solution.py:93
  144.0 2.0 %copy-done = bf16[16,2,16,4224]{3,2,1,0:T(8,128)(2,1)} copy-done((bf16[16,2,16,4224]{3,2,1,0:T(8,128)(2,1)}, bf16[16,2,16,4224]{3,2,1,0:T(8,128)(2,1)S(1)}, u32[]{:S(2)}) %copy-start) | copy-done | bytes 4325400
  146.0 2.6 %slice.8 = bf16[512,4096]{1,0:T(8,128)(2,1)} slice(bf16[512,4224]{1,0:T(8,128)(2,1)S(1)} %bitcast.92), slice={[0:512], [0:4096]} | slice | bytes 8388608 | tf_op jit(solution)/shard_map/slice | solution.py:94
  148.6 6.5 %copy.24 = bf16[512,4096]{0,1:T(8,128)(2,1)} copy(bf16[512,4096]{1,0:T(8,128)(2,1)} %slice.8) | data formatting | bytes 8388608 | tf_op jit(solution)/shard_map/slice | solution.py:94
  155.1 4.8 %copy.25 = bf16[2,16,32,2,2,512]{5,2,1,0,4,3:T(8,128)(2,1)} copy(bf16[2,16,32,2,2,512]{5,2,0,1,4,3:T(8,128)(2,1)} %bitcast.94) | data formatting | bytes 8388608 | tf_op jit(solution)/shard_map/transpose | solution.py:97
  159.8 1.0 convert_reduce_fusion
  162.0 0.7 all_to_all.16
  162.7 2.7 %all_gather.7 = bf16[4,48,1024]{2,1,0:T(8,128)(2,1)S(1)} all-gather(bf16[4,48,512]{2,1,0:T(8,128)(2,1)S(1)} %all_to_all.16), channel_id=1, replica_groups=mesh['grp'=16,'z'=16,'core'=2] {'core'}, dimensions={2}, use_global_device_ids=true | all-gather | bytes 589824 | tf_op jit(solution)/shard_map/all_gather | solution.py:103
  165.4 3.0 %fusion.1 = bf16[2,2,48,2,512]{4,2,0,3,1:T(8,128)(2,1)S(1)} fusion(bf16[1024,2,2,512,1]{3,0,4,2,1:T(8,128)(2,1)} %bitcast.96, f32[512]{0:T(512)S(1)} %convert_reduce_fusion, bf16[4,48,1024]{2,1,0:T(8,128)(2,1)S(1)} %all_gather.7, s32[]{:T(128)S(6)} %select_n.33), kind=kOutput, calls=%fused_computation.5 | convolution fusion | flops 403046400 | bytes 4786180 | tf_op jit(solution)/shard_map/ijc,cabo->iajbo/dot_general | solution.py:107
  168.8 0.9 reshape.50
  (53 shorter events, 20.2 us)
Async XLA Ops:
  6.5 107.9 %all-gather.2.cloned.1.call-start = ((), (), s32[]{:S(2)}) async-start(), calls=%async_computation.1 | async-start | bytes 6488064 | tf_op jit(solution)/shard_map/all_gather | solution.py:85
  8.3 6.7 %collective-permute-start = (bf16[16,4224]{1,0:T(8,128)(2,1)S(1)}, bf16[16,4224]{1,0:T(8,128)(2,1)S(1)}, u32[]{:S(2)}, u32[]{:S(2)}) collective-permute-start(bf16[16,4224]{1,0:T(8,128)(2,1)S(1)} %fusion.5), channel_id=1, source_target_pairs={{0,30},{2,0},{4,2},{6,4},{8,6},{10,8},{12,10},{14,12},{16,14},{18,... | collective-permute-start | bytes 405512 | tf_op jit(solution)/shard_map/ppermute | solution.py:69
  10.2 13.9 %collective-permute-start.8 = (bf16[16,4224]{1,0:T(8,128)(2,1)S(1)}, bf16[16,4224]{1,0:T(8,128)(2,1)S(1)}, u32[]{:S(2)}, u32[]{:S(2)}) collective-permute-start(bf16[16,4224]{1,0:T(8,128)(2,1)S(1)} %fusion.5), channel_id=1, source_target_pairs={{0,2},{2,4},{4,6},{6,8},{8,10},{10,12},{12,14},{14,16},{16,18},{18... | collective-permute-start | bytes 405512 | tf_op jit(solution)/shard_map/ppermute | solution.py:72
  15.0 11.7 %collective-permute-start.1 = (bf16[16,4224]{1,0:T(8,128)(2,1)S(1)}, bf16[16,4224]{1,0:T(8,128)(2,1)S(1)}, u32[]{:S(2)}, u32[]{:S(2)}) collective-permute-start(bf16[16,4224]{1,0:T(8,128)(2,1)S(1)} %collective-permute-done), channel_id=1, source_target_pairs={{0,30},{2,0},{4,2},{6,4},{8,6},{10,8},{12,10},{14,12},{16,14},{18,... | collective-permute-start | bytes 405512 | tf_op jit(solution)/shard_map/ppermute | solution.py:69
  24.1 7.2 %collective-permute-start.9 = (bf16[16,4224]{1,0:T(8,128)(2,1)S(1)}, bf16[16,4224]{1,0:T(8,128)(2,1)S(1)}, u32[]{:S(2)}, u32[]{:S(2)}) collective-permute-start(bf16[16,4224]{1,0:T(8,128)(2,1)S(1)} %collective-permute-done.8), channel_id=1, source_target_pairs={{0,2},{2,4},{4,6},{6,8},{8,10},{10,12},{12,14},{14,16},{16,18},{18... | collective-permute-start | bytes 405512 | tf_op jit(solution)/shard_map/ppermute | solution.py:72
  26.7 7.2 %collective-permute-start.2 = (bf16[16,4224]{1,0:T(8,128)(2,1)S(1)}, bf16[16,4224]{1,0:T(8,128)(2,1)S(1)}, u32[]{:S(2)}, u32[]{:S(2)}) collective-permute-start(bf16[16,4224]{1,0:T(8,128)(2,1)S(1)} %collective-permute-done.1), channel_id=1, source_target_pairs={{0,30},{2,0},{4,2},{6,4},{8,6},{10,8},{12,10},{14,12},{16,14},{18,... | collective-permute-start | bytes 405512 | tf_op jit(solution)/shard_map/ppermute | solution.py:69
  31.3 8.6 %collective-permute-start.10 = (bf16[16,4224]{1,0:T(8,128)(2,1)S(1)}, bf16[16,4224]{1,0:T(8,128)(2,1)S(1)}, u32[]{:S(2)}, u32[]{:S(2)}) collective-permute-start(bf16[16,4224]{1,0:T(8,128)(2,1)S(1)} %collective-permute-done.9), channel_id=1, source_target_pairs={{0,2},{2,4},{4,6},{6,8},{8,10},{10,12},{12,14},{14,16},{16,18},{18... | collective-permute-start | bytes 405512 | tf_op jit(solution)/shard_map/ppermute | solution.py:72
  33.9 8.6 %collective-permute-start.3 = (bf16[16,4224]{1,0:T(8,128)(2,1)S(1)}, bf16[16,4224]{1,0:T(8,128)(2,1)S(1)}, u32[]{:S(2)}, u32[]{:S(2)}) collective-permute-start(bf16[16,4224]{1,0:T(8,128)(2,1)S(1)} %collective-permute-done.2), channel_id=1, source_target_pairs={{0,30},{2,0},{4,2},{6,4},{8,6},{10,8},{12,10},{14,12},{16,14},{18,... | collective-permute-start | bytes 405512 | tf_op jit(solution)/shard_map/ppermute | solution.py:69
  39.9 12.1 %collective-permute-start.11 = (bf16[16,4224]{1,0:T(8,128)(2,1)S(1)}, bf16[16,4224]{1,0:T(8,128)(2,1)S(1)}, u32[]{:S(2)}, u32[]{:S(2)}) collective-permute-start(bf16[16,4224]{1,0:T(8,128)(2,1)S(1)} %collective-permute-done.10), channel_id=1, source_target_pairs={{0,2},{2,4},{4,6},{6,8},{8,10},{10,12},{12,14},{14,16},{16,18},{18... | collective-permute-start | bytes 405512 | tf_op jit(solution)/shard_map/ppermute | solution.py:72
  42.5 12.0 %collective-permute-start.4 = (bf16[16,4224]{1,0:T(8,128)(2,1)S(1)}, bf16[16,4224]{1,0:T(8,128)(2,1)S(1)}, u32[]{:S(2)}, u32[]{:S(2)}) collective-permute-start(bf16[16,4224]{1,0:T(8,128)(2,1)S(1)} %collective-permute-done.3), channel_id=1, source_target_pairs={{0,30},{2,0},{4,2},{6,4},{8,6},{10,8},{12,10},{14,12},{16,14},{18,... | collective-permute-start | bytes 405512 | tf_op jit(solution)/shard_map/ppermute | solution.py:69
  52.0 7.4 %collective-permute-start.12 = (bf16[16,4224]{1,0:T(8,128)(2,1)S(1)}, bf16[16,4224]{1,0:T(8,128)(2,1)S(1)}, u32[]{:S(2)}, u32[]{:S(2)}) collective-permute-start(bf16[16,4224]{1,0:T(8,128)(2,1)S(1)} %collective-permute-done.11), channel_id=1, source_target_pairs={{0,2},{2,4},{4,6},{6,8},{8,10},{10,12},{12,14},{14,16},{16,18},{18... | collective-permute-start | bytes 405512 | tf_op jit(solution)/shard_map/ppermute | solution.py:72
  54.5 7.6 %collective-permute-start.5 = (bf16[16,4224]{1,0:T(8,128)(2,1)S(1)}, bf16[16,4224]{1,0:T(8,128)(2,1)S(1)}, u32[]{:S(2)}, u32[]{:S(2)}) collective-permute-start(bf16[16,4224]{1,0:T(8,128)(2,1)S(1)} %collective-permute-done.4), channel_id=1, source_target_pairs={{0,30},{2,0},{4,2},{6,4},{8,6},{10,8},{12,10},{14,12},{16,14},{18,... | collective-permute-start | bytes 405512 | tf_op jit(solution)/shard_map/ppermute | solution.py:69
  59.3 9.4 %collective-permute-start.13 = (bf16[16,4224]{1,0:T(8,128)(2,1)S(1)}, bf16[16,4224]{1,0:T(8,128)(2,1)S(1)}, u32[]{:S(2)}, u32[]{:S(2)}) collective-permute-start(bf16[16,4224]{1,0:T(8,128)(2,1)S(1)} %collective-permute-done.12), channel_id=1, source_target_pairs={{0,2},{2,4},{4,6},{6,8},{8,10},{10,12},{12,14},{14,16},{16,18},{18... | collective-permute-start | bytes 405512 | tf_op jit(solution)/shard_map/ppermute | solution.py:72
  62.1 9.8 %collective-permute-start.6 = (bf16[16,4224]{1,0:T(8,128)(2,1)S(1)}, bf16[16,4224]{1,0:T(8,128)(2,1)S(1)}, u32[]{:S(2)}, u32[]{:S(2)}) collective-permute-start(bf16[16,4224]{1,0:T(8,128)(2,1)S(1)} %collective-permute-done.5), channel_id=1, source_target_pairs={{0,30},{2,0},{4,2},{6,4},{8,6},{10,8},{12,10},{14,12},{16,14},{18,... | collective-permute-start | bytes 405512 | tf_op jit(solution)/shard_map/ppermute | solution.py:69
  68.7 12.7 %collective-permute-start.14 = (bf16[16,4224]{1,0:T(8,128)(2,1)S(1)}, bf16[16,4224]{1,0:T(8,128)(2,1)S(1)}, u32[]{:S(2)}, u32[]{:S(2)}) collective-permute-start(bf16[16,4224]{1,0:T(8,128)(2,1)S(1)} %collective-permute-done.13), channel_id=1, source_target_pairs={{0,2},{2,4},{4,6},{6,8},{8,10},{10,12},{12,14},{14,16},{16,18},{18... | collective-permute-start | bytes 405512 | tf_op jit(solution)/shard_map/ppermute | solution.py:72
  71.9 8.9 %collective-permute-start.7 = (bf16[16,4224]{1,0:T(8,128)(2,1)S(1)}, bf16[16,4224]{1,0:T(8,128)(2,1)S(1)}, u32[]{:S(2)}, u32[]{:S(2)}) collective-permute-start(bf16[16,4224]{1,0:T(8,128)(2,1)S(1)} %collective-permute-done.6), channel_id=1, source_target_pairs={{0,30},{2,0},{4,2},{6,4},{8,6},{10,8},{12,10},{14,12},{16,14},{18,... | collective-permute-start | bytes 405512 | tf_op jit(solution)/shard_map/ppermute | solution.py:69
  86.1 20.3 %copy-start.1 = (f32[32]{0:T(128)S(1)}, f32[32]{0:T(128)}, u32[]{:S(2)}) copy-start(f32[32]{0:T(128)} %param.9) | copy-start | bytes 388
  86.1 20.9 %copy-start.2 = (f32[32]{0:T(128)S(1)}, f32[32]{0:T(128)}, u32[]{:S(2)}) copy-start(f32[32]{0:T(128)} %param.10) | copy-start | bytes 388
  86.1 21.6 %copy-start.3 = (f32[32]{0:T(128)S(1)}, f32[32]{0:T(128)}, u32[]{:S(2)}) copy-start(f32[32]{0:T(128)} %param.11) | copy-start | bytes 388
  98.5 11.8 %collective-permute-start.15 = (bf16[16,16,4224]{2,1,0:T(8,128)(2,1)S(1)}, bf16[16,16,4224]{2,1,0:T(8,128)(2,1)}, u32[]{:S(2)}, u32[]{:S(2)}) collective-permute-start(bf16[16,16,4224]{2,1,0:T(8,128)(2,1)S(1)} %constant_dynamic-slice_fusion), channel_id=1, source_target_pairs={{0,1},{1,0},{2,3},{3,2},{4,5},{5,4},{6,7},{7,6},{8,9},{9,8},{10,11... | collective-permute-start | bytes 6488072 | tf_op jit(solution)/shard_map/ppermute | solution.py:90
  124.0 36.9 %all-to-all-start = ((bf16[16,2,3072]{2,1,0:T(2,128)(2,1)}), bf16[16,2,3072]{2,1,0:T(2,128)(2,1)S(1)}, u32[]{:S(2)}, u32[]{:S(2)}) async-start(bf16[16,2,3072]{2,1,0:T(2,128)(2,1)} %reshape.55), calls=%async_computation | async-start | bytes 393216 | tf_op jit(solution)/shard_map/all_to_all | solution.py:102
  144.0 2.0 %copy-start = (bf16[16,2,16,4224]{3,2,1,0:T(8,128)(2,1)}, bf16[16,2,16,4224]{3,2,1,0:T(8,128)(2,1)S(1)}, u32[]{:S(2)}) copy-start(bf16[16,2,16,4224]{3,2,1,0:T(8,128)(2,1)S(1)} %pad_maximum_fusion) | copy-start | bytes 12976132
Sparse Core Ops, SparseCore 0:
  13.9 84.7 all-gather.1

commit v6 on v5

--- a/solution.py
+++ b/solution.py
@@ -59,20 +59,28 @@
     )(x, w, col(conv_bias), col(norm_gain), col(norm_shift))
 
 
-def ring_gather(block, axis):
-    chips = lax.axis_size(axis)
-    step_up = [(i, (i - 1) % chips) for i in range(chips)]
-    step_down = [(i, (i + 1) % chips) for i in range(chips)]
-    ahead, behind = block, block
-    from_ahead, from_behind = [], []
+def ring_gather_rows(local):
+    chips = lax.axis_size("z")
+    core = lax.axis_index("core")
+    here = lax.axis_index("z")
+    chip = lax.all_gather(local, "core", axis=0, tiled=True)
+    n = chip.shape[0]
+    whole = jnp.zeros((chips * n,) + chip.shape[1:], chip.dtype)
+    whole = lax.dynamic_update_slice_in_dim(whole, chip, here * n, axis=0)
+    walk = []
+    for z in range(chips):
+        walk.append((2 * z, 2 * ((z - 1) % chips)))
+        walk.append((2 * z + 1, 2 * ((z + 1) % chips) + 1))
+    swap = [(0, 1), (1, 0)]
+    sign = 1 - 2 * core
+    block = chip
     for k in range(1, chips // 2 + 1):
-        ahead = lax.ppermute(ahead, axis, step_up)
-        from_ahead.append(ahead)
+        block = lax.ppermute(block, ("z", "core"), walk)
+        whole = lax.dynamic_update_slice_in_dim(whole, block, ((here + sign * k) % chips) * n, axis=0)
         if k < chips - chips // 2:
-            behind = lax.ppermute(behind, axis, step_down)
-            from_behind.append(behind)
-    stacked = jnp.stack([block] + from_ahead + from_behind[::-1])
-    return jnp.roll(stacked, lax.axis_index(axis), axis=0)
+            other = lax.ppermute(block, "core", swap)
+            whole = lax.dynamic_update_slice_in_dim(whole, other, ((here - sign * k) % chips) * n, axis=0)
+    return whole
 
 
 def body(coarse, conv_weight, conv_bias, norm_gain, norm_shift, up_weight, up_bias):
@@ -82,29 +90,25 @@
     outputs = conv_weight.shape[0]
     slice_out = up_weight.shape[0]
 
-    whole = lax.all_gather(coarse, ("z", "core"), axis=0, tiled=True)
+    whole = ring_gather_rows(coarse)
     height = whole.shape[0]
     flat = up_weight.reshape(slice_out, -1)
     packed = jnp.concatenate([flat, jnp.pad(up_bias[:, None], ((0, 0), (0, 127)))], axis=1)
-    packed_z = ring_gather(packed, "z")
-    packed_other = lax.ppermute(packed_z, "core", [(0, 1), (1, 0)])
-    low = jnp.where(core == 0, packed_z, packed_other)
-    high = jnp.where(core == 0, packed_other, packed_z)
-    packed_all = jnp.stack([low, high], axis=1).reshape(chips * 2 * slice_out, -1)
+    packed_all = lax.all_gather(packed, ("z", "core"), axis=0, tiled=True)
     up_all = packed_all[:, : flat.shape[1]].reshape((chips * 2 * slice_out,) + up_weight.shape[1:])
     bias_all = packed_all[:, flat.shape[1]].astype(jnp.float32)
-    up_all = up_all.reshape(up_all.shape[:3] + (chips, 2, outputs))
-    up_all = jnp.transpose(up_all, (4, 3, 5, 1, 2, 0)).reshape(channels, 2, 2, -1)
 
     activated = conv_norm(whole, conv_weight, conv_bias, norm_gain, norm_shift)
     activated = jnp.transpose(activated).reshape(height, width_cols, outputs)
 
     chip_rows = lax.all_to_all(activated, "z", split_axis=0, concat_axis=2, tiled=True)
-    both = lax.all_gather(chip_rows, "core", axis=2, tiled=True)
+    both = lax.all_gather(chip_rows, "core", axis=0, tiled=False)
     half = chip_rows.shape[0] // 2
-    own = lax.dynamic_slice_in_dim(both, core * half, half, axis=0)
+    own = lax.dynamic_slice_in_dim(both, core * half, half, axis=1)
+    own = own.reshape((2, half, width_cols, chips, outputs))
+    own = jnp.transpose(own, (1, 2, 3, 0, 4)).reshape(half, width_cols, channels)
 
-    decoded = jnp.einsum("ijc,cabo->iajbo", own, up_all, preferred_element_type=jnp.float32)
+    decoded = jnp.einsum("ijc,oabc->iajbo", own, up_all, preferred_element_type=jnp.float32)
     decoded = (decoded + bias_all).astype(jnp.bfloat16)
     return decoded.reshape(2 * half, 2 * width_cols, -1)
 

time: 178 us -> 186 us (1.045)
  the two profiles are of different devices: /device:TPU:47 before, /device:TPU:1 now
where the time goes in v6:
time: 186 us; the launch traced here: 184 us
  waiting for transfers between devices  59 us (32%)
  starting transfers between devices  46.2 us (25%)
  local copies, waits for them, and re-layouts  38.6 us (21%)
  blocking collectives  15.9 us (9%)
  between operations  13.7 us (7%)
  Pallas kernels  6.3 us (3%)
  matrix products  3.04 us (2%)
    ppermute x8, waiting for transfers between devices, ring_gather_rows(): block = lax.ppermute(block, ('z', 'core'), walk)  46.6 us
    ppermute x7, starting transfers between devices, ring_gather_rows(): other = lax.ppermute(block, 'core', swap)  21.4 us
    ppermute x8, starting transfers between devices, ring_gather_rows(): block = lax.ppermute(block, ('z', 'core'), walk)  17.5 us
    all_to_all x1, waiting for transfers between devices, body(): lax.all_to_all(activated, 'z', split_axis=0, concat_axis=2, tiled=True)  12.3 us
    unnamed x10, local copies, waits for them, and re-layouts  9.22 us
    all_gather x1, blocking collectives, ring_gather_rows(): chip = lax.all_gather(local, 'core', axis=0, tiled=True)  8.81 us
    all_to_all x1, starting transfers between devices, body(): lax.all_to_all(activated, 'z', split_axis=0, concat_axis=2, tiled=True)  7.35 us
    all_gather x1, blocking collectives, body(): both = lax.all_gather(chip_rows, 'core', axis=0, tiled=False)  7.07 us
  transfers between devices with their start and end apart: 17, of which 8 were waited for; matrix products, arithmetic and copies ran while one was open for 13% of the time, Pallas kernels for 3%

profile of v6, /device:TPU:1, one launch (start us, length us, event | category | flops | bytes accessed | tf_op | source)
XLA Modules:
  0.0 184.4 jit_solution(6831344309319254708)
XLA Ops:
  6.5 1.0 reshape.44
  9.0 8.8 %all_gather.13 = bf16[4,48,1024]{2,1,0:T(8,128)(2,1)S(1)} all-gather(bf16[2,48,1024]{2,1,0:T(8,128)(2,1)} %param.7), channel_id=1, replica_groups=mesh['grp'=16,'z'=16,'core'=2] {'core'}, dimensions={0}, use_global_device_ids=true | all-gather | bytes 589824 | tf_op jit(solution)/shard_map/all_gather | solution.py:66
  17.8 1.9 %collective-permute-start = (bf16[4,48,1024]{2,1,0:T(8,128)(2,1)S(1)}, bf16[4,48,1024]{2,1,0:T(8,128)(2,1)S(1)}, u32[]{:S(2)}, u32[]{:S(2)}) collective-permute-start(bf16[4,48,1024]{2,1,0:T(8,128)(2,1)S(1)} %all_gather.13), channel_id=1, source_target_pairs={{0,30},{1,3},{2,0},{3,5},{4,2},{5,7},{6,4},{7,9},{8,6},{9,11},{10,... | collective-permute-start | bytes 1179656 | tf_op jit(solution)/shard_map/ppermute | solution.py:78
  19.7 9.0 %collective-permute-done = bf16[4,48,1024]{2,1,0:T(8,128)(2,1)S(1)} collective-permute-done((bf16[4,48,1024]{2,1,0:T(8,128)(2,1)S(1)}, bf16[4,48,1024]{2,1,0:T(8,128)(2,1)S(1)}, u32[]{:S(2)}, u32[]{:S(2)}) %collective-permute-start) | collective-permute-done | bytes 393248 | tf_op jit(solution)/shard_map/ppermute | solution.py:78
  28.7 1.9 %collective-permute-start.2 = (bf16[4,48,1024]{2,1,0:T(8,128)(2,1)S(1)}, bf16[4,48,1024]{2,1,0:T(8,128)(2,1)S(1)}, u32[]{:S(2)}, u32[]{:S(2)}) collective-permute-start(bf16[4,48,1024]{2,1,0:T(8,128)(2,1)S(1)} %collective-permute-done), channel_id=1, source_target_pairs={{0,30},{1,3},{2,0},{3,5},{4,2},{5,7},{6,4},{7,9},{8,6},{9,11},{10,... | collective-permute-start | bytes 1179656 | tf_op jit(solution)/shard_map/ppermute | solution.py:78
  30.6 11.0 %collective-permute-done.2 = bf16[4,48,1024]{2,1,0:T(8,128)(2,1)S(1)} collective-permute-done((bf16[4,48,1024]{2,1,0:T(8,128)(2,1)S(1)}, bf16[4,48,1024]{2,1,0:T(8,128)(2,1)S(1)}, u32[]{:S(2)}, u32[]{:S(2)}) %collective-permute-start.2) | collective-permute-done | bytes 393248 | tf_op jit(solution)/shard_map/ppermute | solution.py:78
  41.6 1.9 %collective-permute-start.4 = (bf16[4,48,1024]{2,1,0:T(8,128)(2,1)S(1)}, bf16[4,48,1024]{2,1,0:T(8,128)(2,1)S(1)}, u32[]{:S(2)}, u32[]{:S(2)}) collective-permute-start(bf16[4,48,1024]{2,1,0:T(8,128)(2,1)S(1)} %collective-permute-done.2), channel_id=1, source_target_pairs={{0,30},{1,3},{2,0},{3,5},{4,2},{5,7},{6,4},{7,9},{8,6},{9,11},{10,... | collective-permute-start | bytes 1179656 | tf_op jit(solution)/shard_map/ppermute | solution.py:78
  43.5 10.5 %collective-permute-done.4 = bf16[4,48,1024]{2,1,0:T(8,128)(2,1)S(1)} collective-permute-done((bf16[4,48,1024]{2,1,0:T(8,128)(2,1)S(1)}, bf16[4,48,1024]{2,1,0:T(8,128)(2,1)S(1)}, u32[]{:S(2)}, u32[]{:S(2)}) %collective-permute-start.4) | collective-permute-done | bytes 393248 | tf_op jit(solution)/shard_map/ppermute | solution.py:78
  54.1 1.9 %collective-permute-start.6 = (bf16[4,48,1024]{2,1,0:T(8,128)(2,1)S(1)}, bf16[4,48,1024]{2,1,0:T(8,128)(2,1)S(1)}, u32[]{:S(2)}, u32[]{:S(2)}) collective-permute-start(bf16[4,48,1024]{2,1,0:T(8,128)(2,1)S(1)} %collective-permute-done.4), channel_id=1, source_target_pairs={{0,30},{1,3},{2,0},{3,5},{4,2},{5,7},{6,4},{7,9},{8,6},{9,11},{10,... | collective-permute-start | bytes 1179656 | tf_op jit(solution)/shard_map/ppermute | solution.py:78
  56.0 11.5 %collective-permute-done.6 = bf16[4,48,1024]{2,1,0:T(8,128)(2,1)S(1)} collective-permute-done((bf16[4,48,1024]{2,1,0:T(8,128)(2,1)S(1)}, bf16[4,48,1024]{2,1,0:T(8,128)(2,1)S(1)}, u32[]{:S(2)}, u32[]{:S(2)}) %collective-permute-start.6) | collective-permute-done | bytes 393248 | tf_op jit(solution)/shard_map/ppermute | solution.py:78
  67.5 1.9 %collective-permute-start.8 = (bf16[4,48,1024]{2,1,0:T(8,128)(2,1)S(1)}, bf16[4,48,1024]{2,1,0:T(8,128)(2,1)S(1)}, u32[]{:S(2)}, u32[]{:S(2)}) collective-permute-start(bf16[4,48,1024]{2,1,0:T(8,128)(2,1)S(1)} %collective-permute-done.6), channel_id=1, source_target_pairs={{0,30},{1,3},{2,0},{3,5},{4,2},{5,7},{6,4},{7,9},{8,6},{9,11},{10,... | collective-permute-start | bytes 1179656 | tf_op jit(solution)/shard_map/ppermute | solution.py:78
  69.4 7.2 %collective-permute-start.1 = (bf16[4,48,1024]{2,1,0:T(8,128)(2,1)S(1)}, bf16[4,48,1024]{2,1,0:T(8,128)(2,1)S(1)}, u32[]{:S(2)}, u32[]{:S(2)}) collective-permute-start(bf16[4,48,1024]{2,1,0:T(8,128)(2,1)S(1)} %collective-permute-done), channel_id=1, source_target_pairs={{0,1},{1,0},{2,3},{3,2},{4,5},{5,4},{6,7},{7,6},{8,9},{9,8},{10,11... | collective-permute-start | bytes 1179656 | tf_op jit(solution)/shard_map/ppermute | solution.py:81
  76.7 1.9 %collective-permute-start.3 = (bf16[4,48,1024]{2,1,0:T(8,128)(2,1)S(1)}, bf16[4,48,1024]{2,1,0:T(8,128)(2,1)S(1)}, u32[]{:S(2)}, u32[]{:S(2)}) collective-permute-start(bf16[4,48,1024]{2,1,0:T(8,128)(2,1)S(1)} %collective-permute-done.2), channel_id=1, source_target_pairs={{0,1},{1,0},{2,3},{3,2},{4,5},{5,4},{6,7},{7,6},{8,9},{9,8},{10,11... | collective-permute-start | bytes 1179656 | tf_op jit(solution)/shard_map/ppermute | solution.py:81
  78.6 3.5 %broadcast_in_dim.8 = bf16[64,48,1024]{2,1,0:T(8,128)(2,1)} broadcast(bf16[]{:T(256)} %constant.84.clone.1), dimensions={} | broadcast | bytes 6291458 | tf_op jit(solution)/shard_map/broadcast_in_dim | solution.py:68
  82.1 0.8 constant_dynamic-update-slice_fusion.15
  85.0 0.8 constant_dynamic-update-slice_fusion.14
  85.8 2.4 %collective-permute-start.5 = (bf16[4,48,1024]{2,1,0:T(8,128)(2,1)S(1)}, bf16[4,48,1024]{2,1,0:T(8,128)(2,1)S(1)}, u32[]{:S(2)}, u32[]{:S(2)}) collective-permute-start(bf16[4,48,1024]{2,1,0:T(8,128)(2,1)S(1)} %collective-permute-done.4), channel_id=1, source_target_pairs={{0,1},{1,0},{2,3},{3,2},{4,5},{5,4},{6,7},{7,6},{8,9},{9,8},{10,11... | collective-permute-start | bytes 1179656 | tf_op jit(solution)/shard_map/ppermute | solution.py:81
  88.1 1.9 %collective-permute-start.10 = (bf16[4,48,1024]{2,1,0:T(8,128)(2,1)S(1)}, bf16[4,48,1024]{2,1,0:T(8,128)(2,1)S(1)}, u32[]{:S(2)}, u32[]{:S(2)}) collective-permute-start(bf16[4,48,1024]{2,1,0:T(8,128)(2,1)S(1)} %collective-permute-done.8), channel_id=1, source_target_pairs={{0,30},{1,3},{2,0},{3,5},{4,2},{5,7},{6,4},{7,9},{8,6},{9,11},{10,... | collective-permute-start | bytes 1179656 | tf_op jit(solution)/shard_map/ppermute | solution.py:78
  90.1 0.8 constant_dynamic-update-slice_fusion.13
  90.9 0.8 constant_dynamic-update-slice_fusion.12
  91.6 2.0 %collective-permute-start.7 = (bf16[4,48,1024]{2,1,0:T(8,128)(2,1)S(1)}, bf16[4,48,1024]{2,1,0:T(8,128)(2,1)S(1)}, u32[]{:S(2)}, u32[]{:S(2)}) collective-permute-start(bf16[4,48,1024]{2,1,0:T(8,128)(2,1)S(1)} %collective-permute-done.6), channel_id=1, source_target_pairs={{0,1},{1,0},{2,3},{3,2},{4,5},{5,4},{6,7},{7,6},{8,9},{9,8},{10,11... | collective-permute-start | bytes 1179656 | tf_op jit(solution)/shard_map/ppermute | solution.py:81
  93.6 0.8 constant_dynamic-update-slice_fusion.11
  95.2 2.3 %collective-permute-start.9 = (bf16[4,48,1024]{2,1,0:T(8,128)(2,1)S(1)}, bf16[4,48,1024]{2,1,0:T(8,128)(2,1)S(1)}, u32[]{:S(2)}, u32[]{:S(2)}) collective-permute-start(bf16[4,48,1024]{2,1,0:T(8,128)(2,1)S(1)} %collective-permute-done.8), channel_id=1, source_target_pairs={{0,1},{1,0},{2,3},{3,2},{4,5},{5,4},{6,7},{7,6},{8,9},{9,8},{10,11... | collective-permute-start | bytes 1179656 | tf_op jit(solution)/shard_map/ppermute | solution.py:81
  97.9 2.9 %collective-permute-start.12 = (bf16[4,48,1024]{2,1,0:T(8,128)(2,1)S(1)}, bf16[4,48,1024]{2,1,0:T(8,128)(2,1)S(1)}, u32[]{:S(2)}, u32[]{:S(2)}) collective-permute-start(bf16[4,48,1024]{2,1,0:T(8,128)(2,1)S(1)} %collective-permute-done.10), channel_id=1, source_target_pairs={{0,30},{1,3},{2,0},{3,5},{4,2},{5,7},{6,4},{7,9},{8,6},{9,11},{10,... | collective-permute-start | bytes 1179656 | tf_op jit(solution)/shard_map/ppermute | solution.py:78
  100.8 0.8 constant_dynamic-update-slice_fusion.9
  101.5 0.8 constant_dynamic-update-slice_fusion.8
  102.3 3.6 %collective-permute-start.11 = (bf16[4,48,1024]{2,1,0:T(8,128)(2,1)S(1)}, bf16[4,48,1024]{2,1,0:T(8,128)(2,1)S(1)}, u32[]{:S(2)}, u32[]{:S(2)}) collective-permute-start(bf16[4,48,1024]{2,1,0:T(8,128)(2,1)S(1)} %collective-permute-done.10), channel_id=1, source_target_pairs={{0,1},{1,0},{2,3},{3,2},{4,5},{5,4},{6,7},{7,6},{8,9},{9,8},{10,11... | collective-permute-start | bytes 1179656 | tf_op jit(solution)/shard_map/ppermute | solution.py:81
  105.9 0.8 constant_dynamic-update-slice_fusion.7
  106.7 0.8 constant_dynamic-update-slice_fusion.6
  107.6 2.0 %collective-permute-start.13 = (bf16[4,48,1024]{2,1,0:T(8,128)(2,1)S(1)}, bf16[4,48,1024]{2,1,0:T(8,128)(2,1)S(1)}, u32[]{:S(2)}, u32[]{:S(2)}) collective-permute-start(bf16[4,48,1024]{2,1,0:T(8,128)(2,1)S(1)} %collective-permute-done.12), channel_id=1, source_target_pairs={{0,1},{1,0},{2,3},{3,2},{4,5},{5,4},{6,7},{7,6},{8,9},{9,8},{10,11... | collective-permute-start | bytes 1179656 | tf_op jit(solution)/shard_map/ppermute | solution.py:81
  109.6 0.8 constant_dynamic-update-slice_fusion.5
  110.4 3.2 %collective-permute-start.14 = (bf16[4,48,1024]{2,1,0:T(8,128)(2,1)S(1)}, bf16[4,48,1024]{2,1,0:T(8,128)(2,1)S(1)}, u32[]{:S(2)}, u32[]{:S(2)}) collective-permute-start(bf16[4,48,1024]{2,1,0:T(8,128)(2,1)S(1)} %collective-permute-done.12), channel_id=1, source_target_pairs={{0,30},{1,3},{2,0},{3,5},{4,2},{5,7},{6,4},{7,9},{8,6},{9,11},{10,... | collective-permute-start | bytes 1179656 | tf_op jit(solution)/shard_map/ppermute | solution.py:78
  113.6 0.8 constant_dynamic-update-slice_fusion.4
  114.4 0.8 constant_dynamic-update-slice_fusion.3
  115.2 0.8 constant_dynamic-update-slice_fusion.2
  116.7 4.1 %collective-permute-done.14 = bf16[4,48,1024]{2,1,0:T(8,128)(2,1)S(1)} collective-permute-done((bf16[4,48,1024]{2,1,0:T(8,128)(2,1)S(1)}, bf16[4,48,1024]{2,1,0:T(8,128)(2,1)S(1)}, u32[]{:S(2)}, u32[]{:S(2)}) %collective-permute-start.14) | collective-permute-done | bytes 393248 | tf_op jit(solution)/shard_map/ppermute | solution.py:78
  120.8 0.8 constant_dynamic-update-slice_fusion
  121.6 6.3 %shard_map.73 = bf16[32,3072]{1,0:T(8,128)(2,1)} custom-call(bf16[3072,1024]{1,0:T(8,128)(2,1)} %bitcast.3.x_ref, bf16[288,1024]{1,0:T(8,128)(2,1)} %bitcast.43, f32[32,1]{1,0:T(8,128)} %copy.23.bias_ref, f32[32,1]{1,0:T(8,128)} %copy.24.gain_ref, f32[32,1]{1,0:T(8,128)} %copy.25.shift_ref), custom_call_target="tpu_custom_call" | custom-call | flops 1811939328 | bytes 7077888 | tf_op jit(solution)/shard_map/pallas_call | solution.py:50
  127.9 1.4 reshape.52
  129.7 1.5 reshape.60
  131.2 7.3 %all-to-all-start = ((bf16[16,2,3072]{2,1,0:T(2,128)(2,1)}), bf16[16,2,3072]{2,1,0:T(2,128)(2,1)S(1)}, u32[]{:S(2)}, u32[]{:S(2)}) async-start(bf16[16,2,3072]{2,1,0:T(2,128)(2,1)} %reshape.60), calls=%async_computation | async-start | bytes 393216 | tf_op jit(solution)/shard_map/all_to_all | solution.py:104
  138.6 12.3 %all-to-all-done = bf16[16,2,3072]{2,1,0:T(2,128)(2,1)S(1)} async-done(((bf16[16,2,3072]{2,1,0:T(2,128)(2,1)}), bf16[16,2,3072]{2,1,0:T(2,128)(2,1)S(1)}, u32[]{:S(2)}, u32[]{:S(2)}) %all-to-all-start) | async-done | bytes 196640 | tf_op jit(solution)/shard_map/all_to_all | solution.py:104
  152.8 7.1 %all_gather.15 = bf16[2,4,48,512]{3,2,1,0:T(8,128)(2,1)S(1)} all-gather(bf16[1,4,48,512]{3,2,1,0:T(8,128)(2,1)S(1)} %all_gather.14), channel_id=1, replica_groups=mesh['grp'=16,'z'=16,'core'=2] {'core'}, dimensions={0}, use_global_device_ids=true | all-gather | bytes 589824 | tf_op jit(solution)/shard_map/all_gather | solution.py:105
  161.0 4.7 %slice.8 = bf16[512,4096]{1,0:T(8,128)(2,1)} slice(bf16[512,4224]{1,0:T(8,128)(2,1)} %all-gather.2.cloned.1.call-done), slice={[0:512], [0:4096]} | slice | bytes 8388608 | tf_op jit(solution)/shard_map/slice | solution.py:98
  165.7 6.5 %copy.37 = bf16[512,4096]{0,1:T(8,128)(2,1)} copy(bf16[512,4096]{1,0:T(8,128)(2,1)} %slice.8) | data formatting | bytes 8388608
  172.2 1.0 convert_reduce_fusion
  173.2 3.0 %fusion.1 = bf16[2,2,48,2,512]{4,2,0,3,1:T(8,128)(2,1)S(1)} fusion(bf16[512,2,2,1024,1]{0,3,4,2,1:T(8,128)(2,1)} %bitcast.36, bf16[2,48,1024,1,1]{1,2,0,4,3:T(8,128)(2,1)S(1)} %bitcast.39, f32[512]{0:T(512)S(1)} %convert_reduce_fusion), kind=kOutput, calls=%fused_computation.2 | convolution fusion | flops 403046400 | bytes 4786176 | tf_op jit(solution)/shard_map/ijc,oabc->iajbo/dot_general | solution.py:111
  176.7 0.9 reshape.55
  (34 shorter events, 9.3 us)
Async XLA Ops:
  6.5 76.4 %copy-start = (f32[32]{0:T(128)S(1)}, f32[32]{0:T(128)}, u32[]{:S(2)}) copy-start(f32[32]{0:T(128)} %param.9) | copy-start | bytes 388
  6.5 77.0 %copy-start.1 = (f32[32]{0:T(128)S(1)}, f32[32]{0:T(128)}, u32[]{:S(2)}) copy-start(f32[32]{0:T(128)} %param.10) | copy-start | bytes 388
  6.5 77.7 %copy-start.2 = (f32[32]{0:T(128)S(1)}, f32[32]{0:T(128)}, u32[]{:S(2)}) copy-start(f32[32]{0:T(128)} %param.11) | copy-start | bytes 388
  6.5 154.5 %all-gather.2.cloned.1.call-start = ((), (), s32[]{:S(2)}) async-start(), calls=%async_computation.1 | async-start | bytes 4460544 | tf_op jit(solution)/shard_map/all_gather | solution.py:97
  17.8 10.9 %collective-permute-start = (bf16[4,48,1024]{2,1,0:T(8,128)(2,1)S(1)}, bf16[4,48,1024]{2,1,0:T(8,128)(2,1)S(1)}, u32[]{:S(2)}, u32[]{:S(2)}) collective-permute-start(bf16[4,48,1024]{2,1,0:T(8,128)(2,1)S(1)} %all_gather.13), channel_id=1, source_target_pairs={{0,30},{1,3},{2,0},{3,5},{4,2},{5,7},{6,4},{7,9},{8,6},{9,11},{10,... | collective-permute-start | bytes 1179656 | tf_op jit(solution)/shard_map/ppermute | solution.py:78
  28.7 12.9 %collective-permute-start.2 = (bf16[4,48,1024]{2,1,0:T(8,128)(2,1)S(1)}, bf16[4,48,1024]{2,1,0:T(8,128)(2,1)S(1)}, u32[]{:S(2)}, u32[]{:S(2)}) collective-permute-start(bf16[4,48,1024]{2,1,0:T(8,128)(2,1)S(1)} %collective-permute-done), channel_id=1, source_target_pairs={{0,30},{1,3},{2,0},{3,5},{4,2},{5,7},{6,4},{7,9},{8,6},{9,11},{10,... | collective-permute-start | bytes 1179656 | tf_op jit(solution)/shard_map/ppermute | solution.py:78
  41.6 12.5 %collective-permute-start.4 = (bf16[4,48,1024]{2,1,0:T(8,128)(2,1)S(1)}, bf16[4,48,1024]{2,1,0:T(8,128)(2,1)S(1)}, u32[]{:S(2)}, u32[]{:S(2)}) collective-permute-start(bf16[4,48,1024]{2,1,0:T(8,128)(2,1)S(1)} %collective-permute-done.2), channel_id=1, source_target_pairs={{0,30},{1,3},{2,0},{3,5},{4,2},{5,7},{6,4},{7,9},{8,6},{9,11},{10,... | collective-permute-start | bytes 1179656 | tf_op jit(solution)/shard_map/ppermute | solution.py:78
  54.1 13.4 %collective-permute-start.6 = (bf16[4,48,1024]{2,1,0:T(8,128)(2,1)S(1)}, bf16[4,48,1024]{2,1,0:T(8,128)(2,1)S(1)}, u32[]{:S(2)}, u32[]{:S(2)}) collective-permute-start(bf16[4,48,1024]{2,1,0:T(8,128)(2,1)S(1)} %collective-permute-done.4), channel_id=1, source_target_pairs={{0,30},{1,3},{2,0},{3,5},{4,2},{5,7},{6,4},{7,9},{8,6},{9,11},{10,... | collective-permute-start | bytes 1179656 | tf_op jit(solution)/shard_map/ppermute | solution.py:78
  67.5 20.6 %collective-permute-start.8 = (bf16[4,48,1024]{2,1,0:T(8,128)(2,1)S(1)}, bf16[4,48,1024]{2,1,0:T(8,128)(2,1)S(1)}, u32[]{:S(2)}, u32[]{:S(2)}) collective-permute-start(bf16[4,48,1024]{2,1,0:T(8,128)(2,1)S(1)} %collective-permute-done.6), channel_id=1, source_target_pairs={{0,30},{1,3},{2,0},{3,5},{4,2},{5,7},{6,4},{7,9},{8,6},{9,11},{10,... | collective-permute-start | bytes 1179656 | tf_op jit(solution)/shard_map/ppermute | solution.py:78
  69.4 20.6 %collective-permute-start.1 = (bf16[4,48,1024]{2,1,0:T(8,128)(2,1)S(1)}, bf16[4,48,1024]{2,1,0:T(8,128)(2,1)S(1)}, u32[]{:S(2)}, u32[]{:S(2)}) collective-permute-start(bf16[4,48,1024]{2,1,0:T(8,128)(2,1)S(1)} %collective-permute-done), channel_id=1, source_target_pairs={{0,1},{1,0},{2,3},{3,2},{4,5},{5,4},{6,7},{7,6},{8,9},{9,8},{10,11... | collective-permute-start | bytes 1179656 | tf_op jit(solution)/shard_map/ppermute | solution.py:81
  76.7 16.9 %collective-permute-start.3 = (bf16[4,48,1024]{2,1,0:T(8,128)(2,1)S(1)}, bf16[4,48,1024]{2,1,0:T(8,128)(2,1)S(1)}, u32[]{:S(2)}, u32[]{:S(2)}) collective-permute-start(bf16[4,48,1024]{2,1,0:T(8,128)(2,1)S(1)} %collective-permute-done.2), channel_id=1, source_target_pairs={{0,1},{1,0},{2,3},{3,2},{4,5},{5,4},{6,7},{7,6},{8,9},{9,8},{10,11... | collective-permute-start | bytes 1179656 | tf_op jit(solution)/shard_map/ppermute | solution.py:81
  85.8 15.0 %collective-permute-start.5 = (bf16[4,48,1024]{2,1,0:T(8,128)(2,1)S(1)}, bf16[4,48,1024]{2,1,0:T(8,128)(2,1)S(1)}, u32[]{:S(2)}, u32[]{:S(2)}) collective-permute-start(bf16[4,48,1024]{2,1,0:T(8,128)(2,1)S(1)} %collective-permute-done.4), channel_id=1, source_target_pairs={{0,1},{1,0},{2,3},{3,2},{4,5},{5,4},{6,7},{7,6},{8,9},{9,8},{10,11... | collective-permute-start | bytes 1179656 | tf_op jit(solution)/shard_map/ppermute | solution.py:81
  88.1 9.7 %collective-permute-start.10 = (bf16[4,48,1024]{2,1,0:T(8,128)(2,1)S(1)}, bf16[4,48,1024]{2,1,0:T(8,128)(2,1)S(1)}, u32[]{:S(2)}, u32[]{:S(2)}) collective-permute-start(bf16[4,48,1024]{2,1,0:T(8,128)(2,1)S(1)} %collective-permute-done.8), channel_id=1, source_target_pairs={{0,30},{1,3},{2,0},{3,5},{4,2},{5,7},{6,4},{7,9},{8,6},{9,11},{10,... | collective-permute-start | bytes 1179656 | tf_op jit(solution)/shard_map/ppermute | solution.py:78
  91.6 14.2 %collective-permute-start.7 = (bf16[4,48,1024]{2,1,0:T(8,128)(2,1)S(1)}, bf16[4,48,1024]{2,1,0:T(8,128)(2,1)S(1)}, u32[]{:S(2)}, u32[]{:S(2)}) collective-permute-start(bf16[4,48,1024]{2,1,0:T(8,128)(2,1)S(1)} %collective-permute-done.6), channel_id=1, source_target_pairs={{0,1},{1,0},{2,3},{3,2},{4,5},{5,4},{6,7},{7,6},{8,9},{9,8},{10,11... | collective-permute-start | bytes 1179656 | tf_op jit(solution)/shard_map/ppermute | solution.py:81
  95.2 14.4 %collective-permute-start.9 = (bf16[4,48,1024]{2,1,0:T(8,128)(2,1)S(1)}, bf16[4,48,1024]{2,1,0:T(8,128)(2,1)S(1)}, u32[]{:S(2)}, u32[]{:S(2)}) collective-permute-start(bf16[4,48,1024]{2,1,0:T(8,128)(2,1)S(1)} %collective-permute-done.8), channel_id=1, source_target_pairs={{0,1},{1,0},{2,3},{3,2},{4,5},{5,4},{6,7},{7,6},{8,9},{9,8},{10,11... | collective-permute-start | bytes 1179656 | tf_op jit(solution)/shard_map/ppermute | solution.py:81
  97.9 9.7 %collective-permute-start.12 = (bf16[4,48,1024]{2,1,0:T(8,128)(2,1)S(1)}, bf16[4,48,1024]{2,1,0:T(8,128)(2,1)S(1)}, u32[]{:S(2)}, u32[]{:S(2)}) collective-permute-start(bf16[4,48,1024]{2,1,0:T(8,128)(2,1)S(1)} %collective-permute-done.10), channel_id=1, source_target_pairs={{0,30},{1,3},{2,0},{3,5},{4,2},{5,7},{6,4},{7,9},{8,6},{9,11},{10,... | collective-permute-start | bytes 1179656 | tf_op jit(solution)/shard_map/ppermute | solution.py:78
  102.3 12.1 %collective-permute-start.11 = (bf16[4,48,1024]{2,1,0:T(8,128)(2,1)S(1)}, bf16[4,48,1024]{2,1,0:T(8,128)(2,1)S(1)}, u32[]{:S(2)}, u32[]{:S(2)}) collective-permute-start(bf16[4,48,1024]{2,1,0:T(8,128)(2,1)S(1)} %collective-permute-done.10), channel_id=1, source_target_pairs={{0,1},{1,0},{2,3},{3,2},{4,5},{5,4},{6,7},{7,6},{8,9},{9,8},{10,11... | collective-permute-start | bytes 1179656 | tf_op jit(solution)/shard_map/ppermute | solution.py:81
  107.6 8.4 %collective-permute-start.13 = (bf16[4,48,1024]{2,1,0:T(8,128)(2,1)S(1)}, bf16[4,48,1024]{2,1,0:T(8,128)(2,1)S(1)}, u32[]{:S(2)}, u32[]{:S(2)}) collective-permute-start(bf16[4,48,1024]{2,1,0:T(8,128)(2,1)S(1)} %collective-permute-done.12), channel_id=1, source_target_pairs={{0,1},{1,0},{2,3},{3,2},{4,5},{5,4},{6,7},{7,6},{8,9},{9,8},{10,11... | collective-permute-start | bytes 1179656 | tf_op jit(solution)/shard_map/ppermute | solution.py:81
  110.4 10.5 %collective-permute-start.14 = (bf16[4,48,1024]{2,1,0:T(8,128)(2,1)S(1)}, bf16[4,48,1024]{2,1,0:T(8,128)(2,1)S(1)}, u32[]{:S(2)}, u32[]{:S(2)}) collective-permute-start(bf16[4,48,1024]{2,1,0:T(8,128)(2,1)S(1)} %collective-permute-done.12), channel_id=1, source_target_pairs={{0,30},{1,3},{2,0},{3,5},{4,2},{5,7},{6,4},{7,9},{8,6},{9,11},{10,... | collective-permute-start | bytes 1179656 | tf_op jit(solution)/shard_map/ppermute | solution.py:78
  131.2 19.7 %all-to-all-start = ((bf16[16,2,3072]{2,1,0:T(2,128)(2,1)}), bf16[16,2,3072]{2,1,0:T(2,128)(2,1)S(1)}, u32[]{:S(2)}, u32[]{:S(2)}) async-start(bf16[16,2,3072]{2,1,0:T(2,128)(2,1)} %reshape.60), calls=%async_computation | async-start | bytes 393216 | tf_op jit(solution)/shard_map/all_to_all | solution.py:104
Sparse Core Ops, SparseCore 0:
  9.5 82.2 all-gather.1

commit v7 on v5

--- a/solution.py
+++ b/solution.py
@@ -59,6 +59,45 @@
     )(x, w, col(conv_bias), col(norm_gain), col(norm_shift))
 
 
+def up_kernel(core_ref, act_ref, own_ref, other_ref, bias_ref, out_ref, wnat_ref, *, width_cols):
+    chips, slab, _ = own_ref.shape
+    channels = act_ref.shape[1]
+    core = core_ref[0]
+    for z in range(chips):
+        mine = pl.multiple_of(2 * slab * z + slab * core, slab)
+        theirs = pl.multiple_of(2 * slab * z + slab * (1 - core), slab)
+        wnat_ref[pl.ds(mine, slab), :] = own_ref[z, :, pl.ds(0, 4 * channels)]
+        wnat_ref[pl.ds(theirs, slab), :] = other_ref[z, :, pl.ds(0, 4 * channels)]
+    act = act_ref[...]
+    rows = out_ref.shape[0]
+    outs = wnat_ref.shape[0]
+    for ab in range(4):
+        a, b = divmod(ab, 2)
+        res = lax.dot_general(act, wnat_ref[:, pl.ds(ab * channels, channels)], (((1,), (1,)), ((), ())),
+                              preferred_element_type=jnp.float32)
+        res = (res + bias_ref[...]).astype(out_ref.dtype)
+        for i in range(rows):
+            out_ref[i, a, :, pl.ds(b * outs, outs)] = res[i * width_cols:(i + 1) * width_cols, :]
+
+
+def up_conv(core, act, own, other, bias_row):
+    rows, width_cols, channels = act.shape
+    chips, slab, _ = own.shape
+    outs = 2 * chips * slab
+    vmem = pl.BlockSpec(memory_space=pltpu.VMEM)
+    smem = pl.BlockSpec(memory_space=pltpu.SMEM)
+    return pl.pallas_call(
+        functools.partial(up_kernel, width_cols=width_cols),
+        out_shape=jax.ShapeDtypeStruct((rows, 2, width_cols, 2 * outs), jnp.bfloat16),
+        in_specs=[smem, vmem, vmem, vmem, vmem],
+        out_specs=vmem,
+        scratch_shapes=[pltpu.VMEM((outs, 4 * channels), jnp.bfloat16)],
+        cost_estimate=pl.CostEstimate(
+            flops=2 * rows * width_cols * channels * 4 * outs, transcendentals=0,
+            bytes_accessed=act.size * 2 + 2 * own.size * 2 + rows * width_cols * 4 * outs * 2),
+    )(jnp.reshape(core, (1,)).astype(jnp.int32), act.reshape(rows * width_cols, channels), own, other, bias_row)
+
+
 def ring_gather(block, axis):
     chips = lax.axis_size(axis)
     step_up = [(i, (i - 1) % chips) for i in range(chips)]
@@ -88,25 +127,22 @@
     packed = jnp.concatenate([flat, jnp.pad(up_bias[:, None], ((0, 0), (0, 127)))], axis=1)
     packed_z = ring_gather(packed, "z")
     packed_other = lax.ppermute(packed_z, "core", [(0, 1), (1, 0)])
-    low = jnp.where(core == 0, packed_z, packed_other)
-    high = jnp.where(core == 0, packed_other, packed_z)
-    packed_all = jnp.stack([low, high], axis=1).reshape(chips * 2 * slice_out, -1)
-    up_all = packed_all[:, : flat.shape[1]].reshape((chips * 2 * slice_out,) + up_weight.shape[1:])
-    bias_all = packed_all[:, flat.shape[1]].astype(jnp.float32)
-    up_all = up_all.reshape(up_all.shape[:3] + (chips, 2, outputs))
-    up_all = jnp.transpose(up_all, (4, 3, 5, 1, 2, 0)).reshape(channels, 2, 2, -1)
+    bias_halves = jnp.stack([packed_z[:, :, flat.shape[1]], packed_other[:, :, flat.shape[1]]], axis=1)
+    bias_halves = jnp.where(core == 0, bias_halves, bias_halves[:, ::-1])
+    bias_row = bias_halves.astype(jnp.float32).reshape(1, -1)
 
     activated = conv_norm(whole, conv_weight, conv_bias, norm_gain, norm_shift)
     activated = jnp.transpose(activated).reshape(height, width_cols, outputs)
 
     chip_rows = lax.all_to_all(activated, "z", split_axis=0, concat_axis=2, tiled=True)
-    both = lax.all_gather(chip_rows, "core", axis=2, tiled=True)
+    both = lax.all_gather(chip_rows, "core", axis=0, tiled=False)
     half = chip_rows.shape[0] // 2
-    own = lax.dynamic_slice_in_dim(both, core * half, half, axis=0)
+    own = lax.dynamic_slice_in_dim(both, core * half, half, axis=1)
+    own = own.reshape((2, half, width_cols, chips, outputs))
+    own = jnp.transpose(own, (1, 2, 3, 0, 4)).reshape(half, width_cols, channels)
 
-    decoded = jnp.einsum("ijc,cabo->iajbo", own, up_all, preferred_element_type=jnp.float32)
-    decoded = (decoded + bias_all).astype(jnp.bfloat16)
-    return decoded.reshape(2 * half, 2 * width_cols, -1)
+    fine = up_conv(core, own, packed_z, packed_other, bias_row)
+    return fine.reshape(2 * half, 2 * width_cols, -1)
 
 
 def solution(mesh):

time: 178 us -> 174 us (0.978)
  the two profiles are of different devices: /device:TPU:47 before, /device:TPU:63 now
where the time goes in v7:
time: 174 us; the launch traced here: 173 us
  starting transfers between devices  84.2 us (48%)
  local copies, waits for them, and re-layouts  38.1 us (22%)
  waiting for transfers between devices  21.7 us (12%)
  between operations  13.7 us (8%)
  Pallas kernels  11 us (6%)
  blocking collectives  2.93 us (2%)
    ppermute x8, starting transfers between devices, ring_gather(): ahead = lax.ppermute(ahead, axis, step_up)  43.3 us
    unnamed x39, local copies, waits for them, and re-layouts  21.3 us
    all_to_all x1, starting transfers between devices, body(): lax.all_to_all(activated, 'z', split_axis=0, concat_axis=2, tiled=True)  17.6 us
    ppermute x7, starting transfers between devices, ring_gather(): behind = lax.ppermute(behind, axis, step_down)  15.9 us
    all_to_all x1, waiting for transfers between devices, body(): lax.all_to_all(activated, 'z', split_axis=0, concat_axis=2, tiled=True)  13.5 us
    ppermute x1, starting transfers between devices, body(): packed_other = lax.ppermute(packed_z, 'core', [(0, 1), (1, 0)])  7.44 us
    pallas_call x1, Pallas kernels, conv_norm(): pl.pallas_call(functools.partial(conv_norm_kernel, height=height, width_c...  6.3 us
    ppermute x8, waiting for transfers between devices, ring_gather(): ahead = lax.ppermute(ahead, axis, step_up)  5.37 us
  transfers between devices with their start and end apart: 18, of which 7 were waited for; matrix products, arithmetic and copies ran while one was open for 18% of the time, Pallas kernels for 4%

profile of v7, /device:TPU:63, one launch (start us, length us, event | category | flops | bytes accessed | tf_op | source)
XLA Modules:
  0.0 173.0 jit_solution(12580566846071538503)
XLA Ops:
  6.5 1.0 reshape.48
  7.5 0.7 copy.67
  8.3 1.9 %collective-permute-start = (bf16[16,4224]{1,0:T(8,128)(2,1)S(1)}, bf16[16,4224]{1,0:T(8,128)(2,1)S(1)}, u32[]{:S(2)}, u32[]{:S(2)}) collective-permute-start(bf16[16,4224]{1,0:T(8,128)(2,1)S(1)} %fusion.1), channel_id=1, source_target_pairs={{0,30},{2,0},{4,2},{6,4},{8,6},{10,8},{12,10},{14,12},{16,14},{18,... | collective-permute-start | bytes 405512 | tf_op jit(solution)/shard_map/ppermute | solution.py:108
  10.2 3.5 %collective-permute-start.8 = (bf16[16,4224]{1,0:T(8,128)(2,1)S(1)}, bf16[16,4224]{1,0:T(8,128)(2,1)S(1)}, u32[]{:S(2)}, u32[]{:S(2)}) collective-permute-start(bf16[16,4224]{1,0:T(8,128)(2,1)S(1)} %fusion.1), channel_id=1, source_target_pairs={{0,2},{2,4},{4,6},{6,8},{8,10},{10,12},{12,14},{14,16},{16,18},{18... | collective-permute-start | bytes 405512 | tf_op jit(solution)/shard_map/ppermute | solution.py:111
  15.0 8.7 %collective-permute-start.1 = (bf16[16,4224]{1,0:T(8,128)(2,1)S(1)}, bf16[16,4224]{1,0:T(8,128)(2,1)S(1)}, u32[]{:S(2)}, u32[]{:S(2)}) collective-permute-start(bf16[16,4224]{1,0:T(8,128)(2,1)S(1)} %collective-permute-done), channel_id=1, source_target_pairs={{0,30},{2,0},{4,2},{6,4},{8,6},{10,8},{12,10},{14,12},{16,14},{18,... | collective-permute-start | bytes 405512 | tf_op jit(solution)/shard_map/ppermute | solution.py:108
  24.4 1.9 %collective-permute-start.9 = (bf16[16,4224]{1,0:T(8,128)(2,1)S(1)}, bf16[16,4224]{1,0:T(8,128)(2,1)S(1)}, u32[]{:S(2)}, u32[]{:S(2)}) collective-permute-start(bf16[16,4224]{1,0:T(8,128)(2,1)S(1)} %collective-permute-done.8), channel_id=1, source_target_pairs={{0,2},{2,4},{4,6},{6,8},{8,10},{10,12},{12,14},{14,16},{16,18},{18... | collective-permute-start | bytes 405512 | tf_op jit(solution)/shard_map/ppermute | solution.py:111
  26.4 4.9 %collective-permute-start.2 = (bf16[16,4224]{1,0:T(8,128)(2,1)S(1)}, bf16[16,4224]{1,0:T(8,128)(2,1)S(1)}, u32[]{:S(2)}, u32[]{:S(2)}) collective-permute-start(bf16[16,4224]{1,0:T(8,128)(2,1)S(1)} %collective-permute-done.1), channel_id=1, source_target_pairs={{0,30},{2,0},{4,2},{6,4},{8,6},{10,8},{12,10},{14,12},{16,14},{18,... | collective-permute-start | bytes 405512 | tf_op jit(solution)/shard_map/ppermute | solution.py:108
  32.0 1.9 %collective-permute-start.10 = (bf16[16,4224]{1,0:T(8,128)(2,1)S(1)}, bf16[16,4224]{1,0:T(8,128)(2,1)S(1)}, u32[]{:S(2)}, u32[]{:S(2)}) collective-permute-start(bf16[16,4224]{1,0:T(8,128)(2,1)S(1)} %collective-permute-done.9), channel_id=1, source_target_pairs={{0,2},{2,4},{4,6},{6,8},{8,10},{10,12},{12,14},{14,16},{16,18},{18... | collective-permute-start | bytes 405512 | tf_op jit(solution)/shard_map/ppermute | solution.py:111
  33.9 6.3 %collective-permute-start.3 = (bf16[16,4224]{1,0:T(8,128)(2,1)S(1)}, bf16[16,4224]{1,0:T(8,128)(2,1)S(1)}, u32[]{:S(2)}, u32[]{:S(2)}) collective-permute-start(bf16[16,4224]{1,0:T(8,128)(2,1)S(1)} %collective-permute-done.2), channel_id=1, source_target_pairs={{0,30},{2,0},{4,2},{6,4},{8,6},{10,8},{12,10},{14,12},{16,14},{18,... | collective-permute-start | bytes 405512 | tf_op jit(solution)/shard_map/ppermute | solution.py:108
  40.9 1.9 %collective-permute-start.11 = (bf16[16,4224]{1,0:T(8,128)(2,1)S(1)}, bf16[16,4224]{1,0:T(8,128)(2,1)S(1)}, u32[]{:S(2)}, u32[]{:S(2)}) collective-permute-start(bf16[16,4224]{1,0:T(8,128)(2,1)S(1)} %collective-permute-done.10), channel_id=1, source_target_pairs={{0,2},{2,4},{4,6},{6,8},{8,10},{10,12},{12,14},{14,16},{16,18},{18... | collective-permute-start | bytes 405512 | tf_op jit(solution)/shard_map/ppermute | solution.py:111
  42.9 6.4 %collective-permute-start.4 = (bf16[16,4224]{1,0:T(8,128)(2,1)S(1)}, bf16[16,4224]{1,0:T(8,128)(2,1)S(1)}, u32[]{:S(2)}, u32[]{:S(2)}) collective-permute-start(bf16[16,4224]{1,0:T(8,128)(2,1)S(1)} %collective-permute-done.3), channel_id=1, source_target_pairs={{0,30},{2,0},{4,2},{6,4},{8,6},{10,8},{12,10},{14,12},{16,14},{18,... | collective-permute-start | bytes 405512 | tf_op jit(solution)/shard_map/ppermute | solution.py:108
  49.2 0.7 bitcast_dynamic-update-slice_fusion.22
  49.9 1.8 %collective-permute-done.11 = bf16[16,4224]{1,0:T(8,128)(2,1)S(1)} collective-permute-done((bf16[16,4224]{1,0:T(8,128)(2,1)S(1)}, bf16[16,4224]{1,0:T(8,128)(2,1)S(1)}, u32[]{:S(2)}, u32[]{:S(2)}) %collective-permute-start.11) | collective-permute-done | bytes 135200 | tf_op jit(solution)/shard_map/ppermute | solution.py:111
  51.7 1.9 %collective-permute-start.12 = (bf16[16,4224]{1,0:T(8,128)(2,1)S(1)}, bf16[16,4224]{1,0:T(8,128)(2,1)S(1)}, u32[]{:S(2)}, u32[]{:S(2)}) collective-permute-start(bf16[16,4224]{1,0:T(8,128)(2,1)S(1)} %collective-permute-done.11), channel_id=1, source_target_pairs={{0,2},{2,4},{4,6},{6,8},{8,10},{10,12},{12,14},{14,16},{16,18},{18... | collective-permute-start | bytes 405512 | tf_op jit(solution)/shard_map/ppermute | solution.py:111
  53.6 4.7 %collective-permute-start.5 = (bf16[16,4224]{1,0:T(8,128)(2,1)S(1)}, bf16[16,4224]{1,0:T(8,128)(2,1)S(1)}, u32[]{:S(2)}, u32[]{:S(2)}) collective-permute-start(bf16[16,4224]{1,0:T(8,128)(2,1)S(1)} %collective-permute-done.4), channel_id=1, source_target_pairs={{0,30},{2,0},{4,2},{6,4},{8,6},{10,8},{12,10},{14,12},{16,14},{18,... | collective-permute-start | bytes 405512 | tf_op jit(solution)/shard_map/ppermute | solution.py:108
  59.4 2.8 %collective-permute-start.13 = (bf16[16,4224]{1,0:T(8,128)(2,1)S(1)}, bf16[16,4224]{1,0:T(8,128)(2,1)S(1)}, u32[]{:S(2)}, u32[]{:S(2)}) collective-permute-start(bf16[16,4224]{1,0:T(8,128)(2,1)S(1)} %collective-permute-done.12), channel_id=1, source_target_pairs={{0,2},{2,4},{4,6},{6,8},{8,10},{10,12},{12,14},{14,16},{16,18},{18... | collective-permute-start | bytes 405512 | tf_op jit(solution)/shard_map/ppermute | solution.py:111
  62.1 5.0 %collective-permute-start.6 = (bf16[16,4224]{1,0:T(8,128)(2,1)S(1)}, bf16[16,4224]{1,0:T(8,128)(2,1)S(1)}, u32[]{:S(2)}, u32[]{:S(2)}) collective-permute-start(bf16[16,4224]{1,0:T(8,128)(2,1)S(1)} %collective-permute-done.5), channel_id=1, source_target_pairs={{0,30},{2,0},{4,2},{6,4},{8,6},{10,8},{12,10},{14,12},{16,14},{18,... | collective-permute-start | bytes 405512 | tf_op jit(solution)/shard_map/ppermute | solution.py:108
  68.4 1.9 %collective-permute-start.14 = (bf16[16,4224]{1,0:T(8,128)(2,1)S(1)}, bf16[16,4224]{1,0:T(8,128)(2,1)S(1)}, u32[]{:S(2)}, u32[]{:S(2)}) collective-permute-start(bf16[16,4224]{1,0:T(8,128)(2,1)S(1)} %collective-permute-done.13), channel_id=1, source_target_pairs={{0,2},{2,4},{4,6},{6,8},{8,10},{10,12},{12,14},{14,16},{16,18},{18... | collective-permute-start | bytes 405512 | tf_op jit(solution)/shard_map/ppermute | solution.py:111
  70.3 0.7 collective-permute-done.6
  71.1 5.3 %collective-permute-start.7 = (bf16[16,4224]{1,0:T(8,128)(2,1)S(1)}, bf16[16,4224]{1,0:T(8,128)(2,1)S(1)}, u32[]{:S(2)}, u32[]{:S(2)}) collective-permute-start(bf16[16,4224]{1,0:T(8,128)(2,1)S(1)} %collective-permute-done.6), channel_id=1, source_target_pairs={{0,30},{2,0},{4,2},{6,4},{8,6},{10,8},{12,10},{14,12},{16,14},{18,... | collective-permute-start | bytes 405512 | tf_op jit(solution)/shard_map/ppermute | solution.py:108
  77.0 4.1 %collective-permute-done.7 = bf16[16,4224]{1,0:T(8,128)(2,1)S(1)} collective-permute-done((bf16[16,4224]{1,0:T(8,128)(2,1)S(1)}, bf16[16,4224]{1,0:T(8,128)(2,1)S(1)}, u32[]{:S(2)}, u32[]{:S(2)}) %collective-permute-start.7) | collective-permute-done | bytes 135200 | tf_op jit(solution)/shard_map/ppermute | solution.py:108
  82.4 0.7 bitcast_dynamic-update-slice_fusion.10
  83.7 0.7 bitcast_dynamic-update-slice_fusion.6
  84.4 0.7 bitcast_dynamic-update-slice_fusion.4
  85.8 0.7 bitcast_dynamic-update-slice_fusion
  88.4 0.7 bitcast_dynamic-update-slice_fusion.25
  91.1 0.7 bitcast_dynamic-update-slice_fusion.17
  93.8 0.7 bitcast_dynamic-update-slice_fusion.9
  95.1 0.7 bitcast_dynamic-update-slice_fusion.5
  95.8 0.7 bitcast_dynamic-update-slice_fusion.3
  97.1 1.8 %constant_dynamic-slice_fusion.own_ref = bf16[16,16,4224]{2,1,0:T(8,128)(2,1)S(1)} fusion(bf16[32,16,4224]{2,1,0:T(8,128)(2,1)} %bitcast_dynamic-update-slice_fusion.1, s32[]{:T(128)S(6)} %select_n.26), kind=kLoop, calls=%fused_computation.40 | loop fusion | bytes 4325380 | tf_op jit(solution)/shard_map/jit(_roll_dynamic)/dynamic_slice | solution.py:114
  98.9 7.4 %collective-permute-start.15 = (bf16[16,16,4224]{2,1,0:T(8,128)(2,1)S(1)}, bf16[16,16,4224]{2,1,0:T(8,128)(2,1)}, u32[]{:S(2)}, u32[]{:S(2)}) collective-permute-start(bf16[16,16,4224]{2,1,0:T(8,128)(2,1)S(1)} %constant_dynamic-slice_fusion.own_ref), channel_id=1, source_target_pairs={{0,1},{1,0},{2,3},{3,2},{4,5},{5,4},{6,7},{7,6},{8,9},{9,8},{10,11... | collective-permute-start | bytes 6488072 | tf_op jit(solution)/shard_map/ppermute | solution.py:129
  106.3 0.7 copy.61.bias_ref
  107.0 0.7 copy.62.gain_ref
  107.7 0.7 copy.63.shift_ref
  108.4 6.3 %shard_map.73 = bf16[32,3072]{1,0:T(8,128)(2,1)} custom-call(bf16[3072,1024]{1,0:T(8,128)(2,1)} %bitcast.77, bf16[288,1024]{1,0:T(8,128)(2,1)} %bitcast.83, f32[32,1]{1,0:T(8,128)} %copy.61.bias_ref, f32[32,1]{1,0:T(8,128)} %copy.62.gain_ref, f32[32,1]{1,0:T(8,128)} %copy.63.shift_ref), custom_call_target="tpu_custom_call" | custom-call | flops 1811939328 | bytes 7077888 | tf_op jit(solution)/shard_map/pallas_call | solution.py:50
  114.7 1.4 reshape.46
  116.5 1.5 reshape.58
  117.9 17.6 %all-to-all-start = ((bf16[16,2,3072]{2,1,0:T(2,128)(2,1)}), bf16[16,2,3072]{2,1,0:T(2,128)(2,1)S(1)}, u32[]{:S(2)}, u32[]{:S(2)}) async-start(bf16[16,2,3072]{2,1,0:T(2,128)(2,1)} %reshape.58), calls=%async_computation | async-start | bytes 393216 | tf_op jit(solution)/shard_map/all_to_all | solution.py:137
  135.5 1.0 dynamic-slice_reduce_fusion
  136.5 1.0 slice_reduce_fusion
  138.1 13.5 %all-to-all-done = bf16[16,2,3072]{2,1,0:T(2,128)(2,1)S(1)} async-done(((bf16[16,2,3072]{2,1,0:T(2,128)(2,1)}), bf16[16,2,3072]{2,1,0:T(2,128)(2,1)S(1)}, u32[]{:S(2)}, u32[]{:S(2)}) %all-to-all-start) | async-done | bytes 196640 | tf_op jit(solution)/shard_map/all_to_all | solution.py:137
  152.8 0.7 all_gather.10
  153.6 2.9 %all_gather.11 = bf16[2,4,48,512]{3,2,1,0:T(8,128)(2,1)S(1)} all-gather(bf16[1,4,48,512]{3,2,1,0:T(8,128)(2,1)S(1)} %all_gather.10), channel_id=1, replica_groups=mesh['grp'=16,'z'=16,'core'=2] {'core'}, dimensions={0}, use_global_device_ids=true | all-gather | bytes 589824 | tf_op jit(solution)/shard_map/all_gather | solution.py:138
  157.0 1.1 copy.70
  158.1 1.5 reshape.54.act_ref
  159.6 4.7 %shard_map.74 = bf16[2,2,48,1024]{3,2,1,0:T(8,128)(2,1)} custom-call(s32[1]{0:T(128)} %bitcast.core_ref, bf16[96,1024]{1,0:T(8,128)(2,1)} %reshape.54.act_ref, bf16[16,16,4224]{2,1,0:T(8,128)(2,1)} %copy-done, bf16[16,16,4224]{2,1,0:T(8,128)(2,1)} %collective-permute-done.15.other_ref, f32[1,512]{1,0:T(1,128)} %reshape.53.bias_ref), custom_call_target="tpu_custom_call" | custom-call | flops 402653184 | bytes 4915200 | tf_op jit(solution)/shard_map/pallas_call | solution.py:89
  164.3 1.9 %reshape.51 = bf16[4,96,512]{2,1,0:T(8,128)(2,1)} reshape(bf16[2,2,48,1024]{3,2,1,0:T(8,128)(2,1)} %shard_map.74) | data formatting | bytes 786432 | tf_op jit(solution)/shard_map/reshape | solution.py:145
  (56 shorter events, 18.8 us)
Async XLA Ops:
  6.5 101.8 %all-gather.2.cloned.1.call-start = ((), (), s32[]{:S(2)}) async-start(), calls=%async_computation.1 | async-start | bytes 6488064 | tf_op jit(solution)/shard_map/all_gather | solution.py:124
  8.3 6.7 %collective-permute-start = (bf16[16,4224]{1,0:T(8,128)(2,1)S(1)}, bf16[16,4224]{1,0:T(8,128)(2,1)S(1)}, u32[]{:S(2)}, u32[]{:S(2)}) collective-permute-start(bf16[16,4224]{1,0:T(8,128)(2,1)S(1)} %fusion.1), channel_id=1, source_target_pairs={{0,30},{2,0},{4,2},{6,4},{8,6},{10,8},{12,10},{14,12},{16,14},{18,... | collective-permute-start | bytes 405512 | tf_op jit(solution)/shard_map/ppermute | solution.py:108
  10.2 14.2 %collective-permute-start.8 = (bf16[16,4224]{1,0:T(8,128)(2,1)S(1)}, bf16[16,4224]{1,0:T(8,128)(2,1)S(1)}, u32[]{:S(2)}, u32[]{:S(2)}) collective-permute-start(bf16[16,4224]{1,0:T(8,128)(2,1)S(1)} %fusion.1), channel_id=1, source_target_pairs={{0,2},{2,4},{4,6},{6,8},{8,10},{10,12},{12,14},{14,16},{16,18},{18... | collective-permute-start | bytes 405512 | tf_op jit(solution)/shard_map/ppermute | solution.py:111
  15.0 11.3 %collective-permute-start.1 = (bf16[16,4224]{1,0:T(8,128)(2,1)S(1)}, bf16[16,4224]{1,0:T(8,128)(2,1)S(1)}, u32[]{:S(2)}, u32[]{:S(2)}) collective-permute-start(bf16[16,4224]{1,0:T(8,128)(2,1)S(1)} %collective-permute-done), channel_id=1, source_target_pairs={{0,30},{2,0},{4,2},{6,4},{8,6},{10,8},{12,10},{14,12},{16,14},{18,... | collective-permute-start | bytes 405512 | tf_op jit(solution)/shard_map/ppermute | solution.py:108
  24.4 7.5 %collective-permute-start.9 = (bf16[16,4224]{1,0:T(8,128)(2,1)S(1)}, bf16[16,4224]{1,0:T(8,128)(2,1)S(1)}, u32[]{:S(2)}, u32[]{:S(2)}) collective-permute-start(bf16[16,4224]{1,0:T(8,128)(2,1)S(1)} %collective-permute-done.8), channel_id=1, source_target_pairs={{0,2},{2,4},{4,6},{6,8},{8,10},{10,12},{12,14},{14,16},{16,18},{18... | collective-permute-start | bytes 405512 | tf_op jit(solution)/shard_map/ppermute | solution.py:111
  26.4 7.5 %collective-permute-start.2 = (bf16[16,4224]{1,0:T(8,128)(2,1)S(1)}, bf16[16,4224]{1,0:T(8,128)(2,1)S(1)}, u32[]{:S(2)}, u32[]{:S(2)}) collective-permute-start(bf16[16,4224]{1,0:T(8,128)(2,1)S(1)} %collective-permute-done.1), channel_id=1, source_target_pairs={{0,30},{2,0},{4,2},{6,4},{8,6},{10,8},{12,10},{14,12},{16,14},{18,... | collective-permute-start | bytes 405512 | tf_op jit(solution)/shard_map/ppermute | solution.py:108
  32.0 8.9 %collective-permute-start.10 = (bf16[16,4224]{1,0:T(8,128)(2,1)S(1)}, bf16[16,4224]{1,0:T(8,128)(2,1)S(1)}, u32[]{:S(2)}, u32[]{:S(2)}) collective-permute-start(bf16[16,4224]{1,0:T(8,128)(2,1)S(1)} %collective-permute-done.9), channel_id=1, source_target_pairs={{0,2},{2,4},{4,6},{6,8},{8,10},{10,12},{12,14},{14,16},{16,18},{18... | collective-permute-start | bytes 405512 | tf_op jit(solution)/shard_map/ppermute | solution.py:111
  33.9 9.0 %collective-permute-start.3 = (bf16[16,4224]{1,0:T(8,128)(2,1)S(1)}, bf16[16,4224]{1,0:T(8,128)(2,1)S(1)}, u32[]{:S(2)}, u32[]{:S(2)}) collective-permute-start(bf16[16,4224]{1,0:T(8,128)(2,1)S(1)} %collective-permute-done.2), channel_id=1, source_target_pairs={{0,30},{2,0},{4,2},{6,4},{8,6},{10,8},{12,10},{14,12},{16,14},{18,... | collective-permute-start | bytes 405512 | tf_op jit(solution)/shard_map/ppermute | solution.py:108
  40.9 10.8 %collective-permute-start.11 = (bf16[16,4224]{1,0:T(8,128)(2,1)S(1)}, bf16[16,4224]{1,0:T(8,128)(2,1)S(1)}, u32[]{:S(2)}, u32[]{:S(2)}) collective-permute-start(bf16[16,4224]{1,0:T(8,128)(2,1)S(1)} %collective-permute-done.10), channel_id=1, source_target_pairs={{0,2},{2,4},{4,6},{6,8},{8,10},{10,12},{12,14},{14,16},{16,18},{18... | collective-permute-start | bytes 405512 | tf_op jit(solution)/shard_map/ppermute | solution.py:111
  42.9 10.7 %collective-permute-start.4 = (bf16[16,4224]{1,0:T(8,128)(2,1)S(1)}, bf16[16,4224]{1,0:T(8,128)(2,1)S(1)}, u32[]{:S(2)}, u32[]{:S(2)}) collective-permute-start(bf16[16,4224]{1,0:T(8,128)(2,1)S(1)} %collective-permute-done.3), channel_id=1, source_target_pairs={{0,30},{2,0},{4,2},{6,4},{8,6},{10,8},{12,10},{14,12},{16,14},{18,... | collective-permute-start | bytes 405512 | tf_op jit(solution)/shard_map/ppermute | solution.py:108
  51.7 7.7 %collective-permute-start.12 = (bf16[16,4224]{1,0:T(8,128)(2,1)S(1)}, bf16[16,4224]{1,0:T(8,128)(2,1)S(1)}, u32[]{:S(2)}, u32[]{:S(2)}) collective-permute-start(bf16[16,4224]{1,0:T(8,128)(2,1)S(1)} %collective-permute-done.11), channel_id=1, source_target_pairs={{0,2},{2,4},{4,6},{6,8},{8,10},{10,12},{12,14},{14,16},{16,18},{18... | collective-permute-start | bytes 405512 | tf_op jit(solution)/shard_map/ppermute | solution.py:111
  53.6 8.5 %collective-permute-start.5 = (bf16[16,4224]{1,0:T(8,128)(2,1)S(1)}, bf16[16,4224]{1,0:T(8,128)(2,1)S(1)}, u32[]{:S(2)}, u32[]{:S(2)}) collective-permute-start(bf16[16,4224]{1,0:T(8,128)(2,1)S(1)} %collective-permute-done.4), channel_id=1, source_target_pairs={{0,30},{2,0},{4,2},{6,4},{8,6},{10,8},{12,10},{14,12},{16,14},{18,... | collective-permute-start | bytes 405512 | tf_op jit(solution)/shard_map/ppermute | solution.py:108
  59.4 9.1 %collective-permute-start.13 = (bf16[16,4224]{1,0:T(8,128)(2,1)S(1)}, bf16[16,4224]{1,0:T(8,128)(2,1)S(1)}, u32[]{:S(2)}, u32[]{:S(2)}) collective-permute-start(bf16[16,4224]{1,0:T(8,128)(2,1)S(1)} %collective-permute-done.12), channel_id=1, source_target_pairs={{0,2},{2,4},{4,6},{6,8},{8,10},{10,12},{12,14},{14,16},{16,18},{18... | collective-permute-start | bytes 405512 | tf_op jit(solution)/shard_map/ppermute | solution.py:111
  62.1 8.9 %collective-permute-start.6 = (bf16[16,4224]{1,0:T(8,128)(2,1)S(1)}, bf16[16,4224]{1,0:T(8,128)(2,1)S(1)}, u32[]{:S(2)}, u32[]{:S(2)}) collective-permute-start(bf16[16,4224]{1,0:T(8,128)(2,1)S(1)} %collective-permute-done.5), channel_id=1, source_target_pairs={{0,30},{2,0},{4,2},{6,4},{8,6},{10,8},{12,10},{14,12},{16,14},{18,... | collective-permute-start | bytes 405512 | tf_op jit(solution)/shard_map/ppermute | solution.py:108
  68.4 13.3 %collective-permute-start.14 = (bf16[16,4224]{1,0:T(8,128)(2,1)S(1)}, bf16[16,4224]{1,0:T(8,128)(2,1)S(1)}, u32[]{:S(2)}, u32[]{:S(2)}) collective-permute-start(bf16[16,4224]{1,0:T(8,128)(2,1)S(1)} %collective-permute-done.13), channel_id=1, source_target_pairs={{0,2},{2,4},{4,6},{6,8},{8,10},{10,12},{12,14},{14,16},{16,18},{18... | collective-permute-start | bytes 405512 | tf_op jit(solution)/shard_map/ppermute | solution.py:111
  71.1 10.0 %collective-permute-start.7 = (bf16[16,4224]{1,0:T(8,128)(2,1)S(1)}, bf16[16,4224]{1,0:T(8,128)(2,1)S(1)}, u32[]{:S(2)}, u32[]{:S(2)}) collective-permute-start(bf16[16,4224]{1,0:T(8,128)(2,1)S(1)} %collective-permute-done.6), channel_id=1, source_target_pairs={{0,30},{2,0},{4,2},{6,4},{8,6},{10,8},{12,10},{14,12},{16,14},{18,... | collective-permute-start | bytes 405512 | tf_op jit(solution)/shard_map/ppermute | solution.py:108
  86.4 19.9 %copy-start.1 = (f32[32]{0:T(128)S(1)}, f32[32]{0:T(128)}, u32[]{:S(2)}) copy-start(f32[32]{0:T(128)} %param.9) | copy-start | bytes 388
  86.4 20.6 %copy-start.2 = (f32[32]{0:T(128)S(1)}, f32[32]{0:T(128)}, u32[]{:S(2)}) copy-start(f32[32]{0:T(128)} %param.10) | copy-start | bytes 388
  86.4 21.3 %copy-start.3 = (f32[32]{0:T(128)S(1)}, f32[32]{0:T(128)}, u32[]{:S(2)}) copy-start(f32[32]{0:T(128)} %param.11) | copy-start | bytes 388
  98.8 17.6 %copy-start = (bf16[16,16,4224]{2,1,0:T(8,128)(2,1)}, bf16[16,16,4224]{2,1,0:T(8,128)(2,1)S(1)}, u32[]{:S(2)}) copy-start(bf16[16,16,4224]{2,1,0:T(8,128)(2,1)S(1)} %constant_dynamic-slice_fusion.own_ref) | copy-start | bytes 6488068
  98.9 37.6 %collective-permute-start.15 = (bf16[16,16,4224]{2,1,0:T(8,128)(2,1)S(1)}, bf16[16,16,4224]{2,1,0:T(8,128)(2,1)}, u32[]{:S(2)}, u32[]{:S(2)}) collective-permute-start(bf16[16,16,4224]{2,1,0:T(8,128)(2,1)S(1)} %constant_dynamic-slice_fusion.own_ref), channel_id=1, source_target_pairs={{0,1},{1,0},{2,3},{3,2},{4,5},{5,4},{6,7},{7,6},{8,9},{9,8},{10,11... | collective-permute-start | bytes 6488072 | tf_op jit(solution)/shard_map/ppermute | solution.py:129
  117.9 33.7 %all-to-all-start = ((bf16[16,2,3072]{2,1,0:T(2,128)(2,1)}), bf16[16,2,3072]{2,1,0:T(2,128)(2,1)S(1)}, u32[]{:S(2)}, u32[]{:S(2)}) async-start(bf16[16,2,3072]{2,1,0:T(2,128)(2,1)} %reshape.58), calls=%async_computation | async-start | bytes 393216 | tf_op jit(solution)/shard_map/all_to_all | solution.py:137
Sparse Core Ops, SparseCore 0:
  13.9 84.2 all-gather.1

commit v8 on v7

--- a/solution.py
+++ b/solution.py
@@ -59,43 +59,51 @@
     )(x, w, col(conv_bias), col(norm_gain), col(norm_shift))
 
 
-def up_kernel(core_ref, act_ref, own_ref, other_ref, bias_ref, out_ref, wnat_ref, *, width_cols):
-    chips, slab, _ = own_ref.shape
-    channels = act_ref.shape[1]
-    core = core_ref[0]
-    for z in range(chips):
-        mine = pl.multiple_of(2 * slab * z + slab * core, slab)
-        theirs = pl.multiple_of(2 * slab * z + slab * (1 - core), slab)
-        wnat_ref[pl.ds(mine, slab), :] = own_ref[z, :, pl.ds(0, 4 * channels)]
-        wnat_ref[pl.ds(theirs, slab), :] = other_ref[z, :, pl.ds(0, 4 * channels)]
+def up_kernel(index_ref, act_ref, own_ref, other_ref, out_ref, wnat_ref, *, width_cols):
+    chips, slab, packed_width = own_ref.shape
+    positions, channels = act_ref.shape
+    core = index_ref[0]
+    here = index_ref[1]
+    for m in range(chips):
+        chip = (here + m) % chips
+        mine = pl.multiple_of(2 * slab * chip + slab * core, slab)
+        theirs = pl.multiple_of(2 * slab * chip + slab * (1 - core), slab)
+        wnat_ref[pl.ds(mine, slab), :] = own_ref[m]
+        wnat_ref[pl.ds(theirs, slab), :] = other_ref[m]
     act = act_ref[...]
     rows = out_ref.shape[0]
     outs = wnat_ref.shape[0]
+    nt = (((1,), (1,)), ((), ()))
+    lane = lax.broadcasted_iota(jnp.int32, (positions, packed_width - 4 * channels), 1)
+    ones = jnp.where(lane == 0, 1.0, 0.0).astype(act.dtype)
+    bias = lax.dot_general(ones, wnat_ref[:, pl.ds(4 * channels, packed_width - 4 * channels)], nt,
+                           preferred_element_type=jnp.float32)
     for ab in range(4):
         a, b = divmod(ab, 2)
-        res = lax.dot_general(act, wnat_ref[:, pl.ds(ab * channels, channels)], (((1,), (1,)), ((), ())),
+        res = lax.dot_general(act, wnat_ref[:, pl.ds(ab * channels, channels)], nt,
                               preferred_element_type=jnp.float32)
-        res = (res + bias_ref[...]).astype(out_ref.dtype)
+        res = (res + bias).astype(out_ref.dtype)
         for i in range(rows):
             out_ref[i, a, :, pl.ds(b * outs, outs)] = res[i * width_cols:(i + 1) * width_cols, :]
 
 
-def up_conv(core, act, own, other, bias_row):
+def up_conv(core, here, act, own, other):
     rows, width_cols, channels = act.shape
-    chips, slab, _ = own.shape
+    chips, slab, packed_width = own.shape
     outs = 2 * chips * slab
     vmem = pl.BlockSpec(memory_space=pltpu.VMEM)
     smem = pl.BlockSpec(memory_space=pltpu.SMEM)
+    index = jnp.stack([core, here]).astype(jnp.int32)
     return pl.pallas_call(
         functools.partial(up_kernel, width_cols=width_cols),
         out_shape=jax.ShapeDtypeStruct((rows, 2, width_cols, 2 * outs), jnp.bfloat16),
-        in_specs=[smem, vmem, vmem, vmem, vmem],
+        in_specs=[smem, vmem, vmem, vmem],
         out_specs=vmem,
-        scratch_shapes=[pltpu.VMEM((outs, 4 * channels), jnp.bfloat16)],
+        scratch_shapes=[pltpu.VMEM((outs, packed_width), jnp.bfloat16)],
         cost_estimate=pl.CostEstimate(
             flops=2 * rows * width_cols * channels * 4 * outs, transcendentals=0,
             bytes_accessed=act.size * 2 + 2 * own.size * 2 + rows * width_cols * 4 * outs * 2),
-    )(jnp.reshape(core, (1,)).astype(jnp.int32), act.reshape(rows * width_cols, channels), own, other, bias_row)
+    )(index, act.reshape(rows * width_cols, channels), own, other)
 
 
 def ring_gather(block, axis):
@@ -110,8 +118,7 @@
         if k < chips - chips // 2:
             behind = lax.ppermute(behind, axis, step_down)
             from_behind.append(behind)
-    stacked = jnp.stack([block] + from_ahead + from_behind[::-1])
-    return jnp.roll(stacked, lax.axis_index(axis), axis=0)
+    return jnp.stack([block] + from_ahead + from_behind[::-1])
 
 
 def body(coarse, conv_weight, conv_bias, norm_gain, norm_shift, up_weight, up_bias):
@@ -127,9 +134,6 @@
     packed = jnp.concatenate([flat, jnp.pad(up_bias[:, None], ((0, 0), (0, 127)))], axis=1)
     packed_z = ring_gather(packed, "z")
     packed_other = lax.ppermute(packed_z, "core", [(0, 1), (1, 0)])
-    bias_halves = jnp.stack([packed_z[:, :, flat.shape[1]], packed_other[:, :, flat.shape[1]]], axis=1)
-    bias_halves = jnp.where(core == 0, bias_halves, bias_halves[:, ::-1])
-    bias_row = bias_halves.astype(jnp.float32).reshape(1, -1)
 
     activated = conv_norm(whole, conv_weight, conv_bias, norm_gain, norm_shift)
     activated = jnp.transpose(activated).reshape(height, width_cols, outputs)
@@ -141,7 +145,7 @@
     own = own.reshape((2, half, width_cols, chips, outputs))
     own = jnp.transpose(own, (1, 2, 3, 0, 4)).reshape(half, width_cols, channels)
 
-    fine = up_conv(core, own, packed_z, packed_other, bias_row)
+    fine = up_conv(core, lax.axis_index("z"), own, packed_z, packed_other)
     return fine.reshape(2 * half, 2 * width_cols, -1)
 
 

time: 174 us -> 161 us (0.925)
  local copies, waits for them, and re-layouts: 38.1 us -> 23.8 us
  waiting for transfers between devices: 21.7 us -> 25.6 us
  starting transfers between devices: 84.2 us -> 82.3 us
    unnamed x39 -> x22, local copies, waits for them, and re-layouts: 21.3 us -> 11.3 us
    all_to_all x1, starting transfers between devices: 17.6 us -> 14.8 us  [body(): lax.all_to_all(activated, 'z', split_axis=0, concat_axis=2, tiled=True)]
    all_gather x1, waiting for transfers between devices: 0.01 us -> 2.18 us  [body(): whole = lax.all_gather(coarse, ('z', 'core'), axis=0, tiled=True)]
    all_to_all x1, waiting for transfers between devices: 13.5 us -> 15.5 us  [body(): lax.all_to_all(activated, 'z', split_axis=0, concat_axis=2, tiled=True)]
    slice x2 -> x0, local copies, waits for them, and re-layouts: 1.9 us -> none  [the longest x1 0.95 us: body(): packed_other[:, :, flat.shape[1]]]
    dynamic_slice x1 -> x0, local copies, waits for them, and re-layouts: 1.76 us -> none  [ring_gather(): return jnp.roll(stacked, lax.axis_index(axis), axis=0)]
  transfers between devices with their start and end apart: 18 -> 18, of which waited for: 7 -> 8; matrix products, arithmetic and copies ran while one was open for 18% -> 13% of each run, Pallas kernels for 4% -> 4%
where the time goes in v8:
time: 161 us
  starting transfers between devices  82.3 us (51%)
  waiting for transfers between devices  25.6 us (16%)
  local copies, waits for them, and re-layouts  23.8 us (15%)
  between operations  13.7 us (9%)
  Pallas kernels  11.1 us (7%)
  blocking collectives  2.76 us (2%)
    ppermute x8, starting transfers between devices, ring_gather(): ahead = lax.ppermute(ahead, axis, step_up)  43.7 us
    ppermute x7, starting transfers between devices, ring_gather(): behind = lax.ppermute(behind, axis, step_down)  15.9 us
    all_to_all x1, waiting for transfers between devices, body(): lax.all_to_all(activated, 'z', split_axis=0, concat_axis=2, tiled=True)  15.5 us
    all_to_all x1, starting transfers between devices, body(): lax.all_to_all(activated, 'z', split_axis=0, concat_axis=2, tiled=True)  14.8 us
    unnamed x22, local copies, waits for them, and re-layouts  11.3 us
    ppermute x1, starting transfers between devices, body(): packed_other = lax.ppermute(packed_z, 'core', [(0, 1), (1, 0)])  7.9 us
    pallas_call x1, Pallas kernels, conv_norm(): pl.pallas_call(functools.partial(conv_norm_kernel, height=height, width_c...  6.3 us
    ppermute x8, waiting for transfers between devices, ring_gather(): ahead = lax.ppermute(ahead, axis, step_up)  5.23 us
  transfers between devices with their start and end apart: 18, of which 8 were waited for; matrix products, arithmetic and copies ran while one was open for 13% of the time, Pallas kernels for 4%

profile of v8, /device:TPU:63, one launch (start us, length us, event | category | flops | bytes accessed | tf_op | source)
XLA Modules:
  0.0 160.6 jit_solution(9710588648114166748)
XLA Ops:
  6.5 0.7 copy.25
  7.3 1.0 reshape.39
  8.3 1.9 %collective-permute-start = (bf16[16,4224]{1,0:T(8,128)(2,1)S(1)}, bf16[16,4224]{1,0:T(8,128)(2,1)S(1)}, u32[]{:S(2)}, u32[]{:S(2)}) collective-permute-start(bf16[16,4224]{1,0:T(8,128)(2,1)S(1)} %fusion.1), channel_id=1, source_target_pairs={{0,30},{2,0},{4,2},{6,4},{8,6},{10,8},{12,10},{14,12},{16,14},{18,... | collective-permute-start | bytes 405512 | tf_op jit(solution)/shard_map/ppermute | solution.py:116
  10.2 3.5 %collective-permute-start.8 = (bf16[16,4224]{1,0:T(8,128)(2,1)S(1)}, bf16[16,4224]{1,0:T(8,128)(2,1)S(1)}, u32[]{:S(2)}, u32[]{:S(2)}) collective-permute-start(bf16[16,4224]{1,0:T(8,128)(2,1)S(1)} %fusion.1), channel_id=1, source_target_pairs={{0,2},{2,4},{4,6},{6,8},{8,10},{10,12},{12,14},{14,16},{16,18},{18... | collective-permute-start | bytes 405512 | tf_op jit(solution)/shard_map/ppermute | solution.py:119
  13.8 0.7 bitcast_dynamic-update-slice_fusion.15
  15.0 8.8 %collective-permute-start.1 = (bf16[16,4224]{1,0:T(8,128)(2,1)S(1)}, bf16[16,4224]{1,0:T(8,128)(2,1)S(1)}, u32[]{:S(2)}, u32[]{:S(2)}) collective-permute-start(bf16[16,4224]{1,0:T(8,128)(2,1)S(1)} %collective-permute-done), channel_id=1, source_target_pairs={{0,30},{2,0},{4,2},{6,4},{8,6},{10,8},{12,10},{14,12},{16,14},{18,... | collective-permute-start | bytes 405512 | tf_op jit(solution)/shard_map/ppermute | solution.py:116
  23.8 0.7 bitcast_dynamic-update-slice_fusion.14
  24.5 1.9 %collective-permute-start.9 = (bf16[16,4224]{1,0:T(8,128)(2,1)S(1)}, bf16[16,4224]{1,0:T(8,128)(2,1)S(1)}, u32[]{:S(2)}, u32[]{:S(2)}) collective-permute-start(bf16[16,4224]{1,0:T(8,128)(2,1)S(1)} %collective-permute-done.8), channel_id=1, source_target_pairs={{0,2},{2,4},{4,6},{6,8},{8,10},{10,12},{12,14},{14,16},{16,18},{18... | collective-permute-start | bytes 405512 | tf_op jit(solution)/shard_map/ppermute | solution.py:119
  26.4 4.9 %collective-permute-start.2 = (bf16[16,4224]{1,0:T(8,128)(2,1)S(1)}, bf16[16,4224]{1,0:T(8,128)(2,1)S(1)}, u32[]{:S(2)}, u32[]{:S(2)}) collective-permute-start(bf16[16,4224]{1,0:T(8,128)(2,1)S(1)} %collective-permute-done.1), channel_id=1, source_target_pairs={{0,30},{2,0},{4,2},{6,4},{8,6},{10,8},{12,10},{14,12},{16,14},{18,... | collective-permute-start | bytes 405512 | tf_op jit(solution)/shard_map/ppermute | solution.py:116
  31.3 0.7 bitcast_dynamic-update-slice_fusion.13
  32.0 1.9 %collective-permute-start.10 = (bf16[16,4224]{1,0:T(8,128)(2,1)S(1)}, bf16[16,4224]{1,0:T(8,128)(2,1)S(1)}, u32[]{:S(2)}, u32[]{:S(2)}) collective-permute-start(bf16[16,4224]{1,0:T(8,128)(2,1)S(1)} %collective-permute-done.9), channel_id=1, source_target_pairs={{0,2},{2,4},{4,6},{6,8},{8,10},{10,12},{12,14},{14,16},{16,18},{18... | collective-permute-start | bytes 405512 | tf_op jit(solution)/shard_map/ppermute | solution.py:119
  33.9 6.3 %collective-permute-start.3 = (bf16[16,4224]{1,0:T(8,128)(2,1)S(1)}, bf16[16,4224]{1,0:T(8,128)(2,1)S(1)}, u32[]{:S(2)}, u32[]{:S(2)}) collective-permute-start(bf16[16,4224]{1,0:T(8,128)(2,1)S(1)} %collective-permute-done.2), channel_id=1, source_target_pairs={{0,30},{2,0},{4,2},{6,4},{8,6},{10,8},{12,10},{14,12},{16,14},{18,... | collective-permute-start | bytes 405512 | tf_op jit(solution)/shard_map/ppermute | solution.py:116
  40.2 0.7 bitcast_dynamic-update-slice_fusion.12
  40.9 2.0 %collective-permute-start.11 = (bf16[16,4224]{1,0:T(8,128)(2,1)S(1)}, bf16[16,4224]{1,0:T(8,128)(2,1)S(1)}, u32[]{:S(2)}, u32[]{:S(2)}) collective-permute-start(bf16[16,4224]{1,0:T(8,128)(2,1)S(1)} %collective-permute-done.10), channel_id=1, source_target_pairs={{0,2},{2,4},{4,6},{6,8},{8,10},{10,12},{12,14},{14,16},{16,18},{18... | collective-permute-start | bytes 405512 | tf_op jit(solution)/shard_map/ppermute | solution.py:119
  42.9 6.4 %collective-permute-start.4 = (bf16[16,4224]{1,0:T(8,128)(2,1)S(1)}, bf16[16,4224]{1,0:T(8,128)(2,1)S(1)}, u32[]{:S(2)}, u32[]{:S(2)}) collective-permute-start(bf16[16,4224]{1,0:T(8,128)(2,1)S(1)} %collective-permute-done.3), channel_id=1, source_target_pairs={{0,30},{2,0},{4,2},{6,4},{8,6},{10,8},{12,10},{14,12},{16,14},{18,... | collective-permute-start | bytes 405512 | tf_op jit(solution)/shard_map/ppermute | solution.py:116
  49.9 1.8 %collective-permute-done.11 = bf16[16,4224]{1,0:T(8,128)(2,1)S(1)} collective-permute-done((bf16[16,4224]{1,0:T(8,128)(2,1)S(1)}, bf16[16,4224]{1,0:T(8,128)(2,1)S(1)}, u32[]{:S(2)}, u32[]{:S(2)}) %collective-permute-start.11) | collective-permute-done | bytes 135200 | tf_op jit(solution)/shard_map/ppermute | solution.py:119
  51.7 1.9 %collective-permute-start.12 = (bf16[16,4224]{1,0:T(8,128)(2,1)S(1)}, bf16[16,4224]{1,0:T(8,128)(2,1)S(1)}, u32[]{:S(2)}, u32[]{:S(2)}) collective-permute-start(bf16[16,4224]{1,0:T(8,128)(2,1)S(1)} %collective-permute-done.11), channel_id=1, source_target_pairs={{0,2},{2,4},{4,6},{6,8},{8,10},{10,12},{12,14},{14,16},{16,18},{18... | collective-permute-start | bytes 405512 | tf_op jit(solution)/shard_map/ppermute | solution.py:119
  53.6 4.8 %collective-permute-start.5 = (bf16[16,4224]{1,0:T(8,128)(2,1)S(1)}, bf16[16,4224]{1,0:T(8,128)(2,1)S(1)}, u32[]{:S(2)}, u32[]{:S(2)}) collective-permute-start(bf16[16,4224]{1,0:T(8,128)(2,1)S(1)} %collective-permute-done.4), channel_id=1, source_target_pairs={{0,30},{2,0},{4,2},{6,4},{8,6},{10,8},{12,10},{14,12},{16,14},{18,... | collective-permute-start | bytes 405512 | tf_op jit(solution)/shard_map/ppermute | solution.py:116
  58.4 0.7 bitcast_dynamic-update-slice_fusion.10
  59.4 2.7 %collective-permute-start.13 = (bf16[16,4224]{1,0:T(8,128)(2,1)S(1)}, bf16[16,4224]{1,0:T(8,128)(2,1)S(1)}, u32[]{:S(2)}, u32[]{:S(2)}) collective-permute-start(bf16[16,4224]{1,0:T(8,128)(2,1)S(1)} %collective-permute-done.12), channel_id=1, source_target_pairs={{0,2},{2,4},{4,6},{6,8},{8,10},{10,12},{12,14},{14,16},{16,18},{18... | collective-permute-start | bytes 405512 | tf_op jit(solution)/shard_map/ppermute | solution.py:119
  62.1 5.1 %collective-permute-start.6 = (bf16[16,4224]{1,0:T(8,128)(2,1)S(1)}, bf16[16,4224]{1,0:T(8,128)(2,1)S(1)}, u32[]{:S(2)}, u32[]{:S(2)}) collective-permute-start(bf16[16,4224]{1,0:T(8,128)(2,1)S(1)} %collective-permute-done.5), channel_id=1, source_target_pairs={{0,30},{2,0},{4,2},{6,4},{8,6},{10,8},{12,10},{14,12},{16,14},{18,... | collective-permute-start | bytes 405512 | tf_op jit(solution)/shard_map/ppermute | solution.py:116
  67.3 0.7 bitcast_dynamic-update-slice_fusion.9
  68.5 1.9 %collective-permute-start.14 = (bf16[16,4224]{1,0:T(8,128)(2,1)S(1)}, bf16[16,4224]{1,0:T(8,128)(2,1)S(1)}, u32[]{:S(2)}, u32[]{:S(2)}) collective-permute-start(bf16[16,4224]{1,0:T(8,128)(2,1)S(1)} %collective-permute-done.13), channel_id=1, source_target_pairs={{0,2},{2,4},{4,6},{6,8},{8,10},{10,12},{12,14},{14,16},{16,18},{18... | collective-permute-start | bytes 405512 | tf_op jit(solution)/shard_map/ppermute | solution.py:119
  70.4 1.2 collective-permute-done.6
  71.6 5.5 %collective-permute-start.7 = (bf16[16,4224]{1,0:T(8,128)(2,1)S(1)}, bf16[16,4224]{1,0:T(8,128)(2,1)S(1)}, u32[]{:S(2)}, u32[]{:S(2)}) collective-permute-start(bf16[16,4224]{1,0:T(8,128)(2,1)S(1)} %collective-permute-done.6), channel_id=1, source_target_pairs={{0,30},{2,0},{4,2},{6,4},{8,6},{10,8},{12,10},{14,12},{16,14},{18,... | collective-permute-start | bytes 405512 | tf_op jit(solution)/shard_map/ppermute | solution.py:116
  77.1 0.7 bitcast_dynamic-update-slice_fusion.8
  77.8 3.5 %collective-permute-done.7 = bf16[16,4224]{1,0:T(8,128)(2,1)S(1)} collective-permute-done((bf16[16,4224]{1,0:T(8,128)(2,1)S(1)}, bf16[16,4224]{1,0:T(8,128)(2,1)S(1)}, u32[]{:S(2)}, u32[]{:S(2)}) %collective-permute-start.7) | collective-permute-done | bytes 135200 | tf_op jit(solution)/shard_map/ppermute | solution.py:116
  83.3 0.7 bitcast_dynamic-update-slice_fusion.4
  84.0 0.7 bitcast_dynamic-update-slice_fusion.3
  84.6 0.7 bitcast_dynamic-update-slice_fusion.2
  85.3 0.7 bitcast_dynamic-update-slice_fusion.1
  86.0 0.7 bitcast_dynamic-update-slice_fusion.own_ref
  86.6 7.9 %collective-permute-start.15 = (bf16[16,16,4224]{2,1,0:T(8,128)(2,1)}, bf16[16,16,4224]{2,1,0:T(8,128)(2,1)}, u32[]{:S(2)}, u32[]{:S(2)}) collective-permute-start(bf16[16,16,4224]{2,1,0:T(8,128)(2,1)} %bitcast_dynamic-update-slice_fusion.own_ref), channel_id=1, source_target_pairs={{0,1},{1,0},{2,3},{3,2},{4,5},{5,4},{6,7},{7,6},{8,9},{9,8},{10,11... | collective-permute-start | bytes 6488072 | tf_op jit(solution)/shard_map/ppermute | solution.py:136
  94.5 0.7 copy.19.bias_ref
  95.2 0.7 copy.20.gain_ref
  95.9 0.7 copy.21.shift_ref
  96.6 2.2 %all-gather.2.cloned.1.call-done = bf16[64,48,1024]{2,1,0:T(8,128)(2,1)} async-done(((bf16[2,48,1024]{2,1,0:T(8,128)(2,1)}), bf16[64,48,1024]{2,1,0:T(8,128)(2,1)}) %all-gather.2.cloned.1.call-update) | async-done | bytes 6291472 | tf_op jit(solution)/shard_map/all_gather | solution.py:131
  98.8 6.3 %shard_map.73 = bf16[32,3072]{1,0:T(8,128)(2,1)} custom-call(bf16[3072,1024]{1,0:T(8,128)(2,1)} %bitcast.60, bf16[288,1024]{1,0:T(8,128)(2,1)} %bitcast.66, f32[32,1]{1,0:T(8,128)} %copy.19.bias_ref, f32[32,1]{1,0:T(8,128)} %copy.20.gain_ref, f32[32,1]{1,0:T(8,128)} %copy.21.shift_ref), custom_call_target="tpu_custom_call" | custom-call | flops 1811939328 | bytes 7077888 | tf_op jit(solution)/shard_map/pallas_call | solution.py:50
  105.1 1.4 reshape.37
  106.9 1.5 reshape.42
  108.3 14.8 %all-to-all-start = ((bf16[16,2,3072]{2,1,0:T(2,128)(2,1)}), bf16[16,2,3072]{2,1,0:T(2,128)(2,1)S(1)}, u32[]{:S(2)}, u32[]{:S(2)}) async-start(bf16[16,2,3072]{2,1,0:T(2,128)(2,1)} %reshape.42), calls=%async_computation | async-start | bytes 393216 | tf_op jit(solution)/shard_map/all_to_all | solution.py:141
  123.8 15.5 %all-to-all-done = bf16[16,2,3072]{2,1,0:T(2,128)(2,1)S(1)} async-done(((bf16[16,2,3072]{2,1,0:T(2,128)(2,1)}), bf16[16,2,3072]{2,1,0:T(2,128)(2,1)S(1)}, u32[]{:S(2)}, u32[]{:S(2)}) %all-to-all-start) | async-done | bytes 196640 | tf_op jit(solution)/shard_map/all_to_all | solution.py:141
  140.5 0.7 all_gather.10
  141.3 2.8 %all_gather.11 = bf16[2,4,48,512]{3,2,1,0:T(8,128)(2,1)S(1)} all-gather(bf16[1,4,48,512]{3,2,1,0:T(8,128)(2,1)S(1)} %all_gather.10), channel_id=1, replica_groups=mesh['grp'=16,'z'=16,'core'=2] {'core'}, dimensions={0}, use_global_device_ids=true | all-gather | bytes 589824 | tf_op jit(solution)/shard_map/all_gather | solution.py:142
  144.5 1.1 copy.27
  145.6 1.5 reshape.41.act_ref
  147.1 4.8 %shard_map.74 = bf16[2,2,48,1024]{3,2,1,0:T(8,128)(2,1)} custom-call(s32[2]{0:T(128)} %pad_add_fusion.index_ref, bf16[96,1024]{1,0:T(8,128)(2,1)} %reshape.41.act_ref, bf16[16,16,4224]{2,1,0:T(8,128)(2,1)} %bitcast_dynamic-update-slice_fusion.own_ref, bf16[16,16,4224]{2,1,0:T(8,128)(2,1)} %collective-permute-done.15.other_ref), custom_call_target="tpu_custom_call" | custom-call | flops 402653184 | bytes 4915200 | tf_op jit(solution)/shard_map/pallas_call | solution.py:97
  151.9 1.9 %reshape.40 = bf16[4,96,512]{2,1,0:T(8,128)(2,1)} reshape(bf16[2,2,48,1024]{3,2,1,0:T(8,128)(2,1)} %shard_map.74) | data formatting | bytes 786432 | tf_op jit(solution)/shard_map/reshape | solution.py:149
  (32 shorter events, 6.7 us)
Async XLA Ops:
  6.5 92.2 %all-gather.2.cloned.1.call-start = ((), (), s32[]{:S(2)}) async-start(), calls=%async_computation.1 | async-start | bytes 6488064 | tf_op jit(solution)/shard_map/all_gather | solution.py:131
  8.3 6.7 %collective-permute-start = (bf16[16,4224]{1,0:T(8,128)(2,1)S(1)}, bf16[16,4224]{1,0:T(8,128)(2,1)S(1)}, u32[]{:S(2)}, u32[]{:S(2)}) collective-permute-start(bf16[16,4224]{1,0:T(8,128)(2,1)S(1)} %fusion.1), channel_id=1, source_target_pairs={{0,30},{2,0},{4,2},{6,4},{8,6},{10,8},{12,10},{14,12},{16,14},{18,... | collective-permute-start | bytes 405512 | tf_op jit(solution)/shard_map/ppermute | solution.py:116
  10.2 14.3 %collective-permute-start.8 = (bf16[16,4224]{1,0:T(8,128)(2,1)S(1)}, bf16[16,4224]{1,0:T(8,128)(2,1)S(1)}, u32[]{:S(2)}, u32[]{:S(2)}) collective-permute-start(bf16[16,4224]{1,0:T(8,128)(2,1)S(1)} %fusion.1), channel_id=1, source_target_pairs={{0,2},{2,4},{4,6},{6,8},{8,10},{10,12},{12,14},{14,16},{16,18},{18... | collective-permute-start | bytes 405512 | tf_op jit(solution)/shard_map/ppermute | solution.py:119
  13.8 80.7 %copy-start = (f32[32]{0:T(128)S(1)}, f32[32]{0:T(128)}, u32[]{:S(2)}) copy-start(f32[32]{0:T(128)} %param.9) | copy-start | bytes 388
  13.8 81.4 %copy-start.1 = (f32[32]{0:T(128)S(1)}, f32[32]{0:T(128)}, u32[]{:S(2)}) copy-start(f32[32]{0:T(128)} %param.10) | copy-start | bytes 388
  13.8 82.1 %copy-start.2 = (f32[32]{0:T(128)S(1)}, f32[32]{0:T(128)}, u32[]{:S(2)}) copy-start(f32[32]{0:T(128)} %param.11) | copy-start | bytes 388
  15.0 11.4 %collective-permute-start.1 = (bf16[16,4224]{1,0:T(8,128)(2,1)S(1)}, bf16[16,4224]{1,0:T(8,128)(2,1)S(1)}, u32[]{:S(2)}, u32[]{:S(2)}) collective-permute-start(bf16[16,4224]{1,0:T(8,128)(2,1)S(1)} %collective-permute-done), channel_id=1, source_target_pairs={{0,30},{2,0},{4,2},{6,4},{8,6},{10,8},{12,10},{14,12},{16,14},{18,... | collective-permute-start | bytes 405512 | tf_op jit(solution)/shard_map/ppermute | solution.py:116
  24.5 7.5 %collective-permute-start.9 = (bf16[16,4224]{1,0:T(8,128)(2,1)S(1)}, bf16[16,4224]{1,0:T(8,128)(2,1)S(1)}, u32[]{:S(2)}, u32[]{:S(2)}) collective-permute-start(bf16[16,4224]{1,0:T(8,128)(2,1)S(1)} %collective-permute-done.8), channel_id=1, source_target_pairs={{0,2},{2,4},{4,6},{6,8},{8,10},{10,12},{12,14},{14,16},{16,18},{18... | collective-permute-start | bytes 405512 | tf_op jit(solution)/shard_map/ppermute | solution.py:119
  26.4 7.5 %collective-permute-start.2 = (bf16[16,4224]{1,0:T(8,128)(2,1)S(1)}, bf16[16,4224]{1,0:T(8,128)(2,1)S(1)}, u32[]{:S(2)}, u32[]{:S(2)}) collective-permute-start(bf16[16,4224]{1,0:T(8,128)(2,1)S(1)} %collective-permute-done.1), channel_id=1, source_target_pairs={{0,30},{2,0},{4,2},{6,4},{8,6},{10,8},{12,10},{14,12},{16,14},{18,... | collective-permute-start | bytes 405512 | tf_op jit(solution)/shard_map/ppermute | solution.py:116
  32.0 8.9 %collective-permute-start.10 = (bf16[16,4224]{1,0:T(8,128)(2,1)S(1)}, bf16[16,4224]{1,0:T(8,128)(2,1)S(1)}, u32[]{:S(2)}, u32[]{:S(2)}) collective-permute-start(bf16[16,4224]{1,0:T(8,128)(2,1)S(1)} %collective-permute-done.9), channel_id=1, source_target_pairs={{0,2},{2,4},{4,6},{6,8},{8,10},{10,12},{12,14},{14,16},{16,18},{18... | collective-permute-start | bytes 405512 | tf_op jit(solution)/shard_map/ppermute | solution.py:119
  33.9 9.0 %collective-permute-start.3 = (bf16[16,4224]{1,0:T(8,128)(2,1)S(1)}, bf16[16,4224]{1,0:T(8,128)(2,1)S(1)}, u32[]{:S(2)}, u32[]{:S(2)}) collective-permute-start(bf16[16,4224]{1,0:T(8,128)(2,1)S(1)} %collective-permute-done.2), channel_id=1, source_target_pairs={{0,30},{2,0},{4,2},{6,4},{8,6},{10,8},{12,10},{14,12},{16,14},{18,... | collective-permute-start | bytes 405512 | tf_op jit(solution)/shard_map/ppermute | solution.py:116
  40.9 10.8 %collective-permute-start.11 = (bf16[16,4224]{1,0:T(8,128)(2,1)S(1)}, bf16[16,4224]{1,0:T(8,128)(2,1)S(1)}, u32[]{:S(2)}, u32[]{:S(2)}) collective-permute-start(bf16[16,4224]{1,0:T(8,128)(2,1)S(1)} %collective-permute-done.10), channel_id=1, source_target_pairs={{0,2},{2,4},{4,6},{6,8},{8,10},{10,12},{12,14},{14,16},{16,18},{18... | collective-permute-start | bytes 405512 | tf_op jit(solution)/shard_map/ppermute | solution.py:119
  42.9 10.7 %collective-permute-start.4 = (bf16[16,4224]{1,0:T(8,128)(2,1)S(1)}, bf16[16,4224]{1,0:T(8,128)(2,1)S(1)}, u32[]{:S(2)}, u32[]{:S(2)}) collective-permute-start(bf16[16,4224]{1,0:T(8,128)(2,1)S(1)} %collective-permute-done.3), channel_id=1, source_target_pairs={{0,30},{2,0},{4,2},{6,4},{8,6},{10,8},{12,10},{14,12},{16,14},{18,... | collective-permute-start | bytes 405512 | tf_op jit(solution)/shard_map/ppermute | solution.py:116
  51.7 7.7 %collective-permute-start.12 = (bf16[16,4224]{1,0:T(8,128)(2,1)S(1)}, bf16[16,4224]{1,0:T(8,128)(2,1)S(1)}, u32[]{:S(2)}, u32[]{:S(2)}) collective-permute-start(bf16[16,4224]{1,0:T(8,128)(2,1)S(1)} %collective-permute-done.11), channel_id=1, source_target_pairs={{0,2},{2,4},{4,6},{6,8},{8,10},{10,12},{12,14},{14,16},{16,18},{18... | collective-permute-start | bytes 405512 | tf_op jit(solution)/shard_map/ppermute | solution.py:119
  53.6 8.5 %collective-permute-start.5 = (bf16[16,4224]{1,0:T(8,128)(2,1)S(1)}, bf16[16,4224]{1,0:T(8,128)(2,1)S(1)}, u32[]{:S(2)}, u32[]{:S(2)}) collective-permute-start(bf16[16,4224]{1,0:T(8,128)(2,1)S(1)} %collective-permute-done.4), channel_id=1, source_target_pairs={{0,30},{2,0},{4,2},{6,4},{8,6},{10,8},{12,10},{14,12},{16,14},{18,... | collective-permute-start | bytes 405512 | tf_op jit(solution)/shard_map/ppermute | solution.py:116
  59.4 9.1 %collective-permute-start.13 = (bf16[16,4224]{1,0:T(8,128)(2,1)S(1)}, bf16[16,4224]{1,0:T(8,128)(2,1)S(1)}, u32[]{:S(2)}, u32[]{:S(2)}) collective-permute-start(bf16[16,4224]{1,0:T(8,128)(2,1)S(1)} %collective-permute-done.12), channel_id=1, source_target_pairs={{0,2},{2,4},{4,6},{6,8},{8,10},{10,12},{12,14},{14,16},{16,18},{18... | collective-permute-start | bytes 405512 | tf_op jit(solution)/shard_map/ppermute | solution.py:119
  62.1 9.5 %collective-permute-start.6 = (bf16[16,4224]{1,0:T(8,128)(2,1)S(1)}, bf16[16,4224]{1,0:T(8,128)(2,1)S(1)}, u32[]{:S(2)}, u32[]{:S(2)}) collective-permute-start(bf16[16,4224]{1,0:T(8,128)(2,1)S(1)} %collective-permute-done.5), channel_id=1, source_target_pairs={{0,30},{2,0},{4,2},{6,4},{8,6},{10,8},{12,10},{14,12},{16,14},{18,... | collective-permute-start | bytes 405512 | tf_op jit(solution)/shard_map/ppermute | solution.py:116
  68.5 13.5 %collective-permute-start.14 = (bf16[16,4224]{1,0:T(8,128)(2,1)S(1)}, bf16[16,4224]{1,0:T(8,128)(2,1)S(1)}, u32[]{:S(2)}, u32[]{:S(2)}) collective-permute-start(bf16[16,4224]{1,0:T(8,128)(2,1)S(1)} %collective-permute-done.13), channel_id=1, source_target_pairs={{0,2},{2,4},{4,6},{6,8},{8,10},{10,12},{12,14},{14,16},{16,18},{18... | collective-permute-start | bytes 405512 | tf_op jit(solution)/shard_map/ppermute | solution.py:119
  71.6 9.7 %collective-permute-start.7 = (bf16[16,4224]{1,0:T(8,128)(2,1)S(1)}, bf16[16,4224]{1,0:T(8,128)(2,1)S(1)}, u32[]{:S(2)}, u32[]{:S(2)}) collective-permute-start(bf16[16,4224]{1,0:T(8,128)(2,1)S(1)} %collective-permute-done.6), channel_id=1, source_target_pairs={{0,30},{2,0},{4,2},{6,4},{8,6},{10,8},{12,10},{14,12},{16,14},{18,... | collective-permute-start | bytes 405512 | tf_op jit(solution)/shard_map/ppermute | solution.py:116
  86.6 60.5 %collective-permute-start.15 = (bf16[16,16,4224]{2,1,0:T(8,128)(2,1)}, bf16[16,16,4224]{2,1,0:T(8,128)(2,1)}, u32[]{:S(2)}, u32[]{:S(2)}) collective-permute-start(bf16[16,16,4224]{2,1,0:T(8,128)(2,1)} %bitcast_dynamic-update-slice_fusion.own_ref), channel_id=1, source_target_pairs={{0,1},{1,0},{2,3},{3,2},{4,5},{5,4},{6,7},{7,6},{8,9},{9,8},{10,11... | collective-permute-start | bytes 6488072 | tf_op jit(solution)/shard_map/ppermute | solution.py:136
  108.3 31.0 %all-to-all-start = ((bf16[16,2,3072]{2,1,0:T(2,128)(2,1)}), bf16[16,2,3072]{2,1,0:T(2,128)(2,1)S(1)}, u32[]{:S(2)}, u32[]{:S(2)}) async-start(bf16[16,2,3072]{2,1,0:T(2,128)(2,1)} %reshape.42), calls=%async_computation | async-start | bytes 393216 | tf_op jit(solution)/shard_map/all_to_all | solution.py:141
Sparse Core Ops, SparseCore 0:
  13.9 84.8 all-gather.1

commit v9 on v8

--- a/solution.py
+++ b/solution.py
@@ -59,9 +59,10 @@
     )(x, w, col(conv_bias), col(norm_gain), col(norm_shift))
 
 
-def up_kernel(index_ref, act_ref, own_ref, other_ref, out_ref, wnat_ref, *, width_cols):
+def up_kernel(index_ref, act_ref, own_ref, other_ref, out_ref, wnat_ref, actn_ref, *, width_cols):
     chips, slab, packed_width = own_ref.shape
-    positions, channels = act_ref.shape
+    channels, positions = act_ref.shape
+    block = channels // (2 * chips)
     core = index_ref[0]
     here = index_ref[1]
     for m in range(chips):
@@ -70,25 +71,31 @@
         theirs = pl.multiple_of(2 * slab * chip + slab * (1 - core), slab)
         wnat_ref[pl.ds(mine, slab), :] = own_ref[m]
         wnat_ref[pl.ds(theirs, slab), :] = other_ref[m]
-    act = act_ref[...]
+    for c in range(2):
+        for z in range(chips):
+            actn_ref[pl.ds((2 * z + c) * block, block), :] = act_ref[pl.ds((c * chips + z) * block, block), :]
     rows = out_ref.shape[0]
     outs = wnat_ref.shape[0]
-    nt = (((1,), (1,)), ((), ()))
-    lane = lax.broadcasted_iota(jnp.int32, (positions, packed_width - 4 * channels), 1)
-    ones = jnp.where(lane == 0, 1.0, 0.0).astype(act.dtype)
-    bias = lax.dot_general(ones, wnat_ref[:, pl.ds(4 * channels, packed_width - 4 * channels)], nt,
+    nn = (((1,), (0,)), ((), ()))
+    sub = lax.broadcasted_iota(jnp.int32, (packed_width - 4 * channels, positions), 0)
+    ones = jnp.where(sub == 0, 1.0, 0.0).astype(actn_ref.dtype)
+    bias = lax.dot_general(wnat_ref[:, pl.ds(4 * channels, packed_width - 4 * channels)], ones, nn,
                            preferred_element_type=jnp.float32)
+    act = actn_ref[...]
     for ab in range(4):
         a, b = divmod(ab, 2)
-        res = lax.dot_general(act, wnat_ref[:, pl.ds(ab * channels, channels)], nt,
+        res = lax.dot_general(wnat_ref[:, pl.ds(ab * channels, channels)], act, nn,
                               preferred_element_type=jnp.float32)
-        res = (res + bias).astype(out_ref.dtype)
+        res = jnp.transpose(res + bias).astype(out_ref.dtype)
+        span = rows * width_cols
+        res = jnp.where(core == 0, res[:span], res[span:])
         for i in range(rows):
             out_ref[i, a, :, pl.ds(b * outs, outs)] = res[i * width_cols:(i + 1) * width_cols, :]
 
 
-def up_conv(core, here, act, own, other):
-    rows, width_cols, channels = act.shape
+def up_conv(core, here, act, own, other, rows):
+    channels, positions = act.shape
+    width_cols = positions // (2 * rows)
     chips, slab, packed_width = own.shape
     outs = 2 * chips * slab
     vmem = pl.BlockSpec(memory_space=pltpu.VMEM)
@@ -99,11 +106,11 @@
         out_shape=jax.ShapeDtypeStruct((rows, 2, width_cols, 2 * outs), jnp.bfloat16),
         in_specs=[smem, vmem, vmem, vmem],
         out_specs=vmem,
-        scratch_shapes=[pltpu.VMEM((outs, packed_width), jnp.bfloat16)],
+        scratch_shapes=[pltpu.VMEM((outs, packed_width), jnp.bfloat16), pltpu.VMEM((channels, positions), act.dtype)],
         cost_estimate=pl.CostEstimate(
-            flops=2 * rows * width_cols * channels * 4 * outs, transcendentals=0,
+            flops=2 * positions * channels * 4 * outs, transcendentals=0,
             bytes_accessed=act.size * 2 + 2 * own.size * 2 + rows * width_cols * 4 * outs * 2),
-    )(index, act.reshape(rows * width_cols, channels), own, other)
+    )(index, act, own, other)
 
 
 def ring_gather(block, axis):
@@ -136,16 +143,10 @@
     packed_other = lax.ppermute(packed_z, "core", [(0, 1), (1, 0)])
 
     activated = conv_norm(whole, conv_weight, conv_bias, norm_gain, norm_shift)
-    activated = jnp.transpose(activated).reshape(height, width_cols, outputs)
-
-    chip_rows = lax.all_to_all(activated, "z", split_axis=0, concat_axis=2, tiled=True)
-    both = lax.all_gather(chip_rows, "core", axis=0, tiled=False)
-    half = chip_rows.shape[0] // 2
-    own = lax.dynamic_slice_in_dim(both, core * half, half, axis=1)
-    own = own.reshape((2, half, width_cols, chips, outputs))
-    own = jnp.transpose(own, (1, 2, 3, 0, 4)).reshape(half, width_cols, channels)
-
-    fine = up_conv(core, lax.axis_index("z"), own, packed_z, packed_other)
+    chip_rows = lax.all_to_all(activated, "z", split_axis=1, concat_axis=0, tiled=True)
+    both = lax.all_gather(chip_rows, "core", axis=0, tiled=True)
+    half = coarse.shape[0]
+    fine = up_conv(core, lax.axis_index("z"), both, packed_z, packed_other, half)
     return fine.reshape(2 * half, 2 * width_cols, -1)
 
 

time: 161 us -> 154 us (0.957)
  the two profiles are of different devices: /device:TPU:63 before, /device:TPU:1 now
where the time goes in v9:
time: 154 us
  starting transfers between devices  77.7 us (50%)
  waiting for transfers between devices  35.7 us (23%)
  between operations  13.7 us (9%)
  Pallas kernels  11.2 us (7%)
  local copies, waits for them, and re-layouts  7.97 us (5%)
  blocking collectives  6.66 us (4%)
    ppermute x8, starting transfers between devices, ring_gather(): ahead = lax.ppermute(ahead, axis, step_up)  45.8 us
    all_to_all x1, waiting for transfers between devices, body(): lax.all_to_all(activated, 'z', split_axis=1, concat_axis=0, tiled=True)  13.8 us
    ppermute x7, starting transfers between devices, ring_gather(): behind = lax.ppermute(behind, axis, step_down)  13.4 us
    all_to_all x1, starting transfers between devices, body(): lax.all_to_all(activated, 'z', split_axis=1, concat_axis=0, tiled=True)  9.86 us
    ppermute x7, waiting for transfers between devices, ring_gather(): behind = lax.ppermute(behind, axis, step_down)  9.26 us
    ppermute x1, starting transfers between devices, body(): packed_other = lax.ppermute(packed_z, 'core', [(0, 1), (1, 0)])  8.66 us
    all_gather x1, waiting for transfers between devices, body(): whole = lax.all_gather(coarse, ('z', 'core'), axis=0, tiled=True)  7.24 us
    all_gather x1, blocking collectives, body(): both = lax.all_gather(chip_rows, 'core', axis=0, tiled=True)  6.66 us
  transfers between devices with their start and end apart: 18, of which 9 were waited for; matrix products, arithmetic and copies ran while one was open for 2% of the time, Pallas kernels for 4%

profile of v9, /device:TPU:1, one launch (start us, length us, event | category | flops | bytes accessed | tf_op | source)
XLA Modules:
  0.0 153.6 jit_solution(6137337039823976995)
XLA Ops:
  6.5 0.7 copy.17
  7.3 1.0 reshape.33
  8.3 12.0 %collective-permute-start = (bf16[16,4224]{1,0:T(8,128)(2,1)S(1)}, bf16[16,4224]{1,0:T(8,128)(2,1)S(1)}, u32[]{:S(2)}, u32[]{:S(2)}) collective-permute-start(bf16[16,4224]{1,0:T(8,128)(2,1)S(1)} %fusion.1), channel_id=1, source_target_pairs={{0,30},{2,0},{4,2},{6,4},{8,6},{10,8},{12,10},{14,12},{16,14},{18,... | collective-permute-start | bytes 405512 | tf_op jit(solution)/shard_map/ppermute | solution.py:123
  20.2 1.9 %collective-permute-start.8 = (bf16[16,4224]{1,0:T(8,128)(2,1)S(1)}, bf16[16,4224]{1,0:T(8,128)(2,1)S(1)}, u32[]{:S(2)}, u32[]{:S(2)}) collective-permute-start(bf16[16,4224]{1,0:T(8,128)(2,1)S(1)} %fusion.1), channel_id=1, source_target_pairs={{0,2},{2,4},{4,6},{6,8},{8,10},{10,12},{12,14},{14,16},{16,18},{18... | collective-permute-start | bytes 405512 | tf_op jit(solution)/shard_map/ppermute | solution.py:126
  22.2 0.0 all-gather.2.cloned.1.call-update
  22.2 0.0 copy-start.1
  22.2 0.0 copy-start.2
  22.2 0.0 copy-start.3
  22.3 0.2 collective-permute-done
  22.5 5.3 %collective-permute-start.1 = (bf16[16,4224]{1,0:T(8,128)(2,1)S(1)}, bf16[16,4224]{1,0:T(8,128)(2,1)S(1)}, u32[]{:S(2)}, u32[]{:S(2)}) collective-permute-start(bf16[16,4224]{1,0:T(8,128)(2,1)S(1)} %collective-permute-done), channel_id=1, source_target_pairs={{0,30},{2,0},{4,2},{6,4},{8,6},{10,8},{12,10},{14,12},{16,14},{18,... | collective-permute-start | bytes 405512 | tf_op jit(solution)/shard_map/ppermute | solution.py:123
  27.8 0.0 collective-permute-done.8
  27.8 1.9 %collective-permute-start.9 = (bf16[16,4224]{1,0:T(8,128)(2,1)S(1)}, bf16[16,4224]{1,0:T(8,128)(2,1)S(1)}, u32[]{:S(2)}, u32[]{:S(2)}) collective-permute-start(bf16[16,4224]{1,0:T(8,128)(2,1)S(1)} %collective-permute-done.8), channel_id=1, source_target_pairs={{0,2},{2,4},{4,6},{6,8},{8,10},{10,12},{12,14},{14,16},{16,18},{18... | collective-permute-start | bytes 405512 | tf_op jit(solution)/shard_map/ppermute | solution.py:126
  29.7 0.0 collective-permute-done.1
  29.8 5.0 %collective-permute-start.2 = (bf16[16,4224]{1,0:T(8,128)(2,1)S(1)}, bf16[16,4224]{1,0:T(8,128)(2,1)S(1)}, u32[]{:S(2)}, u32[]{:S(2)}) collective-permute-start(bf16[16,4224]{1,0:T(8,128)(2,1)S(1)} %collective-permute-done.1), channel_id=1, source_target_pairs={{0,30},{2,0},{4,2},{6,4},{8,6},{10,8},{12,10},{14,12},{16,14},{18,... | collective-permute-start | bytes 405512 | tf_op jit(solution)/shard_map/ppermute | solution.py:123
  34.8 0.0 collective-permute-done.9
  34.8 1.9 %collective-permute-start.10 = (bf16[16,4224]{1,0:T(8,128)(2,1)S(1)}, bf16[16,4224]{1,0:T(8,128)(2,1)S(1)}, u32[]{:S(2)}, u32[]{:S(2)}) collective-permute-start(bf16[16,4224]{1,0:T(8,128)(2,1)S(1)} %collective-permute-done.9), channel_id=1, source_target_pairs={{0,2},{2,4},{4,6},{6,8},{8,10},{10,12},{12,14},{14,16},{16,18},{18... | collective-permute-start | bytes 405512 | tf_op jit(solution)/shard_map/ppermute | solution.py:126
  36.7 0.8 collective-permute-done.2
  37.5 5.0 %collective-permute-start.3 = (bf16[16,4224]{1,0:T(8,128)(2,1)S(1)}, bf16[16,4224]{1,0:T(8,128)(2,1)S(1)}, u32[]{:S(2)}, u32[]{:S(2)}) collective-permute-start(bf16[16,4224]{1,0:T(8,128)(2,1)S(1)} %collective-permute-done.2), channel_id=1, source_target_pairs={{0,30},{2,0},{4,2},{6,4},{8,6},{10,8},{12,10},{14,12},{16,14},{18,... | collective-permute-start | bytes 405512 | tf_op jit(solution)/shard_map/ppermute | solution.py:123
  42.5 2.4 %collective-permute-done.10 = bf16[16,4224]{1,0:T(8,128)(2,1)S(1)} collective-permute-done((bf16[16,4224]{1,0:T(8,128)(2,1)S(1)}, bf16[16,4224]{1,0:T(8,128)(2,1)S(1)}, u32[]{:S(2)}, u32[]{:S(2)}) %collective-permute-start.10) | collective-permute-done | bytes 135200 | tf_op jit(solution)/shard_map/ppermute | solution.py:126
  44.9 1.9 %collective-permute-start.11 = (bf16[16,4224]{1,0:T(8,128)(2,1)S(1)}, bf16[16,4224]{1,0:T(8,128)(2,1)S(1)}, u32[]{:S(2)}, u32[]{:S(2)}) collective-permute-start(bf16[16,4224]{1,0:T(8,128)(2,1)S(1)} %collective-permute-done.10), channel_id=1, source_target_pairs={{0,2},{2,4},{4,6},{6,8},{8,10},{10,12},{12,14},{14,16},{16,18},{18... | collective-permute-start | bytes 405512 | tf_op jit(solution)/shard_map/ppermute | solution.py:126
  46.8 0.0 collective-permute-done.3
  46.8 4.8 %collective-permute-start.4 = (bf16[16,4224]{1,0:T(8,128)(2,1)S(1)}, bf16[16,4224]{1,0:T(8,128)(2,1)S(1)}, u32[]{:S(2)}, u32[]{:S(2)}) collective-permute-start(bf16[16,4224]{1,0:T(8,128)(2,1)S(1)} %collective-permute-done.3), channel_id=1, source_target_pairs={{0,30},{2,0},{4,2},{6,4},{8,6},{10,8},{12,10},{14,12},{16,14},{18,... | collective-permute-start | bytes 405512 | tf_op jit(solution)/shard_map/ppermute | solution.py:123
  51.7 2.1 %collective-permute-done.11 = bf16[16,4224]{1,0:T(8,128)(2,1)S(1)} collective-permute-done((bf16[16,4224]{1,0:T(8,128)(2,1)S(1)}, bf16[16,4224]{1,0:T(8,128)(2,1)S(1)}, u32[]{:S(2)}, u32[]{:S(2)}) %collective-permute-start.11) | collective-permute-done | bytes 135200 | tf_op jit(solution)/shard_map/ppermute | solution.py:126
  53.8 1.9 %collective-permute-start.12 = (bf16[16,4224]{1,0:T(8,128)(2,1)S(1)}, bf16[16,4224]{1,0:T(8,128)(2,1)S(1)}, u32[]{:S(2)}, u32[]{:S(2)}) collective-permute-start(bf16[16,4224]{1,0:T(8,128)(2,1)S(1)} %collective-permute-done.11), channel_id=1, source_target_pairs={{0,2},{2,4},{4,6},{6,8},{8,10},{10,12},{12,14},{14,16},{16,18},{18... | collective-permute-start | bytes 405512 | tf_op jit(solution)/shard_map/ppermute | solution.py:126
  55.7 0.0 collective-permute-done.4
  55.7 4.6 %collective-permute-start.5 = (bf16[16,4224]{1,0:T(8,128)(2,1)S(1)}, bf16[16,4224]{1,0:T(8,128)(2,1)S(1)}, u32[]{:S(2)}, u32[]{:S(2)}) collective-permute-start(bf16[16,4224]{1,0:T(8,128)(2,1)S(1)} %collective-permute-done.4), channel_id=1, source_target_pairs={{0,30},{2,0},{4,2},{6,4},{8,6},{10,8},{12,10},{14,12},{16,14},{18,... | collective-permute-start | bytes 405512 | tf_op jit(solution)/shard_map/ppermute | solution.py:123
  60.3 2.1 %collective-permute-done.12 = bf16[16,4224]{1,0:T(8,128)(2,1)S(1)} collective-permute-done((bf16[16,4224]{1,0:T(8,128)(2,1)S(1)}, bf16[16,4224]{1,0:T(8,128)(2,1)S(1)}, u32[]{:S(2)}, u32[]{:S(2)}) %collective-permute-start.12) | collective-permute-done | bytes 135200 | tf_op jit(solution)/shard_map/ppermute | solution.py:126
  62.5 1.9 %collective-permute-start.13 = (bf16[16,4224]{1,0:T(8,128)(2,1)S(1)}, bf16[16,4224]{1,0:T(8,128)(2,1)S(1)}, u32[]{:S(2)}, u32[]{:S(2)}) collective-permute-start(bf16[16,4224]{1,0:T(8,128)(2,1)S(1)} %collective-permute-done.12), channel_id=1, source_target_pairs={{0,2},{2,4},{4,6},{6,8},{8,10},{10,12},{12,14},{14,16},{16,18},{18... | collective-permute-start | bytes 405512 | tf_op jit(solution)/shard_map/ppermute | solution.py:126
  64.4 4.6 %collective-permute-start.6 = (bf16[16,4224]{1,0:T(8,128)(2,1)S(1)}, bf16[16,4224]{1,0:T(8,128)(2,1)S(1)}, u32[]{:S(2)}, u32[]{:S(2)}) collective-permute-start(bf16[16,4224]{1,0:T(8,128)(2,1)S(1)} %collective-permute-done.5), channel_id=1, source_target_pairs={{0,30},{2,0},{4,2},{6,4},{8,6},{10,8},{12,10},{14,12},{16,14},{18,... | collective-permute-start | bytes 405512 | tf_op jit(solution)/shard_map/ppermute | solution.py:123
  69.0 2.6 %collective-permute-done.13 = bf16[16,4224]{1,0:T(8,128)(2,1)S(1)} collective-permute-done((bf16[16,4224]{1,0:T(8,128)(2,1)S(1)}, bf16[16,4224]{1,0:T(8,128)(2,1)S(1)}, u32[]{:S(2)}, u32[]{:S(2)}) %collective-permute-start.13) | collective-permute-done | bytes 135200 | tf_op jit(solution)/shard_map/ppermute | solution.py:126
  71.6 1.9 %collective-permute-start.14 = (bf16[16,4224]{1,0:T(8,128)(2,1)S(1)}, bf16[16,4224]{1,0:T(8,128)(2,1)S(1)}, u32[]{:S(2)}, u32[]{:S(2)}) collective-permute-start(bf16[16,4224]{1,0:T(8,128)(2,1)S(1)} %collective-permute-done.13), channel_id=1, source_target_pairs={{0,2},{2,4},{4,6},{6,8},{8,10},{10,12},{12,14},{14,16},{16,18},{18... | collective-permute-start | bytes 405512 | tf_op jit(solution)/shard_map/ppermute | solution.py:126
  73.5 0.0 collective-permute-done.6
  73.5 4.6 %collective-permute-start.7 = (bf16[16,4224]{1,0:T(8,128)(2,1)S(1)}, bf16[16,4224]{1,0:T(8,128)(2,1)S(1)}, u32[]{:S(2)}, u32[]{:S(2)}) collective-permute-start(bf16[16,4224]{1,0:T(8,128)(2,1)S(1)} %collective-permute-done.6), channel_id=1, source_target_pairs={{0,30},{2,0},{4,2},{6,4},{8,6},{10,8},{12,10},{14,12},{16,14},{18,... | collective-permute-start | bytes 405512 | tf_op jit(solution)/shard_map/ppermute | solution.py:123
  78.1 4.4 %collective-permute-done.7 = bf16[16,4224]{1,0:T(8,128)(2,1)S(1)} collective-permute-done((bf16[16,4224]{1,0:T(8,128)(2,1)S(1)}, bf16[16,4224]{1,0:T(8,128)(2,1)S(1)}, u32[]{:S(2)}, u32[]{:S(2)}) %collective-permute-start.7) | collective-permute-done | bytes 135200 | tf_op jit(solution)/shard_map/ppermute | solution.py:123
  82.7 8.7 %collective-permute-start.15 = (bf16[16,16,4224]{2,1,0:T(8,128)(2,1)S(1)}, bf16[16,16,4224]{2,1,0:T(8,128)(2,1)}, u32[]{:S(2)}, u32[]{:S(2)}) collective-permute-start(bf16[16,16,4224]{2,1,0:T(8,128)(2,1)S(1)} %bitcast_dynamic-update-slice_fusion.own_ref), channel_id=1, source_target_pairs={{0,1},{1,0},{2,3},{3,2},{4,5},{5,4},{6,7},{7,6},{8,9},{9,8},{10,11... | collective-permute-start | bytes 6488072 | tf_op jit(solution)/shard_map/ppermute | solution.py:143
  91.3 0.7 copy.13.bias_ref
  92.0 0.7 copy.14.gain_ref
  92.7 0.7 copy.15.shift_ref
  93.4 7.2 %all-gather.2.cloned.1.call-done = bf16[64,48,1024]{2,1,0:T(8,128)(2,1)} async-done(((bf16[2,48,1024]{2,1,0:T(8,128)(2,1)}), bf16[64,48,1024]{2,1,0:T(8,128)(2,1)}) %all-gather.2.cloned.1.call-update) | async-done | bytes 6291472 | tf_op jit(solution)/shard_map/all_gather | solution.py:138
  100.6 6.3 %shard_map.73 = bf16[32,3072]{1,0:T(8,128)(2,1)} custom-call(bf16[3072,1024]{1,0:T(8,128)(2,1)} %bitcast.49, bf16[288,1024]{1,0:T(8,128)(2,1)} %bitcast.51, f32[32,1]{1,0:T(8,128)} %copy.13.bias_ref, f32[32,1]{1,0:T(8,128)} %copy.14.gain_ref, f32[32,1]{1,0:T(8,128)} %copy.15.shift_ref), custom_call_target="tpu_custom_call" | custom-call | flops 1811939328 | bytes 7077888 | tf_op jit(solution)/shard_map/pallas_call | solution.py:50
  106.9 1.2 all_to_all.14
  108.2 0.8 copy.16
  109.0 9.9 %all-to-all-start = ((bf16[32,16,192]{2,0,1:T(8,128)(2,1)}), bf16[32,16,192]{2,0,1:T(8,128)(2,1)S(1)}, u32[]{:S(2)}, u32[]{:S(2)}) async-start(bf16[32,16,192]{2,0,1:T(8,128)(2,1)} %copy.16), calls=%async_computation | async-start | bytes 524288 | tf_op jit(solution)/shard_map/all_to_all | solution.py:146
  118.9 0.6 pad_add_fusion.index_ref
  119.5 13.8 %all-to-all-done = bf16[32,16,192]{2,0,1:T(8,128)(2,1)S(1)} async-done(((bf16[32,16,192]{2,0,1:T(8,128)(2,1)}), bf16[32,16,192]{2,0,1:T(8,128)(2,1)S(1)}, u32[]{:S(2)}, u32[]{:S(2)}) %all-to-all-start) | async-done | bytes 196640 | tf_op jit(solution)/shard_map/all_to_all | solution.py:146
  133.3 6.7 %all_gather.7.act_ref = bf16[1024,192]{1,0:T(8,128)(2,1)} all-gather(bf16[512,192]{1,0:T(8,128)(2,1)S(1)} %bitcast.50), channel_id=1, replica_groups=mesh['grp'=16,'z'=16,'core'=2] {'core'}, dimensions={0}, use_global_device_ids=true | all-gather | bytes 589824 | tf_op jit(solution)/shard_map/all_gather | solution.py:147
  139.9 4.9 %shard_map.74 = bf16[2,2,48,1024]{3,2,1,0:T(8,128)(2,1)} custom-call(s32[2]{0:T(128)} %pad_add_fusion.index_ref, bf16[1024,192]{1,0:T(8,128)(2,1)} %all_gather.7.act_ref, bf16[16,16,4224]{2,1,0:T(8,128)(2,1)} %copy-done, bf16[16,16,4224]{2,1,0:T(8,128)(2,1)} %collective-permute-done.15.other_ref), custom_call_target="tpu_custom_call" | custom-call | flops 805306368 | bytes 5111808 | tf_op jit(solution)/shard_map/pallas_call | solution.py:104
  144.9 1.9 %reshape.34 = bf16[4,96,512]{2,1,0:T(8,128)(2,1)} reshape(bf16[2,2,48,1024]{3,2,1,0:T(8,128)(2,1)} %shard_map.74) | data formatting | bytes 786432 | tf_op jit(solution)/shard_map/reshape | solution.py:150
  (26 shorter events, 0.3 us)
Async XLA Ops:
  6.5 94.1 %all-gather.2.cloned.1.call-start = ((), (), s32[]{:S(2)}) async-start(), calls=%async_computation.1 | async-start | bytes 6488064 | tf_op jit(solution)/shard_map/all_gather | solution.py:138
  8.3 14.2 %collective-permute-start = (bf16[16,4224]{1,0:T(8,128)(2,1)S(1)}, bf16[16,4224]{1,0:T(8,128)(2,1)S(1)}, u32[]{:S(2)}, u32[]{:S(2)}) collective-permute-start(bf16[16,4224]{1,0:T(8,128)(2,1)S(1)} %fusion.1), channel_id=1, source_target_pairs={{0,30},{2,0},{4,2},{6,4},{8,6},{10,8},{12,10},{14,12},{16,14},{18,... | collective-permute-start | bytes 405512 | tf_op jit(solution)/shard_map/ppermute | solution.py:123
  20.2 7.6 %collective-permute-start.8 = (bf16[16,4224]{1,0:T(8,128)(2,1)S(1)}, bf16[16,4224]{1,0:T(8,128)(2,1)S(1)}, u32[]{:S(2)}, u32[]{:S(2)}) collective-permute-start(bf16[16,4224]{1,0:T(8,128)(2,1)S(1)} %fusion.1), channel_id=1, source_target_pairs={{0,2},{2,4},{4,6},{6,8},{8,10},{10,12},{12,14},{14,16},{16,18},{18... | collective-permute-start | bytes 405512 | tf_op jit(solution)/shard_map/ppermute | solution.py:126
  22.2 69.1 %copy-start.1 = (f32[32]{0:T(128)S(1)}, f32[32]{0:T(128)}, u32[]{:S(2)}) copy-start(f32[32]{0:T(128)} %param.9) | copy-start | bytes 388
  22.2 69.8 %copy-start.2 = (f32[32]{0:T(128)S(1)}, f32[32]{0:T(128)}, u32[]{:S(2)}) copy-start(f32[32]{0:T(128)} %param.10) | copy-start | bytes 388
  22.2 70.5 %copy-start.3 = (f32[32]{0:T(128)S(1)}, f32[32]{0:T(128)}, u32[]{:S(2)}) copy-start(f32[32]{0:T(128)} %param.11) | copy-start | bytes 388
  22.5 7.3 %collective-permute-start.1 = (bf16[16,4224]{1,0:T(8,128)(2,1)S(1)}, bf16[16,4224]{1,0:T(8,128)(2,1)S(1)}, u32[]{:S(2)}, u32[]{:S(2)}) collective-permute-start(bf16[16,4224]{1,0:T(8,128)(2,1)S(1)} %collective-permute-done), channel_id=1, source_target_pairs={{0,30},{2,0},{4,2},{6,4},{8,6},{10,8},{12,10},{14,12},{16,14},{18,... | collective-permute-start | bytes 405512 | tf_op jit(solution)/shard_map/ppermute | solution.py:123
  27.8 7.0 %collective-permute-start.9 = (bf16[16,4224]{1,0:T(8,128)(2,1)S(1)}, bf16[16,4224]{1,0:T(8,128)(2,1)S(1)}, u32[]{:S(2)}, u32[]{:S(2)}) collective-permute-start(bf16[16,4224]{1,0:T(8,128)(2,1)S(1)} %collective-permute-done.8), channel_id=1, source_target_pairs={{0,2},{2,4},{4,6},{6,8},{8,10},{10,12},{12,14},{14,16},{16,18},{18... | collective-permute-start | bytes 405512 | tf_op jit(solution)/shard_map/ppermute | solution.py:126
  29.8 7.7 %collective-permute-start.2 = (bf16[16,4224]{1,0:T(8,128)(2,1)S(1)}, bf16[16,4224]{1,0:T(8,128)(2,1)S(1)}, u32[]{:S(2)}, u32[]{:S(2)}) collective-permute-start(bf16[16,4224]{1,0:T(8,128)(2,1)S(1)} %collective-permute-done.1), channel_id=1, source_target_pairs={{0,30},{2,0},{4,2},{6,4},{8,6},{10,8},{12,10},{14,12},{16,14},{18,... | collective-permute-start | bytes 405512 | tf_op jit(solution)/shard_map/ppermute | solution.py:123
  34.8 10.1 %collective-permute-start.10 = (bf16[16,4224]{1,0:T(8,128)(2,1)S(1)}, bf16[16,4224]{1,0:T(8,128)(2,1)S(1)}, u32[]{:S(2)}, u32[]{:S(2)}) collective-permute-start(bf16[16,4224]{1,0:T(8,128)(2,1)S(1)} %collective-permute-done.9), channel_id=1, source_target_pairs={{0,2},{2,4},{4,6},{6,8},{8,10},{10,12},{12,14},{14,16},{16,18},{18... | collective-permute-start | bytes 405512 | tf_op jit(solution)/shard_map/ppermute | solution.py:126
  37.5 9.3 %collective-permute-start.3 = (bf16[16,4224]{1,0:T(8,128)(2,1)S(1)}, bf16[16,4224]{1,0:T(8,128)(2,1)S(1)}, u32[]{:S(2)}, u32[]{:S(2)}) collective-permute-start(bf16[16,4224]{1,0:T(8,128)(2,1)S(1)} %collective-permute-done.2), channel_id=1, source_target_pairs={{0,30},{2,0},{4,2},{6,4},{8,6},{10,8},{12,10},{14,12},{16,14},{18,... | collective-permute-start | bytes 405512 | tf_op jit(solution)/shard_map/ppermute | solution.py:123
  44.9 8.9 %collective-permute-start.11 = (bf16[16,4224]{1,0:T(8,128)(2,1)S(1)}, bf16[16,4224]{1,0:T(8,128)(2,1)S(1)}, u32[]{:S(2)}, u32[]{:S(2)}) collective-permute-start(bf16[16,4224]{1,0:T(8,128)(2,1)S(1)} %collective-permute-done.10), channel_id=1, source_target_pairs={{0,2},{2,4},{4,6},{6,8},{8,10},{10,12},{12,14},{14,16},{16,18},{18... | collective-permute-start | bytes 405512 | tf_op jit(solution)/shard_map/ppermute | solution.py:126
  46.8 8.9 %collective-permute-start.4 = (bf16[16,4224]{1,0:T(8,128)(2,1)S(1)}, bf16[16,4224]{1,0:T(8,128)(2,1)S(1)}, u32[]{:S(2)}, u32[]{:S(2)}) collective-permute-start(bf16[16,4224]{1,0:T(8,128)(2,1)S(1)} %collective-permute-done.3), channel_id=1, source_target_pairs={{0,30},{2,0},{4,2},{6,4},{8,6},{10,8},{12,10},{14,12},{16,14},{18,... | collective-permute-start | bytes 405512 | tf_op jit(solution)/shard_map/ppermute | solution.py:123
  53.8 8.7 %collective-permute-start.12 = (bf16[16,4224]{1,0:T(8,128)(2,1)S(1)}, bf16[16,4224]{1,0:T(8,128)(2,1)S(1)}, u32[]{:S(2)}, u32[]{:S(2)}) collective-permute-start(bf16[16,4224]{1,0:T(8,128)(2,1)S(1)} %collective-permute-done.11), channel_id=1, source_target_pairs={{0,2},{2,4},{4,6},{6,8},{8,10},{10,12},{12,14},{14,16},{16,18},{18... | collective-permute-start | bytes 405512 | tf_op jit(solution)/shard_map/ppermute | solution.py:126
  55.7 8.7 %collective-permute-start.5 = (bf16[16,4224]{1,0:T(8,128)(2,1)S(1)}, bf16[16,4224]{1,0:T(8,128)(2,1)S(1)}, u32[]{:S(2)}, u32[]{:S(2)}) collective-permute-start(bf16[16,4224]{1,0:T(8,128)(2,1)S(1)} %collective-permute-done.4), channel_id=1, source_target_pairs={{0,30},{2,0},{4,2},{6,4},{8,6},{10,8},{12,10},{14,12},{16,14},{18,... | collective-permute-start | bytes 405512 | tf_op jit(solution)/shard_map/ppermute | solution.py:123
  62.5 9.1 %collective-permute-start.13 = (bf16[16,4224]{1,0:T(8,128)(2,1)S(1)}, bf16[16,4224]{1,0:T(8,128)(2,1)S(1)}, u32[]{:S(2)}, u32[]{:S(2)}) collective-permute-start(bf16[16,4224]{1,0:T(8,128)(2,1)S(1)} %collective-permute-done.12), channel_id=1, source_target_pairs={{0,2},{2,4},{4,6},{6,8},{8,10},{10,12},{12,14},{14,16},{16,18},{18... | collective-permute-start | bytes 405512 | tf_op jit(solution)/shard_map/ppermute | solution.py:126
  64.4 9.1 %collective-permute-start.6 = (bf16[16,4224]{1,0:T(8,128)(2,1)S(1)}, bf16[16,4224]{1,0:T(8,128)(2,1)S(1)}, u32[]{:S(2)}, u32[]{:S(2)}) collective-permute-start(bf16[16,4224]{1,0:T(8,128)(2,1)S(1)} %collective-permute-done.5), channel_id=1, source_target_pairs={{0,30},{2,0},{4,2},{6,4},{8,6},{10,8},{12,10},{14,12},{16,14},{18,... | collective-permute-start | bytes 405512 | tf_op jit(solution)/shard_map/ppermute | solution.py:123
  71.6 10.9 %collective-permute-start.14 = (bf16[16,4224]{1,0:T(8,128)(2,1)S(1)}, bf16[16,4224]{1,0:T(8,128)(2,1)S(1)}, u32[]{:S(2)}, u32[]{:S(2)}) collective-permute-start(bf16[16,4224]{1,0:T(8,128)(2,1)S(1)} %collective-permute-done.13), channel_id=1, source_target_pairs={{0,2},{2,4},{4,6},{6,8},{8,10},{10,12},{12,14},{14,16},{16,18},{18... | collective-permute-start | bytes 405512 | tf_op jit(solution)/shard_map/ppermute | solution.py:126
  73.5 9.0 %collective-permute-start.7 = (bf16[16,4224]{1,0:T(8,128)(2,1)S(1)}, bf16[16,4224]{1,0:T(8,128)(2,1)S(1)}, u32[]{:S(2)}, u32[]{:S(2)}) collective-permute-start(bf16[16,4224]{1,0:T(8,128)(2,1)S(1)} %collective-permute-done.6), channel_id=1, source_target_pairs={{0,30},{2,0},{4,2},{6,4},{8,6},{10,8},{12,10},{14,12},{16,14},{18,... | collective-permute-start | bytes 405512 | tf_op jit(solution)/shard_map/ppermute | solution.py:123
  82.6 24.3 %copy-start = (bf16[16,16,4224]{2,1,0:T(8,128)(2,1)}, bf16[16,16,4224]{2,1,0:T(8,128)(2,1)S(1)}, u32[]{:S(2)}) copy-start(bf16[16,16,4224]{2,1,0:T(8,128)(2,1)S(1)} %bitcast_dynamic-update-slice_fusion.own_ref) | copy-start | bytes 6488068
  82.7 57.3 %collective-permute-start.15 = (bf16[16,16,4224]{2,1,0:T(8,128)(2,1)S(1)}, bf16[16,16,4224]{2,1,0:T(8,128)(2,1)}, u32[]{:S(2)}, u32[]{:S(2)}) collective-permute-start(bf16[16,16,4224]{2,1,0:T(8,128)(2,1)S(1)} %bitcast_dynamic-update-slice_fusion.own_ref), channel_id=1, source_target_pairs={{0,1},{1,0},{2,3},{3,2},{4,5},{5,4},{6,7},{7,6},{8,9},{9,8},{10,11... | collective-permute-start | bytes 6488072 | tf_op jit(solution)/shard_map/ppermute | solution.py:143
  109.0 24.3 %all-to-all-start = ((bf16[32,16,192]{2,0,1:T(8,128)(2,1)}), bf16[32,16,192]{2,0,1:T(8,128)(2,1)S(1)}, u32[]{:S(2)}, u32[]{:S(2)}) async-start(bf16[32,16,192]{2,0,1:T(8,128)(2,1)} %copy.16), calls=%async_computation | async-start | bytes 524288 | tf_op jit(solution)/shard_map/all_to_all | solution.py:146
Sparse Core Ops, SparseCore 0:
  22.3 78.2 all-gather.1

commit v10 on v9

--- a/solution.py
+++ b/solution.py
@@ -74,7 +74,7 @@
     for c in range(2):
         for z in range(chips):
             actn_ref[pl.ds((2 * z + c) * block, block), :] = act_ref[pl.ds((c * chips + z) * block, block), :]
-    rows = out_ref.shape[0]
+    rows = out_ref.shape[0] // 2
     outs = wnat_ref.shape[0]
     nn = (((1,), (0,)), ((), ()))
     sub = lax.broadcasted_iota(jnp.int32, (packed_width - 4 * channels, positions), 0)
@@ -82,15 +82,20 @@
     bias = lax.dot_general(wnat_ref[:, pl.ds(4 * channels, packed_width - 4 * channels)], ones, nn,
                            preferred_element_type=jnp.float32)
     act = actn_ref[...]
-    for ab in range(4):
-        a, b = divmod(ab, 2)
-        res = lax.dot_general(wnat_ref[:, pl.ds(ab * channels, channels)], act, nn,
-                              preferred_element_type=jnp.float32)
-        res = jnp.transpose(res + bias).astype(out_ref.dtype)
-        span = rows * width_cols
-        res = jnp.where(core == 0, res[:span], res[span:])
+    span = rows * width_cols
+    dest = lax.broadcasted_iota(jnp.int32, (2 * width_cols, 2 * width_cols), 0)
+    src = lax.broadcasted_iota(jnp.int32, (2 * width_cols, 2 * width_cols), 1)
+    interleave = jnp.where(src == (dest % 2) * width_cols + dest // 2, 1.0, 0.0).astype(out_ref.dtype)
+    for a in range(2):
+        phases = []
+        for b in range(2):
+            res = lax.dot_general(wnat_ref[:, pl.ds((2 * a + b) * channels, channels)], act, nn,
+                                  preferred_element_type=jnp.float32)
+            res = jnp.transpose(res + bias).astype(out_ref.dtype)
+            phases.append(jnp.where(core == 0, res[:span], res[span:]))
         for i in range(rows):
-            out_ref[i, a, :, pl.ds(b * outs, outs)] = res[i * width_cols:(i + 1) * width_cols, :]
+            stacked = jnp.concatenate([p[i * width_cols:(i + 1) * width_cols] for p in phases], axis=0)
+            out_ref[2 * i + a] = jnp.dot(interleave, stacked, preferred_element_type=jnp.float32).astype(out_ref.dtype)
 
 
 def up_conv(core, here, act, own, other, rows):
@@ -103,7 +108,7 @@
     index = jnp.stack([core, here]).astype(jnp.int32)
     return pl.pallas_call(
         functools.partial(up_kernel, width_cols=width_cols),
-        out_shape=jax.ShapeDtypeStruct((rows, 2, width_cols, 2 * outs), jnp.bfloat16),
+        out_shape=jax.ShapeDtypeStruct((2 * rows, 2 * width_cols, outs), jnp.bfloat16),
         in_specs=[smem, vmem, vmem, vmem],
         out_specs=vmem,
         scratch_shapes=[pltpu.VMEM((outs, packed_width), jnp.bfloat16), pltpu.VMEM((channels, positions), act.dtype)],

time: 154 us -> 153 us (level)
  local copies, waits for them, and re-layouts: 7.97 us -> 6.1 us
    reshape x1 -> x0, local copies, waits for them, and re-layouts: 1.87 us -> none  [body(): return fine.reshape(2 * half, 2 * width_cols, -1)]
where the time goes in v10:
time: 153 us; the launch traced here: 152 us
  starting transfers between devices  77.7 us (51%)
  waiting for transfers between devices  35.7 us (23%)
  between operations  13.7 us (9%)
  Pallas kernels  11.7 us (8%)
  blocking collectives  6.66 us (4%)
  local copies, waits for them, and re-layouts  6.1 us (4%)
    ppermute x8, starting transfers between devices, ring_gather(): ahead = lax.ppermute(ahead, axis, step_up)  45.8 us
    all_to_all x1, waiting for transfers between devices, body(): lax.all_to_all(activated, 'z', split_axis=1, concat_axis=0, tiled=True)  13.8 us
    ppermute x7, starting transfers between devices, ring_gather(): behind = lax.ppermute(behind, axis, step_down)  13.4 us
    all_to_all x1, starting transfers between devices, body(): lax.all_to_all(activated, 'z', split_axis=1, concat_axis=0, tiled=True)  9.86 us
    ppermute x7, waiting for transfers between devices, ring_gather(): behind = lax.ppermute(behind, axis, step_down)  9.26 us
    ppermute x1, starting transfers between devices, body(): packed_other = lax.ppermute(packed_z, 'core', [(0, 1), (1, 0)])  8.66 us
    all_gather x1, waiting for transfers between devices, body(): whole = lax.all_gather(coarse, ('z', 'core'), axis=0, tiled=True)  7.24 us
    all_gather x1, blocking collectives, body(): both = lax.all_gather(chip_rows, 'core', axis=0, tiled=True)  6.66 us
  transfers between devices with their start and end apart: 18, of which 9 were waited for; matrix products, arithmetic and copies ran while one was open for 2% of the time, Pallas kernels for 4%

profile of v10, /device:TPU:1, one launch (start us, length us, event | category | flops | bytes accessed | tf_op | source)
XLA Modules:
  0.0 152.2 jit_solution(10590153512933642020)
XLA Ops:
  6.5 0.7 copy.17
  7.3 1.0 reshape.30
  8.3 12.0 %collective-permute-start = (bf16[16,4224]{1,0:T(8,128)(2,1)S(1)}, bf16[16,4224]{1,0:T(8,128)(2,1)S(1)}, u32[]{:S(2)}, u32[]{:S(2)}) collective-permute-start(bf16[16,4224]{1,0:T(8,128)(2,1)S(1)} %fusion.1), channel_id=1, source_target_pairs={{0,30},{2,0},{4,2},{6,4},{8,6},{10,8},{12,10},{14,12},{16,14},{18,... | collective-permute-start | bytes 405512 | tf_op jit(solution)/shard_map/ppermute | solution.py:128
  20.2 1.9 %collective-permute-start.8 = (bf16[16,4224]{1,0:T(8,128)(2,1)S(1)}, bf16[16,4224]{1,0:T(8,128)(2,1)S(1)}, u32[]{:S(2)}, u32[]{:S(2)}) collective-permute-start(bf16[16,4224]{1,0:T(8,128)(2,1)S(1)} %fusion.1), channel_id=1, source_target_pairs={{0,2},{2,4},{4,6},{6,8},{8,10},{10,12},{12,14},{14,16},{16,18},{18... | collective-permute-start | bytes 405512 | tf_op jit(solution)/shard_map/ppermute | solution.py:131
  22.2 0.0 all-gather.2.cloned.1.call-update
  22.2 0.0 copy-start.1
  22.2 0.0 copy-start.2
  22.2 0.0 copy-start.3
  22.3 0.2 collective-permute-done
  22.5 5.3 %collective-permute-start.1 = (bf16[16,4224]{1,0:T(8,128)(2,1)S(1)}, bf16[16,4224]{1,0:T(8,128)(2,1)S(1)}, u32[]{:S(2)}, u32[]{:S(2)}) collective-permute-start(bf16[16,4224]{1,0:T(8,128)(2,1)S(1)} %collective-permute-done), channel_id=1, source_target_pairs={{0,30},{2,0},{4,2},{6,4},{8,6},{10,8},{12,10},{14,12},{16,14},{18,... | collective-permute-start | bytes 405512 | tf_op jit(solution)/shard_map/ppermute | solution.py:128
  27.8 0.0 collective-permute-done.8
  27.8 1.9 %collective-permute-start.9 = (bf16[16,4224]{1,0:T(8,128)(2,1)S(1)}, bf16[16,4224]{1,0:T(8,128)(2,1)S(1)}, u32[]{:S(2)}, u32[]{:S(2)}) collective-permute-start(bf16[16,4224]{1,0:T(8,128)(2,1)S(1)} %collective-permute-done.8), channel_id=1, source_target_pairs={{0,2},{2,4},{4,6},{6,8},{8,10},{10,12},{12,14},{14,16},{16,18},{18... | collective-permute-start | bytes 405512 | tf_op jit(solution)/shard_map/ppermute | solution.py:131
  29.7 0.0 collective-permute-done.1
  29.8 5.0 %collective-permute-start.2 = (bf16[16,4224]{1,0:T(8,128)(2,1)S(1)}, bf16[16,4224]{1,0:T(8,128)(2,1)S(1)}, u32[]{:S(2)}, u32[]{:S(2)}) collective-permute-start(bf16[16,4224]{1,0:T(8,128)(2,1)S(1)} %collective-permute-done.1), channel_id=1, source_target_pairs={{0,30},{2,0},{4,2},{6,4},{8,6},{10,8},{12,10},{14,12},{16,14},{18,... | collective-permute-start | bytes 405512 | tf_op jit(solution)/shard_map/ppermute | solution.py:128
  34.8 0.0 collective-permute-done.9
  34.8 1.9 %collective-permute-start.10 = (bf16[16,4224]{1,0:T(8,128)(2,1)S(1)}, bf16[16,4224]{1,0:T(8,128)(2,1)S(1)}, u32[]{:S(2)}, u32[]{:S(2)}) collective-permute-start(bf16[16,4224]{1,0:T(8,128)(2,1)S(1)} %collective-permute-done.9), channel_id=1, source_target_pairs={{0,2},{2,4},{4,6},{6,8},{8,10},{10,12},{12,14},{14,16},{16,18},{18... | collective-permute-start | bytes 405512 | tf_op jit(solution)/shard_map/ppermute | solution.py:131
  36.7 0.8 collective-permute-done.2
  37.5 5.0 %collective-permute-start.3 = (bf16[16,4224]{1,0:T(8,128)(2,1)S(1)}, bf16[16,4224]{1,0:T(8,128)(2,1)S(1)}, u32[]{:S(2)}, u32[]{:S(2)}) collective-permute-start(bf16[16,4224]{1,0:T(8,128)(2,1)S(1)} %collective-permute-done.2), channel_id=1, source_target_pairs={{0,30},{2,0},{4,2},{6,4},{8,6},{10,8},{12,10},{14,12},{16,14},{18,... | collective-permute-start | bytes 405512 | tf_op jit(solution)/shard_map/ppermute | solution.py:128
  42.5 2.4 %collective-permute-done.10 = bf16[16,4224]{1,0:T(8,128)(2,1)S(1)} collective-permute-done((bf16[16,4224]{1,0:T(8,128)(2,1)S(1)}, bf16[16,4224]{1,0:T(8,128)(2,1)S(1)}, u32[]{:S(2)}, u32[]{:S(2)}) %collective-permute-start.10) | collective-permute-done | bytes 135200 | tf_op jit(solution)/shard_map/ppermute | solution.py:131
  44.9 1.9 %collective-permute-start.11 = (bf16[16,4224]{1,0:T(8,128)(2,1)S(1)}, bf16[16,4224]{1,0:T(8,128)(2,1)S(1)}, u32[]{:S(2)}, u32[]{:S(2)}) collective-permute-start(bf16[16,4224]{1,0:T(8,128)(2,1)S(1)} %collective-permute-done.10), channel_id=1, source_target_pairs={{0,2},{2,4},{4,6},{6,8},{8,10},{10,12},{12,14},{14,16},{16,18},{18... | collective-permute-start | bytes 405512 | tf_op jit(solution)/shard_map/ppermute | solution.py:131
  46.8 0.0 collective-permute-done.3
  46.8 4.8 %collective-permute-start.4 = (bf16[16,4224]{1,0:T(8,128)(2,1)S(1)}, bf16[16,4224]{1,0:T(8,128)(2,1)S(1)}, u32[]{:S(2)}, u32[]{:S(2)}) collective-permute-start(bf16[16,4224]{1,0:T(8,128)(2,1)S(1)} %collective-permute-done.3), channel_id=1, source_target_pairs={{0,30},{2,0},{4,2},{6,4},{8,6},{10,8},{12,10},{14,12},{16,14},{18,... | collective-permute-start | bytes 405512 | tf_op jit(solution)/shard_map/ppermute | solution.py:128
  51.7 2.1 %collective-permute-done.11 = bf16[16,4224]{1,0:T(8,128)(2,1)S(1)} collective-permute-done((bf16[16,4224]{1,0:T(8,128)(2,1)S(1)}, bf16[16,4224]{1,0:T(8,128)(2,1)S(1)}, u32[]{:S(2)}, u32[]{:S(2)}) %collective-permute-start.11) | collective-permute-done | bytes 135200 | tf_op jit(solution)/shard_map/ppermute | solution.py:131
  53.8 1.9 %collective-permute-start.12 = (bf16[16,4224]{1,0:T(8,128)(2,1)S(1)}, bf16[16,4224]{1,0:T(8,128)(2,1)S(1)}, u32[]{:S(2)}, u32[]{:S(2)}) collective-permute-start(bf16[16,4224]{1,0:T(8,128)(2,1)S(1)} %collective-permute-done.11), channel_id=1, source_target_pairs={{0,2},{2,4},{4,6},{6,8},{8,10},{10,12},{12,14},{14,16},{16,18},{18... | collective-permute-start | bytes 405512 | tf_op jit(solution)/shard_map/ppermute | solution.py:131
  55.7 0.0 collective-permute-done.4
  55.7 4.6 %collective-permute-start.5 = (bf16[16,4224]{1,0:T(8,128)(2,1)S(1)}, bf16[16,4224]{1,0:T(8,128)(2,1)S(1)}, u32[]{:S(2)}, u32[]{:S(2)}) collective-permute-start(bf16[16,4224]{1,0:T(8,128)(2,1)S(1)} %collective-permute-done.4), channel_id=1, source_target_pairs={{0,30},{2,0},{4,2},{6,4},{8,6},{10,8},{12,10},{14,12},{16,14},{18,... | collective-permute-start | bytes 405512 | tf_op jit(solution)/shard_map/ppermute | solution.py:128
  60.3 2.1 %collective-permute-done.12 = bf16[16,4224]{1,0:T(8,128)(2,1)S(1)} collective-permute-done((bf16[16,4224]{1,0:T(8,128)(2,1)S(1)}, bf16[16,4224]{1,0:T(8,128)(2,1)S(1)}, u32[]{:S(2)}, u32[]{:S(2)}) %collective-permute-start.12) | collective-permute-done | bytes 135200 | tf_op jit(solution)/shard_map/ppermute | solution.py:131
  62.5 1.9 %collective-permute-start.13 = (bf16[16,4224]{1,0:T(8,128)(2,1)S(1)}, bf16[16,4224]{1,0:T(8,128)(2,1)S(1)}, u32[]{:S(2)}, u32[]{:S(2)}) collective-permute-start(bf16[16,4224]{1,0:T(8,128)(2,1)S(1)} %collective-permute-done.12), channel_id=1, source_target_pairs={{0,2},{2,4},{4,6},{6,8},{8,10},{10,12},{12,14},{14,16},{16,18},{18... | collective-permute-start | bytes 405512 | tf_op jit(solution)/shard_map/ppermute | solution.py:131
  64.4 0.0 collective-permute-done.5
  64.4 4.6 %collective-permute-start.6 = (bf16[16,4224]{1,0:T(8,128)(2,1)S(1)}, bf16[16,4224]{1,0:T(8,128)(2,1)S(1)}, u32[]{:S(2)}, u32[]{:S(2)}) collective-permute-start(bf16[16,4224]{1,0:T(8,128)(2,1)S(1)} %collective-permute-done.5), channel_id=1, source_target_pairs={{0,30},{2,0},{4,2},{6,4},{8,6},{10,8},{12,10},{14,12},{16,14},{18,... | collective-permute-start | bytes 405512 | tf_op jit(solution)/shard_map/ppermute | solution.py:128
  69.0 2.6 %collective-permute-done.13 = bf16[16,4224]{1,0:T(8,128)(2,1)S(1)} collective-permute-done((bf16[16,4224]{1,0:T(8,128)(2,1)S(1)}, bf16[16,4224]{1,0:T(8,128)(2,1)S(1)}, u32[]{:S(2)}, u32[]{:S(2)}) %collective-permute-start.13) | collective-permute-done | bytes 135200 | tf_op jit(solution)/shard_map/ppermute | solution.py:131
  71.6 1.9 %collective-permute-start.14 = (bf16[16,4224]{1,0:T(8,128)(2,1)S(1)}, bf16[16,4224]{1,0:T(8,128)(2,1)S(1)}, u32[]{:S(2)}, u32[]{:S(2)}) collective-permute-start(bf16[16,4224]{1,0:T(8,128)(2,1)S(1)} %collective-permute-done.13), channel_id=1, source_target_pairs={{0,2},{2,4},{4,6},{6,8},{8,10},{10,12},{12,14},{14,16},{16,18},{18... | collective-permute-start | bytes 405512 | tf_op jit(solution)/shard_map/ppermute | solution.py:131
  73.5 0.0 collective-permute-done.6
  73.5 4.6 %collective-permute-start.7 = (bf16[16,4224]{1,0:T(8,128)(2,1)S(1)}, bf16[16,4224]{1,0:T(8,128)(2,1)S(1)}, u32[]{:S(2)}, u32[]{:S(2)}) collective-permute-start(bf16[16,4224]{1,0:T(8,128)(2,1)S(1)} %collective-permute-done.6), channel_id=1, source_target_pairs={{0,30},{2,0},{4,2},{6,4},{8,6},{10,8},{12,10},{14,12},{16,14},{18,... | collective-permute-start | bytes 405512 | tf_op jit(solution)/shard_map/ppermute | solution.py:128
  78.1 4.4 %collective-permute-done.7 = bf16[16,4224]{1,0:T(8,128)(2,1)S(1)} collective-permute-done((bf16[16,4224]{1,0:T(8,128)(2,1)S(1)}, bf16[16,4224]{1,0:T(8,128)(2,1)S(1)}, u32[]{:S(2)}, u32[]{:S(2)}) %collective-permute-start.7) | collective-permute-done | bytes 135200 | tf_op jit(solution)/shard_map/ppermute | solution.py:128
  82.7 8.7 %collective-permute-start.15 = (bf16[16,16,4224]{2,1,0:T(8,128)(2,1)S(1)}, bf16[16,16,4224]{2,1,0:T(8,128)(2,1)}, u32[]{:S(2)}, u32[]{:S(2)}) collective-permute-start(bf16[16,16,4224]{2,1,0:T(8,128)(2,1)S(1)} %bitcast_dynamic-update-slice_fusion.own_ref), channel_id=1, source_target_pairs={{0,1},{1,0},{2,3},{3,2},{4,5},{5,4},{6,7},{7,6},{8,9},{9,8},{10,11... | collective-permute-start | bytes 6488072 | tf_op jit(solution)/shard_map/ppermute | solution.py:148
  91.3 0.7 copy.13.bias_ref
  92.0 0.7 copy.14.gain_ref
  92.7 0.7 copy.15.shift_ref
  93.4 7.2 %all-gather.2.cloned.1.call-done = bf16[64,48,1024]{2,1,0:T(8,128)(2,1)} async-done(((bf16[2,48,1024]{2,1,0:T(8,128)(2,1)}), bf16[64,48,1024]{2,1,0:T(8,128)(2,1)}) %all-gather.2.cloned.1.call-update) | async-done | bytes 6291472 | tf_op jit(solution)/shard_map/all_gather | solution.py:143
  100.6 6.3 %shard_map.73 = bf16[32,3072]{1,0:T(8,128)(2,1)} custom-call(bf16[3072,1024]{1,0:T(8,128)(2,1)} %bitcast.47, bf16[288,1024]{1,0:T(8,128)(2,1)} %bitcast.49, f32[32,1]{1,0:T(8,128)} %copy.13.bias_ref, f32[32,1]{1,0:T(8,128)} %copy.14.gain_ref, f32[32,1]{1,0:T(8,128)} %copy.15.shift_ref), custom_call_target="tpu_custom_call" | custom-call | flops 1811939328 | bytes 7077888 | tf_op jit(solution)/shard_map/pallas_call | solution.py:50
  106.9 1.2 all_to_all.14
  108.2 0.8 copy.16
  109.0 9.9 %all-to-all-start = ((bf16[32,16,192]{2,0,1:T(8,128)(2,1)}), bf16[32,16,192]{2,0,1:T(8,128)(2,1)S(1)}, u32[]{:S(2)}, u32[]{:S(2)}) async-start(bf16[32,16,192]{2,0,1:T(8,128)(2,1)} %copy.16), calls=%async_computation | async-start | bytes 524288 | tf_op jit(solution)/shard_map/all_to_all | solution.py:151
  118.9 0.6 pad_add_fusion.index_ref
  119.5 13.8 %all-to-all-done = bf16[32,16,192]{2,0,1:T(8,128)(2,1)S(1)} async-done(((bf16[32,16,192]{2,0,1:T(8,128)(2,1)}), bf16[32,16,192]{2,0,1:T(8,128)(2,1)S(1)}, u32[]{:S(2)}, u32[]{:S(2)}) %all-to-all-start) | async-done | bytes 196640 | tf_op jit(solution)/shard_map/all_to_all | solution.py:151
  133.3 6.7 %all_gather.7.act_ref = bf16[1024,192]{1,0:T(8,128)(2,1)} all-gather(bf16[512,192]{1,0:T(8,128)(2,1)S(1)} %bitcast.48), channel_id=1, replica_groups=mesh['grp'=16,'z'=16,'core'=2] {'core'}, dimensions={0}, use_global_device_ids=true | all-gather | bytes 589824 | tf_op jit(solution)/shard_map/all_gather | solution.py:152
  139.9 5.4 %shard_map.74 = bf16[4,96,512]{2,1,0:T(8,128)(2,1)} custom-call(s32[2]{0:T(128)} %pad_add_fusion.index_ref, bf16[1024,192]{1,0:T(8,128)(2,1)} %all_gather.7.act_ref, bf16[16,16,4224]{2,1,0:T(8,128)(2,1)} %copy-done, bf16[16,16,4224]{2,1,0:T(8,128)(2,1)} %collective-permute-done.15.other_ref), custom_call_target="tpu_custom_call" | custom-call | flops 805306368 | bytes 5111808 | tf_op jit(solution)/shard_map/pallas_call | solution.py:109
  (25 shorter events, 0.3 us)
Async XLA Ops:
  6.5 94.1 %all-gather.2.cloned.1.call-start = ((), (), s32[]{:S(2)}) async-start(), calls=%async_computation.1 | async-start | bytes 6488064 | tf_op jit(solution)/shard_map/all_gather | solution.py:143
  8.3 14.2 %collective-permute-start = (bf16[16,4224]{1,0:T(8,128)(2,1)S(1)}, bf16[16,4224]{1,0:T(8,128)(2,1)S(1)}, u32[]{:S(2)}, u32[]{:S(2)}) collective-permute-start(bf16[16,4224]{1,0:T(8,128)(2,1)S(1)} %fusion.1), channel_id=1, source_target_pairs={{0,30},{2,0},{4,2},{6,4},{8,6},{10,8},{12,10},{14,12},{16,14},{18,... | collective-permute-start | bytes 405512 | tf_op jit(solution)/shard_map/ppermute | solution.py:128
  20.2 7.6 %collective-permute-start.8 = (bf16[16,4224]{1,0:T(8,128)(2,1)S(1)}, bf16[16,4224]{1,0:T(8,128)(2,1)S(1)}, u32[]{:S(2)}, u32[]{:S(2)}) collective-permute-start(bf16[16,4224]{1,0:T(8,128)(2,1)S(1)} %fusion.1), channel_id=1, source_target_pairs={{0,2},{2,4},{4,6},{6,8},{8,10},{10,12},{12,14},{14,16},{16,18},{18... | collective-permute-start | bytes 405512 | tf_op jit(solution)/shard_map/ppermute | solution.py:131
  22.2 69.1 %copy-start.1 = (f32[32]{0:T(128)S(1)}, f32[32]{0:T(128)}, u32[]{:S(2)}) copy-start(f32[32]{0:T(128)} %param.9) | copy-start | bytes 388
  22.2 69.8 %copy-start.2 = (f32[32]{0:T(128)S(1)}, f32[32]{0:T(128)}, u32[]{:S(2)}) copy-start(f32[32]{0:T(128)} %param.10) | copy-start | bytes 388
  22.2 70.5 %copy-start.3 = (f32[32]{0:T(128)S(1)}, f32[32]{0:T(128)}, u32[]{:S(2)}) copy-start(f32[32]{0:T(128)} %param.11) | copy-start | bytes 388
  22.5 7.3 %collective-permute-start.1 = (bf16[16,4224]{1,0:T(8,128)(2,1)S(1)}, bf16[16,4224]{1,0:T(8,128)(2,1)S(1)}, u32[]{:S(2)}, u32[]{:S(2)}) collective-permute-start(bf16[16,4224]{1,0:T(8,128)(2,1)S(1)} %collective-permute-done), channel_id=1, source_target_pairs={{0,30},{2,0},{4,2},{6,4},{8,6},{10,8},{12,10},{14,12},{16,14},{18,... | collective-permute-start | bytes 405512 | tf_op jit(solution)/shard_map/ppermute | solution.py:128
  27.8 7.0 %collective-permute-start.9 = (bf16[16,4224]{1,0:T(8,128)(2,1)S(1)}, bf16[16,4224]{1,0:T(8,128)(2,1)S(1)}, u32[]{:S(2)}, u32[]{:S(2)}) collective-permute-start(bf16[16,4224]{1,0:T(8,128)(2,1)S(1)} %collective-permute-done.8), channel_id=1, source_target_pairs={{0,2},{2,4},{4,6},{6,8},{8,10},{10,12},{12,14},{14,16},{16,18},{18... | collective-permute-start | bytes 405512 | tf_op jit(solution)/shard_map/ppermute | solution.py:131
  29.8 7.7 %collective-permute-start.2 = (bf16[16,4224]{1,0:T(8,128)(2,1)S(1)}, bf16[16,4224]{1,0:T(8,128)(2,1)S(1)}, u32[]{:S(2)}, u32[]{:S(2)}) collective-permute-start(bf16[16,4224]{1,0:T(8,128)(2,1)S(1)} %collective-permute-done.1), channel_id=1, source_target_pairs={{0,30},{2,0},{4,2},{6,4},{8,6},{10,8},{12,10},{14,12},{16,14},{18,... | collective-permute-start | bytes 405512 | tf_op jit(solution)/shard_map/ppermute | solution.py:128
  34.8 10.1 %collective-permute-start.10 = (bf16[16,4224]{1,0:T(8,128)(2,1)S(1)}, bf16[16,4224]{1,0:T(8,128)(2,1)S(1)}, u32[]{:S(2)}, u32[]{:S(2)}) collective-permute-start(bf16[16,4224]{1,0:T(8,128)(2,1)S(1)} %collective-permute-done.9), channel_id=1, source_target_pairs={{0,2},{2,4},{4,6},{6,8},{8,10},{10,12},{12,14},{14,16},{16,18},{18... | collective-permute-start | bytes 405512 | tf_op jit(solution)/shard_map/ppermute | solution.py:131
  37.5 9.3 %collective-permute-start.3 = (bf16[16,4224]{1,0:T(8,128)(2,1)S(1)}, bf16[16,4224]{1,0:T(8,128)(2,1)S(1)}, u32[]{:S(2)}, u32[]{:S(2)}) collective-permute-start(bf16[16,4224]{1,0:T(8,128)(2,1)S(1)} %collective-permute-done.2), channel_id=1, source_target_pairs={{0,30},{2,0},{4,2},{6,4},{8,6},{10,8},{12,10},{14,12},{16,14},{18,... | collective-permute-start | bytes 405512 | tf_op jit(solution)/shard_map/ppermute | solution.py:128
  44.9 8.9 %collective-permute-start.11 = (bf16[16,4224]{1,0:T(8,128)(2,1)S(1)}, bf16[16,4224]{1,0:T(8,128)(2,1)S(1)}, u32[]{:S(2)}, u32[]{:S(2)}) collective-permute-start(bf16[16,4224]{1,0:T(8,128)(2,1)S(1)} %collective-permute-done.10), channel_id=1, source_target_pairs={{0,2},{2,4},{4,6},{6,8},{8,10},{10,12},{12,14},{14,16},{16,18},{18... | collective-permute-start | bytes 405512 | tf_op jit(solution)/shard_map/ppermute | solution.py:131
  46.8 8.9 %collective-permute-start.4 = (bf16[16,4224]{1,0:T(8,128)(2,1)S(1)}, bf16[16,4224]{1,0:T(8,128)(2,1)S(1)}, u32[]{:S(2)}, u32[]{:S(2)}) collective-permute-start(bf16[16,4224]{1,0:T(8,128)(2,1)S(1)} %collective-permute-done.3), channel_id=1, source_target_pairs={{0,30},{2,0},{4,2},{6,4},{8,6},{10,8},{12,10},{14,12},{16,14},{18,... | collective-permute-start | bytes 405512 | tf_op jit(solution)/shard_map/ppermute | solution.py:128
  53.8 8.7 %collective-permute-start.12 = (bf16[16,4224]{1,0:T(8,128)(2,1)S(1)}, bf16[16,4224]{1,0:T(8,128)(2,1)S(1)}, u32[]{:S(2)}, u32[]{:S(2)}) collective-permute-start(bf16[16,4224]{1,0:T(8,128)(2,1)S(1)} %collective-permute-done.11), channel_id=1, source_target_pairs={{0,2},{2,4},{4,6},{6,8},{8,10},{10,12},{12,14},{14,16},{16,18},{18... | collective-permute-start | bytes 405512 | tf_op jit(solution)/shard_map/ppermute | solution.py:131
  55.7 8.7 %collective-permute-start.5 = (bf16[16,4224]{1,0:T(8,128)(2,1)S(1)}, bf16[16,4224]{1,0:T(8,128)(2,1)S(1)}, u32[]{:S(2)}, u32[]{:S(2)}) collective-permute-start(bf16[16,4224]{1,0:T(8,128)(2,1)S(1)} %collective-permute-done.4), channel_id=1, source_target_pairs={{0,30},{2,0},{4,2},{6,4},{8,6},{10,8},{12,10},{14,12},{16,14},{18,... | collective-permute-start | bytes 405512 | tf_op jit(solution)/shard_map/ppermute | solution.py:128
  62.5 9.1 %collective-permute-start.13 = (bf16[16,4224]{1,0:T(8,128)(2,1)S(1)}, bf16[16,4224]{1,0:T(8,128)(2,1)S(1)}, u32[]{:S(2)}, u32[]{:S(2)}) collective-permute-start(bf16[16,4224]{1,0:T(8,128)(2,1)S(1)} %collective-permute-done.12), channel_id=1, source_target_pairs={{0,2},{2,4},{4,6},{6,8},{8,10},{10,12},{12,14},{14,16},{16,18},{18... | collective-permute-start | bytes 405512 | tf_op jit(solution)/shard_map/ppermute | solution.py:131
  64.4 9.1 %collective-permute-start.6 = (bf16[16,4224]{1,0:T(8,128)(2,1)S(1)}, bf16[16,4224]{1,0:T(8,128)(2,1)S(1)}, u32[]{:S(2)}, u32[]{:S(2)}) collective-permute-start(bf16[16,4224]{1,0:T(8,128)(2,1)S(1)} %collective-permute-done.5), channel_id=1, source_target_pairs={{0,30},{2,0},{4,2},{6,4},{8,6},{10,8},{12,10},{14,12},{16,14},{18,... | collective-permute-start | bytes 405512 | tf_op jit(solution)/shard_map/ppermute | solution.py:128
  71.6 10.9 %collective-permute-start.14 = (bf16[16,4224]{1,0:T(8,128)(2,1)S(1)}, bf16[16,4224]{1,0:T(8,128)(2,1)S(1)}, u32[]{:S(2)}, u32[]{:S(2)}) collective-permute-start(bf16[16,4224]{1,0:T(8,128)(2,1)S(1)} %collective-permute-done.13), channel_id=1, source_target_pairs={{0,2},{2,4},{4,6},{6,8},{8,10},{10,12},{12,14},{14,16},{16,18},{18... | collective-permute-start | bytes 405512 | tf_op jit(solution)/shard_map/ppermute | solution.py:131
  73.5 9.0 %collective-permute-start.7 = (bf16[16,4224]{1,0:T(8,128)(2,1)S(1)}, bf16[16,4224]{1,0:T(8,128)(2,1)S(1)}, u32[]{:S(2)}, u32[]{:S(2)}) collective-permute-start(bf16[16,4224]{1,0:T(8,128)(2,1)S(1)} %collective-permute-done.6), channel_id=1, source_target_pairs={{0,30},{2,0},{4,2},{6,4},{8,6},{10,8},{12,10},{14,12},{16,14},{18,... | collective-permute-start | bytes 405512 | tf_op jit(solution)/shard_map/ppermute | solution.py:128
  82.6 24.3 %copy-start = (bf16[16,16,4224]{2,1,0:T(8,128)(2,1)}, bf16[16,16,4224]{2,1,0:T(8,128)(2,1)S(1)}, u32[]{:S(2)}) copy-start(bf16[16,16,4224]{2,1,0:T(8,128)(2,1)S(1)} %bitcast_dynamic-update-slice_fusion.own_ref) | copy-start | bytes 6488068
  82.7 57.3 %collective-permute-start.15 = (bf16[16,16,4224]{2,1,0:T(8,128)(2,1)S(1)}, bf16[16,16,4224]{2,1,0:T(8,128)(2,1)}, u32[]{:S(2)}, u32[]{:S(2)}) collective-permute-start(bf16[16,16,4224]{2,1,0:T(8,128)(2,1)S(1)} %bitcast_dynamic-update-slice_fusion.own_ref), channel_id=1, source_target_pairs={{0,1},{1,0},{2,3},{3,2},{4,5},{5,4},{6,7},{7,6},{8,9},{9,8},{10,11... | collective-permute-start | bytes 6488072 | tf_op jit(solution)/shard_map/ppermute | solution.py:148
  109.0 24.3 %all-to-all-start = ((bf16[32,16,192]{2,0,1:T(8,128)(2,1)}), bf16[32,16,192]{2,0,1:T(8,128)(2,1)S(1)}, u32[]{:S(2)}, u32[]{:S(2)}) async-start(bf16[32,16,192]{2,0,1:T(8,128)(2,1)} %copy.16), calls=%async_computation | async-start | bytes 524288 | tf_op jit(solution)/shard_map/all_to_all | solution.py:151
Sparse Core Ops, SparseCore 0:
  22.3 78.2 all-gather.1

commit v11 on v10

--- a/solution.py
+++ b/solution.py
@@ -10,52 +10,64 @@
 GSIZE = 32
 
 
-def conv_norm_kernel(x_ref, w_ref, bias_ref, gain_ref, shift_ref, out_ref, *, height, width_cols):
+def conv_norm_kernel(x_ref, w_ref, bias_ref, gain_ref, shift_ref, out_ref, taps_ref, *, height, width_cols):
     outputs = out_ref.shape[0]
     positions = height * width_cols
-    taps = lax.dot_general(w_ref[...], x_ref[...], (((1,), (1,)), ((), ())),
-                           preferred_element_type=jnp.float32)
-    pos = lax.broadcasted_iota(jnp.int32, (1, positions), 1)
-    row = pos // width_cols
-    col = pos % width_cols
-    acc = jnp.zeros((outputs, positions), jnp.float32)
-    for t in range(9):
-        r, s = divmod(t, 3)
-        off = (r - 1) * width_cols + (s - 1)
-        part = taps[t * outputs:(t + 1) * outputs, :]
-        if off:
-            part = pltpu.roll(part, (-off) % positions, 1)
-        valid = ((row + (r - 1) >= 0) & (row + (r - 1) < height)
-                 & (col + (s - 1) >= 0) & (col + (s - 1) < width_cols))
-        acc = acc + jnp.where(valid, part, 0.0)
-    conv = acc + bias_ref[...]
-    groups = outputs // GSIZE
-    grouped = conv.reshape(groups, GSIZE, positions)
-    count = GSIZE * positions
-    centre = jnp.sum(jnp.sum(grouped, axis=2, keepdims=True), axis=1, keepdims=True) / count
-    dev = grouped - centre
-    spread = jnp.sum(jnp.sum(dev * dev, axis=2, keepdims=True), axis=1, keepdims=True) / count
-    normed = (dev * lax.rsqrt(spread + 1e-05)).reshape(outputs, positions)
-    v = normed * gain_ref[...] + shift_ref[...]
-    out_ref[...] = (v / (1.0 + jnp.exp(-v))).astype(out_ref.dtype)
+    chunk = x_ref.shape[0]
+    step = pl.program_id(0)
+    at = pl.multiple_of(step * chunk, 128)
+    taps_ref[:, pl.ds(at, chunk)] = lax.dot_general(w_ref[...], x_ref[...], (((1,), (1,)), ((), ())),
+                                                   preferred_element_type=jnp.float32)
+
+    @pl.when(step == pl.num_programs(0) - 1)
+    def _():
+        taps = taps_ref[...]
+        pos = lax.broadcasted_iota(jnp.int32, (1, positions), 1)
+        row = pos // width_cols
+        col = pos % width_cols
+        acc = jnp.zeros((outputs, positions), jnp.float32)
+        for t in range(9):
+            r, s = divmod(t, 3)
+            off = (r - 1) * width_cols + (s - 1)
+            part = taps[t * outputs:(t + 1) * outputs, :]
+            if off:
+                part = pltpu.roll(part, (-off) % positions, 1)
+            valid = ((row + (r - 1) >= 0) & (row + (r - 1) < height)
+                     & (col + (s - 1) >= 0) & (col + (s - 1) < width_cols))
+            acc = acc + jnp.where(valid, part, 0.0)
+        conv = acc + bias_ref[...]
+        groups = outputs // GSIZE
+        grouped = conv.reshape(groups, GSIZE, positions)
+        count = GSIZE * positions
+        centre = jnp.sum(jnp.sum(grouped, axis=2, keepdims=True), axis=1, keepdims=True) / count
+        dev = grouped - centre
+        spread = jnp.sum(jnp.sum(dev * dev, axis=2, keepdims=True), axis=1, keepdims=True) / count
+        normed = (dev * lax.rsqrt(spread + 1e-05)).reshape(outputs, positions)
+        v = normed * gain_ref[...] + shift_ref[...]
+        out_ref[...] = (v / (1.0 + jnp.exp(-v))).astype(out_ref.dtype)
 
 
 def conv_norm(whole, conv_weight, conv_bias, norm_gain, norm_shift):
     height, width_cols, channels = whole.shape
     outputs = conv_weight.shape[0]
-    x = whole.reshape(height * width_cols, channels)
+    positions = height * width_cols
+    chunk = positions // 4
+    x = whole.reshape(positions, channels)
     w = jnp.transpose(conv_weight.reshape(outputs, 9, channels), (1, 0, 2)).reshape(9 * outputs, channels)
     col = lambda v: v.astype(jnp.float32).reshape(outputs, 1)
-    vmem = pl.BlockSpec(memory_space=pltpu.VMEM)
+    fixed = lambda shape: pl.BlockSpec(shape, lambda i: (0, 0))
     return pl.pallas_call(
         functools.partial(conv_norm_kernel, height=height, width_cols=width_cols),
-        out_shape=jax.ShapeDtypeStruct((outputs, height * width_cols), jnp.bfloat16),
-        in_specs=[vmem] * 5,
-        out_specs=vmem,
+        out_shape=jax.ShapeDtypeStruct((outputs, positions), jnp.bfloat16),
+        grid=(positions // chunk,),
+        in_specs=[pl.BlockSpec((chunk, channels), lambda i: (i, 0)), fixed((9 * outputs, channels)),
+                  fixed((outputs, 1)), fixed((outputs, 1)), fixed((outputs, 1))],
+        out_specs=fixed((outputs, positions)),
+        scratch_shapes=[pltpu.VMEM((9 * outputs, positions), jnp.float32)],
         cost_estimate=pl.CostEstimate(
-            flops=2 * height * width_cols * channels * 9 * outputs,
-            transcendentals=height * width_cols * outputs,
-            bytes_accessed=x.size * 2 + w.size * 2 + outputs * height * width_cols * 2),
+            flops=2 * positions * channels * 9 * outputs,
+            transcendentals=positions * outputs,
+            bytes_accessed=x.size * 2 + w.size * 2 + outputs * positions * 2),
     )(x, w, col(conv_bias), col(norm_gain), col(norm_shift))
 
 

time: 153 us -> 154 us (level)
  transfers between devices with their start and end apart: 18 -> 18, of which waited for: 9 -> 9; matrix products, arithmetic and copies ran while one was open for 2% -> 2% of each run, Pallas kernels for 4% -> 5%
where the time goes in v11:
time: 154 us; the launch traced here: 153 us
  starting transfers between devices  77.7 us (50%)
  waiting for transfers between devices  35.7 us (23%)
  between operations  13.7 us (9%)
  Pallas kernels  12.7 us (8%)
  blocking collectives  6.66 us (4%)
  local copies, waits for them, and re-layouts  6.1 us (4%)
    ppermute x8, starting transfers between devices, ring_gather(): ahead = lax.ppermute(ahead, axis, step_up)  45.8 us
    all_to_all x1, waiting for transfers between devices, body(): lax.all_to_all(activated, 'z', split_axis=1, concat_axis=0, tiled=True)  13.8 us
    ppermute x7, starting transfers between devices, ring_gather(): behind = lax.ppermute(behind, axis, step_down)  13.4 us
    all_to_all x1, starting transfers between devices, body(): lax.all_to_all(activated, 'z', split_axis=1, concat_axis=0, tiled=True)  9.87 us
    ppermute x7, waiting for transfers between devices, ring_gather(): behind = lax.ppermute(behind, axis, step_down)  9.26 us
    ppermute x1, starting transfers between devices, body(): packed_other = lax.ppermute(packed_z, 'core', [(0, 1), (1, 0)])  8.66 us
    pallas_call x1, Pallas kernels, conv_norm(): pl.pallas_call(functools.partial(conv_norm_kernel, height=height, width_c...  7.27 us
    all_gather x1, waiting for transfers between devices, body(): whole = lax.all_gather(coarse, ('z', 'core'), axis=0, tiled=True)  7.24 us
  transfers between devices with their start and end apart: 18, of which 9 were waited for; matrix products, arithmetic and copies ran while one was open for 2% of the time, Pallas kernels for 5%

profile of v11, /device:TPU:1, one launch (start us, length us, event | category | flops | bytes accessed | tf_op | source)
XLA Modules:
  0.0 153.2 jit_solution(11281883615017534910)
XLA Ops:
  6.5 0.7 copy.17
  7.3 1.0 reshape.30
  8.3 12.0 %collective-permute-start = (bf16[16,4224]{1,0:T(8,128)(2,1)S(1)}, bf16[16,4224]{1,0:T(8,128)(2,1)S(1)}, u32[]{:S(2)}, u32[]{:S(2)}) collective-permute-start(bf16[16,4224]{1,0:T(8,128)(2,1)S(1)} %fusion.1), channel_id=1, source_target_pairs={{0,30},{2,0},{4,2},{6,4},{8,6},{10,8},{12,10},{14,12},{16,14},{18,... | collective-permute-start | bytes 405512 | tf_op jit(solution)/shard_map/ppermute | solution.py:140
  20.2 1.9 %collective-permute-start.8 = (bf16[16,4224]{1,0:T(8,128)(2,1)S(1)}, bf16[16,4224]{1,0:T(8,128)(2,1)S(1)}, u32[]{:S(2)}, u32[]{:S(2)}) collective-permute-start(bf16[16,4224]{1,0:T(8,128)(2,1)S(1)} %fusion.1), channel_id=1, source_target_pairs={{0,2},{2,4},{4,6},{6,8},{8,10},{10,12},{12,14},{14,16},{16,18},{18... | collective-permute-start | bytes 405512 | tf_op jit(solution)/shard_map/ppermute | solution.py:143
  22.2 0.0 all-gather.2.cloned.1.call-update
  22.2 0.0 copy-start.1
  22.2 0.0 copy-start.2
  22.2 0.0 copy-start.3
  22.3 0.2 collective-permute-done
  22.5 5.3 %collective-permute-start.1 = (bf16[16,4224]{1,0:T(8,128)(2,1)S(1)}, bf16[16,4224]{1,0:T(8,128)(2,1)S(1)}, u32[]{:S(2)}, u32[]{:S(2)}) collective-permute-start(bf16[16,4224]{1,0:T(8,128)(2,1)S(1)} %collective-permute-done), channel_id=1, source_target_pairs={{0,30},{2,0},{4,2},{6,4},{8,6},{10,8},{12,10},{14,12},{16,14},{18,... | collective-permute-start | bytes 405512 | tf_op jit(solution)/shard_map/ppermute | solution.py:140
  27.8 0.0 collective-permute-done.8
  27.8 1.9 %collective-permute-start.9 = (bf16[16,4224]{1,0:T(8,128)(2,1)S(1)}, bf16[16,4224]{1,0:T(8,128)(2,1)S(1)}, u32[]{:S(2)}, u32[]{:S(2)}) collective-permute-start(bf16[16,4224]{1,0:T(8,128)(2,1)S(1)} %collective-permute-done.8), channel_id=1, source_target_pairs={{0,2},{2,4},{4,6},{6,8},{8,10},{10,12},{12,14},{14,16},{16,18},{18... | collective-permute-start | bytes 405512 | tf_op jit(solution)/shard_map/ppermute | solution.py:143
  29.7 0.0 collective-permute-done.1
  29.8 5.0 %collective-permute-start.2 = (bf16[16,4224]{1,0:T(8,128)(2,1)S(1)}, bf16[16,4224]{1,0:T(8,128)(2,1)S(1)}, u32[]{:S(2)}, u32[]{:S(2)}) collective-permute-start(bf16[16,4224]{1,0:T(8,128)(2,1)S(1)} %collective-permute-done.1), channel_id=1, source_target_pairs={{0,30},{2,0},{4,2},{6,4},{8,6},{10,8},{12,10},{14,12},{16,14},{18,... | collective-permute-start | bytes 405512 | tf_op jit(solution)/shard_map/ppermute | solution.py:140
  34.8 0.0 collective-permute-done.9
  34.8 1.9 %collective-permute-start.10 = (bf16[16,4224]{1,0:T(8,128)(2,1)S(1)}, bf16[16,4224]{1,0:T(8,128)(2,1)S(1)}, u32[]{:S(2)}, u32[]{:S(2)}) collective-permute-start(bf16[16,4224]{1,0:T(8,128)(2,1)S(1)} %collective-permute-done.9), channel_id=1, source_target_pairs={{0,2},{2,4},{4,6},{6,8},{8,10},{10,12},{12,14},{14,16},{16,18},{18... | collective-permute-start | bytes 405512 | tf_op jit(solution)/shard_map/ppermute | solution.py:143
  36.7 0.8 collective-permute-done.2
  37.5 5.0 %collective-permute-start.3 = (bf16[16,4224]{1,0:T(8,128)(2,1)S(1)}, bf16[16,4224]{1,0:T(8,128)(2,1)S(1)}, u32[]{:S(2)}, u32[]{:S(2)}) collective-permute-start(bf16[16,4224]{1,0:T(8,128)(2,1)S(1)} %collective-permute-done.2), channel_id=1, source_target_pairs={{0,30},{2,0},{4,2},{6,4},{8,6},{10,8},{12,10},{14,12},{16,14},{18,... | collective-permute-start | bytes 405512 | tf_op jit(solution)/shard_map/ppermute | solution.py:140
  42.5 2.4 %collective-permute-done.10 = bf16[16,4224]{1,0:T(8,128)(2,1)S(1)} collective-permute-done((bf16[16,4224]{1,0:T(8,128)(2,1)S(1)}, bf16[16,4224]{1,0:T(8,128)(2,1)S(1)}, u32[]{:S(2)}, u32[]{:S(2)}) %collective-permute-start.10) | collective-permute-done | bytes 135200 | tf_op jit(solution)/shard_map/ppermute | solution.py:143
  44.9 1.9 %collective-permute-start.11 = (bf16[16,4224]{1,0:T(8,128)(2,1)S(1)}, bf16[16,4224]{1,0:T(8,128)(2,1)S(1)}, u32[]{:S(2)}, u32[]{:S(2)}) collective-permute-start(bf16[16,4224]{1,0:T(8,128)(2,1)S(1)} %collective-permute-done.10), channel_id=1, source_target_pairs={{0,2},{2,4},{4,6},{6,8},{8,10},{10,12},{12,14},{14,16},{16,18},{18... | collective-permute-start | bytes 405512 | tf_op jit(solution)/shard_map/ppermute | solution.py:143
  46.8 0.0 collective-permute-done.3
  46.8 4.8 %collective-permute-start.4 = (bf16[16,4224]{1,0:T(8,128)(2,1)S(1)}, bf16[16,4224]{1,0:T(8,128)(2,1)S(1)}, u32[]{:S(2)}, u32[]{:S(2)}) collective-permute-start(bf16[16,4224]{1,0:T(8,128)(2,1)S(1)} %collective-permute-done.3), channel_id=1, source_target_pairs={{0,30},{2,0},{4,2},{6,4},{8,6},{10,8},{12,10},{14,12},{16,14},{18,... | collective-permute-start | bytes 405512 | tf_op jit(solution)/shard_map/ppermute | solution.py:140
  51.7 2.1 %collective-permute-done.11 = bf16[16,4224]{1,0:T(8,128)(2,1)S(1)} collective-permute-done((bf16[16,4224]{1,0:T(8,128)(2,1)S(1)}, bf16[16,4224]{1,0:T(8,128)(2,1)S(1)}, u32[]{:S(2)}, u32[]{:S(2)}) %collective-permute-start.11) | collective-permute-done | bytes 135200 | tf_op jit(solution)/shard_map/ppermute | solution.py:143
  53.8 1.9 %collective-permute-start.12 = (bf16[16,4224]{1,0:T(8,128)(2,1)S(1)}, bf16[16,4224]{1,0:T(8,128)(2,1)S(1)}, u32[]{:S(2)}, u32[]{:S(2)}) collective-permute-start(bf16[16,4224]{1,0:T(8,128)(2,1)S(1)} %collective-permute-done.11), channel_id=1, source_target_pairs={{0,2},{2,4},{4,6},{6,8},{8,10},{10,12},{12,14},{14,16},{16,18},{18... | collective-permute-start | bytes 405512 | tf_op jit(solution)/shard_map/ppermute | solution.py:143
  55.7 0.0 collective-permute-done.4
  55.7 4.6 %collective-permute-start.5 = (bf16[16,4224]{1,0:T(8,128)(2,1)S(1)}, bf16[16,4224]{1,0:T(8,128)(2,1)S(1)}, u32[]{:S(2)}, u32[]{:S(2)}) collective-permute-start(bf16[16,4224]{1,0:T(8,128)(2,1)S(1)} %collective-permute-done.4), channel_id=1, source_target_pairs={{0,30},{2,0},{4,2},{6,4},{8,6},{10,8},{12,10},{14,12},{16,14},{18,... | collective-permute-start | bytes 405512 | tf_op jit(solution)/shard_map/ppermute | solution.py:140
  60.3 2.1 %collective-permute-done.12 = bf16[16,4224]{1,0:T(8,128)(2,1)S(1)} collective-permute-done((bf16[16,4224]{1,0:T(8,128)(2,1)S(1)}, bf16[16,4224]{1,0:T(8,128)(2,1)S(1)}, u32[]{:S(2)}, u32[]{:S(2)}) %collective-permute-start.12) | collective-permute-done | bytes 135200 | tf_op jit(solution)/shard_map/ppermute | solution.py:143
  62.5 1.9 %collective-permute-start.13 = (bf16[16,4224]{1,0:T(8,128)(2,1)S(1)}, bf16[16,4224]{1,0:T(8,128)(2,1)S(1)}, u32[]{:S(2)}, u32[]{:S(2)}) collective-permute-start(bf16[16,4224]{1,0:T(8,128)(2,1)S(1)} %collective-permute-done.12), channel_id=1, source_target_pairs={{0,2},{2,4},{4,6},{6,8},{8,10},{10,12},{12,14},{14,16},{16,18},{18... | collective-permute-start | bytes 405512 | tf_op jit(solution)/shard_map/ppermute | solution.py:143
  64.4 0.0 collective-permute-done.5
  64.4 4.6 %collective-permute-start.6 = (bf16[16,4224]{1,0:T(8,128)(2,1)S(1)}, bf16[16,4224]{1,0:T(8,128)(2,1)S(1)}, u32[]{:S(2)}, u32[]{:S(2)}) collective-permute-start(bf16[16,4224]{1,0:T(8,128)(2,1)S(1)} %collective-permute-done.5), channel_id=1, source_target_pairs={{0,30},{2,0},{4,2},{6,4},{8,6},{10,8},{12,10},{14,12},{16,14},{18,... | collective-permute-start | bytes 405512 | tf_op jit(solution)/shard_map/ppermute | solution.py:140
  69.0 2.6 %collective-permute-done.13 = bf16[16,4224]{1,0:T(8,128)(2,1)S(1)} collective-permute-done((bf16[16,4224]{1,0:T(8,128)(2,1)S(1)}, bf16[16,4224]{1,0:T(8,128)(2,1)S(1)}, u32[]{:S(2)}, u32[]{:S(2)}) %collective-permute-start.13) | collective-permute-done | bytes 135200 | tf_op jit(solution)/shard_map/ppermute | solution.py:143
  71.6 1.9 %collective-permute-start.14 = (bf16[16,4224]{1,0:T(8,128)(2,1)S(1)}, bf16[16,4224]{1,0:T(8,128)(2,1)S(1)}, u32[]{:S(2)}, u32[]{:S(2)}) collective-permute-start(bf16[16,4224]{1,0:T(8,128)(2,1)S(1)} %collective-permute-done.13), channel_id=1, source_target_pairs={{0,2},{2,4},{4,6},{6,8},{8,10},{10,12},{12,14},{14,16},{16,18},{18... | collective-permute-start | bytes 405512 | tf_op jit(solution)/shard_map/ppermute | solution.py:143
  73.5 0.0 collective-permute-done.6
  73.5 4.6 %collective-permute-start.7 = (bf16[16,4224]{1,0:T(8,128)(2,1)S(1)}, bf16[16,4224]{1,0:T(8,128)(2,1)S(1)}, u32[]{:S(2)}, u32[]{:S(2)}) collective-permute-start(bf16[16,4224]{1,0:T(8,128)(2,1)S(1)} %collective-permute-done.6), channel_id=1, source_target_pairs={{0,30},{2,0},{4,2},{6,4},{8,6},{10,8},{12,10},{14,12},{16,14},{18,... | collective-permute-start | bytes 405512 | tf_op jit(solution)/shard_map/ppermute | solution.py:140
  78.1 4.4 %collective-permute-done.7 = bf16[16,4224]{1,0:T(8,128)(2,1)S(1)} collective-permute-done((bf16[16,4224]{1,0:T(8,128)(2,1)S(1)}, bf16[16,4224]{1,0:T(8,128)(2,1)S(1)}, u32[]{:S(2)}, u32[]{:S(2)}) %collective-permute-start.7) | collective-permute-done | bytes 135200 | tf_op jit(solution)/shard_map/ppermute | solution.py:140
  82.7 8.7 %collective-permute-start.15 = (bf16[16,16,4224]{2,1,0:T(8,128)(2,1)S(1)}, bf16[16,16,4224]{2,1,0:T(8,128)(2,1)}, u32[]{:S(2)}, u32[]{:S(2)}) collective-permute-start(bf16[16,16,4224]{2,1,0:T(8,128)(2,1)S(1)} %bitcast_dynamic-update-slice_fusion.own_ref), channel_id=1, source_target_pairs={{0,1},{1,0},{2,3},{3,2},{4,5},{5,4},{6,7},{7,6},{8,9},{9,8},{10,11... | collective-permute-start | bytes 6488072 | tf_op jit(solution)/shard_map/ppermute | solution.py:160
  91.3 0.7 copy.13.bias_ref
  92.0 0.7 copy.14.gain_ref
  92.7 0.7 copy.15.shift_ref
  93.4 7.2 %all-gather.2.cloned.1.call-done = bf16[64,48,1024]{2,1,0:T(8,128)(2,1)} async-done(((bf16[2,48,1024]{2,1,0:T(8,128)(2,1)}), bf16[64,48,1024]{2,1,0:T(8,128)(2,1)}) %all-gather.2.cloned.1.call-update) | async-done | bytes 6291472 | tf_op jit(solution)/shard_map/all_gather | solution.py:155
  100.6 7.3 %shard_map.73 = bf16[32,3072]{1,0:T(8,128)(2,1)} custom-call(bf16[3072,1024]{1,0:T(8,128)(2,1)} %bitcast.47, bf16[288,1024]{1,0:T(8,128)(2,1)} %bitcast.49, f32[32,1]{1,0:T(8,128)} %copy.13.bias_ref, f32[32,1]{1,0:T(8,128)} %copy.14.gain_ref, f32[32,1]{1,0:T(8,128)} %copy.15.shift_ref), custom_call_target="tpu_custom_call" | custom-call | flops 1811939328 | bytes 7077888 | tf_op jit(solution)/shard_map/pallas_call | solution.py:59
  107.9 1.2 all_to_all.14
  109.2 0.8 copy.16
  110.0 9.9 %all-to-all-start = ((bf16[32,16,192]{2,0,1:T(8,128)(2,1)}), bf16[32,16,192]{2,0,1:T(8,128)(2,1)S(1)}, u32[]{:S(2)}, u32[]{:S(2)}) async-start(bf16[32,16,192]{2,0,1:T(8,128)(2,1)} %copy.16), calls=%async_computation | async-start | bytes 524288 | tf_op jit(solution)/shard_map/all_to_all | solution.py:163
  119.8 0.6 pad_add_fusion.index_ref
  120.5 13.8 %all-to-all-done = bf16[32,16,192]{2,0,1:T(8,128)(2,1)S(1)} async-done(((bf16[32,16,192]{2,0,1:T(8,128)(2,1)}), bf16[32,16,192]{2,0,1:T(8,128)(2,1)S(1)}, u32[]{:S(2)}, u32[]{:S(2)}) %all-to-all-start) | async-done | bytes 196640 | tf_op jit(solution)/shard_map/all_to_all | solution.py:163
  134.3 6.7 %all_gather.7.act_ref = bf16[1024,192]{1,0:T(8,128)(2,1)} all-gather(bf16[512,192]{1,0:T(8,128)(2,1)S(1)} %bitcast.48), channel_id=1, replica_groups=mesh['grp'=16,'z'=16,'core'=2] {'core'}, dimensions={0}, use_global_device_ids=true | all-gather | bytes 589824 | tf_op jit(solution)/shard_map/all_gather | solution.py:164
  140.9 5.4 %shard_map.74 = bf16[4,96,512]{2,1,0:T(8,128)(2,1)} custom-call(s32[2]{0:T(128)} %pad_add_fusion.index_ref, bf16[1024,192]{1,0:T(8,128)(2,1)} %all_gather.7.act_ref, bf16[16,16,4224]{2,1,0:T(8,128)(2,1)} %copy-done, bf16[16,16,4224]{2,1,0:T(8,128)(2,1)} %collective-permute-done.15.other_ref), custom_call_target="tpu_custom_call" | custom-call | flops 805306368 | bytes 5111808 | tf_op jit(solution)/shard_map/pallas_call | solution.py:121
  (25 shorter events, 0.3 us)
Async XLA Ops:
  6.5 94.1 %all-gather.2.cloned.1.call-start = ((), (), s32[]{:S(2)}) async-start(), calls=%async_computation.1 | async-start | bytes 6488064 | tf_op jit(solution)/shard_map/all_gather | solution.py:155
  8.3 14.2 %collective-permute-start = (bf16[16,4224]{1,0:T(8,128)(2,1)S(1)}, bf16[16,4224]{1,0:T(8,128)(2,1)S(1)}, u32[]{:S(2)}, u32[]{:S(2)}) collective-permute-start(bf16[16,4224]{1,0:T(8,128)(2,1)S(1)} %fusion.1), channel_id=1, source_target_pairs={{0,30},{2,0},{4,2},{6,4},{8,6},{10,8},{12,10},{14,12},{16,14},{18,... | collective-permute-start | bytes 405512 | tf_op jit(solution)/shard_map/ppermute | solution.py:140
  20.2 7.6 %collective-permute-start.8 = (bf16[16,4224]{1,0:T(8,128)(2,1)S(1)}, bf16[16,4224]{1,0:T(8,128)(2,1)S(1)}, u32[]{:S(2)}, u32[]{:S(2)}) collective-permute-start(bf16[16,4224]{1,0:T(8,128)(2,1)S(1)} %fusion.1), channel_id=1, source_target_pairs={{0,2},{2,4},{4,6},{6,8},{8,10},{10,12},{12,14},{14,16},{16,18},{18... | collective-permute-start | bytes 405512 | tf_op jit(solution)/shard_map/ppermute | solution.py:143
  22.2 69.1 %copy-start.1 = (f32[32]{0:T(128)S(1)}, f32[32]{0:T(128)}, u32[]{:S(2)}) copy-start(f32[32]{0:T(128)} %param.9) | copy-start | bytes 388
  22.2 69.8 %copy-start.2 = (f32[32]{0:T(128)S(1)}, f32[32]{0:T(128)}, u32[]{:S(2)}) copy-start(f32[32]{0:T(128)} %param.10) | copy-start | bytes 388
  22.2 70.5 %copy-start.3 = (f32[32]{0:T(128)S(1)}, f32[32]{0:T(128)}, u32[]{:S(2)}) copy-start(f32[32]{0:T(128)} %param.11) | copy-start | bytes 388
  22.5 7.3 %collective-permute-start.1 = (bf16[16,4224]{1,0:T(8,128)(2,1)S(1)}, bf16[16,4224]{1,0:T(8,128)(2,1)S(1)}, u32[]{:S(2)}, u32[]{:S(2)}) collective-permute-start(bf16[16,4224]{1,0:T(8,128)(2,1)S(1)} %collective-permute-done), channel_id=1, source_target_pairs={{0,30},{2,0},{4,2},{6,4},{8,6},{10,8},{12,10},{14,12},{16,14},{18,... | collective-permute-start | bytes 405512 | tf_op jit(solution)/shard_map/ppermute | solution.py:140
  27.8 7.0 %collective-permute-start.9 = (bf16[16,4224]{1,0:T(8,128)(2,1)S(1)}, bf16[16,4224]{1,0:T(8,128)(2,1)S(1)}, u32[]{:S(2)}, u32[]{:S(2)}) collective-permute-start(bf16[16,4224]{1,0:T(8,128)(2,1)S(1)} %collective-permute-done.8), channel_id=1, source_target_pairs={{0,2},{2,4},{4,6},{6,8},{8,10},{10,12},{12,14},{14,16},{16,18},{18... | collective-permute-start | bytes 405512 | tf_op jit(solution)/shard_map/ppermute | solution.py:143
  29.8 7.7 %collective-permute-start.2 = (bf16[16,4224]{1,0:T(8,128)(2,1)S(1)}, bf16[16,4224]{1,0:T(8,128)(2,1)S(1)}, u32[]{:S(2)}, u32[]{:S(2)}) collective-permute-start(bf16[16,4224]{1,0:T(8,128)(2,1)S(1)} %collective-permute-done.1), channel_id=1, source_target_pairs={{0,30},{2,0},{4,2},{6,4},{8,6},{10,8},{12,10},{14,12},{16,14},{18,... | collective-permute-start | bytes 405512 | tf_op jit(solution)/shard_map/ppermute | solution.py:140
  34.8 10.1 %collective-permute-start.10 = (bf16[16,4224]{1,0:T(8,128)(2,1)S(1)}, bf16[16,4224]{1,0:T(8,128)(2,1)S(1)}, u32[]{:S(2)}, u32[]{:S(2)}) collective-permute-start(bf16[16,4224]{1,0:T(8,128)(2,1)S(1)} %collective-permute-done.9), channel_id=1, source_target_pairs={{0,2},{2,4},{4,6},{6,8},{8,10},{10,12},{12,14},{14,16},{16,18},{18... | collective-permute-start | bytes 405512 | tf_op jit(solution)/shard_map/ppermute | solution.py:143
  37.5 9.3 %collective-permute-start.3 = (bf16[16,4224]{1,0:T(8,128)(2,1)S(1)}, bf16[16,4224]{1,0:T(8,128)(2,1)S(1)}, u32[]{:S(2)}, u32[]{:S(2)}) collective-permute-start(bf16[16,4224]{1,0:T(8,128)(2,1)S(1)} %collective-permute-done.2), channel_id=1, source_target_pairs={{0,30},{2,0},{4,2},{6,4},{8,6},{10,8},{12,10},{14,12},{16,14},{18,... | collective-permute-start | bytes 405512 | tf_op jit(solution)/shard_map/ppermute | solution.py:140
  44.9 8.9 %collective-permute-start.11 = (bf16[16,4224]{1,0:T(8,128)(2,1)S(1)}, bf16[16,4224]{1,0:T(8,128)(2,1)S(1)}, u32[]{:S(2)}, u32[]{:S(2)}) collective-permute-start(bf16[16,4224]{1,0:T(8,128)(2,1)S(1)} %collective-permute-done.10), channel_id=1, source_target_pairs={{0,2},{2,4},{4,6},{6,8},{8,10},{10,12},{12,14},{14,16},{16,18},{18... | collective-permute-start | bytes 405512 | tf_op jit(solution)/shard_map/ppermute | solution.py:143
  46.8 8.9 %collective-permute-start.4 = (bf16[16,4224]{1,0:T(8,128)(2,1)S(1)}, bf16[16,4224]{1,0:T(8,128)(2,1)S(1)}, u32[]{:S(2)}, u32[]{:S(2)}) collective-permute-start(bf16[16,4224]{1,0:T(8,128)(2,1)S(1)} %collective-permute-done.3), channel_id=1, source_target_pairs={{0,30},{2,0},{4,2},{6,4},{8,6},{10,8},{12,10},{14,12},{16,14},{18,... | collective-permute-start | bytes 405512 | tf_op jit(solution)/shard_map/ppermute | solution.py:140
  53.8 8.7 %collective-permute-start.12 = (bf16[16,4224]{1,0:T(8,128)(2,1)S(1)}, bf16[16,4224]{1,0:T(8,128)(2,1)S(1)}, u32[]{:S(2)}, u32[]{:S(2)}) collective-permute-start(bf16[16,4224]{1,0:T(8,128)(2,1)S(1)} %collective-permute-done.11), channel_id=1, source_target_pairs={{0,2},{2,4},{4,6},{6,8},{8,10},{10,12},{12,14},{14,16},{16,18},{18... | collective-permute-start | bytes 405512 | tf_op jit(solution)/shard_map/ppermute | solution.py:143
  55.7 8.7 %collective-permute-start.5 = (bf16[16,4224]{1,0:T(8,128)(2,1)S(1)}, bf16[16,4224]{1,0:T(8,128)(2,1)S(1)}, u32[]{:S(2)}, u32[]{:S(2)}) collective-permute-start(bf16[16,4224]{1,0:T(8,128)(2,1)S(1)} %collective-permute-done.4), channel_id=1, source_target_pairs={{0,30},{2,0},{4,2},{6,4},{8,6},{10,8},{12,10},{14,12},{16,14},{18,... | collective-permute-start | bytes 405512 | tf_op jit(solution)/shard_map/ppermute | solution.py:140
  62.5 9.1 %collective-permute-start.13 = (bf16[16,4224]{1,0:T(8,128)(2,1)S(1)}, bf16[16,4224]{1,0:T(8,128)(2,1)S(1)}, u32[]{:S(2)}, u32[]{:S(2)}) collective-permute-start(bf16[16,4224]{1,0:T(8,128)(2,1)S(1)} %collective-permute-done.12), channel_id=1, source_target_pairs={{0,2},{2,4},{4,6},{6,8},{8,10},{10,12},{12,14},{14,16},{16,18},{18... | collective-permute-start | bytes 405512 | tf_op jit(solution)/shard_map/ppermute | solution.py:143
  64.4 9.1 %collective-permute-start.6 = (bf16[16,4224]{1,0:T(8,128)(2,1)S(1)}, bf16[16,4224]{1,0:T(8,128)(2,1)S(1)}, u32[]{:S(2)}, u32[]{:S(2)}) collective-permute-start(bf16[16,4224]{1,0:T(8,128)(2,1)S(1)} %collective-permute-done.5), channel_id=1, source_target_pairs={{0,30},{2,0},{4,2},{6,4},{8,6},{10,8},{12,10},{14,12},{16,14},{18,... | collective-permute-start | bytes 405512 | tf_op jit(solution)/shard_map/ppermute | solution.py:140
  71.6 10.9 %collective-permute-start.14 = (bf16[16,4224]{1,0:T(8,128)(2,1)S(1)}, bf16[16,4224]{1,0:T(8,128)(2,1)S(1)}, u32[]{:S(2)}, u32[]{:S(2)}) collective-permute-start(bf16[16,4224]{1,0:T(8,128)(2,1)S(1)} %collective-permute-done.13), channel_id=1, source_target_pairs={{0,2},{2,4},{4,6},{6,8},{8,10},{10,12},{12,14},{14,16},{16,18},{18... | collective-permute-start | bytes 405512 | tf_op jit(solution)/shard_map/ppermute | solution.py:143
  73.5 9.0 %collective-permute-start.7 = (bf16[16,4224]{1,0:T(8,128)(2,1)S(1)}, bf16[16,4224]{1,0:T(8,128)(2,1)S(1)}, u32[]{:S(2)}, u32[]{:S(2)}) collective-permute-start(bf16[16,4224]{1,0:T(8,128)(2,1)S(1)} %collective-permute-done.6), channel_id=1, source_target_pairs={{0,30},{2,0},{4,2},{6,4},{8,6},{10,8},{12,10},{14,12},{16,14},{18,... | collective-permute-start | bytes 405512 | tf_op jit(solution)/shard_map/ppermute | solution.py:140
  82.6 25.3 %copy-start = (bf16[16,16,4224]{2,1,0:T(8,128)(2,1)}, bf16[16,16,4224]{2,1,0:T(8,128)(2,1)S(1)}, u32[]{:S(2)}) copy-start(bf16[16,16,4224]{2,1,0:T(8,128)(2,1)S(1)} %bitcast_dynamic-update-slice_fusion.own_ref) | copy-start | bytes 6488068
  82.7 58.3 %collective-permute-start.15 = (bf16[16,16,4224]{2,1,0:T(8,128)(2,1)S(1)}, bf16[16,16,4224]{2,1,0:T(8,128)(2,1)}, u32[]{:S(2)}, u32[]{:S(2)}) collective-permute-start(bf16[16,16,4224]{2,1,0:T(8,128)(2,1)S(1)} %bitcast_dynamic-update-slice_fusion.own_ref), channel_id=1, source_target_pairs={{0,1},{1,0},{2,3},{3,2},{4,5},{5,4},{6,7},{7,6},{8,9},{9,8},{10,11... | collective-permute-start | bytes 6488072 | tf_op jit(solution)/shard_map/ppermute | solution.py:160
  110.0 24.3 %all-to-all-start = ((bf16[32,16,192]{2,0,1:T(8,128)(2,1)}), bf16[32,16,192]{2,0,1:T(8,128)(2,1)S(1)}, u32[]{:S(2)}, u32[]{:S(2)}) async-start(bf16[32,16,192]{2,0,1:T(8,128)(2,1)} %copy.16), calls=%async_computation | async-start | bytes 524288 | tf_op jit(solution)/shard_map/all_to_all | solution.py:163
Sparse Core Ops, SparseCore 0:
  22.3 78.2 all-gather.1

commit v12 on v10

--- a/solution.py
+++ b/solution.py
@@ -59,10 +59,9 @@
     )(x, w, col(conv_bias), col(norm_gain), col(norm_shift))
 
 
-def up_kernel(index_ref, act_ref, own_ref, other_ref, out_ref, wnat_ref, actn_ref, *, width_cols):
+def up_kernel(index_ref, act_ref, own_ref, other_ref, out_ref, wnat_ref, *, width_cols):
     chips, slab, packed_width = own_ref.shape
     channels, positions = act_ref.shape
-    block = channels // (2 * chips)
     core = index_ref[0]
     here = index_ref[1]
     for m in range(chips):
@@ -71,18 +70,14 @@
         theirs = pl.multiple_of(2 * slab * chip + slab * (1 - core), slab)
         wnat_ref[pl.ds(mine, slab), :] = own_ref[m]
         wnat_ref[pl.ds(theirs, slab), :] = other_ref[m]
-    for c in range(2):
-        for z in range(chips):
-            actn_ref[pl.ds((2 * z + c) * block, block), :] = act_ref[pl.ds((c * chips + z) * block, block), :]
     rows = out_ref.shape[0] // 2
     outs = wnat_ref.shape[0]
     nn = (((1,), (0,)), ((), ()))
     sub = lax.broadcasted_iota(jnp.int32, (packed_width - 4 * channels, positions), 0)
-    ones = jnp.where(sub == 0, 1.0, 0.0).astype(actn_ref.dtype)
+    ones = jnp.where(sub == 0, 1.0, 0.0).astype(act_ref.dtype)
     bias = lax.dot_general(wnat_ref[:, pl.ds(4 * channels, packed_width - 4 * channels)], ones, nn,
                            preferred_element_type=jnp.float32)
-    act = actn_ref[...]
-    span = rows * width_cols
+    act = act_ref[...]
     dest = lax.broadcasted_iota(jnp.int32, (2 * width_cols, 2 * width_cols), 0)
     src = lax.broadcasted_iota(jnp.int32, (2 * width_cols, 2 * width_cols), 1)
     interleave = jnp.where(src == (dest % 2) * width_cols + dest // 2, 1.0, 0.0).astype(out_ref.dtype)
@@ -92,7 +87,7 @@
             res = lax.dot_general(wnat_ref[:, pl.ds((2 * a + b) * channels, channels)], act, nn,
                                   preferred_element_type=jnp.float32)
             res = jnp.transpose(res + bias).astype(out_ref.dtype)
-            phases.append(jnp.where(core == 0, res[:span], res[span:]))
+            phases.append(res)
         for i in range(rows):
             stacked = jnp.concatenate([p[i * width_cols:(i + 1) * width_cols] for p in phases], axis=0)
             out_ref[2 * i + a] = jnp.dot(interleave, stacked, preferred_element_type=jnp.float32).astype(out_ref.dtype)
@@ -100,7 +95,7 @@
 
 def up_conv(core, here, act, own, other, rows):
     channels, positions = act.shape
-    width_cols = positions // (2 * rows)
+    width_cols = positions // rows
     chips, slab, packed_width = own.shape
     outs = 2 * chips * slab
     vmem = pl.BlockSpec(memory_space=pltpu.VMEM)
@@ -111,7 +106,7 @@
         out_shape=jax.ShapeDtypeStruct((2 * rows, 2 * width_cols, outs), jnp.bfloat16),
         in_specs=[smem, vmem, vmem, vmem],
         out_specs=vmem,
-        scratch_shapes=[pltpu.VMEM((outs, packed_width), jnp.bfloat16), pltpu.VMEM((channels, positions), act.dtype)],
+        scratch_shapes=[pltpu.VMEM((outs, packed_width), jnp.bfloat16)],
         cost_estimate=pl.CostEstimate(
             flops=2 * positions * channels * 4 * outs, transcendentals=0,
             bytes_accessed=act.size * 2 + 2 * own.size * 2 + rows * width_cols * 4 * outs * 2),
@@ -148,10 +143,9 @@
     packed_other = lax.ppermute(packed_z, "core", [(0, 1), (1, 0)])
 
     activated = conv_norm(whole, conv_weight, conv_bias, norm_gain, norm_shift)
-    chip_rows = lax.all_to_all(activated, "z", split_axis=1, concat_axis=0, tiled=True)
-    both = lax.all_gather(chip_rows, "core", axis=0, tiled=True)
+    own_rows = lax.all_to_all(activated, ("z", "core"), split_axis=1, concat_axis=0, tiled=True)
     half = coarse.shape[0]
-    fine = up_conv(core, lax.axis_index("z"), both, packed_z, packed_other, half)
+    fine = up_conv(core, lax.axis_index("z"), own_rows, packed_z, packed_other, half)
     return fine.reshape(2 * half, 2 * width_cols, -1)
 
 

time: 153 us -> 155 us (1.013)
  waiting for transfers between devices: 35.7 us -> 43.3 us
  blocking collectives: 6.66 us -> 0 us
    all_to_all x1, waiting for transfers between devices: 13.8 us -> 21.4 us  [body(): lax.all_to_all(activated, ('z', 'core'), split_axis=1, concat_axis=0, til...]
    all_gather x1 -> x0, blocking collectives: 6.66 us -> none  [body(): both = lax.all_gather(chip_rows, 'core', axis=0, tiled=True)]
where the time goes in v12:
time: 155 us; the launch traced here: 154 us
  starting transfers between devices  78.1 us (50%)
  waiting for transfers between devices  43.3 us (28%)
  between operations  13.7 us (9%)
  Pallas kernels  11.4 us (7%)
  local copies, waits for them, and re-layouts  6.77 us (4%)
    ppermute x8, starting transfers between devices, ring_gather(): ahead = lax.ppermute(ahead, axis, step_up)  45.8 us
    all_to_all x1, waiting for transfers between devices, body(): lax.all_to_all(activated, ('z', 'core'), split_axis=1, concat_axis=0, til...  21.4 us
    ppermute x7, starting transfers between devices, ring_gather(): behind = lax.ppermute(behind, axis, step_down)  13.4 us
    all_to_all x1, starting transfers between devices, body(): lax.all_to_all(activated, ('z', 'core'), split_axis=1, concat_axis=0, til...  10.3 us
    ppermute x7, waiting for transfers between devices, ring_gather(): behind = lax.ppermute(behind, axis, step_down)  9.26 us
    ppermute x1, starting transfers between devices, body(): packed_other = lax.ppermute(packed_z, 'core', [(0, 1), (1, 0)])  8.66 us
    all_gather x1, waiting for transfers between devices, body(): whole = lax.all_gather(coarse, ('z', 'core'), axis=0, tiled=True)  7.24 us
    pallas_call x1, Pallas kernels, conv_norm(): pl.pallas_call(functools.partial(conv_norm_kernel, height=height, width_c...  6.3 us
  transfers between devices with their start and end apart: 18, of which 9 were waited for; matrix products, arithmetic and copies ran while one was open for 2% of the time, Pallas kernels for 4%

profile of v12, /device:TPU:1, one launch (start us, length us, event | category | flops | bytes accessed | tf_op | source)
XLA Modules:
  0.0 153.9 jit_solution(2903406964359820757)
XLA Ops:
  6.5 0.7 copy.17
  7.3 1.0 reshape.30
  8.3 12.0 %collective-permute-start = (bf16[16,4224]{1,0:T(8,128)(2,1)S(1)}, bf16[16,4224]{1,0:T(8,128)(2,1)S(1)}, u32[]{:S(2)}, u32[]{:S(2)}) collective-permute-start(bf16[16,4224]{1,0:T(8,128)(2,1)S(1)} %fusion.1), channel_id=1, source_target_pairs={{0,30},{2,0},{4,2},{6,4},{8,6},{10,8},{12,10},{14,12},{16,14},{18,... | collective-permute-start | bytes 405512 | tf_op jit(solution)/shard_map/ppermute | solution.py:123
  20.2 1.9 %collective-permute-start.8 = (bf16[16,4224]{1,0:T(8,128)(2,1)S(1)}, bf16[16,4224]{1,0:T(8,128)(2,1)S(1)}, u32[]{:S(2)}, u32[]{:S(2)}) collective-permute-start(bf16[16,4224]{1,0:T(8,128)(2,1)S(1)} %fusion.1), channel_id=1, source_target_pairs={{0,2},{2,4},{4,6},{6,8},{8,10},{10,12},{12,14},{14,16},{16,18},{18... | collective-permute-start | bytes 405512 | tf_op jit(solution)/shard_map/ppermute | solution.py:126
  22.2 0.0 all-gather.2.cloned.1.call-update
  22.2 0.0 copy-start.2
  22.2 0.0 copy-start.3
  22.2 0.0 copy-start.4
  22.3 0.2 collective-permute-done
  22.5 5.3 %collective-permute-start.1 = (bf16[16,4224]{1,0:T(8,128)(2,1)S(1)}, bf16[16,4224]{1,0:T(8,128)(2,1)S(1)}, u32[]{:S(2)}, u32[]{:S(2)}) collective-permute-start(bf16[16,4224]{1,0:T(8,128)(2,1)S(1)} %collective-permute-done), channel_id=1, source_target_pairs={{0,30},{2,0},{4,2},{6,4},{8,6},{10,8},{12,10},{14,12},{16,14},{18,... | collective-permute-start | bytes 405512 | tf_op jit(solution)/shard_map/ppermute | solution.py:123
  27.8 0.0 collective-permute-done.8
  27.8 1.9 %collective-permute-start.9 = (bf16[16,4224]{1,0:T(8,128)(2,1)S(1)}, bf16[16,4224]{1,0:T(8,128)(2,1)S(1)}, u32[]{:S(2)}, u32[]{:S(2)}) collective-permute-start(bf16[16,4224]{1,0:T(8,128)(2,1)S(1)} %collective-permute-done.8), channel_id=1, source_target_pairs={{0,2},{2,4},{4,6},{6,8},{8,10},{10,12},{12,14},{14,16},{16,18},{18... | collective-permute-start | bytes 405512 | tf_op jit(solution)/shard_map/ppermute | solution.py:126
  29.7 0.0 collective-permute-done.1
  29.8 5.0 %collective-permute-start.2 = (bf16[16,4224]{1,0:T(8,128)(2,1)S(1)}, bf16[16,4224]{1,0:T(8,128)(2,1)S(1)}, u32[]{:S(2)}, u32[]{:S(2)}) collective-permute-start(bf16[16,4224]{1,0:T(8,128)(2,1)S(1)} %collective-permute-done.1), channel_id=1, source_target_pairs={{0,30},{2,0},{4,2},{6,4},{8,6},{10,8},{12,10},{14,12},{16,14},{18,... | collective-permute-start | bytes 405512 | tf_op jit(solution)/shard_map/ppermute | solution.py:123
  34.8 0.0 collective-permute-done.9
  34.8 1.9 %collective-permute-start.10 = (bf16[16,4224]{1,0:T(8,128)(2,1)S(1)}, bf16[16,4224]{1,0:T(8,128)(2,1)S(1)}, u32[]{:S(2)}, u32[]{:S(2)}) collective-permute-start(bf16[16,4224]{1,0:T(8,128)(2,1)S(1)} %collective-permute-done.9), channel_id=1, source_target_pairs={{0,2},{2,4},{4,6},{6,8},{8,10},{10,12},{12,14},{14,16},{16,18},{18... | collective-permute-start | bytes 405512 | tf_op jit(solution)/shard_map/ppermute | solution.py:126
  36.7 0.8 collective-permute-done.2
  37.5 5.0 %collective-permute-start.3 = (bf16[16,4224]{1,0:T(8,128)(2,1)S(1)}, bf16[16,4224]{1,0:T(8,128)(2,1)S(1)}, u32[]{:S(2)}, u32[]{:S(2)}) collective-permute-start(bf16[16,4224]{1,0:T(8,128)(2,1)S(1)} %collective-permute-done.2), channel_id=1, source_target_pairs={{0,30},{2,0},{4,2},{6,4},{8,6},{10,8},{12,10},{14,12},{16,14},{18,... | collective-permute-start | bytes 405512 | tf_op jit(solution)/shard_map/ppermute | solution.py:123
  42.5 2.4 %collective-permute-done.10 = bf16[16,4224]{1,0:T(8,128)(2,1)S(1)} collective-permute-done((bf16[16,4224]{1,0:T(8,128)(2,1)S(1)}, bf16[16,4224]{1,0:T(8,128)(2,1)S(1)}, u32[]{:S(2)}, u32[]{:S(2)}) %collective-permute-start.10) | collective-permute-done | bytes 135200 | tf_op jit(solution)/shard_map/ppermute | solution.py:126
  44.9 1.9 %collective-permute-start.11 = (bf16[16,4224]{1,0:T(8,128)(2,1)S(1)}, bf16[16,4224]{1,0:T(8,128)(2,1)S(1)}, u32[]{:S(2)}, u32[]{:S(2)}) collective-permute-start(bf16[16,4224]{1,0:T(8,128)(2,1)S(1)} %collective-permute-done.10), channel_id=1, source_target_pairs={{0,2},{2,4},{4,6},{6,8},{8,10},{10,12},{12,14},{14,16},{16,18},{18... | collective-permute-start | bytes 405512 | tf_op jit(solution)/shard_map/ppermute | solution.py:126
  46.8 0.0 collective-permute-done.3
  46.8 4.8 %collective-permute-start.4 = (bf16[16,4224]{1,0:T(8,128)(2,1)S(1)}, bf16[16,4224]{1,0:T(8,128)(2,1)S(1)}, u32[]{:S(2)}, u32[]{:S(2)}) collective-permute-start(bf16[16,4224]{1,0:T(8,128)(2,1)S(1)} %collective-permute-done.3), channel_id=1, source_target_pairs={{0,30},{2,0},{4,2},{6,4},{8,6},{10,8},{12,10},{14,12},{16,14},{18,... | collective-permute-start | bytes 405512 | tf_op jit(solution)/shard_map/ppermute | solution.py:123
  51.7 2.1 %collective-permute-done.11 = bf16[16,4224]{1,0:T(8,128)(2,1)S(1)} collective-permute-done((bf16[16,4224]{1,0:T(8,128)(2,1)S(1)}, bf16[16,4224]{1,0:T(8,128)(2,1)S(1)}, u32[]{:S(2)}, u32[]{:S(2)}) %collective-permute-start.11) | collective-permute-done | bytes 135200 | tf_op jit(solution)/shard_map/ppermute | solution.py:126
  53.8 1.9 %collective-permute-start.12 = (bf16[16,4224]{1,0:T(8,128)(2,1)S(1)}, bf16[16,4224]{1,0:T(8,128)(2,1)S(1)}, u32[]{:S(2)}, u32[]{:S(2)}) collective-permute-start(bf16[16,4224]{1,0:T(8,128)(2,1)S(1)} %collective-permute-done.11), channel_id=1, source_target_pairs={{0,2},{2,4},{4,6},{6,8},{8,10},{10,12},{12,14},{14,16},{16,18},{18... | collective-permute-start | bytes 405512 | tf_op jit(solution)/shard_map/ppermute | solution.py:126
  55.7 0.0 collective-permute-done.4
  55.7 4.6 %collective-permute-start.5 = (bf16[16,4224]{1,0:T(8,128)(2,1)S(1)}, bf16[16,4224]{1,0:T(8,128)(2,1)S(1)}, u32[]{:S(2)}, u32[]{:S(2)}) collective-permute-start(bf16[16,4224]{1,0:T(8,128)(2,1)S(1)} %collective-permute-done.4), channel_id=1, source_target_pairs={{0,30},{2,0},{4,2},{6,4},{8,6},{10,8},{12,10},{14,12},{16,14},{18,... | collective-permute-start | bytes 405512 | tf_op jit(solution)/shard_map/ppermute | solution.py:123
  60.3 2.1 %collective-permute-done.12 = bf16[16,4224]{1,0:T(8,128)(2,1)S(1)} collective-permute-done((bf16[16,4224]{1,0:T(8,128)(2,1)S(1)}, bf16[16,4224]{1,0:T(8,128)(2,1)S(1)}, u32[]{:S(2)}, u32[]{:S(2)}) %collective-permute-start.12) | collective-permute-done | bytes 135200 | tf_op jit(solution)/shard_map/ppermute | solution.py:126
  62.5 1.9 %collective-permute-start.13 = (bf16[16,4224]{1,0:T(8,128)(2,1)S(1)}, bf16[16,4224]{1,0:T(8,128)(2,1)S(1)}, u32[]{:S(2)}, u32[]{:S(2)}) collective-permute-start(bf16[16,4224]{1,0:T(8,128)(2,1)S(1)} %collective-permute-done.12), channel_id=1, source_target_pairs={{0,2},{2,4},{4,6},{6,8},{8,10},{10,12},{12,14},{14,16},{16,18},{18... | collective-permute-start | bytes 405512 | tf_op jit(solution)/shard_map/ppermute | solution.py:126
  64.4 0.0 collective-permute-done.5
  64.4 4.6 %collective-permute-start.6 = (bf16[16,4224]{1,0:T(8,128)(2,1)S(1)}, bf16[16,4224]{1,0:T(8,128)(2,1)S(1)}, u32[]{:S(2)}, u32[]{:S(2)}) collective-permute-start(bf16[16,4224]{1,0:T(8,128)(2,1)S(1)} %collective-permute-done.5), channel_id=1, source_target_pairs={{0,30},{2,0},{4,2},{6,4},{8,6},{10,8},{12,10},{14,12},{16,14},{18,... | collective-permute-start | bytes 405512 | tf_op jit(solution)/shard_map/ppermute | solution.py:123
  69.0 2.6 %collective-permute-done.13 = bf16[16,4224]{1,0:T(8,128)(2,1)S(1)} collective-permute-done((bf16[16,4224]{1,0:T(8,128)(2,1)S(1)}, bf16[16,4224]{1,0:T(8,128)(2,1)S(1)}, u32[]{:S(2)}, u32[]{:S(2)}) %collective-permute-start.13) | collective-permute-done | bytes 135200 | tf_op jit(solution)/shard_map/ppermute | solution.py:126
  71.6 1.9 %collective-permute-start.14 = (bf16[16,4224]{1,0:T(8,128)(2,1)S(1)}, bf16[16,4224]{1,0:T(8,128)(2,1)S(1)}, u32[]{:S(2)}, u32[]{:S(2)}) collective-permute-start(bf16[16,4224]{1,0:T(8,128)(2,1)S(1)} %collective-permute-done.13), channel_id=1, source_target_pairs={{0,2},{2,4},{4,6},{6,8},{8,10},{10,12},{12,14},{14,16},{16,18},{18... | collective-permute-start | bytes 405512 | tf_op jit(solution)/shard_map/ppermute | solution.py:126
  73.5 0.0 collective-permute-done.6
  73.5 4.6 %collective-permute-start.7 = (bf16[16,4224]{1,0:T(8,128)(2,1)S(1)}, bf16[16,4224]{1,0:T(8,128)(2,1)S(1)}, u32[]{:S(2)}, u32[]{:S(2)}) collective-permute-start(bf16[16,4224]{1,0:T(8,128)(2,1)S(1)} %collective-permute-done.6), channel_id=1, source_target_pairs={{0,30},{2,0},{4,2},{6,4},{8,6},{10,8},{12,10},{14,12},{16,14},{18,... | collective-permute-start | bytes 405512 | tf_op jit(solution)/shard_map/ppermute | solution.py:123
  78.1 4.4 %collective-permute-done.7 = bf16[16,4224]{1,0:T(8,128)(2,1)S(1)} collective-permute-done((bf16[16,4224]{1,0:T(8,128)(2,1)S(1)}, bf16[16,4224]{1,0:T(8,128)(2,1)S(1)}, u32[]{:S(2)}, u32[]{:S(2)}) %collective-permute-start.7) | collective-permute-done | bytes 135200 | tf_op jit(solution)/shard_map/ppermute | solution.py:123
  82.7 8.7 %collective-permute-start.15 = (bf16[16,16,4224]{2,1,0:T(8,128)(2,1)S(1)}, bf16[16,16,4224]{2,1,0:T(8,128)(2,1)}, u32[]{:S(2)}, u32[]{:S(2)}) collective-permute-start(bf16[16,16,4224]{2,1,0:T(8,128)(2,1)S(1)} %bitcast_dynamic-update-slice_fusion.own_ref), channel_id=1, source_target_pairs={{0,1},{1,0},{2,3},{3,2},{4,5},{5,4},{6,7},{7,6},{8,9},{9,8},{10,11... | collective-permute-start | bytes 6488072 | tf_op jit(solution)/shard_map/ppermute | solution.py:143
  91.3 0.7 copy.13.bias_ref
  92.0 0.7 copy.14.gain_ref
  92.7 0.7 copy.15.shift_ref
  93.4 7.2 %all-gather.2.cloned.1.call-done = bf16[64,48,1024]{2,1,0:T(8,128)(2,1)} async-done(((bf16[2,48,1024]{2,1,0:T(8,128)(2,1)}), bf16[64,48,1024]{2,1,0:T(8,128)(2,1)}) %all-gather.2.cloned.1.call-update) | async-done | bytes 6291472 | tf_op jit(solution)/shard_map/all_gather | solution.py:138
  100.6 6.3 %shard_map.73 = bf16[32,3072]{1,0:T(8,128)(2,1)} custom-call(bf16[3072,1024]{1,0:T(8,128)(2,1)} %bitcast.47, bf16[288,1024]{1,0:T(8,128)(2,1)} %bitcast.49, f32[32,1]{1,0:T(8,128)} %copy.13.bias_ref, f32[32,1]{1,0:T(8,128)} %copy.14.gain_ref, f32[32,1]{1,0:T(8,128)} %copy.15.shift_ref), custom_call_target="tpu_custom_call" | custom-call | flops 1811939328 | bytes 7077888 | tf_op jit(solution)/shard_map/pallas_call | solution.py:50
  106.9 1.2 all_to_all.14
  108.1 0.8 copy.16
  108.9 10.3 %all-to-all-start = ((bf16[32,32,96]{2,0,1:T(8,128)(2,1)}), bf16[32,32,96]{2,0,1:T(8,128)(2,1)S(1)}, u32[]{:S(2)}, u32[]{:S(2)}) async-start(bf16[32,32,96]{2,0,1:T(8,128)(2,1)} %copy.16), calls=%async_computation | async-start | bytes 524288 | tf_op jit(solution)/shard_map/all_to_all | solution.py:146
  119.3 0.6 pad_add_fusion.index_ref
  119.9 21.4 %all-to-all-done = bf16[32,32,96]{2,0,1:T(8,128)(2,1)S(1)} async-done(((bf16[32,32,96]{2,0,1:T(8,128)(2,1)}), bf16[32,32,96]{2,0,1:T(8,128)(2,1)S(1)}, u32[]{:S(2)}, u32[]{:S(2)}) %all-to-all-start) | async-done | bytes 196640 | tf_op jit(solution)/shard_map/all_to_all | solution.py:146
  141.3 0.7 copy-done.1
  142.0 5.1 %shard_map.74 = bf16[4,96,512]{2,1,0:T(8,128)(2,1)} custom-call(s32[2]{0:T(128)} %pad_add_fusion.index_ref, bf16[1024,96]{1,0:T(8,128)(2,1)} %bitcast.48, bf16[16,16,4224]{2,1,0:T(8,128)(2,1)} %copy-done, bf16[16,16,4224]{2,1,0:T(8,128)(2,1)} %collective-permute-done.15.other_ref), custom_call_target="tpu_custom_call" | custom-call | flops 402653184 | bytes 4915200 | tf_op jit(solution)/shard_map/pallas_call | solution.py:104
  (26 shorter events, 0.3 us)
Async XLA Ops:
  6.5 94.1 %all-gather.2.cloned.1.call-start = ((), (), s32[]{:S(2)}) async-start(), calls=%async_computation.1 | async-start | bytes 6488064 | tf_op jit(solution)/shard_map/all_gather | solution.py:138
  8.3 14.2 %collective-permute-start = (bf16[16,4224]{1,0:T(8,128)(2,1)S(1)}, bf16[16,4224]{1,0:T(8,128)(2,1)S(1)}, u32[]{:S(2)}, u32[]{:S(2)}) collective-permute-start(bf16[16,4224]{1,0:T(8,128)(2,1)S(1)} %fusion.1), channel_id=1, source_target_pairs={{0,30},{2,0},{4,2},{6,4},{8,6},{10,8},{12,10},{14,12},{16,14},{18,... | collective-permute-start | bytes 405512 | tf_op jit(solution)/shard_map/ppermute | solution.py:123
  20.2 7.6 %collective-permute-start.8 = (bf16[16,4224]{1,0:T(8,128)(2,1)S(1)}, bf16[16,4224]{1,0:T(8,128)(2,1)S(1)}, u32[]{:S(2)}, u32[]{:S(2)}) collective-permute-start(bf16[16,4224]{1,0:T(8,128)(2,1)S(1)} %fusion.1), channel_id=1, source_target_pairs={{0,2},{2,4},{4,6},{6,8},{8,10},{10,12},{12,14},{14,16},{16,18},{18... | collective-permute-start | bytes 405512 | tf_op jit(solution)/shard_map/ppermute | solution.py:126
  22.2 69.1 %copy-start.2 = (f32[32]{0:T(128)S(1)}, f32[32]{0:T(128)}, u32[]{:S(2)}) copy-start(f32[32]{0:T(128)} %param.9) | copy-start | bytes 388
  22.2 69.8 %copy-start.3 = (f32[32]{0:T(128)S(1)}, f32[32]{0:T(128)}, u32[]{:S(2)}) copy-start(f32[32]{0:T(128)} %param.10) | copy-start | bytes 388
  22.2 70.5 %copy-start.4 = (f32[32]{0:T(128)S(1)}, f32[32]{0:T(128)}, u32[]{:S(2)}) copy-start(f32[32]{0:T(128)} %param.11) | copy-start | bytes 388
  22.5 7.3 %collective-permute-start.1 = (bf16[16,4224]{1,0:T(8,128)(2,1)S(1)}, bf16[16,4224]{1,0:T(8,128)(2,1)S(1)}, u32[]{:S(2)}, u32[]{:S(2)}) collective-permute-start(bf16[16,4224]{1,0:T(8,128)(2,1)S(1)} %collective-permute-done), channel_id=1, source_target_pairs={{0,30},{2,0},{4,2},{6,4},{8,6},{10,8},{12,10},{14,12},{16,14},{18,... | collective-permute-start | bytes 405512 | tf_op jit(solution)/shard_map/ppermute | solution.py:123
  27.8 7.0 %collective-permute-start.9 = (bf16[16,4224]{1,0:T(8,128)(2,1)S(1)}, bf16[16,4224]{1,0:T(8,128)(2,1)S(1)}, u32[]{:S(2)}, u32[]{:S(2)}) collective-permute-start(bf16[16,4224]{1,0:T(8,128)(2,1)S(1)} %collective-permute-done.8), channel_id=1, source_target_pairs={{0,2},{2,4},{4,6},{6,8},{8,10},{10,12},{12,14},{14,16},{16,18},{18... | collective-permute-start | bytes 405512 | tf_op jit(solution)/shard_map/ppermute | solution.py:126
  29.8 7.7 %collective-permute-start.2 = (bf16[16,4224]{1,0:T(8,128)(2,1)S(1)}, bf16[16,4224]{1,0:T(8,128)(2,1)S(1)}, u32[]{:S(2)}, u32[]{:S(2)}) collective-permute-start(bf16[16,4224]{1,0:T(8,128)(2,1)S(1)} %collective-permute-done.1), channel_id=1, source_target_pairs={{0,30},{2,0},{4,2},{6,4},{8,6},{10,8},{12,10},{14,12},{16,14},{18,... | collective-permute-start | bytes 405512 | tf_op jit(solution)/shard_map/ppermute | solution.py:123
  34.8 10.1 %collective-permute-start.10 = (bf16[16,4224]{1,0:T(8,128)(2,1)S(1)}, bf16[16,4224]{1,0:T(8,128)(2,1)S(1)}, u32[]{:S(2)}, u32[]{:S(2)}) collective-permute-start(bf16[16,4224]{1,0:T(8,128)(2,1)S(1)} %collective-permute-done.9), channel_id=1, source_target_pairs={{0,2},{2,4},{4,6},{6,8},{8,10},{10,12},{12,14},{14,16},{16,18},{18... | collective-permute-start | bytes 405512 | tf_op jit(solution)/shard_map/ppermute | solution.py:126
  37.5 9.3 %collective-permute-start.3 = (bf16[16,4224]{1,0:T(8,128)(2,1)S(1)}, bf16[16,4224]{1,0:T(8,128)(2,1)S(1)}, u32[]{:S(2)}, u32[]{:S(2)}) collective-permute-start(bf16[16,4224]{1,0:T(8,128)(2,1)S(1)} %collective-permute-done.2), channel_id=1, source_target_pairs={{0,30},{2,0},{4,2},{6,4},{8,6},{10,8},{12,10},{14,12},{16,14},{18,... | collective-permute-start | bytes 405512 | tf_op jit(solution)/shard_map/ppermute | solution.py:123
  44.9 8.9 %collective-permute-start.11 = (bf16[16,4224]{1,0:T(8,128)(2,1)S(1)}, bf16[16,4224]{1,0:T(8,128)(2,1)S(1)}, u32[]{:S(2)}, u32[]{:S(2)}) collective-permute-start(bf16[16,4224]{1,0:T(8,128)(2,1)S(1)} %collective-permute-done.10), channel_id=1, source_target_pairs={{0,2},{2,4},{4,6},{6,8},{8,10},{10,12},{12,14},{14,16},{16,18},{18... | collective-permute-start | bytes 405512 | tf_op jit(solution)/shard_map/ppermute | solution.py:126
  46.8 8.9 %collective-permute-start.4 = (bf16[16,4224]{1,0:T(8,128)(2,1)S(1)}, bf16[16,4224]{1,0:T(8,128)(2,1)S(1)}, u32[]{:S(2)}, u32[]{:S(2)}) collective-permute-start(bf16[16,4224]{1,0:T(8,128)(2,1)S(1)} %collective-permute-done.3), channel_id=1, source_target_pairs={{0,30},{2,0},{4,2},{6,4},{8,6},{10,8},{12,10},{14,12},{16,14},{18,... | collective-permute-start | bytes 405512 | tf_op jit(solution)/shard_map/ppermute | solution.py:123
  53.8 8.7 %collective-permute-start.12 = (bf16[16,4224]{1,0:T(8,128)(2,1)S(1)}, bf16[16,4224]{1,0:T(8,128)(2,1)S(1)}, u32[]{:S(2)}, u32[]{:S(2)}) collective-permute-start(bf16[16,4224]{1,0:T(8,128)(2,1)S(1)} %collective-permute-done.11), channel_id=1, source_target_pairs={{0,2},{2,4},{4,6},{6,8},{8,10},{10,12},{12,14},{14,16},{16,18},{18... | collective-permute-start | bytes 405512 | tf_op jit(solution)/shard_map/ppermute | solution.py:126
  55.7 8.7 %collective-permute-start.5 = (bf16[16,4224]{1,0:T(8,128)(2,1)S(1)}, bf16[16,4224]{1,0:T(8,128)(2,1)S(1)}, u32[]{:S(2)}, u32[]{:S(2)}) collective-permute-start(bf16[16,4224]{1,0:T(8,128)(2,1)S(1)} %collective-permute-done.4), channel_id=1, source_target_pairs={{0,30},{2,0},{4,2},{6,4},{8,6},{10,8},{12,10},{14,12},{16,14},{18,... | collective-permute-start | bytes 405512 | tf_op jit(solution)/shard_map/ppermute | solution.py:123
  62.5 9.1 %collective-permute-start.13 = (bf16[16,4224]{1,0:T(8,128)(2,1)S(1)}, bf16[16,4224]{1,0:T(8,128)(2,1)S(1)}, u32[]{:S(2)}, u32[]{:S(2)}) collective-permute-start(bf16[16,4224]{1,0:T(8,128)(2,1)S(1)} %collective-permute-done.12), channel_id=1, source_target_pairs={{0,2},{2,4},{4,6},{6,8},{8,10},{10,12},{12,14},{14,16},{16,18},{18... | collective-permute-start | bytes 405512 | tf_op jit(solution)/shard_map/ppermute | solution.py:126
  64.4 9.1 %collective-permute-start.6 = (bf16[16,4224]{1,0:T(8,128)(2,1)S(1)}, bf16[16,4224]{1,0:T(8,128)(2,1)S(1)}, u32[]{:S(2)}, u32[]{:S(2)}) collective-permute-start(bf16[16,4224]{1,0:T(8,128)(2,1)S(1)} %collective-permute-done.5), channel_id=1, source_target_pairs={{0,30},{2,0},{4,2},{6,4},{8,6},{10,8},{12,10},{14,12},{16,14},{18,... | collective-permute-start | bytes 405512 | tf_op jit(solution)/shard_map/ppermute | solution.py:123
  71.6 10.9 %collective-permute-start.14 = (bf16[16,4224]{1,0:T(8,128)(2,1)S(1)}, bf16[16,4224]{1,0:T(8,128)(2,1)S(1)}, u32[]{:S(2)}, u32[]{:S(2)}) collective-permute-start(bf16[16,4224]{1,0:T(8,128)(2,1)S(1)} %collective-permute-done.13), channel_id=1, source_target_pairs={{0,2},{2,4},{4,6},{6,8},{8,10},{10,12},{12,14},{14,16},{16,18},{18... | collective-permute-start | bytes 405512 | tf_op jit(solution)/shard_map/ppermute | solution.py:126
  73.5 9.0 %collective-permute-start.7 = (bf16[16,4224]{1,0:T(8,128)(2,1)S(1)}, bf16[16,4224]{1,0:T(8,128)(2,1)S(1)}, u32[]{:S(2)}, u32[]{:S(2)}) collective-permute-start(bf16[16,4224]{1,0:T(8,128)(2,1)S(1)} %collective-permute-done.6), channel_id=1, source_target_pairs={{0,30},{2,0},{4,2},{6,4},{8,6},{10,8},{12,10},{14,12},{16,14},{18,... | collective-permute-start | bytes 405512 | tf_op jit(solution)/shard_map/ppermute | solution.py:123
  82.6 24.3 %copy-start = (bf16[16,16,4224]{2,1,0:T(8,128)(2,1)}, bf16[16,16,4224]{2,1,0:T(8,128)(2,1)S(1)}, u32[]{:S(2)}) copy-start(bf16[16,16,4224]{2,1,0:T(8,128)(2,1)S(1)} %bitcast_dynamic-update-slice_fusion.own_ref) | copy-start | bytes 6488068
  82.7 37.2 %collective-permute-start.15 = (bf16[16,16,4224]{2,1,0:T(8,128)(2,1)S(1)}, bf16[16,16,4224]{2,1,0:T(8,128)(2,1)}, u32[]{:S(2)}, u32[]{:S(2)}) collective-permute-start(bf16[16,16,4224]{2,1,0:T(8,128)(2,1)S(1)} %bitcast_dynamic-update-slice_fusion.own_ref), channel_id=1, source_target_pairs={{0,1},{1,0},{2,3},{3,2},{4,5},{5,4},{6,7},{7,6},{8,9},{9,8},{10,11... | collective-permute-start | bytes 6488072 | tf_op jit(solution)/shard_map/ppermute | solution.py:143
  108.9 32.3 %all-to-all-start = ((bf16[32,32,96]{2,0,1:T(8,128)(2,1)}), bf16[32,32,96]{2,0,1:T(8,128)(2,1)S(1)}, u32[]{:S(2)}, u32[]{:S(2)}) async-start(bf16[32,32,96]{2,0,1:T(8,128)(2,1)} %copy.16), calls=%async_computation | async-start | bytes 524288 | tf_op jit(solution)/shard_map/all_to_all | solution.py:146
  141.3 0.7 copy-start.1
Sparse Core Ops, SparseCore 0:
  22.3 78.2 all-gather.1

commit v13 on v10

--- a/solution.py
+++ b/solution.py
@@ -11,7 +11,7 @@
 
 
 def conv_norm_kernel(x_ref, w_ref, bias_ref, gain_ref, shift_ref, out_ref, *, height, width_cols):
-    outputs = out_ref.shape[0]
+    outputs = out_ref.shape[1]
     positions = height * width_cols
     taps = lax.dot_general(w_ref[...], x_ref[...], (((1,), (1,)), ((), ())),
                            preferred_element_type=jnp.float32)
@@ -37,10 +37,13 @@
     spread = jnp.sum(jnp.sum(dev * dev, axis=2, keepdims=True), axis=1, keepdims=True) / count
     normed = (dev * lax.rsqrt(spread + 1e-05)).reshape(outputs, positions)
     v = normed * gain_ref[...] + shift_ref[...]
-    out_ref[...] = (v / (1.0 + jnp.exp(-v))).astype(out_ref.dtype)
+    act = (v / (1.0 + jnp.exp(-v))).astype(out_ref.dtype)
+    chips, _, span = out_ref.shape
+    for chip in range(chips):
+        out_ref[chip] = act[:, chip * span:(chip + 1) * span]
 
 
-def conv_norm(whole, conv_weight, conv_bias, norm_gain, norm_shift):
+def conv_norm(whole, conv_weight, conv_bias, norm_gain, norm_shift, chips):
     height, width_cols, channels = whole.shape
     outputs = conv_weight.shape[0]
     x = whole.reshape(height * width_cols, channels)
@@ -49,7 +52,7 @@
     vmem = pl.BlockSpec(memory_space=pltpu.VMEM)
     return pl.pallas_call(
         functools.partial(conv_norm_kernel, height=height, width_cols=width_cols),
-        out_shape=jax.ShapeDtypeStruct((outputs, height * width_cols), jnp.bfloat16),
+        out_shape=jax.ShapeDtypeStruct((chips, outputs, height * width_cols // chips), jnp.bfloat16),
         in_specs=[vmem] * 5,
         out_specs=vmem,
         cost_estimate=pl.CostEstimate(
@@ -147,8 +150,9 @@
     packed_z = ring_gather(packed, "z")
     packed_other = lax.ppermute(packed_z, "core", [(0, 1), (1, 0)])
 
-    activated = conv_norm(whole, conv_weight, conv_bias, norm_gain, norm_shift)
-    chip_rows = lax.all_to_all(activated, "z", split_axis=1, concat_axis=0, tiled=True)
+    activated = conv_norm(whole, conv_weight, conv_bias, norm_gain, norm_shift, chips)
+    chip_rows = lax.all_to_all(activated, "z", split_axis=0, concat_axis=0, tiled=True)
+    chip_rows = chip_rows.reshape(-1, chip_rows.shape[2])
     both = lax.all_gather(chip_rows, "core", axis=0, tiled=True)
     half = coarse.shape[0]
     fine = up_conv(core, lax.axis_index("z"), both, packed_z, packed_other, half)

time: 153 us -> 151 us (0.987)
  local copies, waits for them, and re-layouts: 6.1 us -> 4.07 us
    all_to_all x2 -> x0, local copies, waits for them, and re-layouts: 2.03 us -> none  [body(): lax.all_to_all(activated, 'z', split_axis=1, concat_axis=0, tiled=True)]
where the time goes in v13:
time: 151 us; the launch traced here: 150 us
  starting transfers between devices  77.7 us (51%)
  waiting for transfers between devices  35.7 us (24%)
  between operations  13.7 us (9%)
  Pallas kernels  11.8 us (8%)
  blocking collectives  6.66 us (4%)
  local copies, waits for them, and re-layouts  4.07 us (3%)
    ppermute x8, starting transfers between devices, ring_gather(): ahead = lax.ppermute(ahead, axis, step_up)  45.8 us
    all_to_all x1, waiting for transfers between devices, body(): lax.all_to_all(activated, 'z', split_axis=0, concat_axis=0, tiled=True)  13.8 us
    ppermute x7, starting transfers between devices, ring_gather(): behind = lax.ppermute(behind, axis, step_down)  13.4 us
    all_to_all x1, starting transfers between devices, body(): lax.all_to_all(activated, 'z', split_axis=0, concat_axis=0, tiled=True)  9.86 us
    ppermute x7, waiting for transfers between devices, ring_gather(): behind = lax.ppermute(behind, axis, step_down)  9.26 us
    ppermute x1, starting transfers between devices, body(): packed_other = lax.ppermute(packed_z, 'core', [(0, 1), (1, 0)])  8.66 us
    all_gather x1, waiting for transfers between devices, body(): whole = lax.all_gather(coarse, ('z', 'core'), axis=0, tiled=True)  7.24 us
    all_gather x1, blocking collectives, body(): both = lax.all_gather(chip_rows, 'core', axis=0, tiled=True)  6.66 us
  transfers between devices with their start and end apart: 18, of which 9 were waited for; matrix products, arithmetic and copies ran while one was open for 2% of the time, Pallas kernels for 4%

profile of v13, /device:TPU:1, one launch (start us, length us, event | category | flops | bytes accessed | tf_op | source)
XLA Modules:
  0.0 150.3 jit_solution(15284335847578894271)
XLA Ops:
  6.5 0.7 copy.15
  7.3 1.0 reshape.31
  8.3 12.0 %collective-permute-start = (bf16[16,4224]{1,0:T(8,128)(2,1)S(1)}, bf16[16,4224]{1,0:T(8,128)(2,1)S(1)}, u32[]{:S(2)}, u32[]{:S(2)}) collective-permute-start(bf16[16,4224]{1,0:T(8,128)(2,1)S(1)} %fusion.1), channel_id=1, source_target_pairs={{0,30},{2,0},{4,2},{6,4},{8,6},{10,8},{12,10},{14,12},{16,14},{18,... | collective-permute-start | bytes 405512 | tf_op jit(solution)/shard_map/ppermute | solution.py:131
  20.2 1.9 %collective-permute-start.8 = (bf16[16,4224]{1,0:T(8,128)(2,1)S(1)}, bf16[16,4224]{1,0:T(8,128)(2,1)S(1)}, u32[]{:S(2)}, u32[]{:S(2)}) collective-permute-start(bf16[16,4224]{1,0:T(8,128)(2,1)S(1)} %fusion.1), channel_id=1, source_target_pairs={{0,2},{2,4},{4,6},{6,8},{8,10},{10,12},{12,14},{14,16},{16,18},{18... | collective-permute-start | bytes 405512 | tf_op jit(solution)/shard_map/ppermute | solution.py:134
  22.2 0.0 all-gather.2.cloned.1.call-update
  22.2 0.0 copy-start.1
  22.2 0.0 copy-start.2
  22.2 0.0 copy-start.3
  22.3 0.2 collective-permute-done
  22.5 5.3 %collective-permute-start.1 = (bf16[16,4224]{1,0:T(8,128)(2,1)S(1)}, bf16[16,4224]{1,0:T(8,128)(2,1)S(1)}, u32[]{:S(2)}, u32[]{:S(2)}) collective-permute-start(bf16[16,4224]{1,0:T(8,128)(2,1)S(1)} %collective-permute-done), channel_id=1, source_target_pairs={{0,30},{2,0},{4,2},{6,4},{8,6},{10,8},{12,10},{14,12},{16,14},{18,... | collective-permute-start | bytes 405512 | tf_op jit(solution)/shard_map/ppermute | solution.py:131
  27.8 0.0 collective-permute-done.8
  27.8 1.9 %collective-permute-start.9 = (bf16[16,4224]{1,0:T(8,128)(2,1)S(1)}, bf16[16,4224]{1,0:T(8,128)(2,1)S(1)}, u32[]{:S(2)}, u32[]{:S(2)}) collective-permute-start(bf16[16,4224]{1,0:T(8,128)(2,1)S(1)} %collective-permute-done.8), channel_id=1, source_target_pairs={{0,2},{2,4},{4,6},{6,8},{8,10},{10,12},{12,14},{14,16},{16,18},{18... | collective-permute-start | bytes 405512 | tf_op jit(solution)/shard_map/ppermute | solution.py:134
  29.7 0.0 collective-permute-done.1
  29.8 5.0 %collective-permute-start.2 = (bf16[16,4224]{1,0:T(8,128)(2,1)S(1)}, bf16[16,4224]{1,0:T(8,128)(2,1)S(1)}, u32[]{:S(2)}, u32[]{:S(2)}) collective-permute-start(bf16[16,4224]{1,0:T(8,128)(2,1)S(1)} %collective-permute-done.1), channel_id=1, source_target_pairs={{0,30},{2,0},{4,2},{6,4},{8,6},{10,8},{12,10},{14,12},{16,14},{18,... | collective-permute-start | bytes 405512 | tf_op jit(solution)/shard_map/ppermute | solution.py:131
  34.8 0.0 collective-permute-done.9
  34.8 1.9 %collective-permute-start.10 = (bf16[16,4224]{1,0:T(8,128)(2,1)S(1)}, bf16[16,4224]{1,0:T(8,128)(2,1)S(1)}, u32[]{:S(2)}, u32[]{:S(2)}) collective-permute-start(bf16[16,4224]{1,0:T(8,128)(2,1)S(1)} %collective-permute-done.9), channel_id=1, source_target_pairs={{0,2},{2,4},{4,6},{6,8},{8,10},{10,12},{12,14},{14,16},{16,18},{18... | collective-permute-start | bytes 405512 | tf_op jit(solution)/shard_map/ppermute | solution.py:134
  36.7 0.8 collective-permute-done.2
  37.5 5.0 %collective-permute-start.3 = (bf16[16,4224]{1,0:T(8,128)(2,1)S(1)}, bf16[16,4224]{1,0:T(8,128)(2,1)S(1)}, u32[]{:S(2)}, u32[]{:S(2)}) collective-permute-start(bf16[16,4224]{1,0:T(8,128)(2,1)S(1)} %collective-permute-done.2), channel_id=1, source_target_pairs={{0,30},{2,0},{4,2},{6,4},{8,6},{10,8},{12,10},{14,12},{16,14},{18,... | collective-permute-start | bytes 405512 | tf_op jit(solution)/shard_map/ppermute | solution.py:131
  42.5 2.4 %collective-permute-done.10 = bf16[16,4224]{1,0:T(8,128)(2,1)S(1)} collective-permute-done((bf16[16,4224]{1,0:T(8,128)(2,1)S(1)}, bf16[16,4224]{1,0:T(8,128)(2,1)S(1)}, u32[]{:S(2)}, u32[]{:S(2)}) %collective-permute-start.10) | collective-permute-done | bytes 135200 | tf_op jit(solution)/shard_map/ppermute | solution.py:134
  44.9 1.9 %collective-permute-start.11 = (bf16[16,4224]{1,0:T(8,128)(2,1)S(1)}, bf16[16,4224]{1,0:T(8,128)(2,1)S(1)}, u32[]{:S(2)}, u32[]{:S(2)}) collective-permute-start(bf16[16,4224]{1,0:T(8,128)(2,1)S(1)} %collective-permute-done.10), channel_id=1, source_target_pairs={{0,2},{2,4},{4,6},{6,8},{8,10},{10,12},{12,14},{14,16},{16,18},{18... | collective-permute-start | bytes 405512 | tf_op jit(solution)/shard_map/ppermute | solution.py:134
  46.8 0.0 collective-permute-done.3
  46.8 4.8 %collective-permute-start.4 = (bf16[16,4224]{1,0:T(8,128)(2,1)S(1)}, bf16[16,4224]{1,0:T(8,128)(2,1)S(1)}, u32[]{:S(2)}, u32[]{:S(2)}) collective-permute-start(bf16[16,4224]{1,0:T(8,128)(2,1)S(1)} %collective-permute-done.3), channel_id=1, source_target_pairs={{0,30},{2,0},{4,2},{6,4},{8,6},{10,8},{12,10},{14,12},{16,14},{18,... | collective-permute-start | bytes 405512 | tf_op jit(solution)/shard_map/ppermute | solution.py:131
  51.7 2.1 %collective-permute-done.11 = bf16[16,4224]{1,0:T(8,128)(2,1)S(1)} collective-permute-done((bf16[16,4224]{1,0:T(8,128)(2,1)S(1)}, bf16[16,4224]{1,0:T(8,128)(2,1)S(1)}, u32[]{:S(2)}, u32[]{:S(2)}) %collective-permute-start.11) | collective-permute-done | bytes 135200 | tf_op jit(solution)/shard_map/ppermute | solution.py:134
  53.8 1.9 %collective-permute-start.12 = (bf16[16,4224]{1,0:T(8,128)(2,1)S(1)}, bf16[16,4224]{1,0:T(8,128)(2,1)S(1)}, u32[]{:S(2)}, u32[]{:S(2)}) collective-permute-start(bf16[16,4224]{1,0:T(8,128)(2,1)S(1)} %collective-permute-done.11), channel_id=1, source_target_pairs={{0,2},{2,4},{4,6},{6,8},{8,10},{10,12},{12,14},{14,16},{16,18},{18... | collective-permute-start | bytes 405512 | tf_op jit(solution)/shard_map/ppermute | solution.py:134
  55.7 0.0 collective-permute-done.4
  55.7 4.6 %collective-permute-start.5 = (bf16[16,4224]{1,0:T(8,128)(2,1)S(1)}, bf16[16,4224]{1,0:T(8,128)(2,1)S(1)}, u32[]{:S(2)}, u32[]{:S(2)}) collective-permute-start(bf16[16,4224]{1,0:T(8,128)(2,1)S(1)} %collective-permute-done.4), channel_id=1, source_target_pairs={{0,30},{2,0},{4,2},{6,4},{8,6},{10,8},{12,10},{14,12},{16,14},{18,... | collective-permute-start | bytes 405512 | tf_op jit(solution)/shard_map/ppermute | solution.py:131
  60.3 2.1 %collective-permute-done.12 = bf16[16,4224]{1,0:T(8,128)(2,1)S(1)} collective-permute-done((bf16[16,4224]{1,0:T(8,128)(2,1)S(1)}, bf16[16,4224]{1,0:T(8,128)(2,1)S(1)}, u32[]{:S(2)}, u32[]{:S(2)}) %collective-permute-start.12) | collective-permute-done | bytes 135200 | tf_op jit(solution)/shard_map/ppermute | solution.py:134
  62.5 1.9 %collective-permute-start.13 = (bf16[16,4224]{1,0:T(8,128)(2,1)S(1)}, bf16[16,4224]{1,0:T(8,128)(2,1)S(1)}, u32[]{:S(2)}, u32[]{:S(2)}) collective-permute-start(bf16[16,4224]{1,0:T(8,128)(2,1)S(1)} %collective-permute-done.12), channel_id=1, source_target_pairs={{0,2},{2,4},{4,6},{6,8},{8,10},{10,12},{12,14},{14,16},{16,18},{18... | collective-permute-start | bytes 405512 | tf_op jit(solution)/shard_map/ppermute | solution.py:134
  64.4 0.0 collective-permute-done.5
  64.4 4.6 %collective-permute-start.6 = (bf16[16,4224]{1,0:T(8,128)(2,1)S(1)}, bf16[16,4224]{1,0:T(8,128)(2,1)S(1)}, u32[]{:S(2)}, u32[]{:S(2)}) collective-permute-start(bf16[16,4224]{1,0:T(8,128)(2,1)S(1)} %collective-permute-done.5), channel_id=1, source_target_pairs={{0,30},{2,0},{4,2},{6,4},{8,6},{10,8},{12,10},{14,12},{16,14},{18,... | collective-permute-start | bytes 405512 | tf_op jit(solution)/shard_map/ppermute | solution.py:131
  69.0 2.6 %collective-permute-done.13 = bf16[16,4224]{1,0:T(8,128)(2,1)S(1)} collective-permute-done((bf16[16,4224]{1,0:T(8,128)(2,1)S(1)}, bf16[16,4224]{1,0:T(8,128)(2,1)S(1)}, u32[]{:S(2)}, u32[]{:S(2)}) %collective-permute-start.13) | collective-permute-done | bytes 135200 | tf_op jit(solution)/shard_map/ppermute | solution.py:134
  71.6 1.9 %collective-permute-start.14 = (bf16[16,4224]{1,0:T(8,128)(2,1)S(1)}, bf16[16,4224]{1,0:T(8,128)(2,1)S(1)}, u32[]{:S(2)}, u32[]{:S(2)}) collective-permute-start(bf16[16,4224]{1,0:T(8,128)(2,1)S(1)} %collective-permute-done.13), channel_id=1, source_target_pairs={{0,2},{2,4},{4,6},{6,8},{8,10},{10,12},{12,14},{14,16},{16,18},{18... | collective-permute-start | bytes 405512 | tf_op jit(solution)/shard_map/ppermute | solution.py:134
  73.5 0.0 collective-permute-done.6
  73.5 4.6 %collective-permute-start.7 = (bf16[16,4224]{1,0:T(8,128)(2,1)S(1)}, bf16[16,4224]{1,0:T(8,128)(2,1)S(1)}, u32[]{:S(2)}, u32[]{:S(2)}) collective-permute-start(bf16[16,4224]{1,0:T(8,128)(2,1)S(1)} %collective-permute-done.6), channel_id=1, source_target_pairs={{0,30},{2,0},{4,2},{6,4},{8,6},{10,8},{12,10},{14,12},{16,14},{18,... | collective-permute-start | bytes 405512 | tf_op jit(solution)/shard_map/ppermute | solution.py:131
  78.1 4.4 %collective-permute-done.7 = bf16[16,4224]{1,0:T(8,128)(2,1)S(1)} collective-permute-done((bf16[16,4224]{1,0:T(8,128)(2,1)S(1)}, bf16[16,4224]{1,0:T(8,128)(2,1)S(1)}, u32[]{:S(2)}, u32[]{:S(2)}) %collective-permute-start.7) | collective-permute-done | bytes 135200 | tf_op jit(solution)/shard_map/ppermute | solution.py:131
  82.5 0.0 collective-permute-done.14
  82.7 8.7 %collective-permute-start.15 = (bf16[16,16,4224]{2,1,0:T(8,128)(2,1)S(1)}, bf16[16,16,4224]{2,1,0:T(8,128)(2,1)}, u32[]{:S(2)}, u32[]{:S(2)}) collective-permute-start(bf16[16,16,4224]{2,1,0:T(8,128)(2,1)S(1)} %bitcast_dynamic-update-slice_fusion.own_ref), channel_id=1, source_target_pairs={{0,1},{1,0},{2,3},{3,2},{4,5},{5,4},{6,7},{7,6},{8,9},{9,8},{10,11... | collective-permute-start | bytes 6488072 | tf_op jit(solution)/shard_map/ppermute | solution.py:151
  91.3 0.7 copy.12.bias_ref
  92.0 0.7 copy.13.gain_ref
  92.7 0.7 copy.14.shift_ref
  93.4 7.2 %all-gather.2.cloned.1.call-done = bf16[64,48,1024]{2,1,0:T(8,128)(2,1)} async-done(((bf16[2,48,1024]{2,1,0:T(8,128)(2,1)}), bf16[64,48,1024]{2,1,0:T(8,128)(2,1)}) %all-gather.2.cloned.1.call-update) | async-done | bytes 6291472 | tf_op jit(solution)/shard_map/all_gather | solution.py:146
  100.6 6.4 %shard_map.73 = bf16[16,32,192]{2,1,0:T(8,128)(2,1)} custom-call(bf16[3072,1024]{1,0:T(8,128)(2,1)} %bitcast.45, bf16[288,1024]{1,0:T(8,128)(2,1)} %bitcast.47, f32[32,1]{1,0:T(8,128)} %copy.12.bias_ref, f32[32,1]{1,0:T(8,128)} %copy.13.gain_ref, f32[32,1]{1,0:T(8,128)} %copy.14.shift_ref), custom_call_target="tpu_custom_call" | custom-call | flops 1811939328 | bytes 7077888 | tf_op jit(solution)/shard_map/pallas_call | solution.py:53
  107.0 9.9 %all-to-all-start = ((bf16[16,32,192]{2,1,0:T(8,128)(2,1)}), bf16[16,32,192]{2,1,0:T(8,128)(2,1)S(1)}, u32[]{:S(2)}, u32[]{:S(2)}) async-start(bf16[16,32,192]{2,1,0:T(8,128)(2,1)} %shard_map.73), calls=%async_computation | async-start | bytes 524288 | tf_op jit(solution)/shard_map/all_to_all | solution.py:154
  116.9 0.6 pad_add_fusion.index_ref
  117.6 13.8 %all-to-all-done = bf16[16,32,192]{2,1,0:T(8,128)(2,1)S(1)} async-done(((bf16[16,32,192]{2,1,0:T(8,128)(2,1)}), bf16[16,32,192]{2,1,0:T(8,128)(2,1)S(1)}, u32[]{:S(2)}, u32[]{:S(2)}) %all-to-all-start) | async-done | bytes 196640 | tf_op jit(solution)/shard_map/all_to_all | solution.py:154
  131.3 6.7 %all_gather.7.act_ref = bf16[1024,192]{1,0:T(8,128)(2,1)} all-gather(bf16[512,192]{1,0:T(8,128)(2,1)S(1)} %bitcast.46), channel_id=1, replica_groups=mesh['grp'=16,'z'=16,'core'=2] {'core'}, dimensions={0}, use_global_device_ids=true | all-gather | bytes 589824 | tf_op jit(solution)/shard_map/all_gather | solution.py:156
  138.0 0.0 collective-permute-done.15.other_ref
  138.0 5.4 %shard_map.74 = bf16[4,96,512]{2,1,0:T(8,128)(2,1)} custom-call(s32[2]{0:T(128)} %pad_add_fusion.index_ref, bf16[1024,192]{1,0:T(8,128)(2,1)} %all_gather.7.act_ref, bf16[16,16,4224]{2,1,0:T(8,128)(2,1)} %copy-done, bf16[16,16,4224]{2,1,0:T(8,128)(2,1)} %collective-permute-done.15.other_ref), custom_call_target="tpu_custom_call" | custom-call | flops 805306368 | bytes 5111808 | tf_op jit(solution)/shard_map/pallas_call | solution.py:112
  (23 shorter events, 0.3 us)
Async XLA Ops:
  6.5 94.1 %all-gather.2.cloned.1.call-start = ((), (), s32[]{:S(2)}) async-start(), calls=%async_computation.1 | async-start | bytes 6488064 | tf_op jit(solution)/shard_map/all_gather | solution.py:146
  8.3 14.2 %collective-permute-start = (bf16[16,4224]{1,0:T(8,128)(2,1)S(1)}, bf16[16,4224]{1,0:T(8,128)(2,1)S(1)}, u32[]{:S(2)}, u32[]{:S(2)}) collective-permute-start(bf16[16,4224]{1,0:T(8,128)(2,1)S(1)} %fusion.1), channel_id=1, source_target_pairs={{0,30},{2,0},{4,2},{6,4},{8,6},{10,8},{12,10},{14,12},{16,14},{18,... | collective-permute-start | bytes 405512 | tf_op jit(solution)/shard_map/ppermute | solution.py:131
  20.2 7.6 %collective-permute-start.8 = (bf16[16,4224]{1,0:T(8,128)(2,1)S(1)}, bf16[16,4224]{1,0:T(8,128)(2,1)S(1)}, u32[]{:S(2)}, u32[]{:S(2)}) collective-permute-start(bf16[16,4224]{1,0:T(8,128)(2,1)S(1)} %fusion.1), channel_id=1, source_target_pairs={{0,2},{2,4},{4,6},{6,8},{8,10},{10,12},{12,14},{14,16},{16,18},{18... | collective-permute-start | bytes 405512 | tf_op jit(solution)/shard_map/ppermute | solution.py:134
  22.2 69.1 %copy-start.1 = (f32[32]{0:T(128)S(1)}, f32[32]{0:T(128)}, u32[]{:S(2)}) copy-start(f32[32]{0:T(128)} %param.9) | copy-start | bytes 388
  22.2 69.8 %copy-start.2 = (f32[32]{0:T(128)S(1)}, f32[32]{0:T(128)}, u32[]{:S(2)}) copy-start(f32[32]{0:T(128)} %param.10) | copy-start | bytes 388
  22.2 70.5 %copy-start.3 = (f32[32]{0:T(128)S(1)}, f32[32]{0:T(128)}, u32[]{:S(2)}) copy-start(f32[32]{0:T(128)} %param.11) | copy-start | bytes 388
  22.5 7.3 %collective-permute-start.1 = (bf16[16,4224]{1,0:T(8,128)(2,1)S(1)}, bf16[16,4224]{1,0:T(8,128)(2,1)S(1)}, u32[]{:S(2)}, u32[]{:S(2)}) collective-permute-start(bf16[16,4224]{1,0:T(8,128)(2,1)S(1)} %collective-permute-done), channel_id=1, source_target_pairs={{0,30},{2,0},{4,2},{6,4},{8,6},{10,8},{12,10},{14,12},{16,14},{18,... | collective-permute-start | bytes 405512 | tf_op jit(solution)/shard_map/ppermute | solution.py:131
  27.8 7.0 %collective-permute-start.9 = (bf16[16,4224]{1,0:T(8,128)(2,1)S(1)}, bf16[16,4224]{1,0:T(8,128)(2,1)S(1)}, u32[]{:S(2)}, u32[]{:S(2)}) collective-permute-start(bf16[16,4224]{1,0:T(8,128)(2,1)S(1)} %collective-permute-done.8), channel_id=1, source_target_pairs={{0,2},{2,4},{4,6},{6,8},{8,10},{10,12},{12,14},{14,16},{16,18},{18... | collective-permute-start | bytes 405512 | tf_op jit(solution)/shard_map/ppermute | solution.py:134
  29.8 7.7 %collective-permute-start.2 = (bf16[16,4224]{1,0:T(8,128)(2,1)S(1)}, bf16[16,4224]{1,0:T(8,128)(2,1)S(1)}, u32[]{:S(2)}, u32[]{:S(2)}) collective-permute-start(bf16[16,4224]{1,0:T(8,128)(2,1)S(1)} %collective-permute-done.1), channel_id=1, source_target_pairs={{0,30},{2,0},{4,2},{6,4},{8,6},{10,8},{12,10},{14,12},{16,14},{18,... | collective-permute-start | bytes 405512 | tf_op jit(solution)/shard_map/ppermute | solution.py:131
  34.8 10.1 %collective-permute-start.10 = (bf16[16,4224]{1,0:T(8,128)(2,1)S(1)}, bf16[16,4224]{1,0:T(8,128)(2,1)S(1)}, u32[]{:S(2)}, u32[]{:S(2)}) collective-permute-start(bf16[16,4224]{1,0:T(8,128)(2,1)S(1)} %collective-permute-done.9), channel_id=1, source_target_pairs={{0,2},{2,4},{4,6},{6,8},{8,10},{10,12},{12,14},{14,16},{16,18},{18... | collective-permute-start | bytes 405512 | tf_op jit(solution)/shard_map/ppermute | solution.py:134
  37.5 9.3 %collective-permute-start.3 = (bf16[16,4224]{1,0:T(8,128)(2,1)S(1)}, bf16[16,4224]{1,0:T(8,128)(2,1)S(1)}, u32[]{:S(2)}, u32[]{:S(2)}) collective-permute-start(bf16[16,4224]{1,0:T(8,128)(2,1)S(1)} %collective-permute-done.2), channel_id=1, source_target_pairs={{0,30},{2,0},{4,2},{6,4},{8,6},{10,8},{12,10},{14,12},{16,14},{18,... | collective-permute-start | bytes 405512 | tf_op jit(solution)/shard_map/ppermute | solution.py:131
  44.9 8.9 %collective-permute-start.11 = (bf16[16,4224]{1,0:T(8,128)(2,1)S(1)}, bf16[16,4224]{1,0:T(8,128)(2,1)S(1)}, u32[]{:S(2)}, u32[]{:S(2)}) collective-permute-start(bf16[16,4224]{1,0:T(8,128)(2,1)S(1)} %collective-permute-done.10), channel_id=1, source_target_pairs={{0,2},{2,4},{4,6},{6,8},{8,10},{10,12},{12,14},{14,16},{16,18},{18... | collective-permute-start | bytes 405512 | tf_op jit(solution)/shard_map/ppermute | solution.py:134
  46.8 8.9 %collective-permute-start.4 = (bf16[16,4224]{1,0:T(8,128)(2,1)S(1)}, bf16[16,4224]{1,0:T(8,128)(2,1)S(1)}, u32[]{:S(2)}, u32[]{:S(2)}) collective-permute-start(bf16[16,4224]{1,0:T(8,128)(2,1)S(1)} %collective-permute-done.3), channel_id=1, source_target_pairs={{0,30},{2,0},{4,2},{6,4},{8,6},{10,8},{12,10},{14,12},{16,14},{18,... | collective-permute-start | bytes 405512 | tf_op jit(solution)/shard_map/ppermute | solution.py:131
  53.8 8.7 %collective-permute-start.12 = (bf16[16,4224]{1,0:T(8,128)(2,1)S(1)}, bf16[16,4224]{1,0:T(8,128)(2,1)S(1)}, u32[]{:S(2)}, u32[]{:S(2)}) collective-permute-start(bf16[16,4224]{1,0:T(8,128)(2,1)S(1)} %collective-permute-done.11), channel_id=1, source_target_pairs={{0,2},{2,4},{4,6},{6,8},{8,10},{10,12},{12,14},{14,16},{16,18},{18... | collective-permute-start | bytes 405512 | tf_op jit(solution)/shard_map/ppermute | solution.py:134
  55.7 8.7 %collective-permute-start.5 = (bf16[16,4224]{1,0:T(8,128)(2,1)S(1)}, bf16[16,4224]{1,0:T(8,128)(2,1)S(1)}, u32[]{:S(2)}, u32[]{:S(2)}) collective-permute-start(bf16[16,4224]{1,0:T(8,128)(2,1)S(1)} %collective-permute-done.4), channel_id=1, source_target_pairs={{0,30},{2,0},{4,2},{6,4},{8,6},{10,8},{12,10},{14,12},{16,14},{18,... | collective-permute-start | bytes 405512 | tf_op jit(solution)/shard_map/ppermute | solution.py:131
  62.5 9.1 %collective-permute-start.13 = (bf16[16,4224]{1,0:T(8,128)(2,1)S(1)}, bf16[16,4224]{1,0:T(8,128)(2,1)S(1)}, u32[]{:S(2)}, u32[]{:S(2)}) collective-permute-start(bf16[16,4224]{1,0:T(8,128)(2,1)S(1)} %collective-permute-done.12), channel_id=1, source_target_pairs={{0,2},{2,4},{4,6},{6,8},{8,10},{10,12},{12,14},{14,16},{16,18},{18... | collective-permute-start | bytes 405512 | tf_op jit(solution)/shard_map/ppermute | solution.py:134
  64.4 9.1 %collective-permute-start.6 = (bf16[16,4224]{1,0:T(8,128)(2,1)S(1)}, bf16[16,4224]{1,0:T(8,128)(2,1)S(1)}, u32[]{:S(2)}, u32[]{:S(2)}) collective-permute-start(bf16[16,4224]{1,0:T(8,128)(2,1)S(1)} %collective-permute-done.5), channel_id=1, source_target_pairs={{0,30},{2,0},{4,2},{6,4},{8,6},{10,8},{12,10},{14,12},{16,14},{18,... | collective-permute-start | bytes 405512 | tf_op jit(solution)/shard_map/ppermute | solution.py:131
  71.6 10.9 %collective-permute-start.14 = (bf16[16,4224]{1,0:T(8,128)(2,1)S(1)}, bf16[16,4224]{1,0:T(8,128)(2,1)S(1)}, u32[]{:S(2)}, u32[]{:S(2)}) collective-permute-start(bf16[16,4224]{1,0:T(8,128)(2,1)S(1)} %collective-permute-done.13), channel_id=1, source_target_pairs={{0,2},{2,4},{4,6},{6,8},{8,10},{10,12},{12,14},{14,16},{16,18},{18... | collective-permute-start | bytes 405512 | tf_op jit(solution)/shard_map/ppermute | solution.py:134
  73.5 9.0 %collective-permute-start.7 = (bf16[16,4224]{1,0:T(8,128)(2,1)S(1)}, bf16[16,4224]{1,0:T(8,128)(2,1)S(1)}, u32[]{:S(2)}, u32[]{:S(2)}) collective-permute-start(bf16[16,4224]{1,0:T(8,128)(2,1)S(1)} %collective-permute-done.6), channel_id=1, source_target_pairs={{0,30},{2,0},{4,2},{6,4},{8,6},{10,8},{12,10},{14,12},{16,14},{18,... | collective-permute-start | bytes 405512 | tf_op jit(solution)/shard_map/ppermute | solution.py:131
  82.6 24.4 %copy-start = (bf16[16,16,4224]{2,1,0:T(8,128)(2,1)}, bf16[16,16,4224]{2,1,0:T(8,128)(2,1)S(1)}, u32[]{:S(2)}) copy-start(bf16[16,16,4224]{2,1,0:T(8,128)(2,1)S(1)} %bitcast_dynamic-update-slice_fusion.own_ref) | copy-start | bytes 6488068
  82.7 55.4 %collective-permute-start.15 = (bf16[16,16,4224]{2,1,0:T(8,128)(2,1)S(1)}, bf16[16,16,4224]{2,1,0:T(8,128)(2,1)}, u32[]{:S(2)}, u32[]{:S(2)}) collective-permute-start(bf16[16,16,4224]{2,1,0:T(8,128)(2,1)S(1)} %bitcast_dynamic-update-slice_fusion.own_ref), channel_id=1, source_target_pairs={{0,1},{1,0},{2,3},{3,2},{4,5},{5,4},{6,7},{7,6},{8,9},{9,8},{10,11... | collective-permute-start | bytes 6488072 | tf_op jit(solution)/shard_map/ppermute | solution.py:151
  107.0 24.3 %all-to-all-start = ((bf16[16,32,192]{2,1,0:T(8,128)(2,1)}), bf16[16,32,192]{2,1,0:T(8,128)(2,1)S(1)}, u32[]{:S(2)}, u32[]{:S(2)}) async-start(bf16[16,32,192]{2,1,0:T(8,128)(2,1)} %shard_map.73), calls=%async_computation | async-start | bytes 524288 | tf_op jit(solution)/shard_map/all_to_all | solution.py:154
Sparse Core Ops, SparseCore 0:
  22.3 78.2 all-gather.1

commit v14 on v13

--- a/solution.py
+++ b/solution.py
@@ -62,10 +62,8 @@
     )(x, w, col(conv_bias), col(norm_gain), col(norm_shift))
 
 
-def up_kernel(index_ref, act_ref, own_ref, other_ref, out_ref, wnat_ref, actn_ref, *, width_cols):
-    chips, slab, packed_width = own_ref.shape
-    channels, positions = act_ref.shape
-    block = channels // (2 * chips)
+def assemble_kernel(index_ref, own_ref, other_ref, wnat_ref):
+    chips, slab, _ = own_ref.shape
     core = index_ref[0]
     here = index_ref[1]
     for m in range(chips):
@@ -74,11 +72,31 @@
         theirs = pl.multiple_of(2 * slab * chip + slab * (1 - core), slab)
         wnat_ref[pl.ds(mine, slab), :] = own_ref[m]
         wnat_ref[pl.ds(theirs, slab), :] = other_ref[m]
+
+
+def assemble(index, own, other):
+    chips, slab, packed_width = own.shape
+    vmem = pl.BlockSpec(memory_space=pltpu.VMEM)
+    smem = pl.BlockSpec(memory_space=pltpu.SMEM)
+    return pl.pallas_call(
+        assemble_kernel,
+        out_shape=jax.ShapeDtypeStruct((2 * chips * slab, packed_width), own.dtype),
+        in_specs=[smem, vmem, vmem],
+        out_specs=vmem,
+        cost_estimate=pl.CostEstimate(flops=0, transcendentals=0, bytes_accessed=4 * own.size * 2),
+    )(index, own, other)
+
+
+def up_kernel(index_ref, act_ref, wnat_ref, out_ref, actn_ref, *, width_cols):
+    outs, packed_width = wnat_ref.shape
+    channels, positions = act_ref.shape
+    chips = outs // 32
+    block = channels // (2 * chips)
+    core = index_ref[0]
     for c in range(2):
         for z in range(chips):
             actn_ref[pl.ds((2 * z + c) * block, block), :] = act_ref[pl.ds((c * chips + z) * block, block), :]
     rows = out_ref.shape[0] // 2
-    outs = wnat_ref.shape[0]
     nn = (((1,), (0,)), ((), ()))
     sub = lax.broadcasted_iota(jnp.int32, (packed_width - 4 * channels, positions), 0)
     ones = jnp.where(sub == 0, 1.0, 0.0).astype(actn_ref.dtype)
@@ -101,24 +119,22 @@
             out_ref[2 * i + a] = jnp.dot(interleave, stacked, preferred_element_type=jnp.float32).astype(out_ref.dtype)
 
 
-def up_conv(core, here, act, own, other, rows):
+def up_conv(index, act, wnat, rows):
     channels, positions = act.shape
     width_cols = positions // (2 * rows)
-    chips, slab, packed_width = own.shape
-    outs = 2 * chips * slab
+    outs, packed_width = wnat.shape
     vmem = pl.BlockSpec(memory_space=pltpu.VMEM)
     smem = pl.BlockSpec(memory_space=pltpu.SMEM)
-    index = jnp.stack([core, here]).astype(jnp.int32)
     return pl.pallas_call(
         functools.partial(up_kernel, width_cols=width_cols),
         out_shape=jax.ShapeDtypeStruct((2 * rows, 2 * width_cols, outs), jnp.bfloat16),
-        in_specs=[smem, vmem, vmem, vmem],
+        in_specs=[smem, vmem, vmem],
         out_specs=vmem,
-        scratch_shapes=[pltpu.VMEM((outs, packed_width), jnp.bfloat16), pltpu.VMEM((channels, positions), act.dtype)],
+        scratch_shapes=[pltpu.VMEM((channels, positions), act.dtype)],
         cost_estimate=pl.CostEstimate(
             flops=2 * positions * channels * 4 * outs, transcendentals=0,
-            bytes_accessed=act.size * 2 + 2 * own.size * 2 + rows * width_cols * 4 * outs * 2),
-    )(index, act, own, other)
+            bytes_accessed=act.size * 2 + wnat.size * 2 + rows * width_cols * 4 * outs * 2),
+    )(index, act, wnat)
 
 
 def ring_gather(block, axis):
@@ -149,13 +165,15 @@
     packed = jnp.concatenate([flat, jnp.pad(up_bias[:, None], ((0, 0), (0, 127)))], axis=1)
     packed_z = ring_gather(packed, "z")
     packed_other = lax.ppermute(packed_z, "core", [(0, 1), (1, 0)])
+    index = jnp.stack([core, lax.axis_index("z")]).astype(jnp.int32)
+    wnat = assemble(index, packed_z, packed_other)
 
     activated = conv_norm(whole, conv_weight, conv_bias, norm_gain, norm_shift, chips)
     chip_rows = lax.all_to_all(activated, "z", split_axis=0, concat_axis=0, tiled=True)
     chip_rows = chip_rows.reshape(-1, chip_rows.shape[2])
     both = lax.all_gather(chip_rows, "core", axis=0, tiled=True)
     half = coarse.shape[0]
-    fine = up_conv(core, lax.axis_index("z"), both, packed_z, packed_other, half)
+    fine = up_conv(index, both, wnat, half)
     return fine.reshape(2 * half, 2 * width_cols, -1)
 
 

time: 151 us -> 151 us (level)
  waiting for transfers between devices: 35.7 us -> 29.3 us
  Pallas kernels: 11.8 us -> 16 us
  starting transfers between devices: 77.7 us -> 79.4 us
    all_to_all x1, waiting for transfers between devices: 13.8 us -> 9.21 us  [body(): lax.all_to_all(activated, 'z', split_axis=0, concat_axis=0, tiled=True)]
    pallas_call x0 -> x1, Pallas kernels: none -> 4.57 us  [assemble(): pl.pallas_call(assemble_kernel, out_shape=jax.ShapeDtypeStruct((2 * chips...]
    all_gather x1, waiting for transfers between devices: 7.24 us -> 5.18 us  [body(): whole = lax.all_gather(coarse, ('z', 'core'), axis=0, tiled=True)]
    ppermute x1, starting transfers between devices: 8.66 us -> 10.5 us  [body(): packed_other = lax.ppermute(packed_z, 'core', [(0, 1), (1, 0)])]
  transfers between devices with their start and end apart: 18 -> 18, of which waited for: 9 -> 9; matrix products, arithmetic and copies ran while one was open for 2% -> 2% of each run, Pallas kernels for 4% -> 7%
where the time goes in v14:
time: 151 us; the launch traced here: 150 us
  starting transfers between devices  79.4 us (53%)
  waiting for transfers between devices  29.3 us (19%)
  Pallas kernels  16 us (11%)
  between operations  13.7 us (9%)
  blocking collectives  6.66 us (4%)
  local copies, waits for them, and re-layouts  4.07 us (3%)
    ppermute x8, starting transfers between devices, ring_gather(): ahead = lax.ppermute(ahead, axis, step_up)  45.9 us
    ppermute x7, starting transfers between devices, ring_gather(): behind = lax.ppermute(behind, axis, step_down)  13.4 us
    ppermute x1, starting transfers between devices, body(): packed_other = lax.ppermute(packed_z, 'core', [(0, 1), (1, 0)])  10.5 us
    all_to_all x1, starting transfers between devices, body(): lax.all_to_all(activated, 'z', split_axis=0, concat_axis=0, tiled=True)  9.74 us
    all_to_all x1, waiting for transfers between devices, body(): lax.all_to_all(activated, 'z', split_axis=0, concat_axis=0, tiled=True)  9.21 us
    ppermute x7, waiting for transfers between devices, ring_gather(): behind = lax.ppermute(behind, axis, step_down)  8.94 us
    all_gather x1, blocking collectives, body(): both = lax.all_gather(chip_rows, 'core', axis=0, tiled=True)  6.66 us
    pallas_call x1, Pallas kernels, conv_norm(): pl.pallas_call(functools.partial(conv_norm_kernel, height=height, width_c...  6.4 us
  transfers between devices with their start and end apart: 18, of which 9 were waited for; matrix products, arithmetic and copies ran while one was open for 2% of the time, Pallas kernels for 7%

profile of v14, /device:TPU:1, one launch (start us, length us, event | category | flops | bytes accessed | tf_op | source)
XLA Modules:
  0.0 149.8 jit_solution(8544194692194403814)
XLA Ops:
  6.5 0.7 copy.15
  7.3 1.0 reshape.31
  8.3 12.0 %collective-permute-start = (bf16[16,4224]{1,0:T(8,128)(2,1)S(1)}, bf16[16,4224]{1,0:T(8,128)(2,1)S(1)}, u32[]{:S(2)}, u32[]{:S(2)}) collective-permute-start(bf16[16,4224]{1,0:T(8,128)(2,1)S(1)} %fusion.1), channel_id=1, source_target_pairs={{0,30},{2,0},{4,2},{6,4},{8,6},{10,8},{12,10},{14,12},{16,14},{18,... | collective-permute-start | bytes 405512 | tf_op jit(solution)/shard_map/ppermute | solution.py:147
  20.2 1.9 %collective-permute-start.8 = (bf16[16,4224]{1,0:T(8,128)(2,1)S(1)}, bf16[16,4224]{1,0:T(8,128)(2,1)S(1)}, u32[]{:S(2)}, u32[]{:S(2)}) collective-permute-start(bf16[16,4224]{1,0:T(8,128)(2,1)S(1)} %fusion.1), channel_id=1, source_target_pairs={{0,2},{2,4},{4,6},{6,8},{8,10},{10,12},{12,14},{14,16},{16,18},{18... | collective-permute-start | bytes 405512 | tf_op jit(solution)/shard_map/ppermute | solution.py:150
  22.2 0.0 all-gather.2.cloned.1.call-update
  22.2 0.0 copy-start.1
  22.2 0.0 copy-start.2
  22.2 0.0 copy-start.3
  22.3 0.2 collective-permute-done
  22.5 5.3 %collective-permute-start.1 = (bf16[16,4224]{1,0:T(8,128)(2,1)S(1)}, bf16[16,4224]{1,0:T(8,128)(2,1)S(1)}, u32[]{:S(2)}, u32[]{:S(2)}) collective-permute-start(bf16[16,4224]{1,0:T(8,128)(2,1)S(1)} %collective-permute-done), channel_id=1, source_target_pairs={{0,30},{2,0},{4,2},{6,4},{8,6},{10,8},{12,10},{14,12},{16,14},{18,... | collective-permute-start | bytes 405512 | tf_op jit(solution)/shard_map/ppermute | solution.py:147
  27.8 0.0 collective-permute-done.8
  27.8 1.9 %collective-permute-start.9 = (bf16[16,4224]{1,0:T(8,128)(2,1)S(1)}, bf16[16,4224]{1,0:T(8,128)(2,1)S(1)}, u32[]{:S(2)}, u32[]{:S(2)}) collective-permute-start(bf16[16,4224]{1,0:T(8,128)(2,1)S(1)} %collective-permute-done.8), channel_id=1, source_target_pairs={{0,2},{2,4},{4,6},{6,8},{8,10},{10,12},{12,14},{14,16},{16,18},{18... | collective-permute-start | bytes 405512 | tf_op jit(solution)/shard_map/ppermute | solution.py:150
  29.7 0.0 collective-permute-done.1
  29.8 5.0 %collective-permute-start.2 = (bf16[16,4224]{1,0:T(8,128)(2,1)S(1)}, bf16[16,4224]{1,0:T(8,128)(2,1)S(1)}, u32[]{:S(2)}, u32[]{:S(2)}) collective-permute-start(bf16[16,4224]{1,0:T(8,128)(2,1)S(1)} %collective-permute-done.1), channel_id=1, source_target_pairs={{0,30},{2,0},{4,2},{6,4},{8,6},{10,8},{12,10},{14,12},{16,14},{18,... | collective-permute-start | bytes 405512 | tf_op jit(solution)/shard_map/ppermute | solution.py:147
  34.7 0.0 collective-permute-done.9
  34.8 1.9 %collective-permute-start.10 = (bf16[16,4224]{1,0:T(8,128)(2,1)S(1)}, bf16[16,4224]{1,0:T(8,128)(2,1)S(1)}, u32[]{:S(2)}, u32[]{:S(2)}) collective-permute-start(bf16[16,4224]{1,0:T(8,128)(2,1)S(1)} %collective-permute-done.9), channel_id=1, source_target_pairs={{0,2},{2,4},{4,6},{6,8},{8,10},{10,12},{12,14},{14,16},{16,18},{18... | collective-permute-start | bytes 405512 | tf_op jit(solution)/shard_map/ppermute | solution.py:150
  36.7 0.8 collective-permute-done.2
  37.5 5.0 %collective-permute-start.3 = (bf16[16,4224]{1,0:T(8,128)(2,1)S(1)}, bf16[16,4224]{1,0:T(8,128)(2,1)S(1)}, u32[]{:S(2)}, u32[]{:S(2)}) collective-permute-start(bf16[16,4224]{1,0:T(8,128)(2,1)S(1)} %collective-permute-done.2), channel_id=1, source_target_pairs={{0,30},{2,0},{4,2},{6,4},{8,6},{10,8},{12,10},{14,12},{16,14},{18,... | collective-permute-start | bytes 405512 | tf_op jit(solution)/shard_map/ppermute | solution.py:147
  42.5 2.3 %collective-permute-done.10 = bf16[16,4224]{1,0:T(8,128)(2,1)S(1)} collective-permute-done((bf16[16,4224]{1,0:T(8,128)(2,1)S(1)}, bf16[16,4224]{1,0:T(8,128)(2,1)S(1)}, u32[]{:S(2)}, u32[]{:S(2)}) %collective-permute-start.10) | collective-permute-done | bytes 135200 | tf_op jit(solution)/shard_map/ppermute | solution.py:150
  44.8 1.9 %collective-permute-start.11 = (bf16[16,4224]{1,0:T(8,128)(2,1)S(1)}, bf16[16,4224]{1,0:T(8,128)(2,1)S(1)}, u32[]{:S(2)}, u32[]{:S(2)}) collective-permute-start(bf16[16,4224]{1,0:T(8,128)(2,1)S(1)} %collective-permute-done.10), channel_id=1, source_target_pairs={{0,2},{2,4},{4,6},{6,8},{8,10},{10,12},{12,14},{14,16},{16,18},{18... | collective-permute-start | bytes 405512 | tf_op jit(solution)/shard_map/ppermute | solution.py:150
  46.8 0.0 collective-permute-done.3
  46.8 4.9 %collective-permute-start.4 = (bf16[16,4224]{1,0:T(8,128)(2,1)S(1)}, bf16[16,4224]{1,0:T(8,128)(2,1)S(1)}, u32[]{:S(2)}, u32[]{:S(2)}) collective-permute-start(bf16[16,4224]{1,0:T(8,128)(2,1)S(1)} %collective-permute-done.3), channel_id=1, source_target_pairs={{0,30},{2,0},{4,2},{6,4},{8,6},{10,8},{12,10},{14,12},{16,14},{18,... | collective-permute-start | bytes 405512 | tf_op jit(solution)/shard_map/ppermute | solution.py:147
  51.7 2.3 %collective-permute-done.11 = bf16[16,4224]{1,0:T(8,128)(2,1)S(1)} collective-permute-done((bf16[16,4224]{1,0:T(8,128)(2,1)S(1)}, bf16[16,4224]{1,0:T(8,128)(2,1)S(1)}, u32[]{:S(2)}, u32[]{:S(2)}) %collective-permute-start.11) | collective-permute-done | bytes 135200 | tf_op jit(solution)/shard_map/ppermute | solution.py:150
  54.0 1.9 %collective-permute-start.12 = (bf16[16,4224]{1,0:T(8,128)(2,1)S(1)}, bf16[16,4224]{1,0:T(8,128)(2,1)S(1)}, u32[]{:S(2)}, u32[]{:S(2)}) collective-permute-start(bf16[16,4224]{1,0:T(8,128)(2,1)S(1)} %collective-permute-done.11), channel_id=1, source_target_pairs={{0,2},{2,4},{4,6},{6,8},{8,10},{10,12},{12,14},{14,16},{16,18},{18... | collective-permute-start | bytes 405512 | tf_op jit(solution)/shard_map/ppermute | solution.py:150
  55.9 0.0 collective-permute-done.4
  55.9 4.6 %collective-permute-start.5 = (bf16[16,4224]{1,0:T(8,128)(2,1)S(1)}, bf16[16,4224]{1,0:T(8,128)(2,1)S(1)}, u32[]{:S(2)}, u32[]{:S(2)}) collective-permute-start(bf16[16,4224]{1,0:T(8,128)(2,1)S(1)} %collective-permute-done.4), channel_id=1, source_target_pairs={{0,30},{2,0},{4,2},{6,4},{8,6},{10,8},{12,10},{14,12},{16,14},{18,... | collective-permute-start | bytes 405512 | tf_op jit(solution)/shard_map/ppermute | solution.py:147
  60.5 2.0 %collective-permute-done.12 = bf16[16,4224]{1,0:T(8,128)(2,1)S(1)} collective-permute-done((bf16[16,4224]{1,0:T(8,128)(2,1)S(1)}, bf16[16,4224]{1,0:T(8,128)(2,1)S(1)}, u32[]{:S(2)}, u32[]{:S(2)}) %collective-permute-start.12) | collective-permute-done | bytes 135200 | tf_op jit(solution)/shard_map/ppermute | solution.py:150
  62.5 1.9 %collective-permute-start.13 = (bf16[16,4224]{1,0:T(8,128)(2,1)S(1)}, bf16[16,4224]{1,0:T(8,128)(2,1)S(1)}, u32[]{:S(2)}, u32[]{:S(2)}) collective-permute-start(bf16[16,4224]{1,0:T(8,128)(2,1)S(1)} %collective-permute-done.12), channel_id=1, source_target_pairs={{0,2},{2,4},{4,6},{6,8},{8,10},{10,12},{12,14},{14,16},{16,18},{18... | collective-permute-start | bytes 405512 | tf_op jit(solution)/shard_map/ppermute | solution.py:150
  64.5 0.0 collective-permute-done.5
  64.5 4.6 %collective-permute-start.6 = (bf16[16,4224]{1,0:T(8,128)(2,1)S(1)}, bf16[16,4224]{1,0:T(8,128)(2,1)S(1)}, u32[]{:S(2)}, u32[]{:S(2)}) collective-permute-start(bf16[16,4224]{1,0:T(8,128)(2,1)S(1)} %collective-permute-done.5), channel_id=1, source_target_pairs={{0,30},{2,0},{4,2},{6,4},{8,6},{10,8},{12,10},{14,12},{16,14},{18,... | collective-permute-start | bytes 405512 | tf_op jit(solution)/shard_map/ppermute | solution.py:147
  69.1 2.3 %collective-permute-done.13 = bf16[16,4224]{1,0:T(8,128)(2,1)S(1)} collective-permute-done((bf16[16,4224]{1,0:T(8,128)(2,1)S(1)}, bf16[16,4224]{1,0:T(8,128)(2,1)S(1)}, u32[]{:S(2)}, u32[]{:S(2)}) %collective-permute-start.13) | collective-permute-done | bytes 135200 | tf_op jit(solution)/shard_map/ppermute | solution.py:150
  71.3 1.9 %collective-permute-start.14 = (bf16[16,4224]{1,0:T(8,128)(2,1)S(1)}, bf16[16,4224]{1,0:T(8,128)(2,1)S(1)}, u32[]{:S(2)}, u32[]{:S(2)}) collective-permute-start(bf16[16,4224]{1,0:T(8,128)(2,1)S(1)} %collective-permute-done.13), channel_id=1, source_target_pairs={{0,2},{2,4},{4,6},{6,8},{8,10},{10,12},{12,14},{14,16},{16,18},{18... | collective-permute-start | bytes 405512 | tf_op jit(solution)/shard_map/ppermute | solution.py:150
  73.3 4.6 %collective-permute-start.7 = (bf16[16,4224]{1,0:T(8,128)(2,1)S(1)}, bf16[16,4224]{1,0:T(8,128)(2,1)S(1)}, u32[]{:S(2)}, u32[]{:S(2)}) collective-permute-start(bf16[16,4224]{1,0:T(8,128)(2,1)S(1)} %collective-permute-done.6), channel_id=1, source_target_pairs={{0,30},{2,0},{4,2},{6,4},{8,6},{10,8},{12,10},{14,12},{16,14},{18,... | collective-permute-start | bytes 405512 | tf_op jit(solution)/shard_map/ppermute | solution.py:147
  77.9 4.9 %collective-permute-done.7 = bf16[16,4224]{1,0:T(8,128)(2,1)S(1)} collective-permute-done((bf16[16,4224]{1,0:T(8,128)(2,1)S(1)}, bf16[16,4224]{1,0:T(8,128)(2,1)S(1)}, u32[]{:S(2)}, u32[]{:S(2)}) %collective-permute-start.7) | collective-permute-done | bytes 135200 | tf_op jit(solution)/shard_map/ppermute | solution.py:147
  82.8 0.0 collective-permute-done.14
  83.0 10.5 %collective-permute-start.15 = (bf16[16,16,4224]{2,1,0:T(8,128)(2,1)S(1)}, bf16[16,16,4224]{2,1,0:T(8,128)(2,1)}, u32[]{:S(2)}, u32[]{:S(2)}) collective-permute-start(bf16[16,16,4224]{2,1,0:T(8,128)(2,1)S(1)} %bitcast_dynamic-update-slice_fusion.own_ref), channel_id=1, source_target_pairs={{0,1},{1,0},{2,3},{3,2},{4,5},{5,4},{6,7},{7,6},{8,9},{9,8},{10,11... | collective-permute-start | bytes 6488072 | tf_op jit(solution)/shard_map/ppermute | solution.py:167
  93.4 0.7 copy.12.bias_ref
  94.1 0.7 copy.13.gain_ref
  94.8 0.7 copy.14.shift_ref
  95.5 5.2 %all-gather.2.cloned.1.call-done = bf16[64,48,1024]{2,1,0:T(8,128)(2,1)} async-done(((bf16[2,48,1024]{2,1,0:T(8,128)(2,1)}), bf16[64,48,1024]{2,1,0:T(8,128)(2,1)}) %all-gather.2.cloned.1.call-update) | async-done | bytes 6291472 | tf_op jit(solution)/shard_map/all_gather | solution.py:162
  100.7 6.4 %shard_map.73 = bf16[16,32,192]{2,1,0:T(8,128)(2,1)} custom-call(bf16[3072,1024]{1,0:T(8,128)(2,1)} %bitcast.45, bf16[288,1024]{1,0:T(8,128)(2,1)} %bitcast.47, f32[32,1]{1,0:T(8,128)} %copy.12.bias_ref, f32[32,1]{1,0:T(8,128)} %copy.13.gain_ref, f32[32,1]{1,0:T(8,128)} %copy.14.shift_ref), custom_call_target="tpu_custom_call" | custom-call | flops 1811939328 | bytes 7077888 | tf_op jit(solution)/shard_map/pallas_call | solution.py:53
  107.1 9.7 %all-to-all-start = ((bf16[16,32,192]{2,1,0:T(8,128)(2,1)}), bf16[16,32,192]{2,1,0:T(8,128)(2,1)S(1)}, u32[]{:S(2)}, u32[]{:S(2)}) async-start(bf16[16,32,192]{2,1,0:T(8,128)(2,1)} %shard_map.73), calls=%async_computation | async-start | bytes 524288 | tf_op jit(solution)/shard_map/all_to_all | solution.py:172
  116.8 0.7 pad_add_fusion.index_ref
  117.5 0.0 collective-permute-done.15.other_ref
  117.5 4.6 %shard_map.74.wnat_ref = bf16[512,4224]{1,0:T(8,128)(2,1)} custom-call(s32[2]{0:T(128)} %pad_add_fusion.index_ref, bf16[16,16,4224]{2,1,0:T(8,128)(2,1)} %copy-done, bf16[16,16,4224]{2,1,0:T(8,128)(2,1)} %collective-permute-done.15.other_ref), custom_call_target="tpu_custom_call" | custom-call | bytes 8650752 | tf_op jit(solution)/shard_map/pallas_call | solution.py:81
  122.1 9.2 %all-to-all-done = bf16[16,32,192]{2,1,0:T(8,128)(2,1)S(1)} async-done(((bf16[16,32,192]{2,1,0:T(8,128)(2,1)}), bf16[16,32,192]{2,1,0:T(8,128)(2,1)S(1)}, u32[]{:S(2)}, u32[]{:S(2)}) %all-to-all-start) | async-done | bytes 196640 | tf_op jit(solution)/shard_map/all_to_all | solution.py:172
  131.3 6.7 %all_gather.7.act_ref = bf16[1024,192]{1,0:T(8,128)(2,1)} all-gather(bf16[512,192]{1,0:T(8,128)(2,1)S(1)} %bitcast.46), channel_id=1, replica_groups=mesh['grp'=16,'z'=16,'core'=2] {'core'}, dimensions={0}, use_global_device_ids=true | all-gather | bytes 589824 | tf_op jit(solution)/shard_map/all_gather | solution.py:174
  137.9 5.1 %shard_map.75 = bf16[4,96,512]{2,1,0:T(8,128)(2,1)} custom-call(s32[2]{0:T(128)} %pad_add_fusion.index_ref, bf16[1024,192]{1,0:T(8,128)(2,1)} %all_gather.7.act_ref, bf16[512,4224]{1,0:T(8,128)(2,1)} %shard_map.74.wnat_ref), custom_call_target="tpu_custom_call" | custom-call | flops 805306368 | bytes 5111808 | tf_op jit(solution)/shard_map/pallas_call | solution.py:128
  (24 shorter events, 0.3 us)
Async XLA Ops:
  6.5 94.1 %all-gather.2.cloned.1.call-start = ((), (), s32[]{:S(2)}) async-start(), calls=%async_computation.1 | async-start | bytes 6488064 | tf_op jit(solution)/shard_map/all_gather | solution.py:162
  8.3 14.2 %collective-permute-start = (bf16[16,4224]{1,0:T(8,128)(2,1)S(1)}, bf16[16,4224]{1,0:T(8,128)(2,1)S(1)}, u32[]{:S(2)}, u32[]{:S(2)}) collective-permute-start(bf16[16,4224]{1,0:T(8,128)(2,1)S(1)} %fusion.1), channel_id=1, source_target_pairs={{0,30},{2,0},{4,2},{6,4},{8,6},{10,8},{12,10},{14,12},{16,14},{18,... | collective-permute-start | bytes 405512 | tf_op jit(solution)/shard_map/ppermute | solution.py:147
  20.2 7.5 %collective-permute-start.8 = (bf16[16,4224]{1,0:T(8,128)(2,1)S(1)}, bf16[16,4224]{1,0:T(8,128)(2,1)S(1)}, u32[]{:S(2)}, u32[]{:S(2)}) collective-permute-start(bf16[16,4224]{1,0:T(8,128)(2,1)S(1)} %fusion.1), channel_id=1, source_target_pairs={{0,2},{2,4},{4,6},{6,8},{8,10},{10,12},{12,14},{14,16},{16,18},{18... | collective-permute-start | bytes 405512 | tf_op jit(solution)/shard_map/ppermute | solution.py:150
  22.2 71.2 %copy-start.1 = (f32[32]{0:T(128)S(1)}, f32[32]{0:T(128)}, u32[]{:S(2)}) copy-start(f32[32]{0:T(128)} %param.9) | copy-start | bytes 388
  22.2 71.9 %copy-start.2 = (f32[32]{0:T(128)S(1)}, f32[32]{0:T(128)}, u32[]{:S(2)}) copy-start(f32[32]{0:T(128)} %param.10) | copy-start | bytes 388
  22.2 72.6 %copy-start.3 = (f32[32]{0:T(128)S(1)}, f32[32]{0:T(128)}, u32[]{:S(2)}) copy-start(f32[32]{0:T(128)} %param.11) | copy-start | bytes 388
  22.5 7.3 %collective-permute-start.1 = (bf16[16,4224]{1,0:T(8,128)(2,1)S(1)}, bf16[16,4224]{1,0:T(8,128)(2,1)S(1)}, u32[]{:S(2)}, u32[]{:S(2)}) collective-permute-start(bf16[16,4224]{1,0:T(8,128)(2,1)S(1)} %collective-permute-done), channel_id=1, source_target_pairs={{0,30},{2,0},{4,2},{6,4},{8,6},{10,8},{12,10},{14,12},{16,14},{18,... | collective-permute-start | bytes 405512 | tf_op jit(solution)/shard_map/ppermute | solution.py:147
  27.8 7.0 %collective-permute-start.9 = (bf16[16,4224]{1,0:T(8,128)(2,1)S(1)}, bf16[16,4224]{1,0:T(8,128)(2,1)S(1)}, u32[]{:S(2)}, u32[]{:S(2)}) collective-permute-start(bf16[16,4224]{1,0:T(8,128)(2,1)S(1)} %collective-permute-done.8), channel_id=1, source_target_pairs={{0,2},{2,4},{4,6},{6,8},{8,10},{10,12},{12,14},{14,16},{16,18},{18... | collective-permute-start | bytes 405512 | tf_op jit(solution)/shard_map/ppermute | solution.py:150
  29.8 7.7 %collective-permute-start.2 = (bf16[16,4224]{1,0:T(8,128)(2,1)S(1)}, bf16[16,4224]{1,0:T(8,128)(2,1)S(1)}, u32[]{:S(2)}, u32[]{:S(2)}) collective-permute-start(bf16[16,4224]{1,0:T(8,128)(2,1)S(1)} %collective-permute-done.1), channel_id=1, source_target_pairs={{0,30},{2,0},{4,2},{6,4},{8,6},{10,8},{12,10},{14,12},{16,14},{18,... | collective-permute-start | bytes 405512 | tf_op jit(solution)/shard_map/ppermute | solution.py:147
  34.8 10.1 %collective-permute-start.10 = (bf16[16,4224]{1,0:T(8,128)(2,1)S(1)}, bf16[16,4224]{1,0:T(8,128)(2,1)S(1)}, u32[]{:S(2)}, u32[]{:S(2)}) collective-permute-start(bf16[16,4224]{1,0:T(8,128)(2,1)S(1)} %collective-permute-done.9), channel_id=1, source_target_pairs={{0,2},{2,4},{4,6},{6,8},{8,10},{10,12},{12,14},{14,16},{16,18},{18... | collective-permute-start | bytes 405512 | tf_op jit(solution)/shard_map/ppermute | solution.py:150
  37.5 9.3 %collective-permute-start.3 = (bf16[16,4224]{1,0:T(8,128)(2,1)S(1)}, bf16[16,4224]{1,0:T(8,128)(2,1)S(1)}, u32[]{:S(2)}, u32[]{:S(2)}) collective-permute-start(bf16[16,4224]{1,0:T(8,128)(2,1)S(1)} %collective-permute-done.2), channel_id=1, source_target_pairs={{0,30},{2,0},{4,2},{6,4},{8,6},{10,8},{12,10},{14,12},{16,14},{18,... | collective-permute-start | bytes 405512 | tf_op jit(solution)/shard_map/ppermute | solution.py:147
  44.8 9.2 %collective-permute-start.11 = (bf16[16,4224]{1,0:T(8,128)(2,1)S(1)}, bf16[16,4224]{1,0:T(8,128)(2,1)S(1)}, u32[]{:S(2)}, u32[]{:S(2)}) collective-permute-start(bf16[16,4224]{1,0:T(8,128)(2,1)S(1)} %collective-permute-done.10), channel_id=1, source_target_pairs={{0,2},{2,4},{4,6},{6,8},{8,10},{10,12},{12,14},{14,16},{16,18},{18... | collective-permute-start | bytes 405512 | tf_op jit(solution)/shard_map/ppermute | solution.py:150
  46.8 9.1 %collective-permute-start.4 = (bf16[16,4224]{1,0:T(8,128)(2,1)S(1)}, bf16[16,4224]{1,0:T(8,128)(2,1)S(1)}, u32[]{:S(2)}, u32[]{:S(2)}) collective-permute-start(bf16[16,4224]{1,0:T(8,128)(2,1)S(1)} %collective-permute-done.3), channel_id=1, source_target_pairs={{0,30},{2,0},{4,2},{6,4},{8,6},{10,8},{12,10},{14,12},{16,14},{18,... | collective-permute-start | bytes 405512 | tf_op jit(solution)/shard_map/ppermute | solution.py:147
  54.0 8.5 %collective-permute-start.12 = (bf16[16,4224]{1,0:T(8,128)(2,1)S(1)}, bf16[16,4224]{1,0:T(8,128)(2,1)S(1)}, u32[]{:S(2)}, u32[]{:S(2)}) collective-permute-start(bf16[16,4224]{1,0:T(8,128)(2,1)S(1)} %collective-permute-done.11), channel_id=1, source_target_pairs={{0,2},{2,4},{4,6},{6,8},{8,10},{10,12},{12,14},{14,16},{16,18},{18... | collective-permute-start | bytes 405512 | tf_op jit(solution)/shard_map/ppermute | solution.py:150
  55.9 8.5 %collective-permute-start.5 = (bf16[16,4224]{1,0:T(8,128)(2,1)S(1)}, bf16[16,4224]{1,0:T(8,128)(2,1)S(1)}, u32[]{:S(2)}, u32[]{:S(2)}) collective-permute-start(bf16[16,4224]{1,0:T(8,128)(2,1)S(1)} %collective-permute-done.4), channel_id=1, source_target_pairs={{0,30},{2,0},{4,2},{6,4},{8,6},{10,8},{12,10},{14,12},{16,14},{18,... | collective-permute-start | bytes 405512 | tf_op jit(solution)/shard_map/ppermute | solution.py:147
  62.5 8.8 %collective-permute-start.13 = (bf16[16,4224]{1,0:T(8,128)(2,1)S(1)}, bf16[16,4224]{1,0:T(8,128)(2,1)S(1)}, u32[]{:S(2)}, u32[]{:S(2)}) collective-permute-start(bf16[16,4224]{1,0:T(8,128)(2,1)S(1)} %collective-permute-done.12), channel_id=1, source_target_pairs={{0,2},{2,4},{4,6},{6,8},{8,10},{10,12},{12,14},{14,16},{16,18},{18... | collective-permute-start | bytes 405512 | tf_op jit(solution)/shard_map/ppermute | solution.py:150
  64.5 8.8 %collective-permute-start.6 = (bf16[16,4224]{1,0:T(8,128)(2,1)S(1)}, bf16[16,4224]{1,0:T(8,128)(2,1)S(1)}, u32[]{:S(2)}, u32[]{:S(2)}) collective-permute-start(bf16[16,4224]{1,0:T(8,128)(2,1)S(1)} %collective-permute-done.5), channel_id=1, source_target_pairs={{0,30},{2,0},{4,2},{6,4},{8,6},{10,8},{12,10},{14,12},{16,14},{18,... | collective-permute-start | bytes 405512 | tf_op jit(solution)/shard_map/ppermute | solution.py:147
  71.3 11.5 %collective-permute-start.14 = (bf16[16,4224]{1,0:T(8,128)(2,1)S(1)}, bf16[16,4224]{1,0:T(8,128)(2,1)S(1)}, u32[]{:S(2)}, u32[]{:S(2)}) collective-permute-start(bf16[16,4224]{1,0:T(8,128)(2,1)S(1)} %collective-permute-done.13), channel_id=1, source_target_pairs={{0,2},{2,4},{4,6},{6,8},{8,10},{10,12},{12,14},{14,16},{16,18},{18... | collective-permute-start | bytes 405512 | tf_op jit(solution)/shard_map/ppermute | solution.py:150
  73.3 9.5 %collective-permute-start.7 = (bf16[16,4224]{1,0:T(8,128)(2,1)S(1)}, bf16[16,4224]{1,0:T(8,128)(2,1)S(1)}, u32[]{:S(2)}, u32[]{:S(2)}) collective-permute-start(bf16[16,4224]{1,0:T(8,128)(2,1)S(1)} %collective-permute-done.6), channel_id=1, source_target_pairs={{0,30},{2,0},{4,2},{6,4},{8,6},{10,8},{12,10},{14,12},{16,14},{18,... | collective-permute-start | bytes 405512 | tf_op jit(solution)/shard_map/ppermute | solution.py:147
  82.9 24.1 %copy-start = (bf16[16,16,4224]{2,1,0:T(8,128)(2,1)}, bf16[16,16,4224]{2,1,0:T(8,128)(2,1)S(1)}, u32[]{:S(2)}) copy-start(bf16[16,16,4224]{2,1,0:T(8,128)(2,1)S(1)} %bitcast_dynamic-update-slice_fusion.own_ref) | copy-start | bytes 6488068
  83.0 34.5 %collective-permute-start.15 = (bf16[16,16,4224]{2,1,0:T(8,128)(2,1)S(1)}, bf16[16,16,4224]{2,1,0:T(8,128)(2,1)}, u32[]{:S(2)}, u32[]{:S(2)}) collective-permute-start(bf16[16,16,4224]{2,1,0:T(8,128)(2,1)S(1)} %bitcast_dynamic-update-slice_fusion.own_ref), channel_id=1, source_target_pairs={{0,1},{1,0},{2,3},{3,2},{4,5},{5,4},{6,7},{7,6},{8,9},{9,8},{10,11... | collective-permute-start | bytes 6488072 | tf_op jit(solution)/shard_map/ppermute | solution.py:167
  107.1 24.2 %all-to-all-start = ((bf16[16,32,192]{2,1,0:T(8,128)(2,1)}), bf16[16,32,192]{2,1,0:T(8,128)(2,1)S(1)}, u32[]{:S(2)}, u32[]{:S(2)}) async-start(bf16[16,32,192]{2,1,0:T(8,128)(2,1)} %shard_map.73), calls=%async_computation | async-start | bytes 524288 | tf_op jit(solution)/shard_map/all_to_all | solution.py:172
Sparse Core Ops, SparseCore 0:
  22.3 78.3 all-gather.1

commit v15 on v14

--- a/solution.py
+++ b/solution.py
@@ -93,17 +93,21 @@
     chips = outs // 32
     block = channels // (2 * chips)
     core = index_ref[0]
+    rows = out_ref.shape[0] // 2
+    span = rows * width_cols
+    lanes = actn_ref.shape[1]
+    skip = positions - lanes
     for c in range(2):
         for z in range(chips):
-            actn_ref[pl.ds((2 * z + c) * block, block), :] = act_ref[pl.ds((c * chips + z) * block, block), :]
-    rows = out_ref.shape[0] // 2
+            rows_in = act_ref[pl.ds((c * chips + z) * block, block), :]
+            actn_ref[pl.ds((2 * z + c) * block, block), :] = jnp.where(core == 0, rows_in[:, :lanes], rows_in[:, skip:])
     nn = (((1,), (0,)), ((), ()))
-    sub = lax.broadcasted_iota(jnp.int32, (packed_width - 4 * channels, positions), 0)
+    sub = lax.broadcasted_iota(jnp.int32, (packed_width - 4 * channels, lanes), 0)
     ones = jnp.where(sub == 0, 1.0, 0.0).astype(actn_ref.dtype)
     bias = lax.dot_general(wnat_ref[:, pl.ds(4 * channels, packed_width - 4 * channels)], ones, nn,
                            preferred_element_type=jnp.float32)
     act = actn_ref[...]
-    span = rows * width_cols
+    first = lanes - span
     dest = lax.broadcasted_iota(jnp.int32, (2 * width_cols, 2 * width_cols), 0)
     src = lax.broadcasted_iota(jnp.int32, (2 * width_cols, 2 * width_cols), 1)
     interleave = jnp.where(src == (dest % 2) * width_cols + dest // 2, 1.0, 0.0).astype(out_ref.dtype)
@@ -113,7 +117,7 @@
             res = lax.dot_general(wnat_ref[:, pl.ds((2 * a + b) * channels, channels)], act, nn,
                                   preferred_element_type=jnp.float32)
             res = jnp.transpose(res + bias).astype(out_ref.dtype)
-            phases.append(jnp.where(core == 0, res[:span], res[span:]))
+            phases.append(jnp.where(core == 0, res[:span], res[first:]))
         for i in range(rows):
             stacked = jnp.concatenate([p[i * width_cols:(i + 1) * width_cols] for p in phases], axis=0)
             out_ref[2 * i + a] = jnp.dot(interleave, stacked, preferred_element_type=jnp.float32).astype(out_ref.dtype)
@@ -130,7 +134,7 @@
         out_shape=jax.ShapeDtypeStruct((2 * rows, 2 * width_cols, outs), jnp.bfloat16),
         in_specs=[smem, vmem, vmem],
         out_specs=vmem,
-        scratch_shapes=[pltpu.VMEM((channels, positions), act.dtype)],
+        scratch_shapes=[pltpu.VMEM((channels, -(-positions // 2 // 128) * 128), act.dtype)],
         cost_estimate=pl.CostEstimate(
             flops=2 * positions * channels * 4 * outs, transcendentals=0,
             bytes_accessed=act.size * 2 + wnat.size * 2 + rows * width_cols * 4 * outs * 2),

time: 151 us -> 151 us (level)
  no operation moved by 1% of the time
where the time goes in v15:
time: 151 us; the launch traced here: 150 us
  starting transfers between devices  79.4 us (53%)
  waiting for transfers between devices  29.3 us (19%)
  Pallas kernels  16 us (11%)
  between operations  13.7 us (9%)
  blocking collectives  6.66 us (4%)
  local copies, waits for them, and re-layouts  4.07 us (3%)
    ppermute x8, starting transfers between devices, ring_gather(): ahead = lax.ppermute(ahead, axis, step_up)  45.9 us
    ppermute x7, starting transfers between devices, ring_gather(): behind = lax.ppermute(behind, axis, step_down)  13.4 us
    ppermute x1, starting transfers between devices, body(): packed_other = lax.ppermute(packed_z, 'core', [(0, 1), (1, 0)])  10.5 us
    all_to_all x1, starting transfers between devices, body(): lax.all_to_all(activated, 'z', split_axis=0, concat_axis=0, tiled=True)  9.74 us
    all_to_all x1, waiting for transfers between devices, body(): lax.all_to_all(activated, 'z', split_axis=0, concat_axis=0, tiled=True)  9.21 us
    ppermute x7, waiting for transfers between devices, ring_gather(): behind = lax.ppermute(behind, axis, step_down)  8.94 us
    all_gather x1, blocking collectives, body(): both = lax.all_gather(chip_rows, 'core', axis=0, tiled=True)  6.66 us
    pallas_call x1, Pallas kernels, conv_norm(): pl.pallas_call(functools.partial(conv_norm_kernel, height=height, width_c...  6.4 us
  transfers between devices with their start and end apart: 18, of which 9 were waited for; matrix products, arithmetic and copies ran while one was open for 2% of the time, Pallas kernels for 7%

profile of v15, /device:TPU:1, one launch (start us, length us, event | category | flops | bytes accessed | tf_op | source)
XLA Modules:
  0.0 149.8 jit_solution(13541211913923106306)
XLA Ops:
  6.5 0.7 copy.15
  7.3 1.0 reshape.31
  8.3 12.0 %collective-permute-start = (bf16[16,4224]{1,0:T(8,128)(2,1)S(1)}, bf16[16,4224]{1,0:T(8,128)(2,1)S(1)}, u32[]{:S(2)}, u32[]{:S(2)}) collective-permute-start(bf16[16,4224]{1,0:T(8,128)(2,1)S(1)} %fusion.1), channel_id=1, source_target_pairs={{0,30},{2,0},{4,2},{6,4},{8,6},{10,8},{12,10},{14,12},{16,14},{18,... | collective-permute-start | bytes 405512 | tf_op jit(solution)/shard_map/ppermute | solution.py:151
  20.2 1.9 %collective-permute-start.8 = (bf16[16,4224]{1,0:T(8,128)(2,1)S(1)}, bf16[16,4224]{1,0:T(8,128)(2,1)S(1)}, u32[]{:S(2)}, u32[]{:S(2)}) collective-permute-start(bf16[16,4224]{1,0:T(8,128)(2,1)S(1)} %fusion.1), channel_id=1, source_target_pairs={{0,2},{2,4},{4,6},{6,8},{8,10},{10,12},{12,14},{14,16},{16,18},{18... | collective-permute-start | bytes 405512 | tf_op jit(solution)/shard_map/ppermute | solution.py:154
  22.2 0.0 all-gather.2.cloned.1.call-update
  22.2 0.0 copy-start.1
  22.2 0.0 copy-start.2
  22.2 0.0 copy-start.3
  22.3 0.2 collective-permute-done
  22.5 5.3 %collective-permute-start.1 = (bf16[16,4224]{1,0:T(8,128)(2,1)S(1)}, bf16[16,4224]{1,0:T(8,128)(2,1)S(1)}, u32[]{:S(2)}, u32[]{:S(2)}) collective-permute-start(bf16[16,4224]{1,0:T(8,128)(2,1)S(1)} %collective-permute-done), channel_id=1, source_target_pairs={{0,30},{2,0},{4,2},{6,4},{8,6},{10,8},{12,10},{14,12},{16,14},{18,... | collective-permute-start | bytes 405512 | tf_op jit(solution)/shard_map/ppermute | solution.py:151
  27.8 0.0 collective-permute-done.8
  27.8 1.9 %collective-permute-start.9 = (bf16[16,4224]{1,0:T(8,128)(2,1)S(1)}, bf16[16,4224]{1,0:T(8,128)(2,1)S(1)}, u32[]{:S(2)}, u32[]{:S(2)}) collective-permute-start(bf16[16,4224]{1,0:T(8,128)(2,1)S(1)} %collective-permute-done.8), channel_id=1, source_target_pairs={{0,2},{2,4},{4,6},{6,8},{8,10},{10,12},{12,14},{14,16},{16,18},{18... | collective-permute-start | bytes 405512 | tf_op jit(solution)/shard_map/ppermute | solution.py:154
  29.7 0.0 collective-permute-done.1
  29.8 5.0 %collective-permute-start.2 = (bf16[16,4224]{1,0:T(8,128)(2,1)S(1)}, bf16[16,4224]{1,0:T(8,128)(2,1)S(1)}, u32[]{:S(2)}, u32[]{:S(2)}) collective-permute-start(bf16[16,4224]{1,0:T(8,128)(2,1)S(1)} %collective-permute-done.1), channel_id=1, source_target_pairs={{0,30},{2,0},{4,2},{6,4},{8,6},{10,8},{12,10},{14,12},{16,14},{18,... | collective-permute-start | bytes 405512 | tf_op jit(solution)/shard_map/ppermute | solution.py:151
  34.7 0.0 collective-permute-done.9
  34.8 1.9 %collective-permute-start.10 = (bf16[16,4224]{1,0:T(8,128)(2,1)S(1)}, bf16[16,4224]{1,0:T(8,128)(2,1)S(1)}, u32[]{:S(2)}, u32[]{:S(2)}) collective-permute-start(bf16[16,4224]{1,0:T(8,128)(2,1)S(1)} %collective-permute-done.9), channel_id=1, source_target_pairs={{0,2},{2,4},{4,6},{6,8},{8,10},{10,12},{12,14},{14,16},{16,18},{18... | collective-permute-start | bytes 405512 | tf_op jit(solution)/shard_map/ppermute | solution.py:154
  36.7 0.8 collective-permute-done.2
  37.5 5.0 %collective-permute-start.3 = (bf16[16,4224]{1,0:T(8,128)(2,1)S(1)}, bf16[16,4224]{1,0:T(8,128)(2,1)S(1)}, u32[]{:S(2)}, u32[]{:S(2)}) collective-permute-start(bf16[16,4224]{1,0:T(8,128)(2,1)S(1)} %collective-permute-done.2), channel_id=1, source_target_pairs={{0,30},{2,0},{4,2},{6,4},{8,6},{10,8},{12,10},{14,12},{16,14},{18,... | collective-permute-start | bytes 405512 | tf_op jit(solution)/shard_map/ppermute | solution.py:151
  42.5 2.3 %collective-permute-done.10 = bf16[16,4224]{1,0:T(8,128)(2,1)S(1)} collective-permute-done((bf16[16,4224]{1,0:T(8,128)(2,1)S(1)}, bf16[16,4224]{1,0:T(8,128)(2,1)S(1)}, u32[]{:S(2)}, u32[]{:S(2)}) %collective-permute-start.10) | collective-permute-done | bytes 135200 | tf_op jit(solution)/shard_map/ppermute | solution.py:154
  44.8 1.9 %collective-permute-start.11 = (bf16[16,4224]{1,0:T(8,128)(2,1)S(1)}, bf16[16,4224]{1,0:T(8,128)(2,1)S(1)}, u32[]{:S(2)}, u32[]{:S(2)}) collective-permute-start(bf16[16,4224]{1,0:T(8,128)(2,1)S(1)} %collective-permute-done.10), channel_id=1, source_target_pairs={{0,2},{2,4},{4,6},{6,8},{8,10},{10,12},{12,14},{14,16},{16,18},{18... | collective-permute-start | bytes 405512 | tf_op jit(solution)/shard_map/ppermute | solution.py:154
  46.8 0.0 collective-permute-done.3
  46.8 4.9 %collective-permute-start.4 = (bf16[16,4224]{1,0:T(8,128)(2,1)S(1)}, bf16[16,4224]{1,0:T(8,128)(2,1)S(1)}, u32[]{:S(2)}, u32[]{:S(2)}) collective-permute-start(bf16[16,4224]{1,0:T(8,128)(2,1)S(1)} %collective-permute-done.3), channel_id=1, source_target_pairs={{0,30},{2,0},{4,2},{6,4},{8,6},{10,8},{12,10},{14,12},{16,14},{18,... | collective-permute-start | bytes 405512 | tf_op jit(solution)/shard_map/ppermute | solution.py:151
  51.7 2.3 %collective-permute-done.11 = bf16[16,4224]{1,0:T(8,128)(2,1)S(1)} collective-permute-done((bf16[16,4224]{1,0:T(8,128)(2,1)S(1)}, bf16[16,4224]{1,0:T(8,128)(2,1)S(1)}, u32[]{:S(2)}, u32[]{:S(2)}) %collective-permute-start.11) | collective-permute-done | bytes 135200 | tf_op jit(solution)/shard_map/ppermute | solution.py:154
  54.0 1.9 %collective-permute-start.12 = (bf16[16,4224]{1,0:T(8,128)(2,1)S(1)}, bf16[16,4224]{1,0:T(8,128)(2,1)S(1)}, u32[]{:S(2)}, u32[]{:S(2)}) collective-permute-start(bf16[16,4224]{1,0:T(8,128)(2,1)S(1)} %collective-permute-done.11), channel_id=1, source_target_pairs={{0,2},{2,4},{4,6},{6,8},{8,10},{10,12},{12,14},{14,16},{16,18},{18... | collective-permute-start | bytes 405512 | tf_op jit(solution)/shard_map/ppermute | solution.py:154
  55.9 0.0 collective-permute-done.4
  55.9 4.6 %collective-permute-start.5 = (bf16[16,4224]{1,0:T(8,128)(2,1)S(1)}, bf16[16,4224]{1,0:T(8,128)(2,1)S(1)}, u32[]{:S(2)}, u32[]{:S(2)}) collective-permute-start(bf16[16,4224]{1,0:T(8,128)(2,1)S(1)} %collective-permute-done.4), channel_id=1, source_target_pairs={{0,30},{2,0},{4,2},{6,4},{8,6},{10,8},{12,10},{14,12},{16,14},{18,... | collective-permute-start | bytes 405512 | tf_op jit(solution)/shard_map/ppermute | solution.py:151
  60.5 2.0 %collective-permute-done.12 = bf16[16,4224]{1,0:T(8,128)(2,1)S(1)} collective-permute-done((bf16[16,4224]{1,0:T(8,128)(2,1)S(1)}, bf16[16,4224]{1,0:T(8,128)(2,1)S(1)}, u32[]{:S(2)}, u32[]{:S(2)}) %collective-permute-start.12) | collective-permute-done | bytes 135200 | tf_op jit(solution)/shard_map/ppermute | solution.py:154
  62.5 1.9 %collective-permute-start.13 = (bf16[16,4224]{1,0:T(8,128)(2,1)S(1)}, bf16[16,4224]{1,0:T(8,128)(2,1)S(1)}, u32[]{:S(2)}, u32[]{:S(2)}) collective-permute-start(bf16[16,4224]{1,0:T(8,128)(2,1)S(1)} %collective-permute-done.12), channel_id=1, source_target_pairs={{0,2},{2,4},{4,6},{6,8},{8,10},{10,12},{12,14},{14,16},{16,18},{18... | collective-permute-start | bytes 405512 | tf_op jit(solution)/shard_map/ppermute | solution.py:154
  64.5 0.0 collective-permute-done.5
  64.5 4.6 %collective-permute-start.6 = (bf16[16,4224]{1,0:T(8,128)(2,1)S(1)}, bf16[16,4224]{1,0:T(8,128)(2,1)S(1)}, u32[]{:S(2)}, u32[]{:S(2)}) collective-permute-start(bf16[16,4224]{1,0:T(8,128)(2,1)S(1)} %collective-permute-done.5), channel_id=1, source_target_pairs={{0,30},{2,0},{4,2},{6,4},{8,6},{10,8},{12,10},{14,12},{16,14},{18,... | collective-permute-start | bytes 405512 | tf_op jit(solution)/shard_map/ppermute | solution.py:151
  69.1 2.3 %collective-permute-done.13 = bf16[16,4224]{1,0:T(8,128)(2,1)S(1)} collective-permute-done((bf16[16,4224]{1,0:T(8,128)(2,1)S(1)}, bf16[16,4224]{1,0:T(8,128)(2,1)S(1)}, u32[]{:S(2)}, u32[]{:S(2)}) %collective-permute-start.13) | collective-permute-done | bytes 135200 | tf_op jit(solution)/shard_map/ppermute | solution.py:154
  71.3 1.9 %collective-permute-start.14 = (bf16[16,4224]{1,0:T(8,128)(2,1)S(1)}, bf16[16,4224]{1,0:T(8,128)(2,1)S(1)}, u32[]{:S(2)}, u32[]{:S(2)}) collective-permute-start(bf16[16,4224]{1,0:T(8,128)(2,1)S(1)} %collective-permute-done.13), channel_id=1, source_target_pairs={{0,2},{2,4},{4,6},{6,8},{8,10},{10,12},{12,14},{14,16},{16,18},{18... | collective-permute-start | bytes 405512 | tf_op jit(solution)/shard_map/ppermute | solution.py:154
  73.3 4.6 %collective-permute-start.7 = (bf16[16,4224]{1,0:T(8,128)(2,1)S(1)}, bf16[16,4224]{1,0:T(8,128)(2,1)S(1)}, u32[]{:S(2)}, u32[]{:S(2)}) collective-permute-start(bf16[16,4224]{1,0:T(8,128)(2,1)S(1)} %collective-permute-done.6), channel_id=1, source_target_pairs={{0,30},{2,0},{4,2},{6,4},{8,6},{10,8},{12,10},{14,12},{16,14},{18,... | collective-permute-start | bytes 405512 | tf_op jit(solution)/shard_map/ppermute | solution.py:151
  77.9 4.9 %collective-permute-done.7 = bf16[16,4224]{1,0:T(8,128)(2,1)S(1)} collective-permute-done((bf16[16,4224]{1,0:T(8,128)(2,1)S(1)}, bf16[16,4224]{1,0:T(8,128)(2,1)S(1)}, u32[]{:S(2)}, u32[]{:S(2)}) %collective-permute-start.7) | collective-permute-done | bytes 135200 | tf_op jit(solution)/shard_map/ppermute | solution.py:151
  82.8 0.0 collective-permute-done.14
  83.0 10.5 %collective-permute-start.15 = (bf16[16,16,4224]{2,1,0:T(8,128)(2,1)S(1)}, bf16[16,16,4224]{2,1,0:T(8,128)(2,1)}, u32[]{:S(2)}, u32[]{:S(2)}) collective-permute-start(bf16[16,16,4224]{2,1,0:T(8,128)(2,1)S(1)} %bitcast_dynamic-update-slice_fusion.own_ref), channel_id=1, source_target_pairs={{0,1},{1,0},{2,3},{3,2},{4,5},{5,4},{6,7},{7,6},{8,9},{9,8},{10,11... | collective-permute-start | bytes 6488072 | tf_op jit(solution)/shard_map/ppermute | solution.py:171
  93.4 0.7 copy.12.bias_ref
  94.1 0.7 copy.13.gain_ref
  94.8 0.7 copy.14.shift_ref
  95.5 5.2 %all-gather.2.cloned.1.call-done = bf16[64,48,1024]{2,1,0:T(8,128)(2,1)} async-done(((bf16[2,48,1024]{2,1,0:T(8,128)(2,1)}), bf16[64,48,1024]{2,1,0:T(8,128)(2,1)}) %all-gather.2.cloned.1.call-update) | async-done | bytes 6291472 | tf_op jit(solution)/shard_map/all_gather | solution.py:166
  100.7 6.4 %shard_map.73 = bf16[16,32,192]{2,1,0:T(8,128)(2,1)} custom-call(bf16[3072,1024]{1,0:T(8,128)(2,1)} %bitcast.45, bf16[288,1024]{1,0:T(8,128)(2,1)} %bitcast.47, f32[32,1]{1,0:T(8,128)} %copy.12.bias_ref, f32[32,1]{1,0:T(8,128)} %copy.13.gain_ref, f32[32,1]{1,0:T(8,128)} %copy.14.shift_ref), custom_call_target="tpu_custom_call" | custom-call | flops 1811939328 | bytes 7077888 | tf_op jit(solution)/shard_map/pallas_call | solution.py:53
  107.1 9.7 %all-to-all-start = ((bf16[16,32,192]{2,1,0:T(8,128)(2,1)}), bf16[16,32,192]{2,1,0:T(8,128)(2,1)S(1)}, u32[]{:S(2)}, u32[]{:S(2)}) async-start(bf16[16,32,192]{2,1,0:T(8,128)(2,1)} %shard_map.73), calls=%async_computation | async-start | bytes 524288 | tf_op jit(solution)/shard_map/all_to_all | solution.py:176
  116.8 0.7 pad_add_fusion.index_ref
  117.5 0.0 collective-permute-done.15.other_ref
  117.5 4.6 %shard_map.74.wnat_ref = bf16[512,4224]{1,0:T(8,128)(2,1)} custom-call(s32[2]{0:T(128)} %pad_add_fusion.index_ref, bf16[16,16,4224]{2,1,0:T(8,128)(2,1)} %copy-done, bf16[16,16,4224]{2,1,0:T(8,128)(2,1)} %collective-permute-done.15.other_ref), custom_call_target="tpu_custom_call" | custom-call | bytes 8650752 | tf_op jit(solution)/shard_map/pallas_call | solution.py:81
  122.1 9.2 %all-to-all-done = bf16[16,32,192]{2,1,0:T(8,128)(2,1)S(1)} async-done(((bf16[16,32,192]{2,1,0:T(8,128)(2,1)}), bf16[16,32,192]{2,1,0:T(8,128)(2,1)S(1)}, u32[]{:S(2)}, u32[]{:S(2)}) %all-to-all-start) | async-done | bytes 196640 | tf_op jit(solution)/shard_map/all_to_all | solution.py:176
  131.3 6.7 %all_gather.7.act_ref = bf16[1024,192]{1,0:T(8,128)(2,1)} all-gather(bf16[512,192]{1,0:T(8,128)(2,1)S(1)} %bitcast.46), channel_id=1, replica_groups=mesh['grp'=16,'z'=16,'core'=2] {'core'}, dimensions={0}, use_global_device_ids=true | all-gather | bytes 589824 | tf_op jit(solution)/shard_map/all_gather | solution.py:178
  137.9 5.0 %shard_map.75 = bf16[4,96,512]{2,1,0:T(8,128)(2,1)} custom-call(s32[2]{0:T(128)} %pad_add_fusion.index_ref, bf16[1024,192]{1,0:T(8,128)(2,1)} %all_gather.7.act_ref, bf16[512,4224]{1,0:T(8,128)(2,1)} %shard_map.74.wnat_ref), custom_call_target="tpu_custom_call" | custom-call | flops 805306368 | bytes 5111808 | tf_op jit(solution)/shard_map/pallas_call | solution.py:132
  (24 shorter events, 0.3 us)
Async XLA Ops:
  6.5 94.1 %all-gather.2.cloned.1.call-start = ((), (), s32[]{:S(2)}) async-start(), calls=%async_computation.1 | async-start | bytes 6488064 | tf_op jit(solution)/shard_map/all_gather | solution.py:166
  8.3 14.2 %collective-permute-start = (bf16[16,4224]{1,0:T(8,128)(2,1)S(1)}, bf16[16,4224]{1,0:T(8,128)(2,1)S(1)}, u32[]{:S(2)}, u32[]{:S(2)}) collective-permute-start(bf16[16,4224]{1,0:T(8,128)(2,1)S(1)} %fusion.1), channel_id=1, source_target_pairs={{0,30},{2,0},{4,2},{6,4},{8,6},{10,8},{12,10},{14,12},{16,14},{18,... | collective-permute-start | bytes 405512 | tf_op jit(solution)/shard_map/ppermute | solution.py:151
  20.2 7.5 %collective-permute-start.8 = (bf16[16,4224]{1,0:T(8,128)(2,1)S(1)}, bf16[16,4224]{1,0:T(8,128)(2,1)S(1)}, u32[]{:S(2)}, u32[]{:S(2)}) collective-permute-start(bf16[16,4224]{1,0:T(8,128)(2,1)S(1)} %fusion.1), channel_id=1, source_target_pairs={{0,2},{2,4},{4,6},{6,8},{8,10},{10,12},{12,14},{14,16},{16,18},{18... | collective-permute-start | bytes 405512 | tf_op jit(solution)/shard_map/ppermute | solution.py:154
  22.2 71.2 %copy-start.1 = (f32[32]{0:T(128)S(1)}, f32[32]{0:T(128)}, u32[]{:S(2)}) copy-start(f32[32]{0:T(128)} %param.9) | copy-start | bytes 388
  22.2 71.9 %copy-start.2 = (f32[32]{0:T(128)S(1)}, f32[32]{0:T(128)}, u32[]{:S(2)}) copy-start(f32[32]{0:T(128)} %param.10) | copy-start | bytes 388
  22.2 72.6 %copy-start.3 = (f32[32]{0:T(128)S(1)}, f32[32]{0:T(128)}, u32[]{:S(2)}) copy-start(f32[32]{0:T(128)} %param.11) | copy-start | bytes 388
  22.5 7.3 %collective-permute-start.1 = (bf16[16,4224]{1,0:T(8,128)(2,1)S(1)}, bf16[16,4224]{1,0:T(8,128)(2,1)S(1)}, u32[]{:S(2)}, u32[]{:S(2)}) collective-permute-start(bf16[16,4224]{1,0:T(8,128)(2,1)S(1)} %collective-permute-done), channel_id=1, source_target_pairs={{0,30},{2,0},{4,2},{6,4},{8,6},{10,8},{12,10},{14,12},{16,14},{18,... | collective-permute-start | bytes 405512 | tf_op jit(solution)/shard_map/ppermute | solution.py:151
  27.8 7.0 %collective-permute-start.9 = (bf16[16,4224]{1,0:T(8,128)(2,1)S(1)}, bf16[16,4224]{1,0:T(8,128)(2,1)S(1)}, u32[]{:S(2)}, u32[]{:S(2)}) collective-permute-start(bf16[16,4224]{1,0:T(8,128)(2,1)S(1)} %collective-permute-done.8), channel_id=1, source_target_pairs={{0,2},{2,4},{4,6},{6,8},{8,10},{10,12},{12,14},{14,16},{16,18},{18... | collective-permute-start | bytes 405512 | tf_op jit(solution)/shard_map/ppermute | solution.py:154
  29.8 7.7 %collective-permute-start.2 = (bf16[16,4224]{1,0:T(8,128)(2,1)S(1)}, bf16[16,4224]{1,0:T(8,128)(2,1)S(1)}, u32[]{:S(2)}, u32[]{:S(2)}) collective-permute-start(bf16[16,4224]{1,0:T(8,128)(2,1)S(1)} %collective-permute-done.1), channel_id=1, source_target_pairs={{0,30},{2,0},{4,2},{6,4},{8,6},{10,8},{12,10},{14,12},{16,14},{18,... | collective-permute-start | bytes 405512 | tf_op jit(solution)/shard_map/ppermute | solution.py:151
  34.8 10.1 %collective-permute-start.10 = (bf16[16,4224]{1,0:T(8,128)(2,1)S(1)}, bf16[16,4224]{1,0:T(8,128)(2,1)S(1)}, u32[]{:S(2)}, u32[]{:S(2)}) collective-permute-start(bf16[16,4224]{1,0:T(8,128)(2,1)S(1)} %collective-permute-done.9), channel_id=1, source_target_pairs={{0,2},{2,4},{4,6},{6,8},{8,10},{10,12},{12,14},{14,16},{16,18},{18... | collective-permute-start | bytes 405512 | tf_op jit(solution)/shard_map/ppermute | solution.py:154
  37.5 9.3 %collective-permute-start.3 = (bf16[16,4224]{1,0:T(8,128)(2,1)S(1)}, bf16[16,4224]{1,0:T(8,128)(2,1)S(1)}, u32[]{:S(2)}, u32[]{:S(2)}) collective-permute-start(bf16[16,4224]{1,0:T(8,128)(2,1)S(1)} %collective-permute-done.2), channel_id=1, source_target_pairs={{0,30},{2,0},{4,2},{6,4},{8,6},{10,8},{12,10},{14,12},{16,14},{18,... | collective-permute-start | bytes 405512 | tf_op jit(solution)/shard_map/ppermute | solution.py:151
  44.8 9.2 %collective-permute-start.11 = (bf16[16,4224]{1,0:T(8,128)(2,1)S(1)}, bf16[16,4224]{1,0:T(8,128)(2,1)S(1)}, u32[]{:S(2)}, u32[]{:S(2)}) collective-permute-start(bf16[16,4224]{1,0:T(8,128)(2,1)S(1)} %collective-permute-done.10), channel_id=1, source_target_pairs={{0,2},{2,4},{4,6},{6,8},{8,10},{10,12},{12,14},{14,16},{16,18},{18... | collective-permute-start | bytes 405512 | tf_op jit(solution)/shard_map/ppermute | solution.py:154
  46.8 9.1 %collective-permute-start.4 = (bf16[16,4224]{1,0:T(8,128)(2,1)S(1)}, bf16[16,4224]{1,0:T(8,128)(2,1)S(1)}, u32[]{:S(2)}, u32[]{:S(2)}) collective-permute-start(bf16[16,4224]{1,0:T(8,128)(2,1)S(1)} %collective-permute-done.3), channel_id=1, source_target_pairs={{0,30},{2,0},{4,2},{6,4},{8,6},{10,8},{12,10},{14,12},{16,14},{18,... | collective-permute-start | bytes 405512 | tf_op jit(solution)/shard_map/ppermute | solution.py:151
  54.0 8.5 %collective-permute-start.12 = (bf16[16,4224]{1,0:T(8,128)(2,1)S(1)}, bf16[16,4224]{1,0:T(8,128)(2,1)S(1)}, u32[]{:S(2)}, u32[]{:S(2)}) collective-permute-start(bf16[16,4224]{1,0:T(8,128)(2,1)S(1)} %collective-permute-done.11), channel_id=1, source_target_pairs={{0,2},{2,4},{4,6},{6,8},{8,10},{10,12},{12,14},{14,16},{16,18},{18... | collective-permute-start | bytes 405512 | tf_op jit(solution)/shard_map/ppermute | solution.py:154
  55.9 8.5 %collective-permute-start.5 = (bf16[16,4224]{1,0:T(8,128)(2,1)S(1)}, bf16[16,4224]{1,0:T(8,128)(2,1)S(1)}, u32[]{:S(2)}, u32[]{:S(2)}) collective-permute-start(bf16[16,4224]{1,0:T(8,128)(2,1)S(1)} %collective-permute-done.4), channel_id=1, source_target_pairs={{0,30},{2,0},{4,2},{6,4},{8,6},{10,8},{12,10},{14,12},{16,14},{18,... | collective-permute-start | bytes 405512 | tf_op jit(solution)/shard_map/ppermute | solution.py:151
  62.5 8.8 %collective-permute-start.13 = (bf16[16,4224]{1,0:T(8,128)(2,1)S(1)}, bf16[16,4224]{1,0:T(8,128)(2,1)S(1)}, u32[]{:S(2)}, u32[]{:S(2)}) collective-permute-start(bf16[16,4224]{1,0:T(8,128)(2,1)S(1)} %collective-permute-done.12), channel_id=1, source_target_pairs={{0,2},{2,4},{4,6},{6,8},{8,10},{10,12},{12,14},{14,16},{16,18},{18... | collective-permute-start | bytes 405512 | tf_op jit(solution)/shard_map/ppermute | solution.py:154
  64.5 8.8 %collective-permute-start.6 = (bf16[16,4224]{1,0:T(8,128)(2,1)S(1)}, bf16[16,4224]{1,0:T(8,128)(2,1)S(1)}, u32[]{:S(2)}, u32[]{:S(2)}) collective-permute-start(bf16[16,4224]{1,0:T(8,128)(2,1)S(1)} %collective-permute-done.5), channel_id=1, source_target_pairs={{0,30},{2,0},{4,2},{6,4},{8,6},{10,8},{12,10},{14,12},{16,14},{18,... | collective-permute-start | bytes 405512 | tf_op jit(solution)/shard_map/ppermute | solution.py:151
  71.3 11.5 %collective-permute-start.14 = (bf16[16,4224]{1,0:T(8,128)(2,1)S(1)}, bf16[16,4224]{1,0:T(8,128)(2,1)S(1)}, u32[]{:S(2)}, u32[]{:S(2)}) collective-permute-start(bf16[16,4224]{1,0:T(8,128)(2,1)S(1)} %collective-permute-done.13), channel_id=1, source_target_pairs={{0,2},{2,4},{4,6},{6,8},{8,10},{10,12},{12,14},{14,16},{16,18},{18... | collective-permute-start | bytes 405512 | tf_op jit(solution)/shard_map/ppermute | solution.py:154
  73.3 9.5 %collective-permute-start.7 = (bf16[16,4224]{1,0:T(8,128)(2,1)S(1)}, bf16[16,4224]{1,0:T(8,128)(2,1)S(1)}, u32[]{:S(2)}, u32[]{:S(2)}) collective-permute-start(bf16[16,4224]{1,0:T(8,128)(2,1)S(1)} %collective-permute-done.6), channel_id=1, source_target_pairs={{0,30},{2,0},{4,2},{6,4},{8,6},{10,8},{12,10},{14,12},{16,14},{18,... | collective-permute-start | bytes 405512 | tf_op jit(solution)/shard_map/ppermute | solution.py:151
  82.9 24.1 %copy-start = (bf16[16,16,4224]{2,1,0:T(8,128)(2,1)}, bf16[16,16,4224]{2,1,0:T(8,128)(2,1)S(1)}, u32[]{:S(2)}) copy-start(bf16[16,16,4224]{2,1,0:T(8,128)(2,1)S(1)} %bitcast_dynamic-update-slice_fusion.own_ref) | copy-start | bytes 6488068
  83.0 34.5 %collective-permute-start.15 = (bf16[16,16,4224]{2,1,0:T(8,128)(2,1)S(1)}, bf16[16,16,4224]{2,1,0:T(8,128)(2,1)}, u32[]{:S(2)}, u32[]{:S(2)}) collective-permute-start(bf16[16,16,4224]{2,1,0:T(8,128)(2,1)S(1)} %bitcast_dynamic-update-slice_fusion.own_ref), channel_id=1, source_target_pairs={{0,1},{1,0},{2,3},{3,2},{4,5},{5,4},{6,7},{7,6},{8,9},{9,8},{10,11... | collective-permute-start | bytes 6488072 | tf_op jit(solution)/shard_map/ppermute | solution.py:171
  107.1 24.2 %all-to-all-start = ((bf16[16,32,192]{2,1,0:T(8,128)(2,1)}), bf16[16,32,192]{2,1,0:T(8,128)(2,1)S(1)}, u32[]{:S(2)}, u32[]{:S(2)}) async-start(bf16[16,32,192]{2,1,0:T(8,128)(2,1)} %shard_map.73), calls=%async_computation | async-start | bytes 524288 | tf_op jit(solution)/shard_map/all_to_all | solution.py:176
Sparse Core Ops, SparseCore 0:
  22.3 78.3 all-gather.1

commit v16 on v15

--- a/solution.py
+++ b/solution.py
@@ -10,11 +10,20 @@
 GSIZE = 32
 
 
-def conv_norm_kernel(x_ref, w_ref, bias_ref, gain_ref, shift_ref, out_ref, *, height, width_cols):
+def conv_norm_kernel(x_hbm, w_ref, bias_ref, gain_ref, shift_ref, out_ref, x_buf, taps_ref, sems, *,
+                     height, width_cols):
     outputs = out_ref.shape[1]
     positions = height * width_cols
-    taps = lax.dot_general(w_ref[...], x_ref[...], (((1,), (1,)), ((), ())),
-                           preferred_element_type=jnp.float32)
+    pieces, chunk, _ = x_buf.shape
+    copies = [pltpu.make_async_copy(x_hbm.at[pl.ds(p * chunk, chunk)], x_buf.at[p], sems.at[p])
+              for p in range(pieces)]
+    for copy in copies:
+        copy.start()
+    for p in range(pieces):
+        copies[p].wait()
+        taps_ref[:, pl.ds(p * chunk, chunk)] = lax.dot_general(
+            w_ref[...], x_buf[p], (((1,), (1,)), ((), ())), preferred_element_type=jnp.float32)
+    taps = taps_ref[...]
     pos = lax.broadcasted_iota(jnp.int32, (1, positions), 1)
     row = pos // width_cols
     col = pos % width_cols
@@ -53,8 +62,11 @@
     return pl.pallas_call(
         functools.partial(conv_norm_kernel, height=height, width_cols=width_cols),
         out_shape=jax.ShapeDtypeStruct((chips, outputs, height * width_cols // chips), jnp.bfloat16),
-        in_specs=[vmem] * 5,
+        in_specs=[pl.BlockSpec(memory_space=pl.ANY)] + [vmem] * 4,
         out_specs=vmem,
+        scratch_shapes=[pltpu.VMEM((4, height * width_cols // 4, channels), whole.dtype),
+                        pltpu.VMEM((9 * outputs, height * width_cols), jnp.float32),
+                        pltpu.SemaphoreType.DMA((4,))],
         cost_estimate=pl.CostEstimate(
             flops=2 * height * width_cols * channels * 9 * outputs,
             transcendentals=height * width_cols * outputs,

time: 151 us -> 152 us (level)
  transfers between devices with their start and end apart: 18 -> 18, of which waited for: 9 -> 9; matrix products, arithmetic and copies ran while one was open for 2% -> 2% of each run, Pallas kernels for 7% -> 8%
where the time goes in v16:
time: 152 us; the launch traced here: 151 us
  starting transfers between devices  79.5 us (52%)
  waiting for transfers between devices  29.3 us (19%)
  Pallas kernels  16.9 us (11%)
  between operations  13.7 us (9%)
  blocking collectives  6.68 us (4%)
  local copies, waits for them, and re-layouts  4.07 us (3%)
    ppermute x8, starting transfers between devices, ring_gather(): ahead = lax.ppermute(ahead, axis, step_up)  45.9 us
    ppermute x7, starting transfers between devices, ring_gather(): behind = lax.ppermute(behind, axis, step_down)  13.4 us
    ppermute x1, starting transfers between devices, body(): packed_other = lax.ppermute(packed_z, 'core', [(0, 1), (1, 0)])  10.5 us
    all_to_all x1, starting transfers between devices, body(): lax.all_to_all(activated, 'z', split_axis=0, concat_axis=0, tiled=True)  9.75 us
    all_to_all x1, waiting for transfers between devices, body(): lax.all_to_all(activated, 'z', split_axis=0, concat_axis=0, tiled=True)  9.2 us
    ppermute x7, waiting for transfers between devices, ring_gather(): behind = lax.ppermute(behind, axis, step_down)  8.94 us
    pallas_call x1, Pallas kernels, conv_norm(): pl.pallas_call(functools.partial(conv_norm_kernel, height=height, width_c...  7.29 us
    all_gather x1, blocking collectives, body(): both = lax.all_gather(chip_rows, 'core', axis=0, tiled=True)  6.68 us
  transfers between devices with their start and end apart: 18, of which 9 were waited for; matrix products, arithmetic and copies ran while one was open for 2% of the time, Pallas kernels for 8%

profile of v16, /device:TPU:1, one launch (start us, length us, event | category | flops | bytes accessed | tf_op | source)
XLA Modules:
  0.0 150.7 jit_solution(967890727274433599)
XLA Ops:
  6.5 0.7 copy.15
  7.3 1.0 reshape.31
  8.3 12.0 %collective-permute-start = (bf16[16,4224]{1,0:T(8,128)(2,1)S(1)}, bf16[16,4224]{1,0:T(8,128)(2,1)S(1)}, u32[]{:S(2)}, u32[]{:S(2)}) collective-permute-start(bf16[16,4224]{1,0:T(8,128)(2,1)S(1)} %fusion.1), channel_id=1, source_target_pairs={{0,30},{2,0},{4,2},{6,4},{8,6},{10,8},{12,10},{14,12},{16,14},{18,... | collective-permute-start | bytes 405512 | tf_op jit(solution)/shard_map/ppermute | solution.py:163
  20.2 1.9 %collective-permute-start.8 = (bf16[16,4224]{1,0:T(8,128)(2,1)S(1)}, bf16[16,4224]{1,0:T(8,128)(2,1)S(1)}, u32[]{:S(2)}, u32[]{:S(2)}) collective-permute-start(bf16[16,4224]{1,0:T(8,128)(2,1)S(1)} %fusion.1), channel_id=1, source_target_pairs={{0,2},{2,4},{4,6},{6,8},{8,10},{10,12},{12,14},{14,16},{16,18},{18... | collective-permute-start | bytes 405512 | tf_op jit(solution)/shard_map/ppermute | solution.py:166
  22.2 0.0 all-gather.2.cloned.1.call-update
  22.2 0.0 copy-start.1
  22.2 0.0 copy-start.2
  22.2 0.0 copy-start.3
  22.3 0.2 collective-permute-done
  22.5 5.3 %collective-permute-start.1 = (bf16[16,4224]{1,0:T(8,128)(2,1)S(1)}, bf16[16,4224]{1,0:T(8,128)(2,1)S(1)}, u32[]{:S(2)}, u32[]{:S(2)}) collective-permute-start(bf16[16,4224]{1,0:T(8,128)(2,1)S(1)} %collective-permute-done), channel_id=1, source_target_pairs={{0,30},{2,0},{4,2},{6,4},{8,6},{10,8},{12,10},{14,12},{16,14},{18,... | collective-permute-start | bytes 405512 | tf_op jit(solution)/shard_map/ppermute | solution.py:163
  27.8 0.0 collective-permute-done.8
  27.8 1.9 %collective-permute-start.9 = (bf16[16,4224]{1,0:T(8,128)(2,1)S(1)}, bf16[16,4224]{1,0:T(8,128)(2,1)S(1)}, u32[]{:S(2)}, u32[]{:S(2)}) collective-permute-start(bf16[16,4224]{1,0:T(8,128)(2,1)S(1)} %collective-permute-done.8), channel_id=1, source_target_pairs={{0,2},{2,4},{4,6},{6,8},{8,10},{10,12},{12,14},{14,16},{16,18},{18... | collective-permute-start | bytes 405512 | tf_op jit(solution)/shard_map/ppermute | solution.py:166
  29.7 0.0 collective-permute-done.1
  29.8 5.0 %collective-permute-start.2 = (bf16[16,4224]{1,0:T(8,128)(2,1)S(1)}, bf16[16,4224]{1,0:T(8,128)(2,1)S(1)}, u32[]{:S(2)}, u32[]{:S(2)}) collective-permute-start(bf16[16,4224]{1,0:T(8,128)(2,1)S(1)} %collective-permute-done.1), channel_id=1, source_target_pairs={{0,30},{2,0},{4,2},{6,4},{8,6},{10,8},{12,10},{14,12},{16,14},{18,... | collective-permute-start | bytes 405512 | tf_op jit(solution)/shard_map/ppermute | solution.py:163
  34.7 0.0 collective-permute-done.9
  34.8 1.9 %collective-permute-start.10 = (bf16[16,4224]{1,0:T(8,128)(2,1)S(1)}, bf16[16,4224]{1,0:T(8,128)(2,1)S(1)}, u32[]{:S(2)}, u32[]{:S(2)}) collective-permute-start(bf16[16,4224]{1,0:T(8,128)(2,1)S(1)} %collective-permute-done.9), channel_id=1, source_target_pairs={{0,2},{2,4},{4,6},{6,8},{8,10},{10,12},{12,14},{14,16},{16,18},{18... | collective-permute-start | bytes 405512 | tf_op jit(solution)/shard_map/ppermute | solution.py:166
  36.7 0.8 collective-permute-done.2
  37.5 5.0 %collective-permute-start.3 = (bf16[16,4224]{1,0:T(8,128)(2,1)S(1)}, bf16[16,4224]{1,0:T(8,128)(2,1)S(1)}, u32[]{:S(2)}, u32[]{:S(2)}) collective-permute-start(bf16[16,4224]{1,0:T(8,128)(2,1)S(1)} %collective-permute-done.2), channel_id=1, source_target_pairs={{0,30},{2,0},{4,2},{6,4},{8,6},{10,8},{12,10},{14,12},{16,14},{18,... | collective-permute-start | bytes 405512 | tf_op jit(solution)/shard_map/ppermute | solution.py:163
  42.5 2.3 %collective-permute-done.10 = bf16[16,4224]{1,0:T(8,128)(2,1)S(1)} collective-permute-done((bf16[16,4224]{1,0:T(8,128)(2,1)S(1)}, bf16[16,4224]{1,0:T(8,128)(2,1)S(1)}, u32[]{:S(2)}, u32[]{:S(2)}) %collective-permute-start.10) | collective-permute-done | bytes 135200 | tf_op jit(solution)/shard_map/ppermute | solution.py:166
  44.8 1.9 %collective-permute-start.11 = (bf16[16,4224]{1,0:T(8,128)(2,1)S(1)}, bf16[16,4224]{1,0:T(8,128)(2,1)S(1)}, u32[]{:S(2)}, u32[]{:S(2)}) collective-permute-start(bf16[16,4224]{1,0:T(8,128)(2,1)S(1)} %collective-permute-done.10), channel_id=1, source_target_pairs={{0,2},{2,4},{4,6},{6,8},{8,10},{10,12},{12,14},{14,16},{16,18},{18... | collective-permute-start | bytes 405512 | tf_op jit(solution)/shard_map/ppermute | solution.py:166
  46.8 0.0 collective-permute-done.3
  46.8 4.9 %collective-permute-start.4 = (bf16[16,4224]{1,0:T(8,128)(2,1)S(1)}, bf16[16,4224]{1,0:T(8,128)(2,1)S(1)}, u32[]{:S(2)}, u32[]{:S(2)}) collective-permute-start(bf16[16,4224]{1,0:T(8,128)(2,1)S(1)} %collective-permute-done.3), channel_id=1, source_target_pairs={{0,30},{2,0},{4,2},{6,4},{8,6},{10,8},{12,10},{14,12},{16,14},{18,... | collective-permute-start | bytes 405512 | tf_op jit(solution)/shard_map/ppermute | solution.py:163
  51.7 2.3 %collective-permute-done.11 = bf16[16,4224]{1,0:T(8,128)(2,1)S(1)} collective-permute-done((bf16[16,4224]{1,0:T(8,128)(2,1)S(1)}, bf16[16,4224]{1,0:T(8,128)(2,1)S(1)}, u32[]{:S(2)}, u32[]{:S(2)}) %collective-permute-start.11) | collective-permute-done | bytes 135200 | tf_op jit(solution)/shard_map/ppermute | solution.py:166
  54.0 1.9 %collective-permute-start.12 = (bf16[16,4224]{1,0:T(8,128)(2,1)S(1)}, bf16[16,4224]{1,0:T(8,128)(2,1)S(1)}, u32[]{:S(2)}, u32[]{:S(2)}) collective-permute-start(bf16[16,4224]{1,0:T(8,128)(2,1)S(1)} %collective-permute-done.11), channel_id=1, source_target_pairs={{0,2},{2,4},{4,6},{6,8},{8,10},{10,12},{12,14},{14,16},{16,18},{18... | collective-permute-start | bytes 405512 | tf_op jit(solution)/shard_map/ppermute | solution.py:166
  55.9 0.0 collective-permute-done.4
  55.9 4.6 %collective-permute-start.5 = (bf16[16,4224]{1,0:T(8,128)(2,1)S(1)}, bf16[16,4224]{1,0:T(8,128)(2,1)S(1)}, u32[]{:S(2)}, u32[]{:S(2)}) collective-permute-start(bf16[16,4224]{1,0:T(8,128)(2,1)S(1)} %collective-permute-done.4), channel_id=1, source_target_pairs={{0,30},{2,0},{4,2},{6,4},{8,6},{10,8},{12,10},{14,12},{16,14},{18,... | collective-permute-start | bytes 405512 | tf_op jit(solution)/shard_map/ppermute | solution.py:163
  60.5 2.0 %collective-permute-done.12 = bf16[16,4224]{1,0:T(8,128)(2,1)S(1)} collective-permute-done((bf16[16,4224]{1,0:T(8,128)(2,1)S(1)}, bf16[16,4224]{1,0:T(8,128)(2,1)S(1)}, u32[]{:S(2)}, u32[]{:S(2)}) %collective-permute-start.12) | collective-permute-done | bytes 135200 | tf_op jit(solution)/shard_map/ppermute | solution.py:166
  62.5 1.9 %collective-permute-start.13 = (bf16[16,4224]{1,0:T(8,128)(2,1)S(1)}, bf16[16,4224]{1,0:T(8,128)(2,1)S(1)}, u32[]{:S(2)}, u32[]{:S(2)}) collective-permute-start(bf16[16,4224]{1,0:T(8,128)(2,1)S(1)} %collective-permute-done.12), channel_id=1, source_target_pairs={{0,2},{2,4},{4,6},{6,8},{8,10},{10,12},{12,14},{14,16},{16,18},{18... | collective-permute-start | bytes 405512 | tf_op jit(solution)/shard_map/ppermute | solution.py:166
  64.5 0.0 collective-permute-done.5
  64.5 4.6 %collective-permute-start.6 = (bf16[16,4224]{1,0:T(8,128)(2,1)S(1)}, bf16[16,4224]{1,0:T(8,128)(2,1)S(1)}, u32[]{:S(2)}, u32[]{:S(2)}) collective-permute-start(bf16[16,4224]{1,0:T(8,128)(2,1)S(1)} %collective-permute-done.5), channel_id=1, source_target_pairs={{0,30},{2,0},{4,2},{6,4},{8,6},{10,8},{12,10},{14,12},{16,14},{18,... | collective-permute-start | bytes 405512 | tf_op jit(solution)/shard_map/ppermute | solution.py:163
  69.1 2.3 %collective-permute-done.13 = bf16[16,4224]{1,0:T(8,128)(2,1)S(1)} collective-permute-done((bf16[16,4224]{1,0:T(8,128)(2,1)S(1)}, bf16[16,4224]{1,0:T(8,128)(2,1)S(1)}, u32[]{:S(2)}, u32[]{:S(2)}) %collective-permute-start.13) | collective-permute-done | bytes 135200 | tf_op jit(solution)/shard_map/ppermute | solution.py:166
  71.3 1.9 %collective-permute-start.14 = (bf16[16,4224]{1,0:T(8,128)(2,1)S(1)}, bf16[16,4224]{1,0:T(8,128)(2,1)S(1)}, u32[]{:S(2)}, u32[]{:S(2)}) collective-permute-start(bf16[16,4224]{1,0:T(8,128)(2,1)S(1)} %collective-permute-done.13), channel_id=1, source_target_pairs={{0,2},{2,4},{4,6},{6,8},{8,10},{10,12},{12,14},{14,16},{16,18},{18... | collective-permute-start | bytes 405512 | tf_op jit(solution)/shard_map/ppermute | solution.py:166
  73.2 0.0 collective-permute-done.6
  73.3 4.6 %collective-permute-start.7 = (bf16[16,4224]{1,0:T(8,128)(2,1)S(1)}, bf16[16,4224]{1,0:T(8,128)(2,1)S(1)}, u32[]{:S(2)}, u32[]{:S(2)}) collective-permute-start(bf16[16,4224]{1,0:T(8,128)(2,1)S(1)} %collective-permute-done.6), channel_id=1, source_target_pairs={{0,30},{2,0},{4,2},{6,4},{8,6},{10,8},{12,10},{14,12},{16,14},{18,... | collective-permute-start | bytes 405512 | tf_op jit(solution)/shard_map/ppermute | solution.py:163
  77.9 4.9 %collective-permute-done.7 = bf16[16,4224]{1,0:T(8,128)(2,1)S(1)} collective-permute-done((bf16[16,4224]{1,0:T(8,128)(2,1)S(1)}, bf16[16,4224]{1,0:T(8,128)(2,1)S(1)}, u32[]{:S(2)}, u32[]{:S(2)}) %collective-permute-start.7) | collective-permute-done | bytes 135200 | tf_op jit(solution)/shard_map/ppermute | solution.py:163
  82.8 0.0 collective-permute-done.14
  83.0 10.5 %collective-permute-start.15 = (bf16[16,16,4224]{2,1,0:T(8,128)(2,1)S(1)}, bf16[16,16,4224]{2,1,0:T(8,128)(2,1)}, u32[]{:S(2)}, u32[]{:S(2)}) collective-permute-start(bf16[16,16,4224]{2,1,0:T(8,128)(2,1)S(1)} %bitcast_dynamic-update-slice_fusion.own_ref), channel_id=1, source_target_pairs={{0,1},{1,0},{2,3},{3,2},{4,5},{5,4},{6,7},{7,6},{8,9},{9,8},{10,11... | collective-permute-start | bytes 6488072 | tf_op jit(solution)/shard_map/ppermute | solution.py:183
  93.4 0.7 copy.12.bias_ref
  94.1 0.7 copy.13.gain_ref
  94.8 0.7 copy.14.shift_ref
  95.5 5.2 %all-gather.2.cloned.1.call-done = bf16[64,48,1024]{2,1,0:T(8,128)(2,1)} async-done(((bf16[2,48,1024]{2,1,0:T(8,128)(2,1)}), bf16[64,48,1024]{2,1,0:T(8,128)(2,1)}) %all-gather.2.cloned.1.call-update) | async-done | bytes 6291472 | tf_op jit(solution)/shard_map/all_gather | solution.py:178
  100.7 7.3 %shard_map.73 = bf16[16,32,192]{2,1,0:T(8,128)(2,1)} custom-call(bf16[3072,1024]{1,0:T(8,128)(2,1)} %bitcast.45, bf16[288,1024]{1,0:T(8,128)(2,1)} %bitcast.47, f32[32,1]{1,0:T(8,128)} %copy.12.bias_ref, f32[32,1]{1,0:T(8,128)} %copy.13.gain_ref, f32[32,1]{1,0:T(8,128)} %copy.14.shift_ref), custom_call_target="tpu_custom_call" | custom-call | flops 1811939328 | bytes 7077888 | tf_op jit(solution)/shard_map/pallas_call | solution.py:62
  108.0 9.7 %all-to-all-start = ((bf16[16,32,192]{2,1,0:T(8,128)(2,1)}), bf16[16,32,192]{2,1,0:T(8,128)(2,1)S(1)}, u32[]{:S(2)}, u32[]{:S(2)}) async-start(bf16[16,32,192]{2,1,0:T(8,128)(2,1)} %shard_map.73), calls=%async_computation | async-start | bytes 524288 | tf_op jit(solution)/shard_map/all_to_all | solution.py:188
  117.8 0.7 pad_add_fusion.index_ref
  118.4 4.6 %shard_map.74.wnat_ref = bf16[512,4224]{1,0:T(8,128)(2,1)} custom-call(s32[2]{0:T(128)} %pad_add_fusion.index_ref, bf16[16,16,4224]{2,1,0:T(8,128)(2,1)} %copy-done, bf16[16,16,4224]{2,1,0:T(8,128)(2,1)} %collective-permute-done.15.other_ref), custom_call_target="tpu_custom_call" | custom-call | bytes 8650752 | tf_op jit(solution)/shard_map/pallas_call | solution.py:93
  123.0 9.2 %all-to-all-done = bf16[16,32,192]{2,1,0:T(8,128)(2,1)S(1)} async-done(((bf16[16,32,192]{2,1,0:T(8,128)(2,1)}), bf16[16,32,192]{2,1,0:T(8,128)(2,1)S(1)}, u32[]{:S(2)}, u32[]{:S(2)}) %all-to-all-start) | async-done | bytes 196640 | tf_op jit(solution)/shard_map/all_to_all | solution.py:188
  132.2 6.7 %all_gather.7.act_ref = bf16[1024,192]{1,0:T(8,128)(2,1)} all-gather(bf16[512,192]{1,0:T(8,128)(2,1)S(1)} %bitcast.46), channel_id=1, replica_groups=mesh['grp'=16,'z'=16,'core'=2] {'core'}, dimensions={0}, use_global_device_ids=true | all-gather | bytes 589824 | tf_op jit(solution)/shard_map/all_gather | solution.py:190
  138.9 5.0 %shard_map.75 = bf16[4,96,512]{2,1,0:T(8,128)(2,1)} custom-call(s32[2]{0:T(128)} %pad_add_fusion.index_ref, bf16[1024,192]{1,0:T(8,128)(2,1)} %all_gather.7.act_ref, bf16[512,4224]{1,0:T(8,128)(2,1)} %shard_map.74.wnat_ref), custom_call_target="tpu_custom_call" | custom-call | flops 805306368 | bytes 5111808 | tf_op jit(solution)/shard_map/pallas_call | solution.py:144
  (24 shorter events, 0.3 us)
Async XLA Ops:
  6.5 94.1 %all-gather.2.cloned.1.call-start = ((), (), s32[]{:S(2)}) async-start(), calls=%async_computation.1 | async-start | bytes 6488064 | tf_op jit(solution)/shard_map/all_gather | solution.py:178
  8.3 14.2 %collective-permute-start = (bf16[16,4224]{1,0:T(8,128)(2,1)S(1)}, bf16[16,4224]{1,0:T(8,128)(2,1)S(1)}, u32[]{:S(2)}, u32[]{:S(2)}) collective-permute-start(bf16[16,4224]{1,0:T(8,128)(2,1)S(1)} %fusion.1), channel_id=1, source_target_pairs={{0,30},{2,0},{4,2},{6,4},{8,6},{10,8},{12,10},{14,12},{16,14},{18,... | collective-permute-start | bytes 405512 | tf_op jit(solution)/shard_map/ppermute | solution.py:163
  20.2 7.5 %collective-permute-start.8 = (bf16[16,4224]{1,0:T(8,128)(2,1)S(1)}, bf16[16,4224]{1,0:T(8,128)(2,1)S(1)}, u32[]{:S(2)}, u32[]{:S(2)}) collective-permute-start(bf16[16,4224]{1,0:T(8,128)(2,1)S(1)} %fusion.1), channel_id=1, source_target_pairs={{0,2},{2,4},{4,6},{6,8},{8,10},{10,12},{12,14},{14,16},{16,18},{18... | collective-permute-start | bytes 405512 | tf_op jit(solution)/shard_map/ppermute | solution.py:166
  22.2 71.2 %copy-start.1 = (f32[32]{0:T(128)S(1)}, f32[32]{0:T(128)}, u32[]{:S(2)}) copy-start(f32[32]{0:T(128)} %param.9) | copy-start | bytes 388
  22.2 71.9 %copy-start.2 = (f32[32]{0:T(128)S(1)}, f32[32]{0:T(128)}, u32[]{:S(2)}) copy-start(f32[32]{0:T(128)} %param.10) | copy-start | bytes 388
  22.2 72.6 %copy-start.3 = (f32[32]{0:T(128)S(1)}, f32[32]{0:T(128)}, u32[]{:S(2)}) copy-start(f32[32]{0:T(128)} %param.11) | copy-start | bytes 388
  22.5 7.3 %collective-permute-start.1 = (bf16[16,4224]{1,0:T(8,128)(2,1)S(1)}, bf16[16,4224]{1,0:T(8,128)(2,1)S(1)}, u32[]{:S(2)}, u32[]{:S(2)}) collective-permute-start(bf16[16,4224]{1,0:T(8,128)(2,1)S(1)} %collective-permute-done), channel_id=1, source_target_pairs={{0,30},{2,0},{4,2},{6,4},{8,6},{10,8},{12,10},{14,12},{16,14},{18,... | collective-permute-start | bytes 405512 | tf_op jit(solution)/shard_map/ppermute | solution.py:163
  27.8 7.0 %collective-permute-start.9 = (bf16[16,4224]{1,0:T(8,128)(2,1)S(1)}, bf16[16,4224]{1,0:T(8,128)(2,1)S(1)}, u32[]{:S(2)}, u32[]{:S(2)}) collective-permute-start(bf16[16,4224]{1,0:T(8,128)(2,1)S(1)} %collective-permute-done.8), channel_id=1, source_target_pairs={{0,2},{2,4},{4,6},{6,8},{8,10},{10,12},{12,14},{14,16},{16,18},{18... | collective-permute-start | bytes 405512 | tf_op jit(solution)/shard_map/ppermute | solution.py:166
  29.8 7.7 %collective-permute-start.2 = (bf16[16,4224]{1,0:T(8,128)(2,1)S(1)}, bf16[16,4224]{1,0:T(8,128)(2,1)S(1)}, u32[]{:S(2)}, u32[]{:S(2)}) collective-permute-start(bf16[16,4224]{1,0:T(8,128)(2,1)S(1)} %collective-permute-done.1), channel_id=1, source_target_pairs={{0,30},{2,0},{4,2},{6,4},{8,6},{10,8},{12,10},{14,12},{16,14},{18,... | collective-permute-start | bytes 405512 | tf_op jit(solution)/shard_map/ppermute | solution.py:163
  34.8 10.1 %collective-permute-start.10 = (bf16[16,4224]{1,0:T(8,128)(2,1)S(1)}, bf16[16,4224]{1,0:T(8,128)(2,1)S(1)}, u32[]{:S(2)}, u32[]{:S(2)}) collective-permute-start(bf16[16,4224]{1,0:T(8,128)(2,1)S(1)} %collective-permute-done.9), channel_id=1, source_target_pairs={{0,2},{2,4},{4,6},{6,8},{8,10},{10,12},{12,14},{14,16},{16,18},{18... | collective-permute-start | bytes 405512 | tf_op jit(solution)/shard_map/ppermute | solution.py:166
  37.5 9.3 %collective-permute-start.3 = (bf16[16,4224]{1,0:T(8,128)(2,1)S(1)}, bf16[16,4224]{1,0:T(8,128)(2,1)S(1)}, u32[]{:S(2)}, u32[]{:S(2)}) collective-permute-start(bf16[16,4224]{1,0:T(8,128)(2,1)S(1)} %collective-permute-done.2), channel_id=1, source_target_pairs={{0,30},{2,0},{4,2},{6,4},{8,6},{10,8},{12,10},{14,12},{16,14},{18,... | collective-permute-start | bytes 405512 | tf_op jit(solution)/shard_map/ppermute | solution.py:163
  44.8 9.2 %collective-permute-start.11 = (bf16[16,4224]{1,0:T(8,128)(2,1)S(1)}, bf16[16,4224]{1,0:T(8,128)(2,1)S(1)}, u32[]{:S(2)}, u32[]{:S(2)}) collective-permute-start(bf16[16,4224]{1,0:T(8,128)(2,1)S(1)} %collective-permute-done.10), channel_id=1, source_target_pairs={{0,2},{2,4},{4,6},{6,8},{8,10},{10,12},{12,14},{14,16},{16,18},{18... | collective-permute-start | bytes 405512 | tf_op jit(solution)/shard_map/ppermute | solution.py:166
  46.8 9.1 %collective-permute-start.4 = (bf16[16,4224]{1,0:T(8,128)(2,1)S(1)}, bf16[16,4224]{1,0:T(8,128)(2,1)S(1)}, u32[]{:S(2)}, u32[]{:S(2)}) collective-permute-start(bf16[16,4224]{1,0:T(8,128)(2,1)S(1)} %collective-permute-done.3), channel_id=1, source_target_pairs={{0,30},{2,0},{4,2},{6,4},{8,6},{10,8},{12,10},{14,12},{16,14},{18,... | collective-permute-start | bytes 405512 | tf_op jit(solution)/shard_map/ppermute | solution.py:163
  54.0 8.5 %collective-permute-start.12 = (bf16[16,4224]{1,0:T(8,128)(2,1)S(1)}, bf16[16,4224]{1,0:T(8,128)(2,1)S(1)}, u32[]{:S(2)}, u32[]{:S(2)}) collective-permute-start(bf16[16,4224]{1,0:T(8,128)(2,1)S(1)} %collective-permute-done.11), channel_id=1, source_target_pairs={{0,2},{2,4},{4,6},{6,8},{8,10},{10,12},{12,14},{14,16},{16,18},{18... | collective-permute-start | bytes 405512 | tf_op jit(solution)/shard_map/ppermute | solution.py:166
  55.9 8.5 %collective-permute-start.5 = (bf16[16,4224]{1,0:T(8,128)(2,1)S(1)}, bf16[16,4224]{1,0:T(8,128)(2,1)S(1)}, u32[]{:S(2)}, u32[]{:S(2)}) collective-permute-start(bf16[16,4224]{1,0:T(8,128)(2,1)S(1)} %collective-permute-done.4), channel_id=1, source_target_pairs={{0,30},{2,0},{4,2},{6,4},{8,6},{10,8},{12,10},{14,12},{16,14},{18,... | collective-permute-start | bytes 405512 | tf_op jit(solution)/shard_map/ppermute | solution.py:163
  62.5 8.8 %collective-permute-start.13 = (bf16[16,4224]{1,0:T(8,128)(2,1)S(1)}, bf16[16,4224]{1,0:T(8,128)(2,1)S(1)}, u32[]{:S(2)}, u32[]{:S(2)}) collective-permute-start(bf16[16,4224]{1,0:T(8,128)(2,1)S(1)} %collective-permute-done.12), channel_id=1, source_target_pairs={{0,2},{2,4},{4,6},{6,8},{8,10},{10,12},{12,14},{14,16},{16,18},{18... | collective-permute-start | bytes 405512 | tf_op jit(solution)/shard_map/ppermute | solution.py:166
  64.5 8.8 %collective-permute-start.6 = (bf16[16,4224]{1,0:T(8,128)(2,1)S(1)}, bf16[16,4224]{1,0:T(8,128)(2,1)S(1)}, u32[]{:S(2)}, u32[]{:S(2)}) collective-permute-start(bf16[16,4224]{1,0:T(8,128)(2,1)S(1)} %collective-permute-done.5), channel_id=1, source_target_pairs={{0,30},{2,0},{4,2},{6,4},{8,6},{10,8},{12,10},{14,12},{16,14},{18,... | collective-permute-start | bytes 405512 | tf_op jit(solution)/shard_map/ppermute | solution.py:163
  71.3 11.5 %collective-permute-start.14 = (bf16[16,4224]{1,0:T(8,128)(2,1)S(1)}, bf16[16,4224]{1,0:T(8,128)(2,1)S(1)}, u32[]{:S(2)}, u32[]{:S(2)}) collective-permute-start(bf16[16,4224]{1,0:T(8,128)(2,1)S(1)} %collective-permute-done.13), channel_id=1, source_target_pairs={{0,2},{2,4},{4,6},{6,8},{8,10},{10,12},{12,14},{14,16},{16,18},{18... | collective-permute-start | bytes 405512 | tf_op jit(solution)/shard_map/ppermute | solution.py:166
  73.3 9.5 %collective-permute-start.7 = (bf16[16,4224]{1,0:T(8,128)(2,1)S(1)}, bf16[16,4224]{1,0:T(8,128)(2,1)S(1)}, u32[]{:S(2)}, u32[]{:S(2)}) collective-permute-start(bf16[16,4224]{1,0:T(8,128)(2,1)S(1)} %collective-permute-done.6), channel_id=1, source_target_pairs={{0,30},{2,0},{4,2},{6,4},{8,6},{10,8},{12,10},{14,12},{16,14},{18,... | collective-permute-start | bytes 405512 | tf_op jit(solution)/shard_map/ppermute | solution.py:163
  82.9 25.0 %copy-start = (bf16[16,16,4224]{2,1,0:T(8,128)(2,1)}, bf16[16,16,4224]{2,1,0:T(8,128)(2,1)S(1)}, u32[]{:S(2)}) copy-start(bf16[16,16,4224]{2,1,0:T(8,128)(2,1)S(1)} %bitcast_dynamic-update-slice_fusion.own_ref) | copy-start | bytes 6488068
  83.0 35.5 %collective-permute-start.15 = (bf16[16,16,4224]{2,1,0:T(8,128)(2,1)S(1)}, bf16[16,16,4224]{2,1,0:T(8,128)(2,1)}, u32[]{:S(2)}, u32[]{:S(2)}) collective-permute-start(bf16[16,16,4224]{2,1,0:T(8,128)(2,1)S(1)} %bitcast_dynamic-update-slice_fusion.own_ref), channel_id=1, source_target_pairs={{0,1},{1,0},{2,3},{3,2},{4,5},{5,4},{6,7},{7,6},{8,9},{9,8},{10,11... | collective-permute-start | bytes 6488072 | tf_op jit(solution)/shard_map/ppermute | solution.py:183
  108.0 24.2 %all-to-all-start = ((bf16[16,32,192]{2,1,0:T(8,128)(2,1)}), bf16[16,32,192]{2,1,0:T(8,128)(2,1)S(1)}, u32[]{:S(2)}, u32[]{:S(2)}) async-start(bf16[16,32,192]{2,1,0:T(8,128)(2,1)} %shard_map.73), calls=%async_computation | async-start | bytes 524288 | tf_op jit(solution)/shard_map/all_to_all | solution.py:188
Sparse Core Ops, SparseCore 0:
  22.3 78.3 all-gather.1

commit v17 on v15

--- a/solution.py
+++ b/solution.py
@@ -13,8 +13,8 @@
 def conv_norm_kernel(x_ref, w_ref, bias_ref, gain_ref, shift_ref, out_ref, *, height, width_cols):
     outputs = out_ref.shape[1]
     positions = height * width_cols
-    taps = lax.dot_general(w_ref[...], x_ref[...], (((1,), (1,)), ((), ())),
-                           preferred_element_type=jnp.float32)
+    taps = jnp.transpose(lax.dot_general(x_ref[...], w_ref[...], (((1,), (0,)), ((), ())),
+                                         preferred_element_type=jnp.float32))
     pos = lax.broadcasted_iota(jnp.int32, (1, positions), 1)
     row = pos // width_cols
     col = pos % width_cols
@@ -48,6 +48,7 @@
     outputs = conv_weight.shape[0]
     x = whole.reshape(height * width_cols, channels)
     w = jnp.transpose(conv_weight.reshape(outputs, 9, channels), (1, 0, 2)).reshape(9 * outputs, channels)
+    w = jnp.transpose(jnp.pad(w, ((0, -(-9 * outputs // 128) * 128 - 9 * outputs), (0, 0))))
     col = lambda v: v.astype(jnp.float32).reshape(outputs, 1)
     vmem = pl.BlockSpec(memory_space=pltpu.VMEM)
     return pl.pallas_call(

time: 151 us -> 155 us (1.026)
  Pallas kernels: 16 us -> 19.3 us
    pallas_call x1, Pallas kernels: 6.4 us -> 9.76 us  [conv_norm(): pl.pallas_call(functools.partial(conv_norm_kernel, height=height, width_c...]
    ppermute x1, starting transfers between devices: 10.5 us -> 8.64 us  [body(): packed_other = lax.ppermute(packed_z, 'core', [(0, 1), (1, 0)])]
  transfers between devices with their start and end apart: 18 -> 18, of which waited for: 9 -> 9; matrix products, arithmetic and copies ran while one was open for 2% -> 3% of each run, Pallas kernels for 7% -> 9%
where the time goes in v17:
time: 155 us
  starting transfers between devices  79 us (51%)
  waiting for transfers between devices  29.8 us (19%)
  Pallas kernels  19.3 us (12%)
  between operations  13.7 us (9%)
  blocking collectives  6.66 us (4%)
  local copies, waits for them, and re-layouts  5.39 us (3%)
    ppermute x8, starting transfers between devices, ring_gather(): ahead = lax.ppermute(ahead, axis, step_up)  45.8 us
    ppermute x7, starting transfers between devices, ring_gather(): behind = lax.ppermute(behind, axis, step_down)  13.4 us
    all_to_all x1, starting transfers between devices, body(): lax.all_to_all(activated, 'z', split_axis=0, concat_axis=0, tiled=True)  11.2 us
    pallas_call x1, Pallas kernels, conv_norm(): pl.pallas_call(functools.partial(conv_norm_kernel, height=height, width_c...  9.76 us
    all_to_all x1, waiting for transfers between devices, body(): lax.all_to_all(activated, 'z', split_axis=0, concat_axis=0, tiled=True)  9.2 us
    ppermute x7, waiting for transfers between devices, ring_gather(): behind = lax.ppermute(behind, axis, step_down)  9.19 us
    ppermute x1, starting transfers between devices, body(): packed_other = lax.ppermute(packed_z, 'core', [(0, 1), (1, 0)])  8.64 us
    all_gather x1, blocking collectives, body(): both = lax.all_gather(chip_rows, 'core', axis=0, tiled=True)  6.66 us
  transfers between devices with their start and end apart: 18, of which 9 were waited for; matrix products, arithmetic and copies ran while one was open for 3% of the time, Pallas kernels for 9%

profile of v17, /device:TPU:1, one launch (start us, length us, event | category | flops | bytes accessed | tf_op | source)
XLA Modules:
  0.0 154.6 jit_solution(15068884028286557679)
XLA Ops:
  6.5 0.7 copy.22
  7.3 1.0 reshape.31
  8.3 12.0 %collective-permute-start = (bf16[16,4224]{1,0:T(8,128)(2,1)S(1)}, bf16[16,4224]{1,0:T(8,128)(2,1)S(1)}, u32[]{:S(2)}, u32[]{:S(2)}) collective-permute-start(bf16[16,4224]{1,0:T(8,128)(2,1)S(1)} %fusion.1), channel_id=1, source_target_pairs={{0,30},{2,0},{4,2},{6,4},{8,6},{10,8},{12,10},{14,12},{16,14},{18,... | collective-permute-start | bytes 405512 | tf_op jit(solution)/shard_map/ppermute | solution.py:152
  20.2 1.9 %collective-permute-start.8 = (bf16[16,4224]{1,0:T(8,128)(2,1)S(1)}, bf16[16,4224]{1,0:T(8,128)(2,1)S(1)}, u32[]{:S(2)}, u32[]{:S(2)}) collective-permute-start(bf16[16,4224]{1,0:T(8,128)(2,1)S(1)} %fusion.1), channel_id=1, source_target_pairs={{0,2},{2,4},{4,6},{6,8},{8,10},{10,12},{12,14},{14,16},{16,18},{18... | collective-permute-start | bytes 405512 | tf_op jit(solution)/shard_map/ppermute | solution.py:155
  22.2 0.0 all-gather.2.cloned.1.call-update
  22.2 0.0 copy-start.1
  22.2 0.2 collective-permute-done
  22.5 5.3 %collective-permute-start.1 = (bf16[16,4224]{1,0:T(8,128)(2,1)S(1)}, bf16[16,4224]{1,0:T(8,128)(2,1)S(1)}, u32[]{:S(2)}, u32[]{:S(2)}) collective-permute-start(bf16[16,4224]{1,0:T(8,128)(2,1)S(1)} %collective-permute-done), channel_id=1, source_target_pairs={{0,30},{2,0},{4,2},{6,4},{8,6},{10,8},{12,10},{14,12},{16,14},{18,... | collective-permute-start | bytes 405512 | tf_op jit(solution)/shard_map/ppermute | solution.py:152
  27.8 0.0 collective-permute-done.8
  27.8 1.9 %collective-permute-start.9 = (bf16[16,4224]{1,0:T(8,128)(2,1)S(1)}, bf16[16,4224]{1,0:T(8,128)(2,1)S(1)}, u32[]{:S(2)}, u32[]{:S(2)}) collective-permute-start(bf16[16,4224]{1,0:T(8,128)(2,1)S(1)} %collective-permute-done.8), channel_id=1, source_target_pairs={{0,2},{2,4},{4,6},{6,8},{8,10},{10,12},{12,14},{14,16},{16,18},{18... | collective-permute-start | bytes 405512 | tf_op jit(solution)/shard_map/ppermute | solution.py:155
  29.7 0.0 collective-permute-done.1
  29.8 5.0 %collective-permute-start.2 = (bf16[16,4224]{1,0:T(8,128)(2,1)S(1)}, bf16[16,4224]{1,0:T(8,128)(2,1)S(1)}, u32[]{:S(2)}, u32[]{:S(2)}) collective-permute-start(bf16[16,4224]{1,0:T(8,128)(2,1)S(1)} %collective-permute-done.1), channel_id=1, source_target_pairs={{0,30},{2,0},{4,2},{6,4},{8,6},{10,8},{12,10},{14,12},{16,14},{18,... | collective-permute-start | bytes 405512 | tf_op jit(solution)/shard_map/ppermute | solution.py:152
  34.8 0.0 collective-permute-done.9
  34.8 1.9 %collective-permute-start.10 = (bf16[16,4224]{1,0:T(8,128)(2,1)S(1)}, bf16[16,4224]{1,0:T(8,128)(2,1)S(1)}, u32[]{:S(2)}, u32[]{:S(2)}) collective-permute-start(bf16[16,4224]{1,0:T(8,128)(2,1)S(1)} %collective-permute-done.9), channel_id=1, source_target_pairs={{0,2},{2,4},{4,6},{6,8},{8,10},{10,12},{12,14},{14,16},{16,18},{18... | collective-permute-start | bytes 405512 | tf_op jit(solution)/shard_map/ppermute | solution.py:155
  36.7 0.8 collective-permute-done.2
  37.5 5.0 %collective-permute-start.3 = (bf16[16,4224]{1,0:T(8,128)(2,1)S(1)}, bf16[16,4224]{1,0:T(8,128)(2,1)S(1)}, u32[]{:S(2)}, u32[]{:S(2)}) collective-permute-start(bf16[16,4224]{1,0:T(8,128)(2,1)S(1)} %collective-permute-done.2), channel_id=1, source_target_pairs={{0,30},{2,0},{4,2},{6,4},{8,6},{10,8},{12,10},{14,12},{16,14},{18,... | collective-permute-start | bytes 405512 | tf_op jit(solution)/shard_map/ppermute | solution.py:152
  42.5 2.4 %collective-permute-done.10 = bf16[16,4224]{1,0:T(8,128)(2,1)S(1)} collective-permute-done((bf16[16,4224]{1,0:T(8,128)(2,1)S(1)}, bf16[16,4224]{1,0:T(8,128)(2,1)S(1)}, u32[]{:S(2)}, u32[]{:S(2)}) %collective-permute-start.10) | collective-permute-done | bytes 135200 | tf_op jit(solution)/shard_map/ppermute | solution.py:155
  44.9 1.9 %collective-permute-start.11 = (bf16[16,4224]{1,0:T(8,128)(2,1)S(1)}, bf16[16,4224]{1,0:T(8,128)(2,1)S(1)}, u32[]{:S(2)}, u32[]{:S(2)}) collective-permute-start(bf16[16,4224]{1,0:T(8,128)(2,1)S(1)} %collective-permute-done.10), channel_id=1, source_target_pairs={{0,2},{2,4},{4,6},{6,8},{8,10},{10,12},{12,14},{14,16},{16,18},{18... | collective-permute-start | bytes 405512 | tf_op jit(solution)/shard_map/ppermute | solution.py:155
  46.8 0.0 collective-permute-done.3
  46.8 4.8 %collective-permute-start.4 = (bf16[16,4224]{1,0:T(8,128)(2,1)S(1)}, bf16[16,4224]{1,0:T(8,128)(2,1)S(1)}, u32[]{:S(2)}, u32[]{:S(2)}) collective-permute-start(bf16[16,4224]{1,0:T(8,128)(2,1)S(1)} %collective-permute-done.3), channel_id=1, source_target_pairs={{0,30},{2,0},{4,2},{6,4},{8,6},{10,8},{12,10},{14,12},{16,14},{18,... | collective-permute-start | bytes 405512 | tf_op jit(solution)/shard_map/ppermute | solution.py:152
  51.7 0.0 copy-start.2
  51.7 0.0 copy-start.3
  51.7 0.0 copy-start.4
  51.7 2.1 %collective-permute-done.11 = bf16[16,4224]{1,0:T(8,128)(2,1)S(1)} collective-permute-done((bf16[16,4224]{1,0:T(8,128)(2,1)S(1)}, bf16[16,4224]{1,0:T(8,128)(2,1)S(1)}, u32[]{:S(2)}, u32[]{:S(2)}) %collective-permute-start.11) | collective-permute-done | bytes 135200 | tf_op jit(solution)/shard_map/ppermute | solution.py:155
  53.8 1.9 %collective-permute-start.12 = (bf16[16,4224]{1,0:T(8,128)(2,1)S(1)}, bf16[16,4224]{1,0:T(8,128)(2,1)S(1)}, u32[]{:S(2)}, u32[]{:S(2)}) collective-permute-start(bf16[16,4224]{1,0:T(8,128)(2,1)S(1)} %collective-permute-done.11), channel_id=1, source_target_pairs={{0,2},{2,4},{4,6},{6,8},{8,10},{10,12},{12,14},{14,16},{16,18},{18... | collective-permute-start | bytes 405512 | tf_op jit(solution)/shard_map/ppermute | solution.py:155
  55.7 4.6 %collective-permute-start.5 = (bf16[16,4224]{1,0:T(8,128)(2,1)S(1)}, bf16[16,4224]{1,0:T(8,128)(2,1)S(1)}, u32[]{:S(2)}, u32[]{:S(2)}) collective-permute-start(bf16[16,4224]{1,0:T(8,128)(2,1)S(1)} %collective-permute-done.4), channel_id=1, source_target_pairs={{0,30},{2,0},{4,2},{6,4},{8,6},{10,8},{12,10},{14,12},{16,14},{18,... | collective-permute-start | bytes 405512 | tf_op jit(solution)/shard_map/ppermute | solution.py:152
  60.3 2.1 %collective-permute-done.12 = bf16[16,4224]{1,0:T(8,128)(2,1)S(1)} collective-permute-done((bf16[16,4224]{1,0:T(8,128)(2,1)S(1)}, bf16[16,4224]{1,0:T(8,128)(2,1)S(1)}, u32[]{:S(2)}, u32[]{:S(2)}) %collective-permute-start.12) | collective-permute-done | bytes 135200 | tf_op jit(solution)/shard_map/ppermute | solution.py:155
  62.5 1.9 %collective-permute-start.13 = (bf16[16,4224]{1,0:T(8,128)(2,1)S(1)}, bf16[16,4224]{1,0:T(8,128)(2,1)S(1)}, u32[]{:S(2)}, u32[]{:S(2)}) collective-permute-start(bf16[16,4224]{1,0:T(8,128)(2,1)S(1)} %collective-permute-done.12), channel_id=1, source_target_pairs={{0,2},{2,4},{4,6},{6,8},{8,10},{10,12},{12,14},{14,16},{16,18},{18... | collective-permute-start | bytes 405512 | tf_op jit(solution)/shard_map/ppermute | solution.py:155
  64.4 4.6 %collective-permute-start.6 = (bf16[16,4224]{1,0:T(8,128)(2,1)S(1)}, bf16[16,4224]{1,0:T(8,128)(2,1)S(1)}, u32[]{:S(2)}, u32[]{:S(2)}) collective-permute-start(bf16[16,4224]{1,0:T(8,128)(2,1)S(1)} %collective-permute-done.5), channel_id=1, source_target_pairs={{0,30},{2,0},{4,2},{6,4},{8,6},{10,8},{12,10},{14,12},{16,14},{18,... | collective-permute-start | bytes 405512 | tf_op jit(solution)/shard_map/ppermute | solution.py:152
  69.0 2.5 %collective-permute-done.13 = bf16[16,4224]{1,0:T(8,128)(2,1)S(1)} collective-permute-done((bf16[16,4224]{1,0:T(8,128)(2,1)S(1)}, bf16[16,4224]{1,0:T(8,128)(2,1)S(1)}, u32[]{:S(2)}, u32[]{:S(2)}) %collective-permute-start.13) | collective-permute-done | bytes 135200 | tf_op jit(solution)/shard_map/ppermute | solution.py:155
  71.6 1.9 %collective-permute-start.14 = (bf16[16,4224]{1,0:T(8,128)(2,1)S(1)}, bf16[16,4224]{1,0:T(8,128)(2,1)S(1)}, u32[]{:S(2)}, u32[]{:S(2)}) collective-permute-start(bf16[16,4224]{1,0:T(8,128)(2,1)S(1)} %collective-permute-done.13), channel_id=1, source_target_pairs={{0,2},{2,4},{4,6},{6,8},{8,10},{10,12},{12,14},{14,16},{16,18},{18... | collective-permute-start | bytes 405512 | tf_op jit(solution)/shard_map/ppermute | solution.py:155
  73.5 0.0 collective-permute-done.6
  73.5 4.6 %collective-permute-start.7 = (bf16[16,4224]{1,0:T(8,128)(2,1)S(1)}, bf16[16,4224]{1,0:T(8,128)(2,1)S(1)}, u32[]{:S(2)}, u32[]{:S(2)}) collective-permute-start(bf16[16,4224]{1,0:T(8,128)(2,1)S(1)} %collective-permute-done.6), channel_id=1, source_target_pairs={{0,30},{2,0},{4,2},{6,4},{8,6},{10,8},{12,10},{14,12},{16,14},{18,... | collective-permute-start | bytes 405512 | tf_op jit(solution)/shard_map/ppermute | solution.py:152
  78.1 4.4 %collective-permute-done.7 = bf16[16,4224]{1,0:T(8,128)(2,1)S(1)} collective-permute-done((bf16[16,4224]{1,0:T(8,128)(2,1)S(1)}, bf16[16,4224]{1,0:T(8,128)(2,1)S(1)}, u32[]{:S(2)}, u32[]{:S(2)}) %collective-permute-start.7) | collective-permute-done | bytes 135200 | tf_op jit(solution)/shard_map/ppermute | solution.py:152
  82.7 8.6 %collective-permute-start.15 = (bf16[16,16,4224]{2,1,0:T(8,128)(2,1)S(1)}, bf16[16,16,4224]{2,1,0:T(8,128)(2,1)}, u32[]{:S(2)}, u32[]{:S(2)}) collective-permute-start(bf16[16,16,4224]{2,1,0:T(8,128)(2,1)S(1)} %bitcast_dynamic-update-slice_fusion.own_ref), channel_id=1, source_target_pairs={{0,1},{1,0},{2,3},{3,2},{4,5},{5,4},{6,7},{7,6},{8,9},{9,8},{10,11... | collective-permute-start | bytes 6488072 | tf_op jit(solution)/shard_map/ppermute | solution.py:172
  91.3 0.4 copy.18
  91.7 0.7 copy.19.bias_ref
  92.4 0.7 copy.20.gain_ref
  93.1 0.7 copy.21.shift_ref
  93.7 1.0 pad_bitcast_fusion.w_ref
  94.7 5.9 %all-gather.2.cloned.1.call-done = bf16[64,48,1024]{2,1,0:T(8,128)(2,1)} async-done(((bf16[2,48,1024]{2,1,0:T(8,128)(2,1)}), bf16[64,48,1024]{2,1,0:T(8,128)(2,1)}) %all-gather.2.cloned.1.call-update) | async-done | bytes 6291472 | tf_op jit(solution)/shard_map/all_gather | solution.py:167
  100.6 9.8 %shard_map.73 = bf16[16,32,192]{2,1,0:T(8,128)(2,1)} custom-call(bf16[3072,1024]{1,0:T(8,128)(2,1)} %bitcast.47, bf16[1024,384]{1,0:T(8,128)(2,1)} %pad_bitcast_fusion.w_ref, f32[32,1]{1,0:T(8,128)} %copy.19.bias_ref, f32[32,1]{1,0:T(8,128)} %copy.20.gain_ref, f32[32,1]{1,0:T(8,128)} %copy.21.shift_ref), custom_call_target="tpu_custom_call" | custom-call | flops 1811939328 | bytes 7274496 | tf_op jit(solution)/shard_map/pallas_call | solution.py:54
  110.4 11.2 %all-to-all-start = ((bf16[16,32,192]{2,1,0:T(8,128)(2,1)}), bf16[16,32,192]{2,1,0:T(8,128)(2,1)S(1)}, u32[]{:S(2)}, u32[]{:S(2)}) async-start(bf16[16,32,192]{2,1,0:T(8,128)(2,1)} %shard_map.73), calls=%async_computation | async-start | bytes 524288 | tf_op jit(solution)/shard_map/all_to_all | solution.py:177
  121.6 0.7 pad_add_fusion.index_ref
  122.3 4.6 %shard_map.74.wnat_ref = bf16[512,4224]{1,0:T(8,128)(2,1)} custom-call(s32[2]{0:T(128)} %pad_add_fusion.index_ref, bf16[16,16,4224]{2,1,0:T(8,128)(2,1)} %copy-done, bf16[16,16,4224]{2,1,0:T(8,128)(2,1)} %collective-permute-done.15.other_ref), custom_call_target="tpu_custom_call" | custom-call | bytes 8650752 | tf_op jit(solution)/shard_map/pallas_call | solution.py:82
  126.9 9.2 %all-to-all-done = bf16[16,32,192]{2,1,0:T(8,128)(2,1)S(1)} async-done(((bf16[16,32,192]{2,1,0:T(8,128)(2,1)}), bf16[16,32,192]{2,1,0:T(8,128)(2,1)S(1)}, u32[]{:S(2)}, u32[]{:S(2)}) %all-to-all-start) | async-done | bytes 196640 | tf_op jit(solution)/shard_map/all_to_all | solution.py:177
  136.1 6.7 %all_gather.7.act_ref = bf16[1024,192]{1,0:T(8,128)(2,1)} all-gather(bf16[512,192]{1,0:T(8,128)(2,1)S(1)} %bitcast.48), channel_id=1, replica_groups=mesh['grp'=16,'z'=16,'core'=2] {'core'}, dimensions={0}, use_global_device_ids=true | all-gather | bytes 589824 | tf_op jit(solution)/shard_map/all_gather | solution.py:179
  142.7 5.0 %shard_map.75 = bf16[4,96,512]{2,1,0:T(8,128)(2,1)} custom-call(s32[2]{0:T(128)} %pad_add_fusion.index_ref, bf16[1024,192]{1,0:T(8,128)(2,1)} %all_gather.7.act_ref, bf16[512,4224]{1,0:T(8,128)(2,1)} %shard_map.74.wnat_ref), custom_call_target="tpu_custom_call" | custom-call | flops 805306368 | bytes 5111808 | tf_op jit(solution)/shard_map/pallas_call | solution.py:133
  (28 shorter events, 0.3 us)
Async XLA Ops:
  6.5 94.1 %all-gather.2.cloned.1.call-start = ((), (), s32[]{:S(2)}) async-start(), calls=%async_computation.1 | async-start | bytes 6488064 | tf_op jit(solution)/shard_map/all_gather | solution.py:167
  8.3 14.2 %collective-permute-start = (bf16[16,4224]{1,0:T(8,128)(2,1)S(1)}, bf16[16,4224]{1,0:T(8,128)(2,1)S(1)}, u32[]{:S(2)}, u32[]{:S(2)}) collective-permute-start(bf16[16,4224]{1,0:T(8,128)(2,1)S(1)} %fusion.1), channel_id=1, source_target_pairs={{0,30},{2,0},{4,2},{6,4},{8,6},{10,8},{12,10},{14,12},{16,14},{18,... | collective-permute-start | bytes 405512 | tf_op jit(solution)/shard_map/ppermute | solution.py:152
  20.2 7.6 %collective-permute-start.8 = (bf16[16,4224]{1,0:T(8,128)(2,1)S(1)}, bf16[16,4224]{1,0:T(8,128)(2,1)S(1)}, u32[]{:S(2)}, u32[]{:S(2)}) collective-permute-start(bf16[16,4224]{1,0:T(8,128)(2,1)S(1)} %fusion.1), channel_id=1, source_target_pairs={{0,2},{2,4},{4,6},{6,8},{8,10},{10,12},{12,14},{14,16},{16,18},{18... | collective-permute-start | bytes 405512 | tf_op jit(solution)/shard_map/ppermute | solution.py:155
  22.2 69.1 %copy-start.1 = (bf16[32,3,3,1024]{3,0,2,1:T(8,128)(2,1)S(1)}, bf16[32,3,3,1024]{3,0,2,1:T(8,128)(2,1)}, u32[]{:S(2)}) copy-start(bf16[32,3,3,1024]{3,0,2,1:T(8,128)(2,1)} %param.8) | copy-start | bytes 1769476
  22.5 7.3 %collective-permute-start.1 = (bf16[16,4224]{1,0:T(8,128)(2,1)S(1)}, bf16[16,4224]{1,0:T(8,128)(2,1)S(1)}, u32[]{:S(2)}, u32[]{:S(2)}) collective-permute-start(bf16[16,4224]{1,0:T(8,128)(2,1)S(1)} %collective-permute-done), channel_id=1, source_target_pairs={{0,30},{2,0},{4,2},{6,4},{8,6},{10,8},{12,10},{14,12},{16,14},{18,... | collective-permute-start | bytes 405512 | tf_op jit(solution)/shard_map/ppermute | solution.py:152
  27.8 7.0 %collective-permute-start.9 = (bf16[16,4224]{1,0:T(8,128)(2,1)S(1)}, bf16[16,4224]{1,0:T(8,128)(2,1)S(1)}, u32[]{:S(2)}, u32[]{:S(2)}) collective-permute-start(bf16[16,4224]{1,0:T(8,128)(2,1)S(1)} %collective-permute-done.8), channel_id=1, source_target_pairs={{0,2},{2,4},{4,6},{6,8},{8,10},{10,12},{12,14},{14,16},{16,18},{18... | collective-permute-start | bytes 405512 | tf_op jit(solution)/shard_map/ppermute | solution.py:155
  29.8 7.7 %collective-permute-start.2 = (bf16[16,4224]{1,0:T(8,128)(2,1)S(1)}, bf16[16,4224]{1,0:T(8,128)(2,1)S(1)}, u32[]{:S(2)}, u32[]{:S(2)}) collective-permute-start(bf16[16,4224]{1,0:T(8,128)(2,1)S(1)} %collective-permute-done.1), channel_id=1, source_target_pairs={{0,30},{2,0},{4,2},{6,4},{8,6},{10,8},{12,10},{14,12},{16,14},{18,... | collective-permute-start | bytes 405512 | tf_op jit(solution)/shard_map/ppermute | solution.py:152
  34.8 10.1 %collective-permute-start.10 = (bf16[16,4224]{1,0:T(8,128)(2,1)S(1)}, bf16[16,4224]{1,0:T(8,128)(2,1)S(1)}, u32[]{:S(2)}, u32[]{:S(2)}) collective-permute-start(bf16[16,4224]{1,0:T(8,128)(2,1)S(1)} %collective-permute-done.9), channel_id=1, source_target_pairs={{0,2},{2,4},{4,6},{6,8},{8,10},{10,12},{12,14},{14,16},{16,18},{18... | collective-permute-start | bytes 405512 | tf_op jit(solution)/shard_map/ppermute | solution.py:155
  37.5 9.3 %collective-permute-start.3 = (bf16[16,4224]{1,0:T(8,128)(2,1)S(1)}, bf16[16,4224]{1,0:T(8,128)(2,1)S(1)}, u32[]{:S(2)}, u32[]{:S(2)}) collective-permute-start(bf16[16,4224]{1,0:T(8,128)(2,1)S(1)} %collective-permute-done.2), channel_id=1, source_target_pairs={{0,30},{2,0},{4,2},{6,4},{8,6},{10,8},{12,10},{14,12},{16,14},{18,... | collective-permute-start | bytes 405512 | tf_op jit(solution)/shard_map/ppermute | solution.py:152
  44.9 8.9 %collective-permute-start.11 = (bf16[16,4224]{1,0:T(8,128)(2,1)S(1)}, bf16[16,4224]{1,0:T(8,128)(2,1)S(1)}, u32[]{:S(2)}, u32[]{:S(2)}) collective-permute-start(bf16[16,4224]{1,0:T(8,128)(2,1)S(1)} %collective-permute-done.10), channel_id=1, source_target_pairs={{0,2},{2,4},{4,6},{6,8},{8,10},{10,12},{12,14},{14,16},{16,18},{18... | collective-permute-start | bytes 405512 | tf_op jit(solution)/shard_map/ppermute | solution.py:155
  46.8 8.9 %collective-permute-start.4 = (bf16[16,4224]{1,0:T(8,128)(2,1)S(1)}, bf16[16,4224]{1,0:T(8,128)(2,1)S(1)}, u32[]{:S(2)}, u32[]{:S(2)}) collective-permute-start(bf16[16,4224]{1,0:T(8,128)(2,1)S(1)} %collective-permute-done.3), channel_id=1, source_target_pairs={{0,30},{2,0},{4,2},{6,4},{8,6},{10,8},{12,10},{14,12},{16,14},{18,... | collective-permute-start | bytes 405512 | tf_op jit(solution)/shard_map/ppermute | solution.py:152
  51.7 40.0 %copy-start.2 = (f32[32]{0:T(128)S(1)}, f32[32]{0:T(128)}, u32[]{:S(2)}) copy-start(f32[32]{0:T(128)} %param.9) | copy-start | bytes 388
  51.7 40.7 %copy-start.3 = (f32[32]{0:T(128)S(1)}, f32[32]{0:T(128)}, u32[]{:S(2)}) copy-start(f32[32]{0:T(128)} %param.10) | copy-start | bytes 388
  51.7 41.4 %copy-start.4 = (f32[32]{0:T(128)S(1)}, f32[32]{0:T(128)}, u32[]{:S(2)}) copy-start(f32[32]{0:T(128)} %param.11) | copy-start | bytes 388
  53.8 8.7 %collective-permute-start.12 = (bf16[16,4224]{1,0:T(8,128)(2,1)S(1)}, bf16[16,4224]{1,0:T(8,128)(2,1)S(1)}, u32[]{:S(2)}, u32[]{:S(2)}) collective-permute-start(bf16[16,4224]{1,0:T(8,128)(2,1)S(1)} %collective-permute-done.11), channel_id=1, source_target_pairs={{0,2},{2,4},{4,6},{6,8},{8,10},{10,12},{12,14},{14,16},{16,18},{18... | collective-permute-start | bytes 405512 | tf_op jit(solution)/shard_map/ppermute | solution.py:155
  55.7 8.7 %collective-permute-start.5 = (bf16[16,4224]{1,0:T(8,128)(2,1)S(1)}, bf16[16,4224]{1,0:T(8,128)(2,1)S(1)}, u32[]{:S(2)}, u32[]{:S(2)}) collective-permute-start(bf16[16,4224]{1,0:T(8,128)(2,1)S(1)} %collective-permute-done.4), channel_id=1, source_target_pairs={{0,30},{2,0},{4,2},{6,4},{8,6},{10,8},{12,10},{14,12},{16,14},{18,... | collective-permute-start | bytes 405512 | tf_op jit(solution)/shard_map/ppermute | solution.py:152
  62.5 9.1 %collective-permute-start.13 = (bf16[16,4224]{1,0:T(8,128)(2,1)S(1)}, bf16[16,4224]{1,0:T(8,128)(2,1)S(1)}, u32[]{:S(2)}, u32[]{:S(2)}) collective-permute-start(bf16[16,4224]{1,0:T(8,128)(2,1)S(1)} %collective-permute-done.12), channel_id=1, source_target_pairs={{0,2},{2,4},{4,6},{6,8},{8,10},{10,12},{12,14},{14,16},{16,18},{18... | collective-permute-start | bytes 405512 | tf_op jit(solution)/shard_map/ppermute | solution.py:155
  64.4 9.1 %collective-permute-start.6 = (bf16[16,4224]{1,0:T(8,128)(2,1)S(1)}, bf16[16,4224]{1,0:T(8,128)(2,1)S(1)}, u32[]{:S(2)}, u32[]{:S(2)}) collective-permute-start(bf16[16,4224]{1,0:T(8,128)(2,1)S(1)} %collective-permute-done.5), channel_id=1, source_target_pairs={{0,30},{2,0},{4,2},{6,4},{8,6},{10,8},{12,10},{14,12},{16,14},{18,... | collective-permute-start | bytes 405512 | tf_op jit(solution)/shard_map/ppermute | solution.py:152
  71.6 10.9 %collective-permute-start.14 = (bf16[16,4224]{1,0:T(8,128)(2,1)S(1)}, bf16[16,4224]{1,0:T(8,128)(2,1)S(1)}, u32[]{:S(2)}, u32[]{:S(2)}) collective-permute-start(bf16[16,4224]{1,0:T(8,128)(2,1)S(1)} %collective-permute-done.13), channel_id=1, source_target_pairs={{0,2},{2,4},{4,6},{6,8},{8,10},{10,12},{12,14},{14,16},{16,18},{18... | collective-permute-start | bytes 405512 | tf_op jit(solution)/shard_map/ppermute | solution.py:155
  73.5 9.0 %collective-permute-start.7 = (bf16[16,4224]{1,0:T(8,128)(2,1)S(1)}, bf16[16,4224]{1,0:T(8,128)(2,1)S(1)}, u32[]{:S(2)}, u32[]{:S(2)}) collective-permute-start(bf16[16,4224]{1,0:T(8,128)(2,1)S(1)} %collective-permute-done.6), channel_id=1, source_target_pairs={{0,30},{2,0},{4,2},{6,4},{8,6},{10,8},{12,10},{14,12},{16,14},{18,... | collective-permute-start | bytes 405512 | tf_op jit(solution)/shard_map/ppermute | solution.py:152
  82.6 27.8 %copy-start = (bf16[16,16,4224]{2,1,0:T(8,128)(2,1)}, bf16[16,16,4224]{2,1,0:T(8,128)(2,1)S(1)}, u32[]{:S(2)}) copy-start(bf16[16,16,4224]{2,1,0:T(8,128)(2,1)S(1)} %bitcast_dynamic-update-slice_fusion.own_ref) | copy-start | bytes 6488068
  82.7 39.6 %collective-permute-start.15 = (bf16[16,16,4224]{2,1,0:T(8,128)(2,1)S(1)}, bf16[16,16,4224]{2,1,0:T(8,128)(2,1)}, u32[]{:S(2)}, u32[]{:S(2)}) collective-permute-start(bf16[16,16,4224]{2,1,0:T(8,128)(2,1)S(1)} %bitcast_dynamic-update-slice_fusion.own_ref), channel_id=1, source_target_pairs={{0,1},{1,0},{2,3},{3,2},{4,5},{5,4},{6,7},{7,6},{8,9},{9,8},{10,11... | collective-permute-start | bytes 6488072 | tf_op jit(solution)/shard_map/ppermute | solution.py:172
  110.4 25.6 %all-to-all-start = ((bf16[16,32,192]{2,1,0:T(8,128)(2,1)}), bf16[16,32,192]{2,1,0:T(8,128)(2,1)S(1)}, u32[]{:S(2)}, u32[]{:S(2)}) async-start(bf16[16,32,192]{2,1,0:T(8,128)(2,1)} %shard_map.73), calls=%async_computation | async-start | bytes 524288 | tf_op jit(solution)/shard_map/all_to_all | solution.py:177
Sparse Core Ops, SparseCore 0:
  22.3 78.2 all-gather.1

commit v18 on v15

--- a/solution.py
+++ b/solution.py
@@ -101,12 +101,12 @@
         for z in range(chips):
             rows_in = act_ref[pl.ds((c * chips + z) * block, block), :]
             actn_ref[pl.ds((2 * z + c) * block, block), :] = jnp.where(core == 0, rows_in[:, :lanes], rows_in[:, skip:])
-    nn = (((1,), (0,)), ((), ()))
-    sub = lax.broadcasted_iota(jnp.int32, (packed_width - 4 * channels, lanes), 0)
-    ones = jnp.where(sub == 0, 1.0, 0.0).astype(actn_ref.dtype)
-    bias = lax.dot_general(wnat_ref[:, pl.ds(4 * channels, packed_width - 4 * channels)], ones, nn,
+    nt = (((1,), (1,)), ((), ()))
+    lane = lax.broadcasted_iota(jnp.int32, (lanes, packed_width - 4 * channels), 1)
+    ones = jnp.where(lane == 0, 1.0, 0.0).astype(actn_ref.dtype)
+    bias = lax.dot_general(ones, wnat_ref[:, pl.ds(4 * channels, packed_width - 4 * channels)], nt,
                            preferred_element_type=jnp.float32)
-    act = actn_ref[...]
+    act = jnp.transpose(actn_ref[...].astype(jnp.float32)).astype(actn_ref.dtype)
     first = lanes - span
     dest = lax.broadcasted_iota(jnp.int32, (2 * width_cols, 2 * width_cols), 0)
     src = lax.broadcasted_iota(jnp.int32, (2 * width_cols, 2 * width_cols), 1)
@@ -114,9 +114,9 @@
     for a in range(2):
         phases = []
         for b in range(2):
-            res = lax.dot_general(wnat_ref[:, pl.ds((2 * a + b) * channels, channels)], act, nn,
+            res = lax.dot_general(act, wnat_ref[:, pl.ds((2 * a + b) * channels, channels)], nt,
                                   preferred_element_type=jnp.float32)
-            res = jnp.transpose(res + bias).astype(out_ref.dtype)
+            res = (res + bias).astype(out_ref.dtype)
             phases.append(jnp.where(core == 0, res[:span], res[first:]))
         for i in range(rows):
             stacked = jnp.concatenate([p[i * width_cols:(i + 1) * width_cols] for p in phases], axis=0)

time: 151 us -> 151 us (level)
  no operation moved by 1% of the time
where the time goes in v18:
time: 151 us; the launch traced here: 150 us
  starting transfers between devices  79.4 us (53%)
  waiting for transfers between devices  29.3 us (19%)
  Pallas kernels  16.2 us (11%)
  between operations  13.7 us (9%)
  blocking collectives  6.66 us (4%)
  local copies, waits for them, and re-layouts  4.07 us (3%)
    ppermute x8, starting transfers between devices, ring_gather(): ahead = lax.ppermute(ahead, axis, step_up)  45.9 us
    ppermute x7, starting transfers between devices, ring_gather(): behind = lax.ppermute(behind, axis, step_down)  13.4 us
    ppermute x1, starting transfers between devices, body(): packed_other = lax.ppermute(packed_z, 'core', [(0, 1), (1, 0)])  10.5 us
    all_to_all x1, starting transfers between devices, body(): lax.all_to_all(activated, 'z', split_axis=0, concat_axis=0, tiled=True)  9.74 us
    all_to_all x1, waiting for transfers between devices, body(): lax.all_to_all(activated, 'z', split_axis=0, concat_axis=0, tiled=True)  9.21 us
    ppermute x7, waiting for transfers between devices, ring_gather(): behind = lax.ppermute(behind, axis, step_down)  8.94 us
    all_gather x1, blocking collectives, body(): both = lax.all_gather(chip_rows, 'core', axis=0, tiled=True)  6.66 us
    pallas_call x1, Pallas kernels, conv_norm(): pl.pallas_call(functools.partial(conv_norm_kernel, height=height, width_c...  6.4 us
  transfers between devices with their start and end apart: 18, of which 9 were waited for; matrix products, arithmetic and copies ran while one was open for 2% of the time, Pallas kernels for 7%

profile of v18, /device:TPU:1, one launch (start us, length us, event | category | flops | bytes accessed | tf_op | source)
XLA Modules:
  0.0 150.0 jit_solution(9061710142613054336)
XLA Ops:
  6.5 0.7 copy.15
  7.3 1.0 reshape.31
  8.3 12.0 %collective-permute-start = (bf16[16,4224]{1,0:T(8,128)(2,1)S(1)}, bf16[16,4224]{1,0:T(8,128)(2,1)S(1)}, u32[]{:S(2)}, u32[]{:S(2)}) collective-permute-start(bf16[16,4224]{1,0:T(8,128)(2,1)S(1)} %fusion.1), channel_id=1, source_target_pairs={{0,30},{2,0},{4,2},{6,4},{8,6},{10,8},{12,10},{14,12},{16,14},{18,... | collective-permute-start | bytes 405512 | tf_op jit(solution)/shard_map/ppermute | solution.py:151
  20.2 1.9 %collective-permute-start.8 = (bf16[16,4224]{1,0:T(8,128)(2,1)S(1)}, bf16[16,4224]{1,0:T(8,128)(2,1)S(1)}, u32[]{:S(2)}, u32[]{:S(2)}) collective-permute-start(bf16[16,4224]{1,0:T(8,128)(2,1)S(1)} %fusion.1), channel_id=1, source_target_pairs={{0,2},{2,4},{4,6},{6,8},{8,10},{10,12},{12,14},{14,16},{16,18},{18... | collective-permute-start | bytes 405512 | tf_op jit(solution)/shard_map/ppermute | solution.py:154
  22.2 0.0 all-gather.2.cloned.1.call-update
  22.2 0.0 copy-start.1
  22.2 0.0 copy-start.2
  22.2 0.0 copy-start.3
  22.3 0.2 collective-permute-done
  22.5 5.3 %collective-permute-start.1 = (bf16[16,4224]{1,0:T(8,128)(2,1)S(1)}, bf16[16,4224]{1,0:T(8,128)(2,1)S(1)}, u32[]{:S(2)}, u32[]{:S(2)}) collective-permute-start(bf16[16,4224]{1,0:T(8,128)(2,1)S(1)} %collective-permute-done), channel_id=1, source_target_pairs={{0,30},{2,0},{4,2},{6,4},{8,6},{10,8},{12,10},{14,12},{16,14},{18,... | collective-permute-start | bytes 405512 | tf_op jit(solution)/shard_map/ppermute | solution.py:151
  27.8 0.0 collective-permute-done.8
  27.8 1.9 %collective-permute-start.9 = (bf16[16,4224]{1,0:T(8,128)(2,1)S(1)}, bf16[16,4224]{1,0:T(8,128)(2,1)S(1)}, u32[]{:S(2)}, u32[]{:S(2)}) collective-permute-start(bf16[16,4224]{1,0:T(8,128)(2,1)S(1)} %collective-permute-done.8), channel_id=1, source_target_pairs={{0,2},{2,4},{4,6},{6,8},{8,10},{10,12},{12,14},{14,16},{16,18},{18... | collective-permute-start | bytes 405512 | tf_op jit(solution)/shard_map/ppermute | solution.py:154
  29.7 0.0 collective-permute-done.1
  29.8 5.0 %collective-permute-start.2 = (bf16[16,4224]{1,0:T(8,128)(2,1)S(1)}, bf16[16,4224]{1,0:T(8,128)(2,1)S(1)}, u32[]{:S(2)}, u32[]{:S(2)}) collective-permute-start(bf16[16,4224]{1,0:T(8,128)(2,1)S(1)} %collective-permute-done.1), channel_id=1, source_target_pairs={{0,30},{2,0},{4,2},{6,4},{8,6},{10,8},{12,10},{14,12},{16,14},{18,... | collective-permute-start | bytes 405512 | tf_op jit(solution)/shard_map/ppermute | solution.py:151
  34.7 0.0 collective-permute-done.9
  34.8 1.9 %collective-permute-start.10 = (bf16[16,4224]{1,0:T(8,128)(2,1)S(1)}, bf16[16,4224]{1,0:T(8,128)(2,1)S(1)}, u32[]{:S(2)}, u32[]{:S(2)}) collective-permute-start(bf16[16,4224]{1,0:T(8,128)(2,1)S(1)} %collective-permute-done.9), channel_id=1, source_target_pairs={{0,2},{2,4},{4,6},{6,8},{8,10},{10,12},{12,14},{14,16},{16,18},{18... | collective-permute-start | bytes 405512 | tf_op jit(solution)/shard_map/ppermute | solution.py:154
  36.7 0.8 collective-permute-done.2
  37.5 5.0 %collective-permute-start.3 = (bf16[16,4224]{1,0:T(8,128)(2,1)S(1)}, bf16[16,4224]{1,0:T(8,128)(2,1)S(1)}, u32[]{:S(2)}, u32[]{:S(2)}) collective-permute-start(bf16[16,4224]{1,0:T(8,128)(2,1)S(1)} %collective-permute-done.2), channel_id=1, source_target_pairs={{0,30},{2,0},{4,2},{6,4},{8,6},{10,8},{12,10},{14,12},{16,14},{18,... | collective-permute-start | bytes 405512 | tf_op jit(solution)/shard_map/ppermute | solution.py:151
  42.5 2.3 %collective-permute-done.10 = bf16[16,4224]{1,0:T(8,128)(2,1)S(1)} collective-permute-done((bf16[16,4224]{1,0:T(8,128)(2,1)S(1)}, bf16[16,4224]{1,0:T(8,128)(2,1)S(1)}, u32[]{:S(2)}, u32[]{:S(2)}) %collective-permute-start.10) | collective-permute-done | bytes 135200 | tf_op jit(solution)/shard_map/ppermute | solution.py:154
  44.8 1.9 %collective-permute-start.11 = (bf16[16,4224]{1,0:T(8,128)(2,1)S(1)}, bf16[16,4224]{1,0:T(8,128)(2,1)S(1)}, u32[]{:S(2)}, u32[]{:S(2)}) collective-permute-start(bf16[16,4224]{1,0:T(8,128)(2,1)S(1)} %collective-permute-done.10), channel_id=1, source_target_pairs={{0,2},{2,4},{4,6},{6,8},{8,10},{10,12},{12,14},{14,16},{16,18},{18... | collective-permute-start | bytes 405512 | tf_op jit(solution)/shard_map/ppermute | solution.py:154
  46.8 0.0 collective-permute-done.3
  46.8 4.9 %collective-permute-start.4 = (bf16[16,4224]{1,0:T(8,128)(2,1)S(1)}, bf16[16,4224]{1,0:T(8,128)(2,1)S(1)}, u32[]{:S(2)}, u32[]{:S(2)}) collective-permute-start(bf16[16,4224]{1,0:T(8,128)(2,1)S(1)} %collective-permute-done.3), channel_id=1, source_target_pairs={{0,30},{2,0},{4,2},{6,4},{8,6},{10,8},{12,10},{14,12},{16,14},{18,... | collective-permute-start | bytes 405512 | tf_op jit(solution)/shard_map/ppermute | solution.py:151
  51.7 2.3 %collective-permute-done.11 = bf16[16,4224]{1,0:T(8,128)(2,1)S(1)} collective-permute-done((bf16[16,4224]{1,0:T(8,128)(2,1)S(1)}, bf16[16,4224]{1,0:T(8,128)(2,1)S(1)}, u32[]{:S(2)}, u32[]{:S(2)}) %collective-permute-start.11) | collective-permute-done | bytes 135200 | tf_op jit(solution)/shard_map/ppermute | solution.py:154
  54.0 1.9 %collective-permute-start.12 = (bf16[16,4224]{1,0:T(8,128)(2,1)S(1)}, bf16[16,4224]{1,0:T(8,128)(2,1)S(1)}, u32[]{:S(2)}, u32[]{:S(2)}) collective-permute-start(bf16[16,4224]{1,0:T(8,128)(2,1)S(1)} %collective-permute-done.11), channel_id=1, source_target_pairs={{0,2},{2,4},{4,6},{6,8},{8,10},{10,12},{12,14},{14,16},{16,18},{18... | collective-permute-start | bytes 405512 | tf_op jit(solution)/shard_map/ppermute | solution.py:154
  55.9 0.0 collective-permute-done.4
  55.9 4.6 %collective-permute-start.5 = (bf16[16,4224]{1,0:T(8,128)(2,1)S(1)}, bf16[16,4224]{1,0:T(8,128)(2,1)S(1)}, u32[]{:S(2)}, u32[]{:S(2)}) collective-permute-start(bf16[16,4224]{1,0:T(8,128)(2,1)S(1)} %collective-permute-done.4), channel_id=1, source_target_pairs={{0,30},{2,0},{4,2},{6,4},{8,6},{10,8},{12,10},{14,12},{16,14},{18,... | collective-permute-start | bytes 405512 | tf_op jit(solution)/shard_map/ppermute | solution.py:151
  60.5 2.0 %collective-permute-done.12 = bf16[16,4224]{1,0:T(8,128)(2,1)S(1)} collective-permute-done((bf16[16,4224]{1,0:T(8,128)(2,1)S(1)}, bf16[16,4224]{1,0:T(8,128)(2,1)S(1)}, u32[]{:S(2)}, u32[]{:S(2)}) %collective-permute-start.12) | collective-permute-done | bytes 135200 | tf_op jit(solution)/shard_map/ppermute | solution.py:154
  62.5 1.9 %collective-permute-start.13 = (bf16[16,4224]{1,0:T(8,128)(2,1)S(1)}, bf16[16,4224]{1,0:T(8,128)(2,1)S(1)}, u32[]{:S(2)}, u32[]{:S(2)}) collective-permute-start(bf16[16,4224]{1,0:T(8,128)(2,1)S(1)} %collective-permute-done.12), channel_id=1, source_target_pairs={{0,2},{2,4},{4,6},{6,8},{8,10},{10,12},{12,14},{14,16},{16,18},{18... | collective-permute-start | bytes 405512 | tf_op jit(solution)/shard_map/ppermute | solution.py:154
  64.5 0.0 collective-permute-done.5
  64.5 4.6 %collective-permute-start.6 = (bf16[16,4224]{1,0:T(8,128)(2,1)S(1)}, bf16[16,4224]{1,0:T(8,128)(2,1)S(1)}, u32[]{:S(2)}, u32[]{:S(2)}) collective-permute-start(bf16[16,4224]{1,0:T(8,128)(2,1)S(1)} %collective-permute-done.5), channel_id=1, source_target_pairs={{0,30},{2,0},{4,2},{6,4},{8,6},{10,8},{12,10},{14,12},{16,14},{18,... | collective-permute-start | bytes 405512 | tf_op jit(solution)/shard_map/ppermute | solution.py:151
  69.1 2.3 %collective-permute-done.13 = bf16[16,4224]{1,0:T(8,128)(2,1)S(1)} collective-permute-done((bf16[16,4224]{1,0:T(8,128)(2,1)S(1)}, bf16[16,4224]{1,0:T(8,128)(2,1)S(1)}, u32[]{:S(2)}, u32[]{:S(2)}) %collective-permute-start.13) | collective-permute-done | bytes 135200 | tf_op jit(solution)/shard_map/ppermute | solution.py:154
  71.3 1.9 %collective-permute-start.14 = (bf16[16,4224]{1,0:T(8,128)(2,1)S(1)}, bf16[16,4224]{1,0:T(8,128)(2,1)S(1)}, u32[]{:S(2)}, u32[]{:S(2)}) collective-permute-start(bf16[16,4224]{1,0:T(8,128)(2,1)S(1)} %collective-permute-done.13), channel_id=1, source_target_pairs={{0,2},{2,4},{4,6},{6,8},{8,10},{10,12},{12,14},{14,16},{16,18},{18... | collective-permute-start | bytes 405512 | tf_op jit(solution)/shard_map/ppermute | solution.py:154
  73.3 4.6 %collective-permute-start.7 = (bf16[16,4224]{1,0:T(8,128)(2,1)S(1)}, bf16[16,4224]{1,0:T(8,128)(2,1)S(1)}, u32[]{:S(2)}, u32[]{:S(2)}) collective-permute-start(bf16[16,4224]{1,0:T(8,128)(2,1)S(1)} %collective-permute-done.6), channel_id=1, source_target_pairs={{0,30},{2,0},{4,2},{6,4},{8,6},{10,8},{12,10},{14,12},{16,14},{18,... | collective-permute-start | bytes 405512 | tf_op jit(solution)/shard_map/ppermute | solution.py:151
  77.9 4.9 %collective-permute-done.7 = bf16[16,4224]{1,0:T(8,128)(2,1)S(1)} collective-permute-done((bf16[16,4224]{1,0:T(8,128)(2,1)S(1)}, bf16[16,4224]{1,0:T(8,128)(2,1)S(1)}, u32[]{:S(2)}, u32[]{:S(2)}) %collective-permute-start.7) | collective-permute-done | bytes 135200 | tf_op jit(solution)/shard_map/ppermute | solution.py:151
  82.8 0.0 collective-permute-done.14
  83.0 10.5 %collective-permute-start.15 = (bf16[16,16,4224]{2,1,0:T(8,128)(2,1)S(1)}, bf16[16,16,4224]{2,1,0:T(8,128)(2,1)}, u32[]{:S(2)}, u32[]{:S(2)}) collective-permute-start(bf16[16,16,4224]{2,1,0:T(8,128)(2,1)S(1)} %bitcast_dynamic-update-slice_fusion.own_ref), channel_id=1, source_target_pairs={{0,1},{1,0},{2,3},{3,2},{4,5},{5,4},{6,7},{7,6},{8,9},{9,8},{10,11... | collective-permute-start | bytes 6488072 | tf_op jit(solution)/shard_map/ppermute | solution.py:171
  93.4 0.7 copy.12.bias_ref
  94.1 0.7 copy.13.gain_ref
  94.8 0.7 copy.14.shift_ref
  95.5 5.2 %all-gather.2.cloned.1.call-done = bf16[64,48,1024]{2,1,0:T(8,128)(2,1)} async-done(((bf16[2,48,1024]{2,1,0:T(8,128)(2,1)}), bf16[64,48,1024]{2,1,0:T(8,128)(2,1)}) %all-gather.2.cloned.1.call-update) | async-done | bytes 6291472 | tf_op jit(solution)/shard_map/all_gather | solution.py:166
  100.7 6.4 %shard_map.73 = bf16[16,32,192]{2,1,0:T(8,128)(2,1)} custom-call(bf16[3072,1024]{1,0:T(8,128)(2,1)} %bitcast.45, bf16[288,1024]{1,0:T(8,128)(2,1)} %bitcast.47, f32[32,1]{1,0:T(8,128)} %copy.12.bias_ref, f32[32,1]{1,0:T(8,128)} %copy.13.gain_ref, f32[32,1]{1,0:T(8,128)} %copy.14.shift_ref), custom_call_target="tpu_custom_call" | custom-call | flops 1811939328 | bytes 7077888 | tf_op jit(solution)/shard_map/pallas_call | solution.py:53
  107.1 9.7 %all-to-all-start = ((bf16[16,32,192]{2,1,0:T(8,128)(2,1)}), bf16[16,32,192]{2,1,0:T(8,128)(2,1)S(1)}, u32[]{:S(2)}, u32[]{:S(2)}) async-start(bf16[16,32,192]{2,1,0:T(8,128)(2,1)} %shard_map.73), calls=%async_computation | async-start | bytes 524288 | tf_op jit(solution)/shard_map/all_to_all | solution.py:176
  116.8 0.7 pad_add_fusion.index_ref
  117.5 0.0 collective-permute-done.15.other_ref
  117.5 4.6 %shard_map.74.wnat_ref = bf16[512,4224]{1,0:T(8,128)(2,1)} custom-call(s32[2]{0:T(128)} %pad_add_fusion.index_ref, bf16[16,16,4224]{2,1,0:T(8,128)(2,1)} %copy-done, bf16[16,16,4224]{2,1,0:T(8,128)(2,1)} %collective-permute-done.15.other_ref), custom_call_target="tpu_custom_call" | custom-call | bytes 8650752 | tf_op jit(solution)/shard_map/pallas_call | solution.py:81
  122.1 9.2 %all-to-all-done = bf16[16,32,192]{2,1,0:T(8,128)(2,1)S(1)} async-done(((bf16[16,32,192]{2,1,0:T(8,128)(2,1)}), bf16[16,32,192]{2,1,0:T(8,128)(2,1)S(1)}, u32[]{:S(2)}, u32[]{:S(2)}) %all-to-all-start) | async-done | bytes 196640 | tf_op jit(solution)/shard_map/all_to_all | solution.py:176
  131.3 6.7 %all_gather.7.act_ref = bf16[1024,192]{1,0:T(8,128)(2,1)} all-gather(bf16[512,192]{1,0:T(8,128)(2,1)S(1)} %bitcast.46), channel_id=1, replica_groups=mesh['grp'=16,'z'=16,'core'=2] {'core'}, dimensions={0}, use_global_device_ids=true | all-gather | bytes 589824 | tf_op jit(solution)/shard_map/all_gather | solution.py:178
  137.9 5.3 %shard_map.75 = bf16[4,96,512]{2,1,0:T(8,128)(2,1)} custom-call(s32[2]{0:T(128)} %pad_add_fusion.index_ref, bf16[1024,192]{1,0:T(8,128)(2,1)} %all_gather.7.act_ref, bf16[512,4224]{1,0:T(8,128)(2,1)} %shard_map.74.wnat_ref), custom_call_target="tpu_custom_call" | custom-call | flops 805306368 | bytes 5111808 | tf_op jit(solution)/shard_map/pallas_call | solution.py:132
  (24 shorter events, 0.3 us)
Async XLA Ops:
  6.5 94.1 %all-gather.2.cloned.1.call-start = ((), (), s32[]{:S(2)}) async-start(), calls=%async_computation.1 | async-start | bytes 6488064 | tf_op jit(solution)/shard_map/all_gather | solution.py:166
  8.3 14.2 %collective-permute-start = (bf16[16,4224]{1,0:T(8,128)(2,1)S(1)}, bf16[16,4224]{1,0:T(8,128)(2,1)S(1)}, u32[]{:S(2)}, u32[]{:S(2)}) collective-permute-start(bf16[16,4224]{1,0:T(8,128)(2,1)S(1)} %fusion.1), channel_id=1, source_target_pairs={{0,30},{2,0},{4,2},{6,4},{8,6},{10,8},{12,10},{14,12},{16,14},{18,... | collective-permute-start | bytes 405512 | tf_op jit(solution)/shard_map/ppermute | solution.py:151
  20.2 7.5 %collective-permute-start.8 = (bf16[16,4224]{1,0:T(8,128)(2,1)S(1)}, bf16[16,4224]{1,0:T(8,128)(2,1)S(1)}, u32[]{:S(2)}, u32[]{:S(2)}) collective-permute-start(bf16[16,4224]{1,0:T(8,128)(2,1)S(1)} %fusion.1), channel_id=1, source_target_pairs={{0,2},{2,4},{4,6},{6,8},{8,10},{10,12},{12,14},{14,16},{16,18},{18... | collective-permute-start | bytes 405512 | tf_op jit(solution)/shard_map/ppermute | solution.py:154
  22.2 71.2 %copy-start.1 = (f32[32]{0:T(128)S(1)}, f32[32]{0:T(128)}, u32[]{:S(2)}) copy-start(f32[32]{0:T(128)} %param.9) | copy-start | bytes 388
  22.2 71.9 %copy-start.2 = (f32[32]{0:T(128)S(1)}, f32[32]{0:T(128)}, u32[]{:S(2)}) copy-start(f32[32]{0:T(128)} %param.10) | copy-start | bytes 388
  22.2 72.6 %copy-start.3 = (f32[32]{0:T(128)S(1)}, f32[32]{0:T(128)}, u32[]{:S(2)}) copy-start(f32[32]{0:T(128)} %param.11) | copy-start | bytes 388
  22.5 7.3 %collective-permute-start.1 = (bf16[16,4224]{1,0:T(8,128)(2,1)S(1)}, bf16[16,4224]{1,0:T(8,128)(2,1)S(1)}, u32[]{:S(2)}, u32[]{:S(2)}) collective-permute-start(bf16[16,4224]{1,0:T(8,128)(2,1)S(1)} %collective-permute-done), channel_id=1, source_target_pairs={{0,30},{2,0},{4,2},{6,4},{8,6},{10,8},{12,10},{14,12},{16,14},{18,... | collective-permute-start | bytes 405512 | tf_op jit(solution)/shard_map/ppermute | solution.py:151
  27.8 7.0 %collective-permute-start.9 = (bf16[16,4224]{1,0:T(8,128)(2,1)S(1)}, bf16[16,4224]{1,0:T(8,128)(2,1)S(1)}, u32[]{:S(2)}, u32[]{:S(2)}) collective-permute-start(bf16[16,4224]{1,0:T(8,128)(2,1)S(1)} %collective-permute-done.8), channel_id=1, source_target_pairs={{0,2},{2,4},{4,6},{6,8},{8,10},{10,12},{12,14},{14,16},{16,18},{18... | collective-permute-start | bytes 405512 | tf_op jit(solution)/shard_map/ppermute | solution.py:154
  29.8 7.7 %collective-permute-start.2 = (bf16[16,4224]{1,0:T(8,128)(2,1)S(1)}, bf16[16,4224]{1,0:T(8,128)(2,1)S(1)}, u32[]{:S(2)}, u32[]{:S(2)}) collective-permute-start(bf16[16,4224]{1,0:T(8,128)(2,1)S(1)} %collective-permute-done.1), channel_id=1, source_target_pairs={{0,30},{2,0},{4,2},{6,4},{8,6},{10,8},{12,10},{14,12},{16,14},{18,... | collective-permute-start | bytes 405512 | tf_op jit(solution)/shard_map/ppermute | solution.py:151
  34.8 10.1 %collective-permute-start.10 = (bf16[16,4224]{1,0:T(8,128)(2,1)S(1)}, bf16[16,4224]{1,0:T(8,128)(2,1)S(1)}, u32[]{:S(2)}, u32[]{:S(2)}) collective-permute-start(bf16[16,4224]{1,0:T(8,128)(2,1)S(1)} %collective-permute-done.9), channel_id=1, source_target_pairs={{0,2},{2,4},{4,6},{6,8},{8,10},{10,12},{12,14},{14,16},{16,18},{18... | collective-permute-start | bytes 405512 | tf_op jit(solution)/shard_map/ppermute | solution.py:154
  37.5 9.3 %collective-permute-start.3 = (bf16[16,4224]{1,0:T(8,128)(2,1)S(1)}, bf16[16,4224]{1,0:T(8,128)(2,1)S(1)}, u32[]{:S(2)}, u32[]{:S(2)}) collective-permute-start(bf16[16,4224]{1,0:T(8,128)(2,1)S(1)} %collective-permute-done.2), channel_id=1, source_target_pairs={{0,30},{2,0},{4,2},{6,4},{8,6},{10,8},{12,10},{14,12},{16,14},{18,... | collective-permute-start | bytes 405512 | tf_op jit(solution)/shard_map/ppermute | solution.py:151
  44.8 9.2 %collective-permute-start.11 = (bf16[16,4224]{1,0:T(8,128)(2,1)S(1)}, bf16[16,4224]{1,0:T(8,128)(2,1)S(1)}, u32[]{:S(2)}, u32[]{:S(2)}) collective-permute-start(bf16[16,4224]{1,0:T(8,128)(2,1)S(1)} %collective-permute-done.10), channel_id=1, source_target_pairs={{0,2},{2,4},{4,6},{6,8},{8,10},{10,12},{12,14},{14,16},{16,18},{18... | collective-permute-start | bytes 405512 | tf_op jit(solution)/shard_map/ppermute | solution.py:154
  46.8 9.1 %collective-permute-start.4 = (bf16[16,4224]{1,0:T(8,128)(2,1)S(1)}, bf16[16,4224]{1,0:T(8,128)(2,1)S(1)}, u32[]{:S(2)}, u32[]{:S(2)}) collective-permute-start(bf16[16,4224]{1,0:T(8,128)(2,1)S(1)} %collective-permute-done.3), channel_id=1, source_target_pairs={{0,30},{2,0},{4,2},{6,4},{8,6},{10,8},{12,10},{14,12},{16,14},{18,... | collective-permute-start | bytes 405512 | tf_op jit(solution)/shard_map/ppermute | solution.py:151
  54.0 8.5 %collective-permute-start.12 = (bf16[16,4224]{1,0:T(8,128)(2,1)S(1)}, bf16[16,4224]{1,0:T(8,128)(2,1)S(1)}, u32[]{:S(2)}, u32[]{:S(2)}) collective-permute-start(bf16[16,4224]{1,0:T(8,128)(2,1)S(1)} %collective-permute-done.11), channel_id=1, source_target_pairs={{0,2},{2,4},{4,6},{6,8},{8,10},{10,12},{12,14},{14,16},{16,18},{18... | collective-permute-start | bytes 405512 | tf_op jit(solution)/shard_map/ppermute | solution.py:154
  55.9 8.5 %collective-permute-start.5 = (bf16[16,4224]{1,0:T(8,128)(2,1)S(1)}, bf16[16,4224]{1,0:T(8,128)(2,1)S(1)}, u32[]{:S(2)}, u32[]{:S(2)}) collective-permute-start(bf16[16,4224]{1,0:T(8,128)(2,1)S(1)} %collective-permute-done.4), channel_id=1, source_target_pairs={{0,30},{2,0},{4,2},{6,4},{8,6},{10,8},{12,10},{14,12},{16,14},{18,... | collective-permute-start | bytes 405512 | tf_op jit(solution)/shard_map/ppermute | solution.py:151
  62.5 8.8 %collective-permute-start.13 = (bf16[16,4224]{1,0:T(8,128)(2,1)S(1)}, bf16[16,4224]{1,0:T(8,128)(2,1)S(1)}, u32[]{:S(2)}, u32[]{:S(2)}) collective-permute-start(bf16[16,4224]{1,0:T(8,128)(2,1)S(1)} %collective-permute-done.12), channel_id=1, source_target_pairs={{0,2},{2,4},{4,6},{6,8},{8,10},{10,12},{12,14},{14,16},{16,18},{18... | collective-permute-start | bytes 405512 | tf_op jit(solution)/shard_map/ppermute | solution.py:154
  64.5 8.8 %collective-permute-start.6 = (bf16[16,4224]{1,0:T(8,128)(2,1)S(1)}, bf16[16,4224]{1,0:T(8,128)(2,1)S(1)}, u32[]{:S(2)}, u32[]{:S(2)}) collective-permute-start(bf16[16,4224]{1,0:T(8,128)(2,1)S(1)} %collective-permute-done.5), channel_id=1, source_target_pairs={{0,30},{2,0},{4,2},{6,4},{8,6},{10,8},{12,10},{14,12},{16,14},{18,... | collective-permute-start | bytes 405512 | tf_op jit(solution)/shard_map/ppermute | solution.py:151
  71.3 11.5 %collective-permute-start.14 = (bf16[16,4224]{1,0:T(8,128)(2,1)S(1)}, bf16[16,4224]{1,0:T(8,128)(2,1)S(1)}, u32[]{:S(2)}, u32[]{:S(2)}) collective-permute-start(bf16[16,4224]{1,0:T(8,128)(2,1)S(1)} %collective-permute-done.13), channel_id=1, source_target_pairs={{0,2},{2,4},{4,6},{6,8},{8,10},{10,12},{12,14},{14,16},{16,18},{18... | collective-permute-start | bytes 405512 | tf_op jit(solution)/shard_map/ppermute | solution.py:154
  73.3 9.5 %collective-permute-start.7 = (bf16[16,4224]{1,0:T(8,128)(2,1)S(1)}, bf16[16,4224]{1,0:T(8,128)(2,1)S(1)}, u32[]{:S(2)}, u32[]{:S(2)}) collective-permute-start(bf16[16,4224]{1,0:T(8,128)(2,1)S(1)} %collective-permute-done.6), channel_id=1, source_target_pairs={{0,30},{2,0},{4,2},{6,4},{8,6},{10,8},{12,10},{14,12},{16,14},{18,... | collective-permute-start | bytes 405512 | tf_op jit(solution)/shard_map/ppermute | solution.py:151
  82.9 24.1 %copy-start = (bf16[16,16,4224]{2,1,0:T(8,128)(2,1)}, bf16[16,16,4224]{2,1,0:T(8,128)(2,1)S(1)}, u32[]{:S(2)}) copy-start(bf16[16,16,4224]{2,1,0:T(8,128)(2,1)S(1)} %bitcast_dynamic-update-slice_fusion.own_ref) | copy-start | bytes 6488068
  83.0 34.5 %collective-permute-start.15 = (bf16[16,16,4224]{2,1,0:T(8,128)(2,1)S(1)}, bf16[16,16,4224]{2,1,0:T(8,128)(2,1)}, u32[]{:S(2)}, u32[]{:S(2)}) collective-permute-start(bf16[16,16,4224]{2,1,0:T(8,128)(2,1)S(1)} %bitcast_dynamic-update-slice_fusion.own_ref), channel_id=1, source_target_pairs={{0,1},{1,0},{2,3},{3,2},{4,5},{5,4},{6,7},{7,6},{8,9},{9,8},{10,11... | collective-permute-start | bytes 6488072 | tf_op jit(solution)/shard_map/ppermute | solution.py:171
  107.1 24.2 %all-to-all-start = ((bf16[16,32,192]{2,1,0:T(8,128)(2,1)}), bf16[16,32,192]{2,1,0:T(8,128)(2,1)S(1)}, u32[]{:S(2)}, u32[]{:S(2)}) async-start(bf16[16,32,192]{2,1,0:T(8,128)(2,1)} %shard_map.73), calls=%async_computation | async-start | bytes 524288 | tf_op jit(solution)/shard_map/all_to_all | solution.py:176
Sparse Core Ops, SparseCore 0:
  22.3 78.3 all-gather.1

commit v19 on v15

--- a/solution.py
+++ b/solution.py
@@ -87,12 +87,18 @@
     )(index, own, other)
 
 
-def up_kernel(index_ref, act_ref, wnat_ref, out_ref, actn_ref, *, width_cols):
-    outs, packed_width = wnat_ref.shape
+def up_kernel(index_ref, act_ref, wnat_hbm, out_ref, actn_ref, w_buf, b_buf, sems, *, width_cols):
+    outs, packed_width = wnat_hbm.shape
     channels, positions = act_ref.shape
     chips = outs // 32
     block = channels // (2 * chips)
     core = index_ref[0]
+    copies = [pltpu.make_async_copy(wnat_hbm.at[:, pl.ds(ab * channels, channels)], w_buf.at[ab], sems.at[ab])
+              for ab in range(4)]
+    copies.append(pltpu.make_async_copy(wnat_hbm.at[:, pl.ds(4 * channels, packed_width - 4 * channels)],
+                                        b_buf, sems.at[4]))
+    for copy in copies:
+        copy.start()
     rows = out_ref.shape[0] // 2
     span = rows * width_cols
     lanes = actn_ref.shape[1]
@@ -104,8 +110,8 @@
     nn = (((1,), (0,)), ((), ()))
     sub = lax.broadcasted_iota(jnp.int32, (packed_width - 4 * channels, lanes), 0)
     ones = jnp.where(sub == 0, 1.0, 0.0).astype(actn_ref.dtype)
-    bias = lax.dot_general(wnat_ref[:, pl.ds(4 * channels, packed_width - 4 * channels)], ones, nn,
-                           preferred_element_type=jnp.float32)
+    copies[4].wait()
+    bias = lax.dot_general(b_buf[...], ones, nn, preferred_element_type=jnp.float32)
     act = actn_ref[...]
     first = lanes - span
     dest = lax.broadcasted_iota(jnp.int32, (2 * width_cols, 2 * width_cols), 0)
@@ -114,8 +120,8 @@
     for a in range(2):
         phases = []
         for b in range(2):
-            res = lax.dot_general(wnat_ref[:, pl.ds((2 * a + b) * channels, channels)], act, nn,
-                                  preferred_element_type=jnp.float32)
+            copies[2 * a + b].wait()
+            res = lax.dot_general(w_buf[2 * a + b], act, nn, preferred_element_type=jnp.float32)
             res = jnp.transpose(res + bias).astype(out_ref.dtype)
             phases.append(jnp.where(core == 0, res[:span], res[first:]))
         for i in range(rows):
@@ -132,9 +138,12 @@
     return pl.pallas_call(
         functools.partial(up_kernel, width_cols=width_cols),
         out_shape=jax.ShapeDtypeStruct((2 * rows, 2 * width_cols, outs), jnp.bfloat16),
-        in_specs=[smem, vmem, vmem],
+        in_specs=[smem, vmem, pl.BlockSpec(memory_space=pl.ANY)],
         out_specs=vmem,
-        scratch_shapes=[pltpu.VMEM((channels, -(-positions // 2 // 128) * 128), act.dtype)],
+        scratch_shapes=[pltpu.VMEM((channels, -(-positions // 2 // 128) * 128), act.dtype),
+                        pltpu.VMEM((4, outs, channels), wnat.dtype),
+                        pltpu.VMEM((outs, packed_width - 4 * channels), wnat.dtype),
+                        pltpu.SemaphoreType.DMA((5,))],
         cost_estimate=pl.CostEstimate(
             flops=2 * positions * channels * 4 * outs, transcendentals=0,
             bytes_accessed=act.size * 2 + wnat.size * 2 + rows * width_cols * 4 * outs * 2),

time: 151 us -> 153 us (1.013)
  Pallas kernels: 16 us -> 18.6 us
    pallas_call x1, Pallas kernels: 5 us -> 7.59 us  [up_conv(): pl.pallas_call(functools.partial(up_kernel, width_cols=width_cols), out_s...]
where the time goes in v19:
time: 153 us; the launch traced here: 152 us
  starting transfers between devices  79.4 us (52%)
  waiting for transfers between devices  29.3 us (19%)
  Pallas kernels  18.6 us (12%)
  between operations  13.7 us (9%)
  blocking collectives  6.66 us (4%)
  local copies, waits for them, and re-layouts  4.07 us (3%)
    ppermute x8, starting transfers between devices, ring_gather(): ahead = lax.ppermute(ahead, axis, step_up)  45.9 us
    ppermute x7, starting transfers between devices, ring_gather(): behind = lax.ppermute(behind, axis, step_down)  13.4 us
    ppermute x1, starting transfers between devices, body(): packed_other = lax.ppermute(packed_z, 'core', [(0, 1), (1, 0)])  10.5 us
    all_to_all x1, starting transfers between devices, body(): lax.all_to_all(activated, 'z', split_axis=0, concat_axis=0, tiled=True)  9.74 us
    all_to_all x1, waiting for transfers between devices, body(): lax.all_to_all(activated, 'z', split_axis=0, concat_axis=0, tiled=True)  9.21 us
    ppermute x7, waiting for transfers between devices, ring_gather(): behind = lax.ppermute(behind, axis, step_down)  8.94 us
    pallas_call x1, Pallas kernels, up_conv(): pl.pallas_call(functools.partial(up_kernel, width_cols=width_cols), out_s...  7.59 us
    all_gather x1, blocking collectives, body(): both = lax.all_gather(chip_rows, 'core', axis=0, tiled=True)  6.66 us
  transfers between devices with their start and end apart: 18, of which 9 were waited for; matrix products, arithmetic and copies ran while one was open for 2% of the time, Pallas kernels for 7%

profile of v19, /device:TPU:1, one launch (start us, length us, event | category | flops | bytes accessed | tf_op | source)
XLA Modules:
  0.0 152.4 jit_solution(11062500162332472313)
XLA Ops:
  6.5 0.7 copy.15
  7.3 1.0 reshape.31
  8.3 12.0 %collective-permute-start = (bf16[16,4224]{1,0:T(8,128)(2,1)S(1)}, bf16[16,4224]{1,0:T(8,128)(2,1)S(1)}, u32[]{:S(2)}, u32[]{:S(2)}) collective-permute-start(bf16[16,4224]{1,0:T(8,128)(2,1)S(1)} %fusion.1), channel_id=1, source_target_pairs={{0,30},{2,0},{4,2},{6,4},{8,6},{10,8},{12,10},{14,12},{16,14},{18,... | collective-permute-start | bytes 405512 | tf_op jit(solution)/shard_map/ppermute | solution.py:160
  20.2 1.9 %collective-permute-start.8 = (bf16[16,4224]{1,0:T(8,128)(2,1)S(1)}, bf16[16,4224]{1,0:T(8,128)(2,1)S(1)}, u32[]{:S(2)}, u32[]{:S(2)}) collective-permute-start(bf16[16,4224]{1,0:T(8,128)(2,1)S(1)} %fusion.1), channel_id=1, source_target_pairs={{0,2},{2,4},{4,6},{6,8},{8,10},{10,12},{12,14},{14,16},{16,18},{18... | collective-permute-start | bytes 405512 | tf_op jit(solution)/shard_map/ppermute | solution.py:163
  22.2 0.0 all-gather.2.cloned.1.call-update
  22.2 0.0 copy-start.1
  22.2 0.0 copy-start.2
  22.2 0.0 copy-start.3
  22.3 0.2 collective-permute-done
  22.5 5.3 %collective-permute-start.1 = (bf16[16,4224]{1,0:T(8,128)(2,1)S(1)}, bf16[16,4224]{1,0:T(8,128)(2,1)S(1)}, u32[]{:S(2)}, u32[]{:S(2)}) collective-permute-start(bf16[16,4224]{1,0:T(8,128)(2,1)S(1)} %collective-permute-done), channel_id=1, source_target_pairs={{0,30},{2,0},{4,2},{6,4},{8,6},{10,8},{12,10},{14,12},{16,14},{18,... | collective-permute-start | bytes 405512 | tf_op jit(solution)/shard_map/ppermute | solution.py:160
  27.8 0.0 collective-permute-done.8
  27.8 1.9 %collective-permute-start.9 = (bf16[16,4224]{1,0:T(8,128)(2,1)S(1)}, bf16[16,4224]{1,0:T(8,128)(2,1)S(1)}, u32[]{:S(2)}, u32[]{:S(2)}) collective-permute-start(bf16[16,4224]{1,0:T(8,128)(2,1)S(1)} %collective-permute-done.8), channel_id=1, source_target_pairs={{0,2},{2,4},{4,6},{6,8},{8,10},{10,12},{12,14},{14,16},{16,18},{18... | collective-permute-start | bytes 405512 | tf_op jit(solution)/shard_map/ppermute | solution.py:163
  29.7 0.0 collective-permute-done.1
  29.8 5.0 %collective-permute-start.2 = (bf16[16,4224]{1,0:T(8,128)(2,1)S(1)}, bf16[16,4224]{1,0:T(8,128)(2,1)S(1)}, u32[]{:S(2)}, u32[]{:S(2)}) collective-permute-start(bf16[16,4224]{1,0:T(8,128)(2,1)S(1)} %collective-permute-done.1), channel_id=1, source_target_pairs={{0,30},{2,0},{4,2},{6,4},{8,6},{10,8},{12,10},{14,12},{16,14},{18,... | collective-permute-start | bytes 405512 | tf_op jit(solution)/shard_map/ppermute | solution.py:160
  34.7 0.0 collective-permute-done.9
  34.8 1.9 %collective-permute-start.10 = (bf16[16,4224]{1,0:T(8,128)(2,1)S(1)}, bf16[16,4224]{1,0:T(8,128)(2,1)S(1)}, u32[]{:S(2)}, u32[]{:S(2)}) collective-permute-start(bf16[16,4224]{1,0:T(8,128)(2,1)S(1)} %collective-permute-done.9), channel_id=1, source_target_pairs={{0,2},{2,4},{4,6},{6,8},{8,10},{10,12},{12,14},{14,16},{16,18},{18... | collective-permute-start | bytes 405512 | tf_op jit(solution)/shard_map/ppermute | solution.py:163
  36.7 0.8 collective-permute-done.2
  37.5 5.0 %collective-permute-start.3 = (bf16[16,4224]{1,0:T(8,128)(2,1)S(1)}, bf16[16,4224]{1,0:T(8,128)(2,1)S(1)}, u32[]{:S(2)}, u32[]{:S(2)}) collective-permute-start(bf16[16,4224]{1,0:T(8,128)(2,1)S(1)} %collective-permute-done.2), channel_id=1, source_target_pairs={{0,30},{2,0},{4,2},{6,4},{8,6},{10,8},{12,10},{14,12},{16,14},{18,... | collective-permute-start | bytes 405512 | tf_op jit(solution)/shard_map/ppermute | solution.py:160
  42.5 2.3 %collective-permute-done.10 = bf16[16,4224]{1,0:T(8,128)(2,1)S(1)} collective-permute-done((bf16[16,4224]{1,0:T(8,128)(2,1)S(1)}, bf16[16,4224]{1,0:T(8,128)(2,1)S(1)}, u32[]{:S(2)}, u32[]{:S(2)}) %collective-permute-start.10) | collective-permute-done | bytes 135200 | tf_op jit(solution)/shard_map/ppermute | solution.py:163
  44.8 1.9 %collective-permute-start.11 = (bf16[16,4224]{1,0:T(8,128)(2,1)S(1)}, bf16[16,4224]{1,0:T(8,128)(2,1)S(1)}, u32[]{:S(2)}, u32[]{:S(2)}) collective-permute-start(bf16[16,4224]{1,0:T(8,128)(2,1)S(1)} %collective-permute-done.10), channel_id=1, source_target_pairs={{0,2},{2,4},{4,6},{6,8},{8,10},{10,12},{12,14},{14,16},{16,18},{18... | collective-permute-start | bytes 405512 | tf_op jit(solution)/shard_map/ppermute | solution.py:163
  46.8 0.0 collective-permute-done.3
  46.8 4.9 %collective-permute-start.4 = (bf16[16,4224]{1,0:T(8,128)(2,1)S(1)}, bf16[16,4224]{1,0:T(8,128)(2,1)S(1)}, u32[]{:S(2)}, u32[]{:S(2)}) collective-permute-start(bf16[16,4224]{1,0:T(8,128)(2,1)S(1)} %collective-permute-done.3), channel_id=1, source_target_pairs={{0,30},{2,0},{4,2},{6,4},{8,6},{10,8},{12,10},{14,12},{16,14},{18,... | collective-permute-start | bytes 405512 | tf_op jit(solution)/shard_map/ppermute | solution.py:160
  51.7 2.3 %collective-permute-done.11 = bf16[16,4224]{1,0:T(8,128)(2,1)S(1)} collective-permute-done((bf16[16,4224]{1,0:T(8,128)(2,1)S(1)}, bf16[16,4224]{1,0:T(8,128)(2,1)S(1)}, u32[]{:S(2)}, u32[]{:S(2)}) %collective-permute-start.11) | collective-permute-done | bytes 135200 | tf_op jit(solution)/shard_map/ppermute | solution.py:163
  54.0 1.9 %collective-permute-start.12 = (bf16[16,4224]{1,0:T(8,128)(2,1)S(1)}, bf16[16,4224]{1,0:T(8,128)(2,1)S(1)}, u32[]{:S(2)}, u32[]{:S(2)}) collective-permute-start(bf16[16,4224]{1,0:T(8,128)(2,1)S(1)} %collective-permute-done.11), channel_id=1, source_target_pairs={{0,2},{2,4},{4,6},{6,8},{8,10},{10,12},{12,14},{14,16},{16,18},{18... | collective-permute-start | bytes 405512 | tf_op jit(solution)/shard_map/ppermute | solution.py:163
  55.9 0.0 collective-permute-done.4
  55.9 4.6 %collective-permute-start.5 = (bf16[16,4224]{1,0:T(8,128)(2,1)S(1)}, bf16[16,4224]{1,0:T(8,128)(2,1)S(1)}, u32[]{:S(2)}, u32[]{:S(2)}) collective-permute-start(bf16[16,4224]{1,0:T(8,128)(2,1)S(1)} %collective-permute-done.4), channel_id=1, source_target_pairs={{0,30},{2,0},{4,2},{6,4},{8,6},{10,8},{12,10},{14,12},{16,14},{18,... | collective-permute-start | bytes 405512 | tf_op jit(solution)/shard_map/ppermute | solution.py:160
  60.5 2.0 %collective-permute-done.12 = bf16[16,4224]{1,0:T(8,128)(2,1)S(1)} collective-permute-done((bf16[16,4224]{1,0:T(8,128)(2,1)S(1)}, bf16[16,4224]{1,0:T(8,128)(2,1)S(1)}, u32[]{:S(2)}, u32[]{:S(2)}) %collective-permute-start.12) | collective-permute-done | bytes 135200 | tf_op jit(solution)/shard_map/ppermute | solution.py:163
  62.5 1.9 %collective-permute-start.13 = (bf16[16,4224]{1,0:T(8,128)(2,1)S(1)}, bf16[16,4224]{1,0:T(8,128)(2,1)S(1)}, u32[]{:S(2)}, u32[]{:S(2)}) collective-permute-start(bf16[16,4224]{1,0:T(8,128)(2,1)S(1)} %collective-permute-done.12), channel_id=1, source_target_pairs={{0,2},{2,4},{4,6},{6,8},{8,10},{10,12},{12,14},{14,16},{16,18},{18... | collective-permute-start | bytes 405512 | tf_op jit(solution)/shard_map/ppermute | solution.py:163
  64.5 0.0 collective-permute-done.5
  64.5 4.6 %collective-permute-start.6 = (bf16[16,4224]{1,0:T(8,128)(2,1)S(1)}, bf16[16,4224]{1,0:T(8,128)(2,1)S(1)}, u32[]{:S(2)}, u32[]{:S(2)}) collective-permute-start(bf16[16,4224]{1,0:T(8,128)(2,1)S(1)} %collective-permute-done.5), channel_id=1, source_target_pairs={{0,30},{2,0},{4,2},{6,4},{8,6},{10,8},{12,10},{14,12},{16,14},{18,... | collective-permute-start | bytes 405512 | tf_op jit(solution)/shard_map/ppermute | solution.py:160
  69.1 2.3 %collective-permute-done.13 = bf16[16,4224]{1,0:T(8,128)(2,1)S(1)} collective-permute-done((bf16[16,4224]{1,0:T(8,128)(2,1)S(1)}, bf16[16,4224]{1,0:T(8,128)(2,1)S(1)}, u32[]{:S(2)}, u32[]{:S(2)}) %collective-permute-start.13) | collective-permute-done | bytes 135200 | tf_op jit(solution)/shard_map/ppermute | solution.py:163
  71.3 1.9 %collective-permute-start.14 = (bf16[16,4224]{1,0:T(8,128)(2,1)S(1)}, bf16[16,4224]{1,0:T(8,128)(2,1)S(1)}, u32[]{:S(2)}, u32[]{:S(2)}) collective-permute-start(bf16[16,4224]{1,0:T(8,128)(2,1)S(1)} %collective-permute-done.13), channel_id=1, source_target_pairs={{0,2},{2,4},{4,6},{6,8},{8,10},{10,12},{12,14},{14,16},{16,18},{18... | collective-permute-start | bytes 405512 | tf_op jit(solution)/shard_map/ppermute | solution.py:163
  73.3 4.6 %collective-permute-start.7 = (bf16[16,4224]{1,0:T(8,128)(2,1)S(1)}, bf16[16,4224]{1,0:T(8,128)(2,1)S(1)}, u32[]{:S(2)}, u32[]{:S(2)}) collective-permute-start(bf16[16,4224]{1,0:T(8,128)(2,1)S(1)} %collective-permute-done.6), channel_id=1, source_target_pairs={{0,30},{2,0},{4,2},{6,4},{8,6},{10,8},{12,10},{14,12},{16,14},{18,... | collective-permute-start | bytes 405512 | tf_op jit(solution)/shard_map/ppermute | solution.py:160
  77.9 4.9 %collective-permute-done.7 = bf16[16,4224]{1,0:T(8,128)(2,1)S(1)} collective-permute-done((bf16[16,4224]{1,0:T(8,128)(2,1)S(1)}, bf16[16,4224]{1,0:T(8,128)(2,1)S(1)}, u32[]{:S(2)}, u32[]{:S(2)}) %collective-permute-start.7) | collective-permute-done | bytes 135200 | tf_op jit(solution)/shard_map/ppermute | solution.py:160
  82.8 0.0 collective-permute-done.14
  83.0 10.5 %collective-permute-start.15 = (bf16[16,16,4224]{2,1,0:T(8,128)(2,1)S(1)}, bf16[16,16,4224]{2,1,0:T(8,128)(2,1)}, u32[]{:S(2)}, u32[]{:S(2)}) collective-permute-start(bf16[16,16,4224]{2,1,0:T(8,128)(2,1)S(1)} %bitcast_dynamic-update-slice_fusion.own_ref), channel_id=1, source_target_pairs={{0,1},{1,0},{2,3},{3,2},{4,5},{5,4},{6,7},{7,6},{8,9},{9,8},{10,11... | collective-permute-start | bytes 6488072 | tf_op jit(solution)/shard_map/ppermute | solution.py:180
  93.4 0.7 copy.12.bias_ref
  94.1 0.7 copy.13.gain_ref
  94.8 0.7 copy.14.shift_ref
  95.5 5.2 %all-gather.2.cloned.1.call-done = bf16[64,48,1024]{2,1,0:T(8,128)(2,1)} async-done(((bf16[2,48,1024]{2,1,0:T(8,128)(2,1)}), bf16[64,48,1024]{2,1,0:T(8,128)(2,1)}) %all-gather.2.cloned.1.call-update) | async-done | bytes 6291472 | tf_op jit(solution)/shard_map/all_gather | solution.py:175
  100.7 6.4 %shard_map.73 = bf16[16,32,192]{2,1,0:T(8,128)(2,1)} custom-call(bf16[3072,1024]{1,0:T(8,128)(2,1)} %bitcast.45, bf16[288,1024]{1,0:T(8,128)(2,1)} %bitcast.47, f32[32,1]{1,0:T(8,128)} %copy.12.bias_ref, f32[32,1]{1,0:T(8,128)} %copy.13.gain_ref, f32[32,1]{1,0:T(8,128)} %copy.14.shift_ref), custom_call_target="tpu_custom_call" | custom-call | flops 1811939328 | bytes 7077888 | tf_op jit(solution)/shard_map/pallas_call | solution.py:53
  107.1 9.7 %all-to-all-start = ((bf16[16,32,192]{2,1,0:T(8,128)(2,1)}), bf16[16,32,192]{2,1,0:T(8,128)(2,1)S(1)}, u32[]{:S(2)}, u32[]{:S(2)}) async-start(bf16[16,32,192]{2,1,0:T(8,128)(2,1)} %shard_map.73), calls=%async_computation | async-start | bytes 524288 | tf_op jit(solution)/shard_map/all_to_all | solution.py:185
  116.8 0.7 pad_add_fusion.index_ref
  117.5 0.0 collective-permute-done.15.other_ref
  117.5 4.6 %shard_map.74.wnat_hbm = bf16[512,4224]{1,0:T(8,128)(2,1)} custom-call(s32[2]{0:T(128)} %pad_add_fusion.index_ref, bf16[16,16,4224]{2,1,0:T(8,128)(2,1)} %copy-done, bf16[16,16,4224]{2,1,0:T(8,128)(2,1)} %collective-permute-done.15.other_ref), custom_call_target="tpu_custom_call" | custom-call | bytes 8650752 | tf_op jit(solution)/shard_map/pallas_call | solution.py:81
  122.1 9.2 %all-to-all-done = bf16[16,32,192]{2,1,0:T(8,128)(2,1)S(1)} async-done(((bf16[16,32,192]{2,1,0:T(8,128)(2,1)}), bf16[16,32,192]{2,1,0:T(8,128)(2,1)S(1)}, u32[]{:S(2)}, u32[]{:S(2)}) %all-to-all-start) | async-done | bytes 196640 | tf_op jit(solution)/shard_map/all_to_all | solution.py:185
  131.3 6.7 %all_gather.7.act_ref = bf16[1024,192]{1,0:T(8,128)(2,1)} all-gather(bf16[512,192]{1,0:T(8,128)(2,1)S(1)} %bitcast.46), channel_id=1, replica_groups=mesh['grp'=16,'z'=16,'core'=2] {'core'}, dimensions={0}, use_global_device_ids=true | all-gather | bytes 589824 | tf_op jit(solution)/shard_map/all_gather | solution.py:187
  137.9 7.6 %shard_map.75 = bf16[4,96,512]{2,1,0:T(8,128)(2,1)} custom-call(s32[2]{0:T(128)} %pad_add_fusion.index_ref, bf16[1024,192]{1,0:T(8,128)(2,1)} %all_gather.7.act_ref, bf16[512,4224]{1,0:T(8,128)(2,1)} %shard_map.74.wnat_hbm), custom_call_target="tpu_custom_call" | custom-call | flops 805306368 | bytes 5111808 | tf_op jit(solution)/shard_map/pallas_call | solution.py:138
  (24 shorter events, 0.3 us)
Async XLA Ops:
  6.5 94.1 %all-gather.2.cloned.1.call-start = ((), (), s32[]{:S(2)}) async-start(), calls=%async_computation.1 | async-start | bytes 6488064 | tf_op jit(solution)/shard_map/all_gather | solution.py:175
  8.3 14.2 %collective-permute-start = (bf16[16,4224]{1,0:T(8,128)(2,1)S(1)}, bf16[16,4224]{1,0:T(8,128)(2,1)S(1)}, u32[]{:S(2)}, u32[]{:S(2)}) collective-permute-start(bf16[16,4224]{1,0:T(8,128)(2,1)S(1)} %fusion.1), channel_id=1, source_target_pairs={{0,30},{2,0},{4,2},{6,4},{8,6},{10,8},{12,10},{14,12},{16,14},{18,... | collective-permute-start | bytes 405512 | tf_op jit(solution)/shard_map/ppermute | solution.py:160
  20.2 7.5 %collective-permute-start.8 = (bf16[16,4224]{1,0:T(8,128)(2,1)S(1)}, bf16[16,4224]{1,0:T(8,128)(2,1)S(1)}, u32[]{:S(2)}, u32[]{:S(2)}) collective-permute-start(bf16[16,4224]{1,0:T(8,128)(2,1)S(1)} %fusion.1), channel_id=1, source_target_pairs={{0,2},{2,4},{4,6},{6,8},{8,10},{10,12},{12,14},{14,16},{16,18},{18... | collective-permute-start | bytes 405512 | tf_op jit(solution)/shard_map/ppermute | solution.py:163
  22.2 71.2 %copy-start.1 = (f32[32]{0:T(128)S(1)}, f32[32]{0:T(128)}, u32[]{:S(2)}) copy-start(f32[32]{0:T(128)} %param.9) | copy-start | bytes 388
  22.2 71.9 %copy-start.2 = (f32[32]{0:T(128)S(1)}, f32[32]{0:T(128)}, u32[]{:S(2)}) copy-start(f32[32]{0:T(128)} %param.10) | copy-start | bytes 388
  22.2 72.6 %copy-start.3 = (f32[32]{0:T(128)S(1)}, f32[32]{0:T(128)}, u32[]{:S(2)}) copy-start(f32[32]{0:T(128)} %param.11) | copy-start | bytes 388
  22.5 7.3 %collective-permute-start.1 = (bf16[16,4224]{1,0:T(8,128)(2,1)S(1)}, bf16[16,4224]{1,0:T(8,128)(2,1)S(1)}, u32[]{:S(2)}, u32[]{:S(2)}) collective-permute-start(bf16[16,4224]{1,0:T(8,128)(2,1)S(1)} %collective-permute-done), channel_id=1, source_target_pairs={{0,30},{2,0},{4,2},{6,4},{8,6},{10,8},{12,10},{14,12},{16,14},{18,... | collective-permute-start | bytes 405512 | tf_op jit(solution)/shard_map/ppermute | solution.py:160
  27.8 7.0 %collective-permute-start.9 = (bf16[16,4224]{1,0:T(8,128)(2,1)S(1)}, bf16[16,4224]{1,0:T(8,128)(2,1)S(1)}, u32[]{:S(2)}, u32[]{:S(2)}) collective-permute-start(bf16[16,4224]{1,0:T(8,128)(2,1)S(1)} %collective-permute-done.8), channel_id=1, source_target_pairs={{0,2},{2,4},{4,6},{6,8},{8,10},{10,12},{12,14},{14,16},{16,18},{18... | collective-permute-start | bytes 405512 | tf_op jit(solution)/shard_map/ppermute | solution.py:163
  29.8 7.7 %collective-permute-start.2 = (bf16[16,4224]{1,0:T(8,128)(2,1)S(1)}, bf16[16,4224]{1,0:T(8,128)(2,1)S(1)}, u32[]{:S(2)}, u32[]{:S(2)}) collective-permute-start(bf16[16,4224]{1,0:T(8,128)(2,1)S(1)} %collective-permute-done.1), channel_id=1, source_target_pairs={{0,30},{2,0},{4,2},{6,4},{8,6},{10,8},{12,10},{14,12},{16,14},{18,... | collective-permute-start | bytes 405512 | tf_op jit(solution)/shard_map/ppermute | solution.py:160
  34.8 10.1 %collective-permute-start.10 = (bf16[16,4224]{1,0:T(8,128)(2,1)S(1)}, bf16[16,4224]{1,0:T(8,128)(2,1)S(1)}, u32[]{:S(2)}, u32[]{:S(2)}) collective-permute-start(bf16[16,4224]{1,0:T(8,128)(2,1)S(1)} %collective-permute-done.9), channel_id=1, source_target_pairs={{0,2},{2,4},{4,6},{6,8},{8,10},{10,12},{12,14},{14,16},{16,18},{18... | collective-permute-start | bytes 405512 | tf_op jit(solution)/shard_map/ppermute | solution.py:163
  37.5 9.3 %collective-permute-start.3 = (bf16[16,4224]{1,0:T(8,128)(2,1)S(1)}, bf16[16,4224]{1,0:T(8,128)(2,1)S(1)}, u32[]{:S(2)}, u32[]{:S(2)}) collective-permute-start(bf16[16,4224]{1,0:T(8,128)(2,1)S(1)} %collective-permute-done.2), channel_id=1, source_target_pairs={{0,30},{2,0},{4,2},{6,4},{8,6},{10,8},{12,10},{14,12},{16,14},{18,... | collective-permute-start | bytes 405512 | tf_op jit(solution)/shard_map/ppermute | solution.py:160
  44.8 9.2 %collective-permute-start.11 = (bf16[16,4224]{1,0:T(8,128)(2,1)S(1)}, bf16[16,4224]{1,0:T(8,128)(2,1)S(1)}, u32[]{:S(2)}, u32[]{:S(2)}) collective-permute-start(bf16[16,4224]{1,0:T(8,128)(2,1)S(1)} %collective-permute-done.10), channel_id=1, source_target_pairs={{0,2},{2,4},{4,6},{6,8},{8,10},{10,12},{12,14},{14,16},{16,18},{18... | collective-permute-start | bytes 405512 | tf_op jit(solution)/shard_map/ppermute | solution.py:163
  46.8 9.1 %collective-permute-start.4 = (bf16[16,4224]{1,0:T(8,128)(2,1)S(1)}, bf16[16,4224]{1,0:T(8,128)(2,1)S(1)}, u32[]{:S(2)}, u32[]{:S(2)}) collective-permute-start(bf16[16,4224]{1,0:T(8,128)(2,1)S(1)} %collective-permute-done.3), channel_id=1, source_target_pairs={{0,30},{2,0},{4,2},{6,4},{8,6},{10,8},{12,10},{14,12},{16,14},{18,... | collective-permute-start | bytes 405512 | tf_op jit(solution)/shard_map/ppermute | solution.py:160
  54.0 8.5 %collective-permute-start.12 = (bf16[16,4224]{1,0:T(8,128)(2,1)S(1)}, bf16[16,4224]{1,0:T(8,128)(2,1)S(1)}, u32[]{:S(2)}, u32[]{:S(2)}) collective-permute-start(bf16[16,4224]{1,0:T(8,128)(2,1)S(1)} %collective-permute-done.11), channel_id=1, source_target_pairs={{0,2},{2,4},{4,6},{6,8},{8,10},{10,12},{12,14},{14,16},{16,18},{18... | collective-permute-start | bytes 405512 | tf_op jit(solution)/shard_map/ppermute | solution.py:163
  55.9 8.5 %collective-permute-start.5 = (bf16[16,4224]{1,0:T(8,128)(2,1)S(1)}, bf16[16,4224]{1,0:T(8,128)(2,1)S(1)}, u32[]{:S(2)}, u32[]{:S(2)}) collective-permute-start(bf16[16,4224]{1,0:T(8,128)(2,1)S(1)} %collective-permute-done.4), channel_id=1, source_target_pairs={{0,30},{2,0},{4,2},{6,4},{8,6},{10,8},{12,10},{14,12},{16,14},{18,... | collective-permute-start | bytes 405512 | tf_op jit(solution)/shard_map/ppermute | solution.py:160
  62.5 8.8 %collective-permute-start.13 = (bf16[16,4224]{1,0:T(8,128)(2,1)S(1)}, bf16[16,4224]{1,0:T(8,128)(2,1)S(1)}, u32[]{:S(2)}, u32[]{:S(2)}) collective-permute-start(bf16[16,4224]{1,0:T(8,128)(2,1)S(1)} %collective-permute-done.12), channel_id=1, source_target_pairs={{0,2},{2,4},{4,6},{6,8},{8,10},{10,12},{12,14},{14,16},{16,18},{18... | collective-permute-start | bytes 405512 | tf_op jit(solution)/shard_map/ppermute | solution.py:163
  64.5 8.8 %collective-permute-start.6 = (bf16[16,4224]{1,0:T(8,128)(2,1)S(1)}, bf16[16,4224]{1,0:T(8,128)(2,1)S(1)}, u32[]{:S(2)}, u32[]{:S(2)}) collective-permute-start(bf16[16,4224]{1,0:T(8,128)(2,1)S(1)} %collective-permute-done.5), channel_id=1, source_target_pairs={{0,30},{2,0},{4,2},{6,4},{8,6},{10,8},{12,10},{14,12},{16,14},{18,... | collective-permute-start | bytes 405512 | tf_op jit(solution)/shard_map/ppermute | solution.py:160
  71.3 11.5 %collective-permute-start.14 = (bf16[16,4224]{1,0:T(8,128)(2,1)S(1)}, bf16[16,4224]{1,0:T(8,128)(2,1)S(1)}, u32[]{:S(2)}, u32[]{:S(2)}) collective-permute-start(bf16[16,4224]{1,0:T(8,128)(2,1)S(1)} %collective-permute-done.13), channel_id=1, source_target_pairs={{0,2},{2,4},{4,6},{6,8},{8,10},{10,12},{12,14},{14,16},{16,18},{18... | collective-permute-start | bytes 405512 | tf_op jit(solution)/shard_map/ppermute | solution.py:163
  73.3 9.5 %collective-permute-start.7 = (bf16[16,4224]{1,0:T(8,128)(2,1)S(1)}, bf16[16,4224]{1,0:T(8,128)(2,1)S(1)}, u32[]{:S(2)}, u32[]{:S(2)}) collective-permute-start(bf16[16,4224]{1,0:T(8,128)(2,1)S(1)} %collective-permute-done.6), channel_id=1, source_target_pairs={{0,30},{2,0},{4,2},{6,4},{8,6},{10,8},{12,10},{14,12},{16,14},{18,... | collective-permute-start | bytes 405512 | tf_op jit(solution)/shard_map/ppermute | solution.py:160
  82.9 24.1 %copy-start = (bf16[16,16,4224]{2,1,0:T(8,128)(2,1)}, bf16[16,16,4224]{2,1,0:T(8,128)(2,1)S(1)}, u32[]{:S(2)}) copy-start(bf16[16,16,4224]{2,1,0:T(8,128)(2,1)S(1)} %bitcast_dynamic-update-slice_fusion.own_ref) | copy-start | bytes 6488068
  83.0 34.5 %collective-permute-start.15 = (bf16[16,16,4224]{2,1,0:T(8,128)(2,1)S(1)}, bf16[16,16,4224]{2,1,0:T(8,128)(2,1)}, u32[]{:S(2)}, u32[]{:S(2)}) collective-permute-start(bf16[16,16,4224]{2,1,0:T(8,128)(2,1)S(1)} %bitcast_dynamic-update-slice_fusion.own_ref), channel_id=1, source_target_pairs={{0,1},{1,0},{2,3},{3,2},{4,5},{5,4},{6,7},{7,6},{8,9},{9,8},{10,11... | collective-permute-start | bytes 6488072 | tf_op jit(solution)/shard_map/ppermute | solution.py:180
  107.1 24.2 %all-to-all-start = ((bf16[16,32,192]{2,1,0:T(8,128)(2,1)}), bf16[16,32,192]{2,1,0:T(8,128)(2,1)S(1)}, u32[]{:S(2)}, u32[]{:S(2)}) async-start(bf16[16,32,192]{2,1,0:T(8,128)(2,1)} %shard_map.73), calls=%async_computation | async-start | bytes 524288 | tf_op jit(solution)/shard_map/all_to_all | solution.py:185
Sparse Core Ops, SparseCore 0:
  22.3 78.3 all-gather.1

commit v20 on v15

--- a/solution.py
+++ b/solution.py
@@ -16,8 +16,8 @@
     taps = lax.dot_general(w_ref[...], x_ref[...], (((1,), (1,)), ((), ())),
                            preferred_element_type=jnp.float32)
     pos = lax.broadcasted_iota(jnp.int32, (1, positions), 1)
-    row = pos // width_cols
-    col = pos % width_cols
+    posf = pos.astype(jnp.float32)
+    col = (posf - width_cols * jnp.floor((posf + 0.5) * (1.0 / width_cols))).astype(jnp.int32)
     acc = jnp.zeros((outputs, positions), jnp.float32)
     for t in range(9):
         r, s = divmod(t, 3)
@@ -25,7 +25,7 @@
         part = taps[t * outputs:(t + 1) * outputs, :]
         if off:
             part = pltpu.roll(part, (-off) % positions, 1)
-        valid = ((row + (r - 1) >= 0) & (row + (r - 1) < height)
+        valid = ((pos + (r - 1) * width_cols >= 0) & (pos + (r - 1) * width_cols < positions)
                  & (col + (s - 1) >= 0) & (col + (s - 1) < width_cols))
         acc = acc + jnp.where(valid, part, 0.0)
     conv = acc + bias_ref[...]

time: 151 us -> 151 us (level)
  no operation moved by 1% of the time
where the time goes in v20:
time: 151 us; the launch traced here: 150 us
  starting transfers between devices  79.4 us (53%)
  waiting for transfers between devices  29.3 us (19%)
  Pallas kernels  15.9 us (11%)
  between operations  13.7 us (9%)
  blocking collectives  6.66 us (4%)
  local copies, waits for them, and re-layouts  4.07 us (3%)
    ppermute x8, starting transfers between devices, ring_gather(): ahead = lax.ppermute(ahead, axis, step_up)  45.9 us
    ppermute x7, starting transfers between devices, ring_gather(): behind = lax.ppermute(behind, axis, step_down)  13.4 us
    ppermute x1, starting transfers between devices, body(): packed_other = lax.ppermute(packed_z, 'core', [(0, 1), (1, 0)])  10.5 us
    all_to_all x1, starting transfers between devices, body(): lax.all_to_all(activated, 'z', split_axis=0, concat_axis=0, tiled=True)  9.74 us
    all_to_all x1, waiting for transfers between devices, body(): lax.all_to_all(activated, 'z', split_axis=0, concat_axis=0, tiled=True)  9.21 us
    ppermute x7, waiting for transfers between devices, ring_gather(): behind = lax.ppermute(behind, axis, step_down)  8.94 us
    all_gather x1, blocking collectives, body(): both = lax.all_gather(chip_rows, 'core', axis=0, tiled=True)  6.66 us
    pallas_call x1, Pallas kernels, conv_norm(): pl.pallas_call(functools.partial(conv_norm_kernel, height=height, width_c...  6.37 us
  transfers between devices with their start and end apart: 18, of which 9 were waited for; matrix products, arithmetic and copies ran while one was open for 2% of the time, Pallas kernels for 7%

profile of v20, /device:TPU:1, one launch (start us, length us, event | category | flops | bytes accessed | tf_op | source)
XLA Modules:
  0.0 149.8 jit_solution(519494121511290618)
XLA Ops:
  6.5 0.7 copy.15
  7.3 1.0 reshape.31
  8.3 12.0 %collective-permute-start = (bf16[16,4224]{1,0:T(8,128)(2,1)S(1)}, bf16[16,4224]{1,0:T(8,128)(2,1)S(1)}, u32[]{:S(2)}, u32[]{:S(2)}) collective-permute-start(bf16[16,4224]{1,0:T(8,128)(2,1)S(1)} %fusion.1), channel_id=1, source_target_pairs={{0,30},{2,0},{4,2},{6,4},{8,6},{10,8},{12,10},{14,12},{16,14},{18,... | collective-permute-start | bytes 405512 | tf_op jit(solution)/shard_map/ppermute | solution.py:151
  20.2 1.9 %collective-permute-start.8 = (bf16[16,4224]{1,0:T(8,128)(2,1)S(1)}, bf16[16,4224]{1,0:T(8,128)(2,1)S(1)}, u32[]{:S(2)}, u32[]{:S(2)}) collective-permute-start(bf16[16,4224]{1,0:T(8,128)(2,1)S(1)} %fusion.1), channel_id=1, source_target_pairs={{0,2},{2,4},{4,6},{6,8},{8,10},{10,12},{12,14},{14,16},{16,18},{18... | collective-permute-start | bytes 405512 | tf_op jit(solution)/shard_map/ppermute | solution.py:154
  22.2 0.0 all-gather.2.cloned.1.call-update
  22.2 0.0 copy-start.1
  22.2 0.0 copy-start.2
  22.2 0.0 copy-start.3
  22.3 0.2 collective-permute-done
  22.5 5.3 %collective-permute-start.1 = (bf16[16,4224]{1,0:T(8,128)(2,1)S(1)}, bf16[16,4224]{1,0:T(8,128)(2,1)S(1)}, u32[]{:S(2)}, u32[]{:S(2)}) collective-permute-start(bf16[16,4224]{1,0:T(8,128)(2,1)S(1)} %collective-permute-done), channel_id=1, source_target_pairs={{0,30},{2,0},{4,2},{6,4},{8,6},{10,8},{12,10},{14,12},{16,14},{18,... | collective-permute-start | bytes 405512 | tf_op jit(solution)/shard_map/ppermute | solution.py:151
  27.8 0.0 collective-permute-done.8
  27.8 1.9 %collective-permute-start.9 = (bf16[16,4224]{1,0:T(8,128)(2,1)S(1)}, bf16[16,4224]{1,0:T(8,128)(2,1)S(1)}, u32[]{:S(2)}, u32[]{:S(2)}) collective-permute-start(bf16[16,4224]{1,0:T(8,128)(2,1)S(1)} %collective-permute-done.8), channel_id=1, source_target_pairs={{0,2},{2,4},{4,6},{6,8},{8,10},{10,12},{12,14},{14,16},{16,18},{18... | collective-permute-start | bytes 405512 | tf_op jit(solution)/shard_map/ppermute | solution.py:154
  29.7 0.0 collective-permute-done.1
  29.8 5.0 %collective-permute-start.2 = (bf16[16,4224]{1,0:T(8,128)(2,1)S(1)}, bf16[16,4224]{1,0:T(8,128)(2,1)S(1)}, u32[]{:S(2)}, u32[]{:S(2)}) collective-permute-start(bf16[16,4224]{1,0:T(8,128)(2,1)S(1)} %collective-permute-done.1), channel_id=1, source_target_pairs={{0,30},{2,0},{4,2},{6,4},{8,6},{10,8},{12,10},{14,12},{16,14},{18,... | collective-permute-start | bytes 405512 | tf_op jit(solution)/shard_map/ppermute | solution.py:151
  34.7 0.0 collective-permute-done.9
  34.8 1.9 %collective-permute-start.10 = (bf16[16,4224]{1,0:T(8,128)(2,1)S(1)}, bf16[16,4224]{1,0:T(8,128)(2,1)S(1)}, u32[]{:S(2)}, u32[]{:S(2)}) collective-permute-start(bf16[16,4224]{1,0:T(8,128)(2,1)S(1)} %collective-permute-done.9), channel_id=1, source_target_pairs={{0,2},{2,4},{4,6},{6,8},{8,10},{10,12},{12,14},{14,16},{16,18},{18... | collective-permute-start | bytes 405512 | tf_op jit(solution)/shard_map/ppermute | solution.py:154
  36.7 0.8 collective-permute-done.2
  37.5 5.0 %collective-permute-start.3 = (bf16[16,4224]{1,0:T(8,128)(2,1)S(1)}, bf16[16,4224]{1,0:T(8,128)(2,1)S(1)}, u32[]{:S(2)}, u32[]{:S(2)}) collective-permute-start(bf16[16,4224]{1,0:T(8,128)(2,1)S(1)} %collective-permute-done.2), channel_id=1, source_target_pairs={{0,30},{2,0},{4,2},{6,4},{8,6},{10,8},{12,10},{14,12},{16,14},{18,... | collective-permute-start | bytes 405512 | tf_op jit(solution)/shard_map/ppermute | solution.py:151
  42.5 2.3 %collective-permute-done.10 = bf16[16,4224]{1,0:T(8,128)(2,1)S(1)} collective-permute-done((bf16[16,4224]{1,0:T(8,128)(2,1)S(1)}, bf16[16,4224]{1,0:T(8,128)(2,1)S(1)}, u32[]{:S(2)}, u32[]{:S(2)}) %collective-permute-start.10) | collective-permute-done | bytes 135200 | tf_op jit(solution)/shard_map/ppermute | solution.py:154
  44.8 1.9 %collective-permute-start.11 = (bf16[16,4224]{1,0:T(8,128)(2,1)S(1)}, bf16[16,4224]{1,0:T(8,128)(2,1)S(1)}, u32[]{:S(2)}, u32[]{:S(2)}) collective-permute-start(bf16[16,4224]{1,0:T(8,128)(2,1)S(1)} %collective-permute-done.10), channel_id=1, source_target_pairs={{0,2},{2,4},{4,6},{6,8},{8,10},{10,12},{12,14},{14,16},{16,18},{18... | collective-permute-start | bytes 405512 | tf_op jit(solution)/shard_map/ppermute | solution.py:154
  46.8 0.0 collective-permute-done.3
  46.8 4.9 %collective-permute-start.4 = (bf16[16,4224]{1,0:T(8,128)(2,1)S(1)}, bf16[16,4224]{1,0:T(8,128)(2,1)S(1)}, u32[]{:S(2)}, u32[]{:S(2)}) collective-permute-start(bf16[16,4224]{1,0:T(8,128)(2,1)S(1)} %collective-permute-done.3), channel_id=1, source_target_pairs={{0,30},{2,0},{4,2},{6,4},{8,6},{10,8},{12,10},{14,12},{16,14},{18,... | collective-permute-start | bytes 405512 | tf_op jit(solution)/shard_map/ppermute | solution.py:151
  51.7 2.3 %collective-permute-done.11 = bf16[16,4224]{1,0:T(8,128)(2,1)S(1)} collective-permute-done((bf16[16,4224]{1,0:T(8,128)(2,1)S(1)}, bf16[16,4224]{1,0:T(8,128)(2,1)S(1)}, u32[]{:S(2)}, u32[]{:S(2)}) %collective-permute-start.11) | collective-permute-done | bytes 135200 | tf_op jit(solution)/shard_map/ppermute | solution.py:154
  54.0 1.9 %collective-permute-start.12 = (bf16[16,4224]{1,0:T(8,128)(2,1)S(1)}, bf16[16,4224]{1,0:T(8,128)(2,1)S(1)}, u32[]{:S(2)}, u32[]{:S(2)}) collective-permute-start(bf16[16,4224]{1,0:T(8,128)(2,1)S(1)} %collective-permute-done.11), channel_id=1, source_target_pairs={{0,2},{2,4},{4,6},{6,8},{8,10},{10,12},{12,14},{14,16},{16,18},{18... | collective-permute-start | bytes 405512 | tf_op jit(solution)/shard_map/ppermute | solution.py:154
  55.9 0.0 collective-permute-done.4
  55.9 4.6 %collective-permute-start.5 = (bf16[16,4224]{1,0:T(8,128)(2,1)S(1)}, bf16[16,4224]{1,0:T(8,128)(2,1)S(1)}, u32[]{:S(2)}, u32[]{:S(2)}) collective-permute-start(bf16[16,4224]{1,0:T(8,128)(2,1)S(1)} %collective-permute-done.4), channel_id=1, source_target_pairs={{0,30},{2,0},{4,2},{6,4},{8,6},{10,8},{12,10},{14,12},{16,14},{18,... | collective-permute-start | bytes 405512 | tf_op jit(solution)/shard_map/ppermute | solution.py:151
  60.5 2.0 %collective-permute-done.12 = bf16[16,4224]{1,0:T(8,128)(2,1)S(1)} collective-permute-done((bf16[16,4224]{1,0:T(8,128)(2,1)S(1)}, bf16[16,4224]{1,0:T(8,128)(2,1)S(1)}, u32[]{:S(2)}, u32[]{:S(2)}) %collective-permute-start.12) | collective-permute-done | bytes 135200 | tf_op jit(solution)/shard_map/ppermute | solution.py:154
  62.5 1.9 %collective-permute-start.13 = (bf16[16,4224]{1,0:T(8,128)(2,1)S(1)}, bf16[16,4224]{1,0:T(8,128)(2,1)S(1)}, u32[]{:S(2)}, u32[]{:S(2)}) collective-permute-start(bf16[16,4224]{1,0:T(8,128)(2,1)S(1)} %collective-permute-done.12), channel_id=1, source_target_pairs={{0,2},{2,4},{4,6},{6,8},{8,10},{10,12},{12,14},{14,16},{16,18},{18... | collective-permute-start | bytes 405512 | tf_op jit(solution)/shard_map/ppermute | solution.py:154
  64.5 0.0 collective-permute-done.5
  64.5 4.6 %collective-permute-start.6 = (bf16[16,4224]{1,0:T(8,128)(2,1)S(1)}, bf16[16,4224]{1,0:T(8,128)(2,1)S(1)}, u32[]{:S(2)}, u32[]{:S(2)}) collective-permute-start(bf16[16,4224]{1,0:T(8,128)(2,1)S(1)} %collective-permute-done.5), channel_id=1, source_target_pairs={{0,30},{2,0},{4,2},{6,4},{8,6},{10,8},{12,10},{14,12},{16,14},{18,... | collective-permute-start | bytes 405512 | tf_op jit(solution)/shard_map/ppermute | solution.py:151
  69.1 2.3 %collective-permute-done.13 = bf16[16,4224]{1,0:T(8,128)(2,1)S(1)} collective-permute-done((bf16[16,4224]{1,0:T(8,128)(2,1)S(1)}, bf16[16,4224]{1,0:T(8,128)(2,1)S(1)}, u32[]{:S(2)}, u32[]{:S(2)}) %collective-permute-start.13) | collective-permute-done | bytes 135200 | tf_op jit(solution)/shard_map/ppermute | solution.py:154
  71.3 1.9 %collective-permute-start.14 = (bf16[16,4224]{1,0:T(8,128)(2,1)S(1)}, bf16[16,4224]{1,0:T(8,128)(2,1)S(1)}, u32[]{:S(2)}, u32[]{:S(2)}) collective-permute-start(bf16[16,4224]{1,0:T(8,128)(2,1)S(1)} %collective-permute-done.13), channel_id=1, source_target_pairs={{0,2},{2,4},{4,6},{6,8},{8,10},{10,12},{12,14},{14,16},{16,18},{18... | collective-permute-start | bytes 405512 | tf_op jit(solution)/shard_map/ppermute | solution.py:154
  73.2 0.0 collective-permute-done.6
  73.3 4.6 %collective-permute-start.7 = (bf16[16,4224]{1,0:T(8,128)(2,1)S(1)}, bf16[16,4224]{1,0:T(8,128)(2,1)S(1)}, u32[]{:S(2)}, u32[]{:S(2)}) collective-permute-start(bf16[16,4224]{1,0:T(8,128)(2,1)S(1)} %collective-permute-done.6), channel_id=1, source_target_pairs={{0,30},{2,0},{4,2},{6,4},{8,6},{10,8},{12,10},{14,12},{16,14},{18,... | collective-permute-start | bytes 405512 | tf_op jit(solution)/shard_map/ppermute | solution.py:151
  77.9 4.9 %collective-permute-done.7 = bf16[16,4224]{1,0:T(8,128)(2,1)S(1)} collective-permute-done((bf16[16,4224]{1,0:T(8,128)(2,1)S(1)}, bf16[16,4224]{1,0:T(8,128)(2,1)S(1)}, u32[]{:S(2)}, u32[]{:S(2)}) %collective-permute-start.7) | collective-permute-done | bytes 135200 | tf_op jit(solution)/shard_map/ppermute | solution.py:151
  82.8 0.0 collective-permute-done.14
  83.0 10.5 %collective-permute-start.15 = (bf16[16,16,4224]{2,1,0:T(8,128)(2,1)S(1)}, bf16[16,16,4224]{2,1,0:T(8,128)(2,1)}, u32[]{:S(2)}, u32[]{:S(2)}) collective-permute-start(bf16[16,16,4224]{2,1,0:T(8,128)(2,1)S(1)} %bitcast_dynamic-update-slice_fusion.own_ref), channel_id=1, source_target_pairs={{0,1},{1,0},{2,3},{3,2},{4,5},{5,4},{6,7},{7,6},{8,9},{9,8},{10,11... | collective-permute-start | bytes 6488072 | tf_op jit(solution)/shard_map/ppermute | solution.py:171
  93.4 0.7 copy.12.bias_ref
  94.1 0.7 copy.13.gain_ref
  94.8 0.7 copy.14.shift_ref
  95.5 5.2 %all-gather.2.cloned.1.call-done = bf16[64,48,1024]{2,1,0:T(8,128)(2,1)} async-done(((bf16[2,48,1024]{2,1,0:T(8,128)(2,1)}), bf16[64,48,1024]{2,1,0:T(8,128)(2,1)}) %all-gather.2.cloned.1.call-update) | async-done | bytes 6291472 | tf_op jit(solution)/shard_map/all_gather | solution.py:166
  100.7 6.4 %shard_map.73 = bf16[16,32,192]{2,1,0:T(8,128)(2,1)} custom-call(bf16[3072,1024]{1,0:T(8,128)(2,1)} %bitcast.45, bf16[288,1024]{1,0:T(8,128)(2,1)} %bitcast.47, f32[32,1]{1,0:T(8,128)} %copy.12.bias_ref, f32[32,1]{1,0:T(8,128)} %copy.13.gain_ref, f32[32,1]{1,0:T(8,128)} %copy.14.shift_ref), custom_call_target="tpu_custom_call" | custom-call | flops 1811939328 | bytes 7077888 | tf_op jit(solution)/shard_map/pallas_call | solution.py:53
  107.1 9.7 %all-to-all-start = ((bf16[16,32,192]{2,1,0:T(8,128)(2,1)}), bf16[16,32,192]{2,1,0:T(8,128)(2,1)S(1)}, u32[]{:S(2)}, u32[]{:S(2)}) async-start(bf16[16,32,192]{2,1,0:T(8,128)(2,1)} %shard_map.73), calls=%async_computation | async-start | bytes 524288 | tf_op jit(solution)/shard_map/all_to_all | solution.py:176
  116.8 0.7 pad_add_fusion.index_ref
  117.5 4.6 %shard_map.74.wnat_ref = bf16[512,4224]{1,0:T(8,128)(2,1)} custom-call(s32[2]{0:T(128)} %pad_add_fusion.index_ref, bf16[16,16,4224]{2,1,0:T(8,128)(2,1)} %copy-done, bf16[16,16,4224]{2,1,0:T(8,128)(2,1)} %collective-permute-done.15.other_ref), custom_call_target="tpu_custom_call" | custom-call | bytes 8650752 | tf_op jit(solution)/shard_map/pallas_call | solution.py:81
  122.0 9.2 %all-to-all-done = bf16[16,32,192]{2,1,0:T(8,128)(2,1)S(1)} async-done(((bf16[16,32,192]{2,1,0:T(8,128)(2,1)}), bf16[16,32,192]{2,1,0:T(8,128)(2,1)S(1)}, u32[]{:S(2)}, u32[]{:S(2)}) %all-to-all-start) | async-done | bytes 196640 | tf_op jit(solution)/shard_map/all_to_all | solution.py:176
  131.2 6.7 %all_gather.7.act_ref = bf16[1024,192]{1,0:T(8,128)(2,1)} all-gather(bf16[512,192]{1,0:T(8,128)(2,1)S(1)} %bitcast.46), channel_id=1, replica_groups=mesh['grp'=16,'z'=16,'core'=2] {'core'}, dimensions={0}, use_global_device_ids=true | all-gather | bytes 589824 | tf_op jit(solution)/shard_map/all_gather | solution.py:178
  137.9 5.0 %shard_map.75 = bf16[4,96,512]{2,1,0:T(8,128)(2,1)} custom-call(s32[2]{0:T(128)} %pad_add_fusion.index_ref, bf16[1024,192]{1,0:T(8,128)(2,1)} %all_gather.7.act_ref, bf16[512,4224]{1,0:T(8,128)(2,1)} %shard_map.74.wnat_ref), custom_call_target="tpu_custom_call" | custom-call | flops 805306368 | bytes 5111808 | tf_op jit(solution)/shard_map/pallas_call | solution.py:132
  (24 shorter events, 0.3 us)
Async XLA Ops:
  6.5 94.1 %all-gather.2.cloned.1.call-start = ((), (), s32[]{:S(2)}) async-start(), calls=%async_computation.1 | async-start | bytes 6488064 | tf_op jit(solution)/shard_map/all_gather | solution.py:166
  8.3 14.2 %collective-permute-start = (bf16[16,4224]{1,0:T(8,128)(2,1)S(1)}, bf16[16,4224]{1,0:T(8,128)(2,1)S(1)}, u32[]{:S(2)}, u32[]{:S(2)}) collective-permute-start(bf16[16,4224]{1,0:T(8,128)(2,1)S(1)} %fusion.1), channel_id=1, source_target_pairs={{0,30},{2,0},{4,2},{6,4},{8,6},{10,8},{12,10},{14,12},{16,14},{18,... | collective-permute-start | bytes 405512 | tf_op jit(solution)/shard_map/ppermute | solution.py:151
  20.2 7.5 %collective-permute-start.8 = (bf16[16,4224]{1,0:T(8,128)(2,1)S(1)}, bf16[16,4224]{1,0:T(8,128)(2,1)S(1)}, u32[]{:S(2)}, u32[]{:S(2)}) collective-permute-start(bf16[16,4224]{1,0:T(8,128)(2,1)S(1)} %fusion.1), channel_id=1, source_target_pairs={{0,2},{2,4},{4,6},{6,8},{8,10},{10,12},{12,14},{14,16},{16,18},{18... | collective-permute-start | bytes 405512 | tf_op jit(solution)/shard_map/ppermute | solution.py:154
  22.2 71.2 %copy-start.1 = (f32[32]{0:T(128)S(1)}, f32[32]{0:T(128)}, u32[]{:S(2)}) copy-start(f32[32]{0:T(128)} %param.9) | copy-start | bytes 388
  22.2 71.9 %copy-start.2 = (f32[32]{0:T(128)S(1)}, f32[32]{0:T(128)}, u32[]{:S(2)}) copy-start(f32[32]{0:T(128)} %param.10) | copy-start | bytes 388
  22.2 72.6 %copy-start.3 = (f32[32]{0:T(128)S(1)}, f32[32]{0:T(128)}, u32[]{:S(2)}) copy-start(f32[32]{0:T(128)} %param.11) | copy-start | bytes 388
  22.5 7.3 %collective-permute-start.1 = (bf16[16,4224]{1,0:T(8,128)(2,1)S(1)}, bf16[16,4224]{1,0:T(8,128)(2,1)S(1)}, u32[]{:S(2)}, u32[]{:S(2)}) collective-permute-start(bf16[16,4224]{1,0:T(8,128)(2,1)S(1)} %collective-permute-done), channel_id=1, source_target_pairs={{0,30},{2,0},{4,2},{6,4},{8,6},{10,8},{12,10},{14,12},{16,14},{18,... | collective-permute-start | bytes 405512 | tf_op jit(solution)/shard_map/ppermute | solution.py:151
  27.8 7.0 %collective-permute-start.9 = (bf16[16,4224]{1,0:T(8,128)(2,1)S(1)}, bf16[16,4224]{1,0:T(8,128)(2,1)S(1)}, u32[]{:S(2)}, u32[]{:S(2)}) collective-permute-start(bf16[16,4224]{1,0:T(8,128)(2,1)S(1)} %collective-permute-done.8), channel_id=1, source_target_pairs={{0,2},{2,4},{4,6},{6,8},{8,10},{10,12},{12,14},{14,16},{16,18},{18... | collective-permute-start | bytes 405512 | tf_op jit(solution)/shard_map/ppermute | solution.py:154
  29.8 7.7 %collective-permute-start.2 = (bf16[16,4224]{1,0:T(8,128)(2,1)S(1)}, bf16[16,4224]{1,0:T(8,128)(2,1)S(1)}, u32[]{:S(2)}, u32[]{:S(2)}) collective-permute-start(bf16[16,4224]{1,0:T(8,128)(2,1)S(1)} %collective-permute-done.1), channel_id=1, source_target_pairs={{0,30},{2,0},{4,2},{6,4},{8,6},{10,8},{12,10},{14,12},{16,14},{18,... | collective-permute-start | bytes 405512 | tf_op jit(solution)/shard_map/ppermute | solution.py:151
  34.8 10.1 %collective-permute-start.10 = (bf16[16,4224]{1,0:T(8,128)(2,1)S(1)}, bf16[16,4224]{1,0:T(8,128)(2,1)S(1)}, u32[]{:S(2)}, u32[]{:S(2)}) collective-permute-start(bf16[16,4224]{1,0:T(8,128)(2,1)S(1)} %collective-permute-done.9), channel_id=1, source_target_pairs={{0,2},{2,4},{4,6},{6,8},{8,10},{10,12},{12,14},{14,16},{16,18},{18... | collective-permute-start | bytes 405512 | tf_op jit(solution)/shard_map/ppermute | solution.py:154
  37.5 9.3 %collective-permute-start.3 = (bf16[16,4224]{1,0:T(8,128)(2,1)S(1)}, bf16[16,4224]{1,0:T(8,128)(2,1)S(1)}, u32[]{:S(2)}, u32[]{:S(2)}) collective-permute-start(bf16[16,4224]{1,0:T(8,128)(2,1)S(1)} %collective-permute-done.2), channel_id=1, source_target_pairs={{0,30},{2,0},{4,2},{6,4},{8,6},{10,8},{12,10},{14,12},{16,14},{18,... | collective-permute-start | bytes 405512 | tf_op jit(solution)/shard_map/ppermute | solution.py:151
  44.8 9.2 %collective-permute-start.11 = (bf16[16,4224]{1,0:T(8,128)(2,1)S(1)}, bf16[16,4224]{1,0:T(8,128)(2,1)S(1)}, u32[]{:S(2)}, u32[]{:S(2)}) collective-permute-start(bf16[16,4224]{1,0:T(8,128)(2,1)S(1)} %collective-permute-done.10), channel_id=1, source_target_pairs={{0,2},{2,4},{4,6},{6,8},{8,10},{10,12},{12,14},{14,16},{16,18},{18... | collective-permute-start | bytes 405512 | tf_op jit(solution)/shard_map/ppermute | solution.py:154
  46.8 9.1 %collective-permute-start.4 = (bf16[16,4224]{1,0:T(8,128)(2,1)S(1)}, bf16[16,4224]{1,0:T(8,128)(2,1)S(1)}, u32[]{:S(2)}, u32[]{:S(2)}) collective-permute-start(bf16[16,4224]{1,0:T(8,128)(2,1)S(1)} %collective-permute-done.3), channel_id=1, source_target_pairs={{0,30},{2,0},{4,2},{6,4},{8,6},{10,8},{12,10},{14,12},{16,14},{18,... | collective-permute-start | bytes 405512 | tf_op jit(solution)/shard_map/ppermute | solution.py:151
  54.0 8.5 %collective-permute-start.12 = (bf16[16,4224]{1,0:T(8,128)(2,1)S(1)}, bf16[16,4224]{1,0:T(8,128)(2,1)S(1)}, u32[]{:S(2)}, u32[]{:S(2)}) collective-permute-start(bf16[16,4224]{1,0:T(8,128)(2,1)S(1)} %collective-permute-done.11), channel_id=1, source_target_pairs={{0,2},{2,4},{4,6},{6,8},{8,10},{10,12},{12,14},{14,16},{16,18},{18... | collective-permute-start | bytes 405512 | tf_op jit(solution)/shard_map/ppermute | solution.py:154
  55.9 8.5 %collective-permute-start.5 = (bf16[16,4224]{1,0:T(8,128)(2,1)S(1)}, bf16[16,4224]{1,0:T(8,128)(2,1)S(1)}, u32[]{:S(2)}, u32[]{:S(2)}) collective-permute-start(bf16[16,4224]{1,0:T(8,128)(2,1)S(1)} %collective-permute-done.4), channel_id=1, source_target_pairs={{0,30},{2,0},{4,2},{6,4},{8,6},{10,8},{12,10},{14,12},{16,14},{18,... | collective-permute-start | bytes 405512 | tf_op jit(solution)/shard_map/ppermute | solution.py:151
  62.5 8.8 %collective-permute-start.13 = (bf16[16,4224]{1,0:T(8,128)(2,1)S(1)}, bf16[16,4224]{1,0:T(8,128)(2,1)S(1)}, u32[]{:S(2)}, u32[]{:S(2)}) collective-permute-start(bf16[16,4224]{1,0:T(8,128)(2,1)S(1)} %collective-permute-done.12), channel_id=1, source_target_pairs={{0,2},{2,4},{4,6},{6,8},{8,10},{10,12},{12,14},{14,16},{16,18},{18... | collective-permute-start | bytes 405512 | tf_op jit(solution)/shard_map/ppermute | solution.py:154
  64.5 8.8 %collective-permute-start.6 = (bf16[16,4224]{1,0:T(8,128)(2,1)S(1)}, bf16[16,4224]{1,0:T(8,128)(2,1)S(1)}, u32[]{:S(2)}, u32[]{:S(2)}) collective-permute-start(bf16[16,4224]{1,0:T(8,128)(2,1)S(1)} %collective-permute-done.5), channel_id=1, source_target_pairs={{0,30},{2,0},{4,2},{6,4},{8,6},{10,8},{12,10},{14,12},{16,14},{18,... | collective-permute-start | bytes 405512 | tf_op jit(solution)/shard_map/ppermute | solution.py:151
  71.3 11.5 %collective-permute-start.14 = (bf16[16,4224]{1,0:T(8,128)(2,1)S(1)}, bf16[16,4224]{1,0:T(8,128)(2,1)S(1)}, u32[]{:S(2)}, u32[]{:S(2)}) collective-permute-start(bf16[16,4224]{1,0:T(8,128)(2,1)S(1)} %collective-permute-done.13), channel_id=1, source_target_pairs={{0,2},{2,4},{4,6},{6,8},{8,10},{10,12},{12,14},{14,16},{16,18},{18... | collective-permute-start | bytes 405512 | tf_op jit(solution)/shard_map/ppermute | solution.py:154
  73.3 9.5 %collective-permute-start.7 = (bf16[16,4224]{1,0:T(8,128)(2,1)S(1)}, bf16[16,4224]{1,0:T(8,128)(2,1)S(1)}, u32[]{:S(2)}, u32[]{:S(2)}) collective-permute-start(bf16[16,4224]{1,0:T(8,128)(2,1)S(1)} %collective-permute-done.6), channel_id=1, source_target_pairs={{0,30},{2,0},{4,2},{6,4},{8,6},{10,8},{12,10},{14,12},{16,14},{18,... | collective-permute-start | bytes 405512 | tf_op jit(solution)/shard_map/ppermute | solution.py:151
  82.9 24.1 %copy-start = (bf16[16,16,4224]{2,1,0:T(8,128)(2,1)}, bf16[16,16,4224]{2,1,0:T(8,128)(2,1)S(1)}, u32[]{:S(2)}) copy-start(bf16[16,16,4224]{2,1,0:T(8,128)(2,1)S(1)} %bitcast_dynamic-update-slice_fusion.own_ref) | copy-start | bytes 6488068
  83.0 34.5 %collective-permute-start.15 = (bf16[16,16,4224]{2,1,0:T(8,128)(2,1)S(1)}, bf16[16,16,4224]{2,1,0:T(8,128)(2,1)}, u32[]{:S(2)}, u32[]{:S(2)}) collective-permute-start(bf16[16,16,4224]{2,1,0:T(8,128)(2,1)S(1)} %bitcast_dynamic-update-slice_fusion.own_ref), channel_id=1, source_target_pairs={{0,1},{1,0},{2,3},{3,2},{4,5},{5,4},{6,7},{7,6},{8,9},{9,8},{10,11... | collective-permute-start | bytes 6488072 | tf_op jit(solution)/shard_map/ppermute | solution.py:171
  107.1 24.2 %all-to-all-start = ((bf16[16,32,192]{2,1,0:T(8,128)(2,1)}), bf16[16,32,192]{2,1,0:T(8,128)(2,1)S(1)}, u32[]{:S(2)}, u32[]{:S(2)}) async-start(bf16[16,32,192]{2,1,0:T(8,128)(2,1)} %shard_map.73), calls=%async_computation | async-start | bytes 524288 | tf_op jit(solution)/shard_map/all_to_all | solution.py:176
Sparse Core Ops, SparseCore 0:
  22.3 78.3 all-gather.1

commit v21 on v15

--- a/solution.py
+++ b/solution.py
@@ -37,7 +37,7 @@
     spread = jnp.sum(jnp.sum(dev * dev, axis=2, keepdims=True), axis=1, keepdims=True) / count
     normed = (dev * lax.rsqrt(spread + 1e-05)).reshape(outputs, positions)
     v = normed * gain_ref[...] + shift_ref[...]
-    act = (v / (1.0 + jnp.exp(-v))).astype(out_ref.dtype)
+    act = (v * (0.5 + 0.5 * jnp.tanh(0.5 * v))).astype(out_ref.dtype)
     chips, _, span = out_ref.shape
     for chip in range(chips):
         out_ref[chip] = act[:, chip * span:(chip + 1) * span]

time: 151 us -> 151 us (level)
  no operation moved by 1% of the time
where the time goes in v21:
time: 151 us; the launch traced here: 150 us
  starting transfers between devices  79.4 us (53%)
  waiting for transfers between devices  29.3 us (19%)
  Pallas kernels  15.9 us (11%)
  between operations  13.7 us (9%)
  blocking collectives  6.66 us (4%)
  local copies, waits for them, and re-layouts  4.07 us (3%)
    ppermute x8, starting transfers between devices, ring_gather(): ahead = lax.ppermute(ahead, axis, step_up)  45.9 us
    ppermute x7, starting transfers between devices, ring_gather(): behind = lax.ppermute(behind, axis, step_down)  13.4 us
    ppermute x1, starting transfers between devices, body(): packed_other = lax.ppermute(packed_z, 'core', [(0, 1), (1, 0)])  10.5 us
    all_to_all x1, starting transfers between devices, body(): lax.all_to_all(activated, 'z', split_axis=0, concat_axis=0, tiled=True)  9.74 us
    all_to_all x1, waiting for transfers between devices, body(): lax.all_to_all(activated, 'z', split_axis=0, concat_axis=0, tiled=True)  9.21 us
    ppermute x7, waiting for transfers between devices, ring_gather(): behind = lax.ppermute(behind, axis, step_down)  8.94 us
    all_gather x1, blocking collectives, body(): both = lax.all_gather(chip_rows, 'core', axis=0, tiled=True)  6.66 us
    pallas_call x1, Pallas kernels, conv_norm(): pl.pallas_call(functools.partial(conv_norm_kernel, height=height, width_c...  6.38 us
  transfers between devices with their start and end apart: 18, of which 9 were waited for; matrix products, arithmetic and copies ran while one was open for 2% of the time, Pallas kernels for 7%

profile of v21, /device:TPU:1, one launch (start us, length us, event | category | flops | bytes accessed | tf_op | source)
XLA Modules:
  0.0 149.8 jit_solution(1429436938971953341)
XLA Ops:
  6.5 0.7 copy.15
  7.3 1.0 reshape.31
  8.3 12.0 %collective-permute-start = (bf16[16,4224]{1,0:T(8,128)(2,1)S(1)}, bf16[16,4224]{1,0:T(8,128)(2,1)S(1)}, u32[]{:S(2)}, u32[]{:S(2)}) collective-permute-start(bf16[16,4224]{1,0:T(8,128)(2,1)S(1)} %fusion.1), channel_id=1, source_target_pairs={{0,30},{2,0},{4,2},{6,4},{8,6},{10,8},{12,10},{14,12},{16,14},{18,... | collective-permute-start | bytes 405512 | tf_op jit(solution)/shard_map/ppermute | solution.py:151
  20.2 1.9 %collective-permute-start.8 = (bf16[16,4224]{1,0:T(8,128)(2,1)S(1)}, bf16[16,4224]{1,0:T(8,128)(2,1)S(1)}, u32[]{:S(2)}, u32[]{:S(2)}) collective-permute-start(bf16[16,4224]{1,0:T(8,128)(2,1)S(1)} %fusion.1), channel_id=1, source_target_pairs={{0,2},{2,4},{4,6},{6,8},{8,10},{10,12},{12,14},{14,16},{16,18},{18... | collective-permute-start | bytes 405512 | tf_op jit(solution)/shard_map/ppermute | solution.py:154
  22.2 0.0 all-gather.2.cloned.1.call-update
  22.2 0.0 copy-start.1
  22.2 0.0 copy-start.2
  22.2 0.0 copy-start.3
  22.3 0.2 collective-permute-done
  22.5 5.3 %collective-permute-start.1 = (bf16[16,4224]{1,0:T(8,128)(2,1)S(1)}, bf16[16,4224]{1,0:T(8,128)(2,1)S(1)}, u32[]{:S(2)}, u32[]{:S(2)}) collective-permute-start(bf16[16,4224]{1,0:T(8,128)(2,1)S(1)} %collective-permute-done), channel_id=1, source_target_pairs={{0,30},{2,0},{4,2},{6,4},{8,6},{10,8},{12,10},{14,12},{16,14},{18,... | collective-permute-start | bytes 405512 | tf_op jit(solution)/shard_map/ppermute | solution.py:151
  27.8 0.0 collective-permute-done.8
  27.8 1.9 %collective-permute-start.9 = (bf16[16,4224]{1,0:T(8,128)(2,1)S(1)}, bf16[16,4224]{1,0:T(8,128)(2,1)S(1)}, u32[]{:S(2)}, u32[]{:S(2)}) collective-permute-start(bf16[16,4224]{1,0:T(8,128)(2,1)S(1)} %collective-permute-done.8), channel_id=1, source_target_pairs={{0,2},{2,4},{4,6},{6,8},{8,10},{10,12},{12,14},{14,16},{16,18},{18... | collective-permute-start | bytes 405512 | tf_op jit(solution)/shard_map/ppermute | solution.py:154
  29.7 0.0 collective-permute-done.1
  29.8 5.0 %collective-permute-start.2 = (bf16[16,4224]{1,0:T(8,128)(2,1)S(1)}, bf16[16,4224]{1,0:T(8,128)(2,1)S(1)}, u32[]{:S(2)}, u32[]{:S(2)}) collective-permute-start(bf16[16,4224]{1,0:T(8,128)(2,1)S(1)} %collective-permute-done.1), channel_id=1, source_target_pairs={{0,30},{2,0},{4,2},{6,4},{8,6},{10,8},{12,10},{14,12},{16,14},{18,... | collective-permute-start | bytes 405512 | tf_op jit(solution)/shard_map/ppermute | solution.py:151
  34.7 0.0 collective-permute-done.9
  34.8 1.9 %collective-permute-start.10 = (bf16[16,4224]{1,0:T(8,128)(2,1)S(1)}, bf16[16,4224]{1,0:T(8,128)(2,1)S(1)}, u32[]{:S(2)}, u32[]{:S(2)}) collective-permute-start(bf16[16,4224]{1,0:T(8,128)(2,1)S(1)} %collective-permute-done.9), channel_id=1, source_target_pairs={{0,2},{2,4},{4,6},{6,8},{8,10},{10,12},{12,14},{14,16},{16,18},{18... | collective-permute-start | bytes 405512 | tf_op jit(solution)/shard_map/ppermute | solution.py:154
  36.7 0.8 collective-permute-done.2
  37.5 5.0 %collective-permute-start.3 = (bf16[16,4224]{1,0:T(8,128)(2,1)S(1)}, bf16[16,4224]{1,0:T(8,128)(2,1)S(1)}, u32[]{:S(2)}, u32[]{:S(2)}) collective-permute-start(bf16[16,4224]{1,0:T(8,128)(2,1)S(1)} %collective-permute-done.2), channel_id=1, source_target_pairs={{0,30},{2,0},{4,2},{6,4},{8,6},{10,8},{12,10},{14,12},{16,14},{18,... | collective-permute-start | bytes 405512 | tf_op jit(solution)/shard_map/ppermute | solution.py:151
  42.5 2.3 %collective-permute-done.10 = bf16[16,4224]{1,0:T(8,128)(2,1)S(1)} collective-permute-done((bf16[16,4224]{1,0:T(8,128)(2,1)S(1)}, bf16[16,4224]{1,0:T(8,128)(2,1)S(1)}, u32[]{:S(2)}, u32[]{:S(2)}) %collective-permute-start.10) | collective-permute-done | bytes 135200 | tf_op jit(solution)/shard_map/ppermute | solution.py:154
  44.8 1.9 %collective-permute-start.11 = (bf16[16,4224]{1,0:T(8,128)(2,1)S(1)}, bf16[16,4224]{1,0:T(8,128)(2,1)S(1)}, u32[]{:S(2)}, u32[]{:S(2)}) collective-permute-start(bf16[16,4224]{1,0:T(8,128)(2,1)S(1)} %collective-permute-done.10), channel_id=1, source_target_pairs={{0,2},{2,4},{4,6},{6,8},{8,10},{10,12},{12,14},{14,16},{16,18},{18... | collective-permute-start | bytes 405512 | tf_op jit(solution)/shard_map/ppermute | solution.py:154
  46.8 0.0 collective-permute-done.3
  46.8 4.9 %collective-permute-start.4 = (bf16[16,4224]{1,0:T(8,128)(2,1)S(1)}, bf16[16,4224]{1,0:T(8,128)(2,1)S(1)}, u32[]{:S(2)}, u32[]{:S(2)}) collective-permute-start(bf16[16,4224]{1,0:T(8,128)(2,1)S(1)} %collective-permute-done.3), channel_id=1, source_target_pairs={{0,30},{2,0},{4,2},{6,4},{8,6},{10,8},{12,10},{14,12},{16,14},{18,... | collective-permute-start | bytes 405512 | tf_op jit(solution)/shard_map/ppermute | solution.py:151
  51.7 2.3 %collective-permute-done.11 = bf16[16,4224]{1,0:T(8,128)(2,1)S(1)} collective-permute-done((bf16[16,4224]{1,0:T(8,128)(2,1)S(1)}, bf16[16,4224]{1,0:T(8,128)(2,1)S(1)}, u32[]{:S(2)}, u32[]{:S(2)}) %collective-permute-start.11) | collective-permute-done | bytes 135200 | tf_op jit(solution)/shard_map/ppermute | solution.py:154
  54.0 1.9 %collective-permute-start.12 = (bf16[16,4224]{1,0:T(8,128)(2,1)S(1)}, bf16[16,4224]{1,0:T(8,128)(2,1)S(1)}, u32[]{:S(2)}, u32[]{:S(2)}) collective-permute-start(bf16[16,4224]{1,0:T(8,128)(2,1)S(1)} %collective-permute-done.11), channel_id=1, source_target_pairs={{0,2},{2,4},{4,6},{6,8},{8,10},{10,12},{12,14},{14,16},{16,18},{18... | collective-permute-start | bytes 405512 | tf_op jit(solution)/shard_map/ppermute | solution.py:154
  55.9 0.0 collective-permute-done.4
  55.9 4.6 %collective-permute-start.5 = (bf16[16,4224]{1,0:T(8,128)(2,1)S(1)}, bf16[16,4224]{1,0:T(8,128)(2,1)S(1)}, u32[]{:S(2)}, u32[]{:S(2)}) collective-permute-start(bf16[16,4224]{1,0:T(8,128)(2,1)S(1)} %collective-permute-done.4), channel_id=1, source_target_pairs={{0,30},{2,0},{4,2},{6,4},{8,6},{10,8},{12,10},{14,12},{16,14},{18,... | collective-permute-start | bytes 405512 | tf_op jit(solution)/shard_map/ppermute | solution.py:151
  60.5 2.0 %collective-permute-done.12 = bf16[16,4224]{1,0:T(8,128)(2,1)S(1)} collective-permute-done((bf16[16,4224]{1,0:T(8,128)(2,1)S(1)}, bf16[16,4224]{1,0:T(8,128)(2,1)S(1)}, u32[]{:S(2)}, u32[]{:S(2)}) %collective-permute-start.12) | collective-permute-done | bytes 135200 | tf_op jit(solution)/shard_map/ppermute | solution.py:154
  62.5 1.9 %collective-permute-start.13 = (bf16[16,4224]{1,0:T(8,128)(2,1)S(1)}, bf16[16,4224]{1,0:T(8,128)(2,1)S(1)}, u32[]{:S(2)}, u32[]{:S(2)}) collective-permute-start(bf16[16,4224]{1,0:T(8,128)(2,1)S(1)} %collective-permute-done.12), channel_id=1, source_target_pairs={{0,2},{2,4},{4,6},{6,8},{8,10},{10,12},{12,14},{14,16},{16,18},{18... | collective-permute-start | bytes 405512 | tf_op jit(solution)/shard_map/ppermute | solution.py:154
  64.5 0.0 collective-permute-done.5
  64.5 4.6 %collective-permute-start.6 = (bf16[16,4224]{1,0:T(8,128)(2,1)S(1)}, bf16[16,4224]{1,0:T(8,128)(2,1)S(1)}, u32[]{:S(2)}, u32[]{:S(2)}) collective-permute-start(bf16[16,4224]{1,0:T(8,128)(2,1)S(1)} %collective-permute-done.5), channel_id=1, source_target_pairs={{0,30},{2,0},{4,2},{6,4},{8,6},{10,8},{12,10},{14,12},{16,14},{18,... | collective-permute-start | bytes 405512 | tf_op jit(solution)/shard_map/ppermute | solution.py:151
  69.1 2.3 %collective-permute-done.13 = bf16[16,4224]{1,0:T(8,128)(2,1)S(1)} collective-permute-done((bf16[16,4224]{1,0:T(8,128)(2,1)S(1)}, bf16[16,4224]{1,0:T(8,128)(2,1)S(1)}, u32[]{:S(2)}, u32[]{:S(2)}) %collective-permute-start.13) | collective-permute-done | bytes 135200 | tf_op jit(solution)/shard_map/ppermute | solution.py:154
  71.3 1.9 %collective-permute-start.14 = (bf16[16,4224]{1,0:T(8,128)(2,1)S(1)}, bf16[16,4224]{1,0:T(8,128)(2,1)S(1)}, u32[]{:S(2)}, u32[]{:S(2)}) collective-permute-start(bf16[16,4224]{1,0:T(8,128)(2,1)S(1)} %collective-permute-done.13), channel_id=1, source_target_pairs={{0,2},{2,4},{4,6},{6,8},{8,10},{10,12},{12,14},{14,16},{16,18},{18... | collective-permute-start | bytes 405512 | tf_op jit(solution)/shard_map/ppermute | solution.py:154
  73.2 0.0 collective-permute-done.6
  73.3 4.6 %collective-permute-start.7 = (bf16[16,4224]{1,0:T(8,128)(2,1)S(1)}, bf16[16,4224]{1,0:T(8,128)(2,1)S(1)}, u32[]{:S(2)}, u32[]{:S(2)}) collective-permute-start(bf16[16,4224]{1,0:T(8,128)(2,1)S(1)} %collective-permute-done.6), channel_id=1, source_target_pairs={{0,30},{2,0},{4,2},{6,4},{8,6},{10,8},{12,10},{14,12},{16,14},{18,... | collective-permute-start | bytes 405512 | tf_op jit(solution)/shard_map/ppermute | solution.py:151
  77.9 4.9 %collective-permute-done.7 = bf16[16,4224]{1,0:T(8,128)(2,1)S(1)} collective-permute-done((bf16[16,4224]{1,0:T(8,128)(2,1)S(1)}, bf16[16,4224]{1,0:T(8,128)(2,1)S(1)}, u32[]{:S(2)}, u32[]{:S(2)}) %collective-permute-start.7) | collective-permute-done | bytes 135200 | tf_op jit(solution)/shard_map/ppermute | solution.py:151
  82.8 0.0 collective-permute-done.14
  83.0 10.5 %collective-permute-start.15 = (bf16[16,16,4224]{2,1,0:T(8,128)(2,1)S(1)}, bf16[16,16,4224]{2,1,0:T(8,128)(2,1)}, u32[]{:S(2)}, u32[]{:S(2)}) collective-permute-start(bf16[16,16,4224]{2,1,0:T(8,128)(2,1)S(1)} %bitcast_dynamic-update-slice_fusion.own_ref), channel_id=1, source_target_pairs={{0,1},{1,0},{2,3},{3,2},{4,5},{5,4},{6,7},{7,6},{8,9},{9,8},{10,11... | collective-permute-start | bytes 6488072 | tf_op jit(solution)/shard_map/ppermute | solution.py:171
  93.4 0.7 copy.12.bias_ref
  94.1 0.7 copy.13.gain_ref
  94.8 0.7 copy.14.shift_ref
  95.5 5.2 %all-gather.2.cloned.1.call-done = bf16[64,48,1024]{2,1,0:T(8,128)(2,1)} async-done(((bf16[2,48,1024]{2,1,0:T(8,128)(2,1)}), bf16[64,48,1024]{2,1,0:T(8,128)(2,1)}) %all-gather.2.cloned.1.call-update) | async-done | bytes 6291472 | tf_op jit(solution)/shard_map/all_gather | solution.py:166
  100.7 6.4 %shard_map.73 = bf16[16,32,192]{2,1,0:T(8,128)(2,1)} custom-call(bf16[3072,1024]{1,0:T(8,128)(2,1)} %bitcast.45, bf16[288,1024]{1,0:T(8,128)(2,1)} %bitcast.47, f32[32,1]{1,0:T(8,128)} %copy.12.bias_ref, f32[32,1]{1,0:T(8,128)} %copy.13.gain_ref, f32[32,1]{1,0:T(8,128)} %copy.14.shift_ref), custom_call_target="tpu_custom_call" | custom-call | flops 1811939328 | bytes 7077888 | tf_op jit(solution)/shard_map/pallas_call | solution.py:53
  107.1 9.7 %all-to-all-start = ((bf16[16,32,192]{2,1,0:T(8,128)(2,1)}), bf16[16,32,192]{2,1,0:T(8,128)(2,1)S(1)}, u32[]{:S(2)}, u32[]{:S(2)}) async-start(bf16[16,32,192]{2,1,0:T(8,128)(2,1)} %shard_map.73), calls=%async_computation | async-start | bytes 524288 | tf_op jit(solution)/shard_map/all_to_all | solution.py:176
  116.8 0.7 pad_add_fusion.index_ref
  117.5 4.6 %shard_map.74.wnat_ref = bf16[512,4224]{1,0:T(8,128)(2,1)} custom-call(s32[2]{0:T(128)} %pad_add_fusion.index_ref, bf16[16,16,4224]{2,1,0:T(8,128)(2,1)} %copy-done, bf16[16,16,4224]{2,1,0:T(8,128)(2,1)} %collective-permute-done.15.other_ref), custom_call_target="tpu_custom_call" | custom-call | bytes 8650752 | tf_op jit(solution)/shard_map/pallas_call | solution.py:81
  122.0 9.2 %all-to-all-done = bf16[16,32,192]{2,1,0:T(8,128)(2,1)S(1)} async-done(((bf16[16,32,192]{2,1,0:T(8,128)(2,1)}), bf16[16,32,192]{2,1,0:T(8,128)(2,1)S(1)}, u32[]{:S(2)}, u32[]{:S(2)}) %all-to-all-start) | async-done | bytes 196640 | tf_op jit(solution)/shard_map/all_to_all | solution.py:176
  131.2 6.7 %all_gather.7.act_ref = bf16[1024,192]{1,0:T(8,128)(2,1)} all-gather(bf16[512,192]{1,0:T(8,128)(2,1)S(1)} %bitcast.46), channel_id=1, replica_groups=mesh['grp'=16,'z'=16,'core'=2] {'core'}, dimensions={0}, use_global_device_ids=true | all-gather | bytes 589824 | tf_op jit(solution)/shard_map/all_gather | solution.py:178
  137.9 5.0 %shard_map.75 = bf16[4,96,512]{2,1,0:T(8,128)(2,1)} custom-call(s32[2]{0:T(128)} %pad_add_fusion.index_ref, bf16[1024,192]{1,0:T(8,128)(2,1)} %all_gather.7.act_ref, bf16[512,4224]{1,0:T(8,128)(2,1)} %shard_map.74.wnat_ref), custom_call_target="tpu_custom_call" | custom-call | flops 805306368 | bytes 5111808 | tf_op jit(solution)/shard_map/pallas_call | solution.py:132
  (24 shorter events, 0.3 us)
Async XLA Ops:
  6.5 94.1 %all-gather.2.cloned.1.call-start = ((), (), s32[]{:S(2)}) async-start(), calls=%async_computation.1 | async-start | bytes 6488064 | tf_op jit(solution)/shard_map/all_gather | solution.py:166
  8.3 14.2 %collective-permute-start = (bf16[16,4224]{1,0:T(8,128)(2,1)S(1)}, bf16[16,4224]{1,0:T(8,128)(2,1)S(1)}, u32[]{:S(2)}, u32[]{:S(2)}) collective-permute-start(bf16[16,4224]{1,0:T(8,128)(2,1)S(1)} %fusion.1), channel_id=1, source_target_pairs={{0,30},{2,0},{4,2},{6,4},{8,6},{10,8},{12,10},{14,12},{16,14},{18,... | collective-permute-start | bytes 405512 | tf_op jit(solution)/shard_map/ppermute | solution.py:151
  20.2 7.5 %collective-permute-start.8 = (bf16[16,4224]{1,0:T(8,128)(2,1)S(1)}, bf16[16,4224]{1,0:T(8,128)(2,1)S(1)}, u32[]{:S(2)}, u32[]{:S(2)}) collective-permute-start(bf16[16,4224]{1,0:T(8,128)(2,1)S(1)} %fusion.1), channel_id=1, source_target_pairs={{0,2},{2,4},{4,6},{6,8},{8,10},{10,12},{12,14},{14,16},{16,18},{18... | collective-permute-start | bytes 405512 | tf_op jit(solution)/shard_map/ppermute | solution.py:154
  22.2 71.2 %copy-start.1 = (f32[32]{0:T(128)S(1)}, f32[32]{0:T(128)}, u32[]{:S(2)}) copy-start(f32[32]{0:T(128)} %param.9) | copy-start | bytes 388
  22.2 71.9 %copy-start.2 = (f32[32]{0:T(128)S(1)}, f32[32]{0:T(128)}, u32[]{:S(2)}) copy-start(f32[32]{0:T(128)} %param.10) | copy-start | bytes 388
  22.2 72.6 %copy-start.3 = (f32[32]{0:T(128)S(1)}, f32[32]{0:T(128)}, u32[]{:S(2)}) copy-start(f32[32]{0:T(128)} %param.11) | copy-start | bytes 388
  22.5 7.3 %collective-permute-start.1 = (bf16[16,4224]{1,0:T(8,128)(2,1)S(1)}, bf16[16,4224]{1,0:T(8,128)(2,1)S(1)}, u32[]{:S(2)}, u32[]{:S(2)}) collective-permute-start(bf16[16,4224]{1,0:T(8,128)(2,1)S(1)} %collective-permute-done), channel_id=1, source_target_pairs={{0,30},{2,0},{4,2},{6,4},{8,6},{10,8},{12,10},{14,12},{16,14},{18,... | collective-permute-start | bytes 405512 | tf_op jit(solution)/shard_map/ppermute | solution.py:151
  27.8 7.0 %collective-permute-start.9 = (bf16[16,4224]{1,0:T(8,128)(2,1)S(1)}, bf16[16,4224]{1,0:T(8,128)(2,1)S(1)}, u32[]{:S(2)}, u32[]{:S(2)}) collective-permute-start(bf16[16,4224]{1,0:T(8,128)(2,1)S(1)} %collective-permute-done.8), channel_id=1, source_target_pairs={{0,2},{2,4},{4,6},{6,8},{8,10},{10,12},{12,14},{14,16},{16,18},{18... | collective-permute-start | bytes 405512 | tf_op jit(solution)/shard_map/ppermute | solution.py:154
  29.8 7.7 %collective-permute-start.2 = (bf16[16,4224]{1,0:T(8,128)(2,1)S(1)}, bf16[16,4224]{1,0:T(8,128)(2,1)S(1)}, u32[]{:S(2)}, u32[]{:S(2)}) collective-permute-start(bf16[16,4224]{1,0:T(8,128)(2,1)S(1)} %collective-permute-done.1), channel_id=1, source_target_pairs={{0,30},{2,0},{4,2},{6,4},{8,6},{10,8},{12,10},{14,12},{16,14},{18,... | collective-permute-start | bytes 405512 | tf_op jit(solution)/shard_map/ppermute | solution.py:151
  34.8 10.1 %collective-permute-start.10 = (bf16[16,4224]{1,0:T(8,128)(2,1)S(1)}, bf16[16,4224]{1,0:T(8,128)(2,1)S(1)}, u32[]{:S(2)}, u32[]{:S(2)}) collective-permute-start(bf16[16,4224]{1,0:T(8,128)(2,1)S(1)} %collective-permute-done.9), channel_id=1, source_target_pairs={{0,2},{2,4},{4,6},{6,8},{8,10},{10,12},{12,14},{14,16},{16,18},{18... | collective-permute-start | bytes 405512 | tf_op jit(solution)/shard_map/ppermute | solution.py:154
  37.5 9.3 %collective-permute-start.3 = (bf16[16,4224]{1,0:T(8,128)(2,1)S(1)}, bf16[16,4224]{1,0:T(8,128)(2,1)S(1)}, u32[]{:S(2)}, u32[]{:S(2)}) collective-permute-start(bf16[16,4224]{1,0:T(8,128)(2,1)S(1)} %collective-permute-done.2), channel_id=1, source_target_pairs={{0,30},{2,0},{4,2},{6,4},{8,6},{10,8},{12,10},{14,12},{16,14},{18,... | collective-permute-start | bytes 405512 | tf_op jit(solution)/shard_map/ppermute | solution.py:151
  44.8 9.2 %collective-permute-start.11 = (bf16[16,4224]{1,0:T(8,128)(2,1)S(1)}, bf16[16,4224]{1,0:T(8,128)(2,1)S(1)}, u32[]{:S(2)}, u32[]{:S(2)}) collective-permute-start(bf16[16,4224]{1,0:T(8,128)(2,1)S(1)} %collective-permute-done.10), channel_id=1, source_target_pairs={{0,2},{2,4},{4,6},{6,8},{8,10},{10,12},{12,14},{14,16},{16,18},{18... | collective-permute-start | bytes 405512 | tf_op jit(solution)/shard_map/ppermute | solution.py:154
  46.8 9.1 %collective-permute-start.4 = (bf16[16,4224]{1,0:T(8,128)(2,1)S(1)}, bf16[16,4224]{1,0:T(8,128)(2,1)S(1)}, u32[]{:S(2)}, u32[]{:S(2)}) collective-permute-start(bf16[16,4224]{1,0:T(8,128)(2,1)S(1)} %collective-permute-done.3), channel_id=1, source_target_pairs={{0,30},{2,0},{4,2},{6,4},{8,6},{10,8},{12,10},{14,12},{16,14},{18,... | collective-permute-start | bytes 405512 | tf_op jit(solution)/shard_map/ppermute | solution.py:151
  54.0 8.5 %collective-permute-start.12 = (bf16[16,4224]{1,0:T(8,128)(2,1)S(1)}, bf16[16,4224]{1,0:T(8,128)(2,1)S(1)}, u32[]{:S(2)}, u32[]{:S(2)}) collective-permute-start(bf16[16,4224]{1,0:T(8,128)(2,1)S(1)} %collective-permute-done.11), channel_id=1, source_target_pairs={{0,2},{2,4},{4,6},{6,8},{8,10},{10,12},{12,14},{14,16},{16,18},{18... | collective-permute-start | bytes 405512 | tf_op jit(solution)/shard_map/ppermute | solution.py:154
  55.9 8.5 %collective-permute-start.5 = (bf16[16,4224]{1,0:T(8,128)(2,1)S(1)}, bf16[16,4224]{1,0:T(8,128)(2,1)S(1)}, u32[]{:S(2)}, u32[]{:S(2)}) collective-permute-start(bf16[16,4224]{1,0:T(8,128)(2,1)S(1)} %collective-permute-done.4), channel_id=1, source_target_pairs={{0,30},{2,0},{4,2},{6,4},{8,6},{10,8},{12,10},{14,12},{16,14},{18,... | collective-permute-start | bytes 405512 | tf_op jit(solution)/shard_map/ppermute | solution.py:151
  62.5 8.8 %collective-permute-start.13 = (bf16[16,4224]{1,0:T(8,128)(2,1)S(1)}, bf16[16,4224]{1,0:T(8,128)(2,1)S(1)}, u32[]{:S(2)}, u32[]{:S(2)}) collective-permute-start(bf16[16,4224]{1,0:T(8,128)(2,1)S(1)} %collective-permute-done.12), channel_id=1, source_target_pairs={{0,2},{2,4},{4,6},{6,8},{8,10},{10,12},{12,14},{14,16},{16,18},{18... | collective-permute-start | bytes 405512 | tf_op jit(solution)/shard_map/ppermute | solution.py:154
  64.5 8.8 %collective-permute-start.6 = (bf16[16,4224]{1,0:T(8,128)(2,1)S(1)}, bf16[16,4224]{1,0:T(8,128)(2,1)S(1)}, u32[]{:S(2)}, u32[]{:S(2)}) collective-permute-start(bf16[16,4224]{1,0:T(8,128)(2,1)S(1)} %collective-permute-done.5), channel_id=1, source_target_pairs={{0,30},{2,0},{4,2},{6,4},{8,6},{10,8},{12,10},{14,12},{16,14},{18,... | collective-permute-start | bytes 405512 | tf_op jit(solution)/shard_map/ppermute | solution.py:151
  71.3 11.5 %collective-permute-start.14 = (bf16[16,4224]{1,0:T(8,128)(2,1)S(1)}, bf16[16,4224]{1,0:T(8,128)(2,1)S(1)}, u32[]{:S(2)}, u32[]{:S(2)}) collective-permute-start(bf16[16,4224]{1,0:T(8,128)(2,1)S(1)} %collective-permute-done.13), channel_id=1, source_target_pairs={{0,2},{2,4},{4,6},{6,8},{8,10},{10,12},{12,14},{14,16},{16,18},{18... | collective-permute-start | bytes 405512 | tf_op jit(solution)/shard_map/ppermute | solution.py:154
  73.3 9.5 %collective-permute-start.7 = (bf16[16,4224]{1,0:T(8,128)(2,1)S(1)}, bf16[16,4224]{1,0:T(8,128)(2,1)S(1)}, u32[]{:S(2)}, u32[]{:S(2)}) collective-permute-start(bf16[16,4224]{1,0:T(8,128)(2,1)S(1)} %collective-permute-done.6), channel_id=1, source_target_pairs={{0,30},{2,0},{4,2},{6,4},{8,6},{10,8},{12,10},{14,12},{16,14},{18,... | collective-permute-start | bytes 405512 | tf_op jit(solution)/shard_map/ppermute | solution.py:151
  82.9 24.1 %copy-start = (bf16[16,16,4224]{2,1,0:T(8,128)(2,1)}, bf16[16,16,4224]{2,1,0:T(8,128)(2,1)S(1)}, u32[]{:S(2)}) copy-start(bf16[16,16,4224]{2,1,0:T(8,128)(2,1)S(1)} %bitcast_dynamic-update-slice_fusion.own_ref) | copy-start | bytes 6488068
  83.0 34.5 %collective-permute-start.15 = (bf16[16,16,4224]{2,1,0:T(8,128)(2,1)S(1)}, bf16[16,16,4224]{2,1,0:T(8,128)(2,1)}, u32[]{:S(2)}, u32[]{:S(2)}) collective-permute-start(bf16[16,16,4224]{2,1,0:T(8,128)(2,1)S(1)} %bitcast_dynamic-update-slice_fusion.own_ref), channel_id=1, source_target_pairs={{0,1},{1,0},{2,3},{3,2},{4,5},{5,4},{6,7},{7,6},{8,9},{9,8},{10,11... | collective-permute-start | bytes 6488072 | tf_op jit(solution)/shard_map/ppermute | solution.py:171
  107.1 24.2 %all-to-all-start = ((bf16[16,32,192]{2,1,0:T(8,128)(2,1)}), bf16[16,32,192]{2,1,0:T(8,128)(2,1)S(1)}, u32[]{:S(2)}, u32[]{:S(2)}) async-start(bf16[16,32,192]{2,1,0:T(8,128)(2,1)} %shard_map.73), calls=%async_computation | async-start | bytes 524288 | tf_op jit(solution)/shard_map/all_to_all | solution.py:176
Sparse Core Ops, SparseCore 0:
  22.3 78.3 all-gather.1
